TPU v7x, 512 devices: a whole 4x8x8 slice. The times are simulated.
512 devices in a mesh: space: 32 (over z, y_lo), chan: 16 (over x, y_hi, core).
Axes of the slice: x: 4, y: 8 (y_hi: 2, y_lo: 4; y = y_hi * 4 + y_lo), z: 8, core: 2. Of those that a mesh axis runs over, the one named last changes fastest.
Arguments:
- frames: bfloat16 [4, 48, 320, 512], P(None, None, 'space', 'chan'), may hold values from -120 to 120
- cache: bfloat16 [2, 48, 320, 512], P(None, None, 'space', 'chan'), may hold values from -6 to 6
- gamma: float32 [512], P('chan'), may hold values from 0.5 to 2
- beta: float32 [512], P('chan'), may hold values from -3 to 3
- kernel: bfloat16 [3, 3, 3, 512, 512], P(None, None, None, 'chan'), may hold values from -0.0546875 to 0.0546875
- bias: float32 [512], P('chan'), may hold values from -3 to 3
Outputs:
- output: bfloat16 [4, 48, 320, 512], P(None, None, 'space', 'chan')
All inputs are finite; a program needn't handle non-finite values.
Results may differ from a plain program's by a relative error of at most 0.004.
Values may be sent and summed in bfloat16 or wider, within the bound.
A program may use at most 192 MiB of HBM per device.

v0:
```python
import jax
import jax.numpy as jnp
from jax import lax
from jax.sharding import PartitionSpec as P

CH = 512
GROUPS = 32


epsilon = 1e-06


def extended(value, sides, width):
    for axis, dim in sides:
        peers, length = (lax.axis_size(axis), value.shape[dim])
        up = [(i, (i + 1) % peers) for i in range(peers - 1)]
        down = [(j, i) for i, j in up]
        last = lax.slice_in_dim(value, length - width, length, axis=dim)
        first = lax.slice_in_dim(value, 0, width, axis=dim)
        before = lax.ppermute(last, axis, up)
        after = lax.ppermute(first, axis, down)
        value = jnp.concatenate([before, value, after], axis=dim)
    return value


def unfold_taps(source, row_count, col_count):
    return jnp.concatenate(
        [
            source[:, row_tap : row_tap + row_count, col_tap : col_tap + col_count, :]
            for row_tap in range(3)
            for col_tap in range(3)
        ],
        axis=3,
    )


def local(frames, cache, gamma, beta, kernel, bias):
    nframes, row_count, col_count, local_ch = frames.shape
    group_size = CH // GROUPS
    local_groups = local_ch // group_size
    full_width = col_count * lax.axis_size("space")
    members = float(nframes * row_count * full_width * group_size)
    values = frames.astype(jnp.float32).reshape(
        nframes, row_count, col_count, local_groups, group_size
    )
    first_moment = lax.psum(jnp.sum(values, axis=(0, 1, 2, 4)), "space")
    group_mean = first_moment / members
    centred = values - group_mean[:, None]
    spread = lax.psum(jnp.sum(centred * centred, axis=(0, 1, 2, 4)), "space")
    group_var = spread / members
    scaled = centred * lax.rsqrt(group_var + epsilon)[:, None]
    normed = scaled.reshape(nframes, row_count, col_count, local_ch) * gamma + beta
    active = jax.nn.silu(normed).astype(jnp.bfloat16)
    joined = jnp.concatenate([cache, active], axis=0)
    bordered = extended(joined, (("space", 2),), 1)
    bordered = jnp.pad(bordered, ((0, 0), (1, 1), (0, 0), (0, 0)))
    cell_count = nframes * row_count * col_count
    columns_in = unfold_taps(bordered, row_count, col_count)
    tap_width = columns_in.shape[3]
    flat_kernel = kernel.reshape(3, tap_width, kernel.shape[4])
    running = jnp.zeros((bias.shape[0] * lax.axis_size("chan"), cell_count), jnp.float32)
    for depth in range(3):
        tap_weight = flat_kernel[depth]
        window = columns_in[depth : depth + nframes].reshape(cell_count, tap_width)
        running = running + lax.dot_general(
            tap_weight, window, (((0,), (1,)), ((), ())), preferred_element_type=jnp.float32
        )
    summed = lax.psum_scatter(running, "chan", scatter_dimension=0, tiled=True)
    result = summed.T + bias
    return result.astype(jnp.bfloat16).reshape(nframes, row_count, col_count, -1)


def solution(mesh):
    placed = (
        P(None, None, "space", "chan"),
        P(None, None, "space", "chan"),
        P("chan"),
        P("chan"),
        P(None, None, None, "chan", None),
        P("chan"),
    )
    return jax.shard_map(
        local, mesh=mesh, in_specs=placed, out_specs=P(None, None, "space", "chan"), check_vma=False
    )
```

profile of v0, /device:TPU:6, one launch (start us, length us, event | category | flops | bytes accessed | tf_op | source)
XLA Modules:
  0.0 339.7 jit_solution(13974662160841745628)
XLA Ops:
  6.5 1.2 convert_reduce_fusion
  7.9 86.8 %psum.14 = f32[2]{0:T(128)S(1)} all-reduce(f32[2]{0:T(128)S(1)} %reduce_sum.25), channel_id=1, replica_groups=mesh['space'=32,'chan'=16] {'space'}, use_global_device_ids=true, to_apply=%region_2.0 | all-reduce | flops 2 | bytes 16 | tf_op jit(solution)/shard_map/psum | solution.py:46
  94.9 1.3 fusion.3
  96.4 74.8 %psum.15 = f32[2]{0:T(128)S(1)} all-reduce(f32[2]{0:T(128)S(1)} %reduce_sum.37), channel_id=1, replica_groups=mesh['space'=32,'chan'=16] {'space'}, use_global_device_ids=true, to_apply=%region_5.6 | all-reduce | flops 2 | bytes 16 | tf_op jit(solution)/shard_map/psum | solution.py:49
  171.3 1.3 fusion.11
  172.6 0.8 fusion.19
  173.4 3.9 %collective-permute-start = (bf16[6,48,1,32]{1,3,2,0:T(8,128)(2,1)S(1)}, bf16[6,48,1,32]{1,3,2,0:T(8,128)(2,1)S(1)}, u32[]{:S(2)}, u32[]{:S(2)}) collective-permute-start(bf16[6,48,1,32]{1,3,2,0:T(8,128)(2,1)S(1)} %get-tuple-element.11), channel_id=1, source_target_pairs={{0,16},{16,32},{32,48},{48,64},{64,80},{80,96},{96,112},{112,128},... | collective-permute-start | bytes 55304 | tf_op jit(solution)/shard_map/ppermute | solution.py:20
  177.3 1.3 collective-permute-start.1
  178.6 1.9 fusion.22
  180.5 2.7 collective-permute-done.1
  183.3 1.3 select_maximum_fusion
  184.8 0.1 fusion.18
  184.9 0.1 fusion.15
  185.0 0.1 fusion.17
  185.2 0.3 slice_dynamic-update-slice_fusion.2
  185.4 0.3 slice_dynamic-update-slice_fusion.1
  185.7 0.3 slice_dynamic-update-slice_fusion
  186.0 2.9 fusion.21
  188.9 5.2 %copy.12 = bf16[4,48,10,288]{3,2,1,0:T(8,128)(2,1)} copy(bf16[4,48,10,288]{1,3,2,0:T(8,128)(2,1)} %get-tuple-element.7) | data formatting | bytes 2211840 | tf_op jit(solution)/shard_map/slice | solution.py:64
  194.1 4.0 %reshape.31 = bf16[1920,288]{1,0:T(8,128)(2,1)} reshape(bf16[4,48,10,288]{3,2,1,0:T(8,128)(2,1)} %copy.12) | data formatting | bytes 2211840 | tf_op jit(solution)/shard_map/reshape | solution.py:64
  198.1 5.2 %copy.13 = bf16[4,48,10,288]{3,2,1,0:T(8,128)(2,1)} copy(bf16[4,48,10,288]{1,3,2,0:T(8,128)(2,1)} %get-tuple-element.6) | data formatting | bytes 2211840 | tf_op jit(solution)/shard_map/slice | solution.py:64
  203.2 3.9 %reshape.32 = bf16[1920,288]{1,0:T(8,128)(2,1)} reshape(bf16[4,48,10,288]{3,2,1,0:T(8,128)(2,1)} %copy.13) | data formatting | bytes 2211840 | tf_op jit(solution)/shard_map/reshape | solution.py:64
  207.2 3.6 %copy.14 = bf16[4,48,10,288]{3,2,1,0:T(8,128)(2,1)} copy(bf16[4,48,10,288]{1,3,2,0:T(8,128)(2,1)S(1)} %get-tuple-element.5) | data formatting | bytes 2211840 | tf_op jit(solution)/shard_map/slice | solution.py:64
  210.8 3.0 reshape.33
  213.8 2.2 fusion.23
  216.1 1.2 fusion.24
  217.3 3.2 add_bitcast_fusion
  220.5 5.5 %copy.16 = f32[512,1920]{1,0:T(8,128)} copy(f32[512,1920]{0,1:T(8,128)} %add_bitcast_fusion) | data formatting | bytes 7864320
  226.1 104.1 %reduce-scatter.4.cloned.1.call-done = f32[32,1920]{1,0:T(8,128)} async-done(((f32[512,1920]{1,0:T(8,128)}), f32[32,1920]{1,0:T(8,128)}) %reduce-scatter.4.cloned.1.call-update) | async-done | bytes 245776
  330.1 1.3 copy.17
  331.5 0.2 reshape.34
  331.7 1.2 copy.15
  (25 shorter events, 1.0 us)
Async XLA Ops:
  6.5 178.2 %copy-start.2 = (bf16[2,48,10,32]{1,3,2,0:T(8,128)(2,1)S(1)}, bf16[2,48,10,32]{1,3,2,0:T(8,128)(2,1)}, u32[]{:S(2)}) copy-start(bf16[2,48,10,32]{1,3,2,0:T(8,128)(2,1)} %param.7) | copy-start | bytes 184324
  6.5 323.6 %reduce-scatter.4.cloned.1.call-start = ((), (), s32[]{:S(2)}) async-start(), calls=%async_computation.1 | async-start | bytes 4177920
  173.4 7.1 %collective-permute-start = (bf16[6,48,1,32]{1,3,2,0:T(8,128)(2,1)S(1)}, bf16[6,48,1,32]{1,3,2,0:T(8,128)(2,1)S(1)}, u32[]{:S(2)}, u32[]{:S(2)}) collective-permute-start(bf16[6,48,1,32]{1,3,2,0:T(8,128)(2,1)S(1)} %get-tuple-element.11), channel_id=1, source_target_pairs={{0,16},{16,32},{32,48},{48,64},{64,80},{80,96},{96,112},{112,128},... | collective-permute-start | bytes 55304 | tf_op jit(solution)/shard_map/ppermute | solution.py:20
  177.3 6.0 %collective-permute-start.1 = (bf16[6,48,1,32]{1,3,2,0:T(8,128)(2,1)S(1)}, bf16[6,48,1,32]{1,3,2,0:T(8,128)(2,1)S(1)}, u32[]{:S(2)}, u32[]{:S(2)}) collective-permute-start(bf16[6,48,1,32]{1,3,2,0:T(8,128)(2,1)S(1)} %get-tuple-element.12), channel_id=1, source_target_pairs={{16,0},{32,16},{48,32},{64,48},{80,64},{96,80},{112,96},{128,112},... | collective-permute-start | bytes 55304 | tf_op jit(solution)/shard_map/ppermute | solution.py:21
  210.8 3.0 copy-start
  213.8 2.3 copy-start.1
  226.0 105.4 %copy-start.3 = (f32[32]{0:T(128)S(1)}, f32[32]{0:T(128)}, u32[]{:S(2)}) copy-start(f32[32]{0:T(128)} %param.11) | copy-start | bytes 388
Sparse Core Ops, SparseCore 0:
  226.2 103.9 reduce-scatter.3
where the time goes:
time: 342 us; the launch traced here: 340 us
  blocking collectives  162 us (47%)
  waiting for transfers between devices  107 us (31%)
  local copies, waits for them, and re-layouts  39.4 us (12%)
  between operations  13.6 us (4%)
  matrix products  6.67 us (2%)
  other arithmetic  6.52 us (2%)
  starting transfers between devices  5.17 us (2%)
    unnamed x2, waiting for transfers between devices  104 us
    psum x1, blocking collectives, local(): first_moment = lax.psum(jnp.sum(values, axis=(0, 1, 2, 4)), 'space')  86.8 us
    psum x1, blocking collectives, local(): spread = lax.psum(jnp.sum(centred * centred, axis=(0, 1, 2, 4)), 'space')  74.8 us
    slice x4, local copies, waits for them, and re-layouts, local(): window = columns_in[depth:depth + nframes].reshape(cell_count, tap_width)  16.9 us
    reshape x3, local copies, waits for them, and re-layouts, local(): window = columns_in[depth:depth + nframes].reshape(cell_count, tap_width)  10.9 us
    unnamed x15, local copies, waits for them, and re-layouts  7.5 us
  transfers between devices with their start and end apart: 3, of which 2 were waited for; matrix products, arithmetic and copies ran while one was open for 1% of the time, Pallas kernels for 0%

commit v1 on v0

v1 whole, which is shorter than its diff:
```python
import functools

import jax
import jax.numpy as jnp
from jax import lax
from jax.experimental import pallas as pl
from jax.experimental.pallas import tpu as pltpu
from jax.sharding import PartitionSpec as P

CH = 512
GROUPS = 32
MESH = pl.DeviceIdType.MESH

epsilon = 1e-06


def gather_kernel(n, x_ref, o_ref, buf, send_sem, recv_sem):
    me = lax.axis_index("space")
    ch = lax.axis_index("chan")
    barrier = pltpu.get_barrier_semaphore()

    def signal(k, carry):
        peer = lax.rem(me + k, n)
        pl.semaphore_signal(barrier, 1, device_id=(peer, ch), device_id_type=MESH)
        return carry

    lax.fori_loop(1, n, signal, 0)
    pl.semaphore_wait(barrier, n - 1)

    def copy_to(peer):
        return pltpu.make_async_remote_copy(
            src_ref=x_ref,
            dst_ref=buf.at[me],
            send_sem=send_sem.at[peer],
            recv_sem=recv_sem.at[me],
            device_id=(peer, ch),
            device_id_type=MESH,
        )

    def copy_from(peer):
        return pltpu.make_async_remote_copy(
            src_ref=x_ref,
            dst_ref=buf.at[peer],
            send_sem=send_sem.at[peer],
            recv_sem=recv_sem.at[peer],
            device_id=(peer, ch),
            device_id_type=MESH,
        )

    def start(k, carry):
        copy_to(lax.rem(me + k, n)).start()
        return carry

    lax.fori_loop(1, n, start, 0)

    def finish(k, carry):
        peer = lax.rem(me + k, n)
        copy_to(peer).wait_send()
        copy_from(peer).wait_recv()
        return carry

    lax.fori_loop(1, n, finish, 0)
    buf[me] = x_ref[...]
    o_ref[...] = buf[...]


def gather_space(tile):
    n = lax.axis_size("space")
    return pl.pallas_call(
        functools.partial(gather_kernel, n),
        out_shape=jax.ShapeDtypeStruct((n,) + tile.shape, tile.dtype),
        in_specs=[pl.BlockSpec(memory_space=pltpu.VMEM)],
        out_specs=pl.BlockSpec(memory_space=pltpu.VMEM),
        scratch_shapes=[
            pltpu.VMEM((n,) + tile.shape, tile.dtype),
            pltpu.SemaphoreType.DMA((n,)),
            pltpu.SemaphoreType.DMA((n,)),
        ],
        compiler_params=pltpu.CompilerParams(collective_id=0, has_side_effects=True),
    )(tile)


def edge_exchange(edges_last, edges_first, axis):
    peers = lax.axis_size(axis)
    up = [(i, (i + 1) % peers) for i in range(peers - 1)]
    down = [(j, i) for i, j in up]
    before = lax.ppermute(edges_last, axis, up)
    after = lax.ppermute(edges_first, axis, down)
    return before, after


def unfold_taps(source, row_count, col_count):
    return jnp.concatenate(
        [
            source[:, row_tap : row_tap + row_count, col_tap : col_tap + col_count, :]
            for row_tap in range(3)
            for col_tap in range(3)
        ],
        axis=3,
    )


def local(frames, cache, gamma, beta, kernel, bias):
    nframes, row_count, col_count, local_ch = frames.shape
    ncache = cache.shape[0]
    group_size = CH // GROUPS
    local_groups = local_ch // group_size
    nspace = lax.axis_size("space")
    me = lax.axis_index("space")
    local_members = float(nframes * row_count * col_count * group_size)

    raw = jnp.concatenate([cache, frames], axis=0)
    before, after = edge_exchange(raw[:, :, col_count - 1 :], raw[:, :, :1], "space")

    values = frames.astype(jnp.float32).reshape(
        nframes, row_count, col_count, local_groups, group_size
    )
    local_mean = jnp.sum(values, axis=(0, 1, 2, 4)) / local_members
    local_dev = values - local_mean[:, None]
    local_m2 = jnp.sum(local_dev * local_dev, axis=(0, 1, 2, 4))
    tile = jnp.zeros((8, 128), jnp.float32)
    tile = tile.at[0, :local_groups].set(local_mean).at[1, :local_groups].set(local_m2)
    gathered = gather_space(tile)
    means = gathered[:, 0, :local_groups]
    m2s = gathered[:, 1, :local_groups]
    group_mean = jnp.mean(means, axis=0)
    spread = jnp.sum(m2s, axis=0) + local_members * jnp.sum(
        (means - group_mean) ** 2, axis=0
    )
    group_var = spread / (local_members * nspace)
    inv = lax.rsqrt(group_var + epsilon)

    def activate(x):
        shape = x.shape
        v = x.astype(jnp.float32).reshape(shape[:-1] + (local_groups, group_size))
        scaled = (v - group_mean[:, None]) * inv[:, None]
        normed = scaled.reshape(shape) * gamma + beta
        return jax.nn.silu(normed).astype(jnp.bfloat16)

    active = activate(frames)
    joined = jnp.concatenate([cache, active], axis=0)
    left = jnp.concatenate([before[:ncache], activate(before[ncache:])], axis=0)
    right = jnp.concatenate([after[:ncache], activate(after[ncache:])], axis=0)
    left = jnp.where(me == 0, jnp.zeros_like(left), left)
    right = jnp.where(me == nspace - 1, jnp.zeros_like(right), right)
    bordered = jnp.concatenate([left, joined, right], axis=2)
    bordered = jnp.pad(bordered, ((0, 0), (1, 1), (0, 0), (0, 0)))
    cell_count = nframes * row_count * col_count
    columns_in = unfold_taps(bordered, row_count, col_count)
    tap_width = columns_in.shape[3]
    flat_kernel = kernel.reshape(3, tap_width, kernel.shape[4])
    running = jnp.zeros((bias.shape[0] * lax.axis_size("chan"), cell_count), jnp.float32)
    for depth in range(3):
        tap_weight = flat_kernel[depth]
        window = columns_in[depth : depth + nframes].reshape(cell_count, tap_width)
        running = running + lax.dot_general(
            tap_weight, window, (((0,), (1,)), ((), ())), preferred_element_type=jnp.float32
        )
    summed = lax.psum_scatter(running, "chan", scatter_dimension=0, tiled=True)
    result = summed.T + bias
    return result.astype(jnp.bfloat16).reshape(nframes, row_count, col_count, -1)


def solution(mesh):
    placed = (
        P(None, None, "space", "chan"),
        P(None, None, "space", "chan"),
        P("chan"),
        P("chan"),
        P(None, None, None, "chan", None),
        P("chan"),
    )
    return jax.shard_map(
        local, mesh=mesh, in_specs=placed, out_specs=P(None, None, "space", "chan"), check_vma=False
    )
```

time: 342 us -> 206 us (0.60)
  blocking collectives: 162 us -> 0 us
  Pallas kernels: 0 us -> 23.7 us
    psum x2 -> x0, blocking collectives: 162 us -> none  [the longest x1 86.8 us: local(): first_moment = lax.psum(jnp.sum(values, axis=(0, 1, 2, 4)), 'space')]
    pallas_call x0 -> x1, Pallas kernels: none -> 23.7 us  [gather_space(): pl.pallas_call(functools.partial(gather_kernel, n), out_shape=jax.ShapeDt...]
    unnamed x15 -> x24, local copies, waits for them, and re-layouts: 7.5 us -> 9.07 us
  transfers between devices with their start and end apart: 3 -> 3, of which waited for: 2 -> 1; matrix products, arithmetic and copies ran while one was open for 1% -> 4% of each run, Pallas kernels for 0% -> 12%
where the time goes in v1:
time: 206 us; the launch traced here: 204 us
  waiting for transfers between devices  106 us (51%)
  local copies, waits for them, and re-layouts  42.4 us (21%)
  Pallas kernels  23.7 us (12%)
  between operations  13.7 us (7%)
  matrix products  6.69 us (3%)
  other arithmetic  5.87 us (3%)
  starting transfers between devices  4.81 us (2%)
    unnamed x2, waiting for transfers between devices  106 us
    pallas_call x1, Pallas kernels, gather_space(): pl.pallas_call(functools.partial(gather_kernel, n), out_shape=jax.ShapeDt...  23.7 us
    slice x4, local copies, waits for them, and re-layouts, local(): window = columns_in[depth:depth + nframes].reshape(cell_count, tap_width)  16.9 us
    reshape x3, local copies, waits for them, and re-layouts, local(): window = columns_in[depth:depth + nframes].reshape(cell_count, tap_width)  10.9 us
    unnamed x24, local copies, waits for them, and re-layouts  9.07 us
    dot_general x3, matrix products, local(): lax.dot_general(tap_weight, window, (((0,), (1,)), ((), ())), preferred_e...  6.69 us
  transfers between devices with their start and end apart: 3, of which 1 were waited for; matrix products, arithmetic and copies ran while one was open for 4% of the time, Pallas kernels for 12%

profile of v1, /device:TPU:6, one launch (start us, length us, event | category | flops | bytes accessed | tf_op | source)
XLA Modules:
  0.0 203.5 jit_solution(8005842480078148758)
XLA Ops:
  6.6 1.0 constant_dynamic-update-slice_fusion.1
  7.6 1.0 constant_dynamic-update-slice_fusion
  8.6 3.5 %collective-permute-start = (bf16[6,48,1,32]{1,3,2,0:T(8,128)(2,1)S(1)}, bf16[6,48,1,32]{1,3,2,0:T(8,128)(2,1)S(1)}, u32[]{:S(2)}, u32[]{:S(2)}) collective-permute-start(bf16[6,48,1,32]{1,3,2,0:T(8,128)(2,1)S(1)} %get-tuple-element.37), channel_id=1, source_target_pairs={{0,16},{16,32},{32,48},{48,64},{64,80},{80,96},{96,112},{112,128},... | collective-permute-start | bytes 55304 | tf_op jit(solution)/shard_map/ppermute | solution.py:87
  12.1 1.3 collective-permute-start.1
  13.4 1.2 convert_reduce_fusion
  14.9 1.3 fusion.2
  16.4 0.2 scatter.9.x_ref
  16.6 0.6 copy-done.4
  17.2 23.7 %shard_map.64 = f32[32,8,128]{2,1,0:T(8,128)} custom-call(f32[8,128]{1,0:T(8,128)} %copy-done.4), custom_call_target="tpu_custom_call" | custom-call | tf_op jit(solution)/shard_map/pallas_call | solution.py:69
  40.9 1.0 slice_reduce_fusion.1
  42.0 0.2 fusion.19
  42.5 1.9 fusion.22
  44.4 1.0 fusion.11
  45.7 0.4 select_maximum_fusion
  46.7 0.3 slice_dynamic-update-slice_fusion.2
  46.9 0.3 slice_dynamic-update-slice_fusion.1
  47.2 0.3 slice_dynamic-update-slice_fusion
  47.5 2.9 %fusion.21 = (bf16[4,48,10,288]{1,3,2,0:T(8,128)(2,1)S(1)}, bf16[4,48,10,288]{1,3,2,0:T(8,128)(2,1)}, bf16[4,48,10,288]{1,3,2,0:T(8,128)(2,1)}) fusion(bf16[6,48,10,288]{1,3,2,0:T(8,128)(2,1)S(1)} %slice_dynamic-update-slice_fusion), kind=kLoop, calls=%fused_computation.53 | loop fusion | bytes 6635520 | tf_op jit(solution)/shard_map/slice | solution.py:155
  50.4 5.2 %copy.15 = bf16[4,48,10,288]{3,2,1,0:T(8,128)(2,1)} copy(bf16[4,48,10,288]{1,3,2,0:T(8,128)(2,1)} %get-tuple-element.33) | data formatting | bytes 2211840 | tf_op jit(solution)/shard_map/slice | solution.py:155
  55.6 4.0 %reshape.208 = bf16[1920,288]{1,0:T(8,128)(2,1)} reshape(bf16[4,48,10,288]{3,2,1,0:T(8,128)(2,1)} %copy.15) | data formatting | bytes 2211840 | tf_op jit(solution)/shard_map/reshape | solution.py:155
  59.6 5.2 %copy.16 = bf16[4,48,10,288]{3,2,1,0:T(8,128)(2,1)} copy(bf16[4,48,10,288]{1,3,2,0:T(8,128)(2,1)} %get-tuple-element.32) | data formatting | bytes 2211840 | tf_op jit(solution)/shard_map/slice | solution.py:155
  64.7 3.9 %reshape.209 = bf16[1920,288]{1,0:T(8,128)(2,1)} reshape(bf16[4,48,10,288]{3,2,1,0:T(8,128)(2,1)} %copy.16) | data formatting | bytes 2211840 | tf_op jit(solution)/shard_map/reshape | solution.py:155
  68.7 3.6 %copy.17 = bf16[4,48,10,288]{3,2,1,0:T(8,128)(2,1)} copy(bf16[4,48,10,288]{1,3,2,0:T(8,128)(2,1)S(1)} %get-tuple-element.31) | data formatting | bytes 2211840 | tf_op jit(solution)/shard_map/slice | solution.py:155
  72.3 3.0 %reshape.210 = bf16[1920,288]{1,0:T(8,128)(2,1)S(1)} reshape(bf16[4,48,10,288]{3,2,1,0:T(8,128)(2,1)} %copy.17) | data formatting | bytes 2211840 | tf_op jit(solution)/shard_map/reshape | solution.py:155
  75.3 2.3 %fusion.24 = f32[1920,512]{1,0:T(8,128)S(1)} fusion(bf16[1920,288]{1,0:T(8,128)(2,1)S(1)} %copy-done, bf16[288,512]{1,0:T(8,128)(2,1)} %bitcast.25), kind=kOutput, calls=%fused_computation.56 | convolution fusion | flops 566231040 | bytes 5332992 | tf_op jit(solution)/shard_map/dot_general | solution.py:156
  77.6 1.2 fusion.25
  78.8 3.3 %add_bitcast_fusion = f32[512,1920]{0,1:T(8,128)} fusion(f32[1920,512]{1,0:T(8,128)S(1)} %fusion.24, f32[1920,512]{1,0:T(8,128)S(1)} %fusion.25, bf16[1920,288]{1,0:T(8,128)(2,1)S(1)} %reshape.210, bf16[288,512]{1,0:T(8,128)(2,1)S(1)} %bitcast.23), kind=kOutput, calls=%fused_computation | convolution fusion | flops 568197120 | bytes 13197312 | tf_op jit(solution)/shard_map/dot_general | solution.py:156
  82.0 5.5 %copy.19 = f32[512,1920]{1,0:T(8,128)} copy(f32[512,1920]{0,1:T(8,128)} %add_bitcast_fusion) | data formatting | bytes 7864320
  87.6 106.4 %reduce-scatter.4.cloned.1.call-done = f32[32,1920]{1,0:T(8,128)} async-done(((f32[512,1920]{1,0:T(8,128)}), f32[32,1920]{1,0:T(8,128)}) %reduce-scatter.4.cloned.1.call-update) | async-done | bytes 245776
  193.9 1.3 copy.20
  195.3 0.2 reshape.211
  195.5 1.2 copy.18
  (46 shorter events, 1.9 us)
Async XLA Ops:
  6.5 39.1 %copy-start.3 = (bf16[2,48,10,32]{1,3,2,0:T(8,128)(2,1)S(1)}, bf16[2,48,10,32]{1,3,2,0:T(8,128)(2,1)}, u32[]{:S(2)}) copy-start(bf16[2,48,10,32]{1,3,2,0:T(8,128)(2,1)} %param.11) | copy-start | bytes 184324
  6.5 37.9 %copy-start.2 = (bf16[4,48,10,32]{1,3,2,0:T(8,128)(2,1)S(1)}, bf16[4,48,10,32]{1,3,2,0:T(8,128)(2,1)}, u32[]{:S(2)}) copy-start(bf16[4,48,10,32]{1,3,2,0:T(8,128)(2,1)} %param.10) | copy-start | bytes 368644
  6.5 38.9 %copy-start.6 = (f32[32]{0:T(128)S(1)}, f32[32]{0:T(128)}, u32[]{:S(2)}) copy-start(f32[32]{0:T(128)} %param.12) | copy-start | bytes 388
  6.5 38.9 %copy-start.5 = (f32[32]{0:T(128)S(1)}, f32[32]{0:T(128)}, u32[]{:S(2)}) copy-start(f32[32]{0:T(128)} %param.13) | copy-start | bytes 388
  6.5 187.4 %reduce-scatter.4.cloned.1.call-start = ((), (), s32[]{:S(2)}) async-start(), calls=%async_computation.1 | async-start | bytes 4177920
  8.6 36.8 %collective-permute-start = (bf16[6,48,1,32]{1,3,2,0:T(8,128)(2,1)S(1)}, bf16[6,48,1,32]{1,3,2,0:T(8,128)(2,1)S(1)}, u32[]{:S(2)}, u32[]{:S(2)}) collective-permute-start(bf16[6,48,1,32]{1,3,2,0:T(8,128)(2,1)S(1)} %get-tuple-element.37), channel_id=1, source_target_pairs={{0,16},{16,32},{32,48},{48,64},{64,80},{80,96},{96,112},{112,128},... | collective-permute-start | bytes 55304 | tf_op jit(solution)/shard_map/ppermute | solution.py:87
  12.1 33.4 %collective-permute-start.1 = (bf16[6,48,1,32]{1,3,2,0:T(8,128)(2,1)S(1)}, bf16[6,48,1,32]{1,3,2,0:T(8,128)(2,1)S(1)}, u32[]{:S(2)}, u32[]{:S(2)}) collective-permute-start(bf16[6,48,1,32]{1,3,2,0:T(8,128)(2,1)S(1)} %get-tuple-element.38), channel_id=1, source_target_pairs={{16,0},{32,16},{48,32},{64,48},{80,64},{96,80},{112,96},{128,112},... | collective-permute-start | bytes 55304 | tf_op jit(solution)/shard_map/ppermute | solution.py:88
  16.6 0.6 copy-start.4
  72.3 3.0 %copy-start = (bf16[1920,288]{1,0:T(8,128)(2,1)S(1)}, bf16[1920,288]{1,0:T(8,128)(2,1)}, u32[]{:S(2)}) copy-start(bf16[1920,288]{1,0:T(8,128)(2,1)} %reshape.208) | copy-start | bytes 3317764
  75.3 2.3 %copy-start.1 = (bf16[1920,288]{1,0:T(8,128)(2,1)S(1)}, bf16[1920,288]{1,0:T(8,128)(2,1)}, u32[]{:S(2)}) copy-start(bf16[1920,288]{1,0:T(8,128)(2,1)} %reshape.209) | copy-start | bytes 3317764
  87.5 107.7 %copy-start.7 = (f32[32]{0:T(128)S(1)}, f32[32]{0:T(128)}, u32[]{:S(2)}) copy-start(f32[32]{0:T(128)} %param.15) | copy-start | bytes 388
Sparse Core Ops, SparseCore 0:
  87.7 106.1 reduce-scatter.3

commit v2 on v1

--- a/solution.py
+++ b/solution.py
@@ -80,6 +80,86 @@
     )(tile)
 
 
+def scatter_kernel(x_ref, o_ref, recv1, acc1, recv2, acc2, recv3, send_sem, recv_sem):
+    sp = lax.axis_index("space")
+    c = lax.axis_index("chan")
+    core = c % 2
+    yh = (c // 2) % 2
+    xx = c // 4
+    nx = x_ref.shape[1]
+
+    def dev(x_, yh_, core_):
+        return (sp, x_ * 4 + yh_ * 2 + core_)
+
+    peers = [dev(xx, yh, 1 - core)]
+    peers += [dev(lax.rem(xx + k, nx), yh, core) for k in range(1, nx)]
+    peers += [dev(xx, 1 - yh, core)]
+    barrier = pltpu.get_barrier_semaphore()
+    for p in peers:
+        pl.semaphore_signal(barrier, 1, device_id=p, device_id_type=MESH)
+    pl.semaphore_wait(barrier, len(peers))
+
+    first = pltpu.make_async_remote_copy(
+        src_ref=x_ref.at[1 - core], dst_ref=recv1, send_sem=send_sem.at[0],
+        recv_sem=recv_sem.at[0], device_id=peers[0], device_id_type=MESH)
+    first.start()
+    first.wait()
+
+    sends = []
+    for k in range(1, nx):
+        dest = lax.rem(xx + k, nx)
+        acc1[dest] = x_ref[core, dest] + recv1[dest]
+        slot = nx - 1 - k
+        cp = pltpu.make_async_remote_copy(
+            src_ref=acc1.at[dest], dst_ref=recv2.at[slot], send_sem=send_sem.at[k],
+            recv_sem=recv_sem.at[1 + slot], device_id=peers[k], device_id_type=MESH)
+        cp.start()
+        sends.append(cp)
+    acc1[xx] = x_ref[core, xx] + recv1[xx]
+    for slot in range(nx - 1):
+        pltpu.make_async_remote_copy(
+            src_ref=acc1.at[xx], dst_ref=recv2.at[slot], send_sem=send_sem.at[1 + slot],
+            recv_sem=recv_sem.at[1 + slot], device_id=peers[0], device_id_type=MESH).wait_recv()
+    other = 1 - yh
+    total = acc1[xx, other]
+    for slot in range(nx - 1):
+        total = total + recv2[slot, other]
+    acc2[other] = total
+    last = pltpu.make_async_remote_copy(
+        src_ref=acc2.at[other], dst_ref=recv3, send_sem=send_sem.at[nx],
+        recv_sem=recv_sem.at[nx], device_id=peers[nx], device_id_type=MESH)
+    last.start()
+    total = acc1[xx, yh]
+    for slot in range(nx - 1):
+        total = total + recv2[slot, yh]
+    for cp in sends:
+        cp.wait_send()
+    last.wait()
+    o_ref[...] = total + recv3[...]
+
+
+def scatter_chan(parts):
+    ncore, nx, nyh, rows, cells = parts.shape
+    f32 = jnp.float32
+    return pl.pallas_call(
+        scatter_kernel,
+        out_shape=jax.ShapeDtypeStruct((rows, cells), f32),
+        in_specs=[pl.BlockSpec(memory_space=pltpu.VMEM)],
+        out_specs=pl.BlockSpec(memory_space=pltpu.VMEM),
+        scratch_shapes=[
+            pltpu.VMEM((nx, nyh, rows, cells), f32),
+            pltpu.VMEM((nx, nyh, rows, cells), f32),
+            pltpu.VMEM((nx - 1, nyh, rows, cells), f32),
+            pltpu.VMEM((nyh, rows, cells), f32),
+            pltpu.VMEM((rows, cells), f32),
+            pltpu.SemaphoreType.DMA((nx + 1,)),
+            pltpu.SemaphoreType.DMA((nx + 1,)),
+        ],
+        compiler_params=pltpu.CompilerParams(
+            collective_id=1, has_side_effects=True, vmem_limit_bytes=48 * 1024 * 1024),
+    )(parts)
+
+
 def edge_exchange(edges_last, edges_first, axis):
     peers = lax.axis_size(axis)
     up = [(i, (i + 1) % peers) for i in range(peers - 1)]
@@ -148,15 +228,19 @@
     cell_count = nframes * row_count * col_count
     columns_in = unfold_taps(bordered, row_count, col_count)
     tap_width = columns_in.shape[3]
-    flat_kernel = kernel.reshape(3, tap_width, kernel.shape[4])
-    running = jnp.zeros((bias.shape[0] * lax.axis_size("chan"), cell_count), jnp.float32)
+    nchan = lax.axis_size("chan")
+    nx = nchan // 4
+    perm_kernel = kernel.reshape(kernel.shape[:4] + (nx, 2, 2, local_ch))
+    perm_kernel = perm_kernel.transpose(0, 1, 2, 3, 6, 4, 5, 7)
+    flat_kernel = perm_kernel.reshape(3, tap_width, kernel.shape[4])
+    running = jnp.zeros((bias.shape[0] * nchan, cell_count), jnp.float32)
     for depth in range(3):
         tap_weight = flat_kernel[depth]
         window = columns_in[depth : depth + nframes].reshape(cell_count, tap_width)
         running = running + lax.dot_general(
             tap_weight, window, (((0,), (1,)), ((), ())), preferred_element_type=jnp.float32
         )
-    summed = lax.psum_scatter(running, "chan", scatter_dimension=0, tiled=True)
+    summed = scatter_chan(running.reshape(2, nx, 2, local_ch, cell_count))
     result = summed.T + bias
     return result.astype(jnp.bfloat16).reshape(nframes, row_count, col_count, -1)
 

time: 206 us -> 145 us (0.70)
  waiting for transfers between devices: 106 us -> 0.01 us
  Pallas kernels: 23.7 us -> 70.9 us
  local copies, waits for them, and re-layouts: 42.4 us -> 57.8 us
  between operations: 13.7 us -> 0.34 us
  matrix products: 6.69 us -> 3.82 us
    unnamed x2 -> x0, waiting for transfers between devices: 106 us -> none
    pallas_call x0 -> x1, Pallas kernels: none -> 47.9 us  [scatter_chan(): pl.pallas_call(scatter_kernel, out_shape=jax.ShapeDtypeStruct((rows, cell...]
    reshape x0 -> x2, local copies, waits for them, and re-layouts: none -> 11.3 us  [local(): perm_kernel = kernel.reshape(kernel.shape[:4] + (nx, 2, 2, local_ch))]
    squeeze x0 -> x3, local copies, waits for them, and re-layouts: none -> 7.07 us  [local(): tap_weight = flat_kernel[depth]]
    unnamed x24 -> x22, local copies, waits for them, and re-layouts: 9.07 us -> 2.34 us
    dot_general x3, matrix products: 6.69 us -> 3.82 us  [local(): lax.dot_general(tap_weight, window, (((0,), (1,)), ((), ())), preferred_e...]
    slice x1, local copies, waits for them, and re-layouts: 1.94 us -> 4.4 us  [local(): tap_weight = flat_kernel[depth]]
  transfers between devices with their start and end apart: 3 -> 2, of which waited for: 1 -> 0; matrix products, arithmetic and copies ran while one was open for 4% -> 20% of each run, Pallas kernels for 12% -> 16%
where the time goes in v2:
time: 145 us; the launch traced here: 144 us
  Pallas kernels  70.9 us (49%)
  local copies, waits for them, and re-layouts  57.8 us (40%)
  other arithmetic  6 us (4%)
  starting transfers between devices  5.37 us (4%)
  matrix products  3.82 us (3%)
    pallas_call x1, Pallas kernels, scatter_chan(): pl.pallas_call(scatter_kernel, out_shape=jax.ShapeDtypeStruct((rows, cell...  47.9 us
    pallas_call x1, Pallas kernels, gather_space(): pl.pallas_call(functools.partial(gather_kernel, n), out_shape=jax.ShapeDt...  23.1 us
    slice x4, local copies, waits for them, and re-layouts, local(): window = columns_in[depth:depth + nframes].reshape(cell_count, tap_width)  16.8 us
    reshape x2, local copies, waits for them, and re-layouts, local(): perm_kernel = kernel.reshape(kernel.shape[:4] + (nx, 2, 2, local_ch))  11.3 us
    reshape x3, local copies, waits for them, and re-layouts, local(): window = columns_in[depth:depth + nframes].reshape(cell_count, tap_width)  9.95 us
    squeeze x3, local copies, waits for them, and re-layouts, local(): tap_weight = flat_kernel[depth]  7.07 us
    slice x1, local copies, waits for them, and re-layouts, local(): tap_weight = flat_kernel[depth]  4.4 us
    ppermute x1, starting transfers between devices, edge_exchange(): before = lax.ppermute(edges_last, axis, up)  4.09 us
  transfers between devices with their start and end apart: 2, of which 0 were waited for; matrix products, arithmetic and copies ran while one was open for 20% of the time, Pallas kernels for 16%

profile of v2, /device:TPU:6, one launch (start us, length us, event | category | flops | bytes accessed | tf_op | source)
XLA Modules:
  0.0 144.2 jit_solution(5185482097668583732)
XLA Ops:
  0.0 0.9 constant_dynamic-update-slice_fusion.1
  0.9 1.0 constant_dynamic-update-slice_fusion
  2.0 0.6 fusion.23
  2.6 4.1 %collective-permute-start = (bf16[6,48,1,32]{1,3,2,0:T(8,128)(2,1)}, bf16[6,48,1,32]{1,3,2,0:T(8,128)(2,1)}, u32[]{:S(2)}, u32[]{:S(2)}) collective-permute-start(bf16[6,48,1,32]{1,3,2,0:T(8,128)(2,1)} %get-tuple-element.37), channel_id=1, source_target_pairs={{0,16},{16,32},{32,48},{48,64},{64,80},{80,96},{96,112},{112,128},... | collective-permute-start | bytes 55304 | tf_op jit(solution)/shard_map/ppermute | solution.py:167
  6.7 1.3 collective-permute-start.1
  8.0 1.2 convert_reduce_fusion
  9.5 1.3 fusion.2
  11.2 0.6 copy-done.4
  11.8 23.1 %shard_map.64 = f32[32,8,128]{2,1,0:T(8,128)} custom-call(f32[8,128]{1,0:T(8,128)} %copy-done.4), custom_call_target="tpu_custom_call" | custom-call | tf_op jit(solution)/shard_map/pallas_call | solution.py:69
  34.8 1.0 slice_reduce_fusion.1
  36.5 7.8 %reshape.215 = bf16[3,3,3,32,4,2,2,32]{7,6,5,4,3,2,1,0:T(2,128)(2,1)S(1)} reshape(bf16[3,3,3,32,512]{4,3,2,1,0:T(8,128)(2,1)} %param.14) | data formatting | bytes 1769472 | tf_op jit(solution)/shard_map/reshape | solution.py:233
  44.3 3.4 %copy.17 = bf16[3,3,3,32,4,2,2,32]{7,5,4,6,3,2,1,0:T(2,128)(2,1)S(1)} copy(bf16[3,3,3,32,4,2,2,32]{7,6,5,4,3,2,1,0:T(2,128)(2,1)S(1)} %reshape.215) | data formatting | bytes 1769472 | tf_op jit(solution)/shard_map/reshape | solution.py:233
  47.8 4.4 %fusion.22 = (bf16[1,3,3,32,2,4,2,32]{7,6,5,4,3,2,1,0:T(2,128)(2,1)}, bf16[1,3,3,32,2,4,2,32]{7,6,5,4,3,2,1,0:T(2,128)(2,1)S(1)}, bf16[1,3,3,32,2,4,2,32]{7,6,5,4,3,2,1,0:T(2,128)(2,1)S(1)}) fusion(bf16[3,3,3,32,2,4,2,32]{7,6,5,4,3,2,1,0:T(2,128)(2,1)S(1)} %bitcast.26), kind=kLoop, calls=%fused_computation.55 | loop fusion | bytes 1769472 | tf_op jit(solution)/shard_map/slice | solution.py:238
  52.5 4.1 %squeeze.16 = bf16[288,512]{1,0:T(8,128)(2,1)S(1)} reshape(bf16[1,3,3,32,2,4,2,32]{7,6,5,4,3,2,1,0:T(2,128)(2,1)} %get-tuple-element.34) | data formatting | bytes 589824 | tf_op jit(solution)/shard_map/squeeze | solution.py:238
  56.6 1.1 squeeze.15
  57.8 1.9 %squeeze.14 = bf16[288,512]{1,0:T(8,128)(2,1)} reshape(bf16[1,3,3,32,2,4,2,32]{7,6,5,4,3,2,1,0:T(2,128)(2,1)S(1)} %get-tuple-element.36) | data formatting | bytes 589824 | tf_op jit(solution)/shard_map/squeeze | solution.py:238
  59.6 0.7 slice.133
  60.3 0.9 multiply_convert_fusion.1
  61.2 0.7 slice.136
  62.0 0.4 select_maximum_fusion
  63.8 2.9 %fusion.21 = (bf16[4,48,10,288]{1,3,2,0:T(8,128)(2,1)}, bf16[4,48,10,288]{1,3,2,0:T(8,128)(2,1)S(1)}, bf16[4,48,10,288]{1,3,2,0:T(8,128)(2,1)}) fusion(bf16[6,48,10,288]{1,3,2,0:T(8,128)(2,1)S(1)} %slice_dynamic-update-slice_fusion), kind=kLoop, calls=%fused_computation.54 | loop fusion | bytes 6635520 | tf_op jit(solution)/shard_map/slice | solution.py:239
  66.7 5.2 %copy.13 = bf16[4,48,10,288]{3,2,1,0:T(8,128)(2,1)} copy(bf16[4,48,10,288]{1,3,2,0:T(8,128)(2,1)} %get-tuple-element.31) | data formatting | bytes 2211840 | tf_op jit(solution)/shard_map/slice | solution.py:239
  71.8 3.9 %reshape.217 = bf16[1920,288]{1,0:T(8,128)(2,1)} reshape(bf16[4,48,10,288]{3,2,1,0:T(8,128)(2,1)} %copy.13) | data formatting | bytes 2211840 | tf_op jit(solution)/shard_map/reshape | solution.py:239
  75.8 3.6 %copy.12 = bf16[4,48,10,288]{3,2,1,0:T(8,128)(2,1)} copy(bf16[4,48,10,288]{1,3,2,0:T(8,128)(2,1)S(1)} %get-tuple-element.32) | data formatting | bytes 2211840 | tf_op jit(solution)/shard_map/slice | solution.py:239
  79.4 2.9 %reshape.216 = bf16[1920,288]{1,0:T(8,128)(2,1)S(1)} reshape(bf16[4,48,10,288]{3,2,1,0:T(8,128)(2,1)} %copy.12) | data formatting | bytes 2211840 | tf_op jit(solution)/shard_map/reshape | solution.py:239
  82.3 5.2 %copy.10 = bf16[4,48,10,288]{3,2,1,0:T(8,128)(2,1)} copy(bf16[4,48,10,288]{1,3,2,0:T(8,128)(2,1)} %get-tuple-element.33) | data formatting | bytes 2211840 | tf_op jit(solution)/shard_map/slice | solution.py:239
  87.5 3.1 %reshape.214 = bf16[1920,288]{1,0:T(8,128)(2,1)S(1)} reshape(bf16[4,48,10,288]{3,2,1,0:T(8,128)(2,1)} %copy.10) | data formatting | bytes 2211840 | tf_op jit(solution)/shard_map/reshape | solution.py:239
  90.6 1.3 fusion.25
  91.9 1.3 fusion.24
  93.3 1.3 add_add_fusion
  94.6 47.9 %shard_map.65 = f32[32,1920]{1,0:T(8,128)S(1)} custom-call(f32[2,4,2,32,1920]{4,3,2,1,0:T(8,128)S(1)} %bitcast.25), custom_call_target="tpu_custom_call" | custom-call | tf_op jit(solution)/shard_map/pallas_call | solution.py:144
  143.0 1.2 copy.15
  (48 shorter events, 3.7 us)
Async XLA Ops:
  2.6 57.0 %collective-permute-start = (bf16[6,48,1,32]{1,3,2,0:T(8,128)(2,1)}, bf16[6,48,1,32]{1,3,2,0:T(8,128)(2,1)}, u32[]{:S(2)}, u32[]{:S(2)}) collective-permute-start(bf16[6,48,1,32]{1,3,2,0:T(8,128)(2,1)} %get-tuple-element.37), channel_id=1, source_target_pairs={{0,16},{16,32},{32,48},{48,64},{64,80},{80,96},{96,112},{112,128},... | collective-permute-start | bytes 55304 | tf_op jit(solution)/shard_map/ppermute | solution.py:167
  6.7 53.7 %collective-permute-start.1 = (bf16[6,48,1,32]{1,3,2,0:T(8,128)(2,1)}, bf16[6,48,1,32]{1,3,2,0:T(8,128)(2,1)}, u32[]{:S(2)}, u32[]{:S(2)}) collective-permute-start(bf16[6,48,1,32]{1,3,2,0:T(8,128)(2,1)} %get-tuple-element.38), channel_id=1, source_target_pairs={{16,0},{32,16},{48,32},{64,48},{80,64},{96,80},{112,96},{128,112},... | collective-permute-start | bytes 55304 | tf_op jit(solution)/shard_map/ppermute | solution.py:168
  11.2 0.6 copy-start.4
  47.7 4.4 %copy-start.1 = (bf16[4,48,10,32]{1,3,2,0:T(8,128)(2,1)S(1)}, bf16[4,48,10,32]{1,3,2,0:T(8,128)(2,1)}, u32[]{:S(2)}) copy-start(bf16[4,48,10,32]{1,3,2,0:T(8,128)(2,1)} %param.10) | copy-start | bytes 368644
  47.8 4.4 %copy-start.5 = (f32[32]{0:T(128)S(1)}, f32[32]{0:T(128)}, u32[]{:S(2)}) copy-start(f32[32]{0:T(128)} %param.13) | copy-start | bytes 388
  47.8 4.4 %copy-start.6 = (f32[32]{0:T(128)S(1)}, f32[32]{0:T(128)}, u32[]{:S(2)}) copy-start(f32[32]{0:T(128)} %param.12) | copy-start | bytes 388
  52.2 9.8 %copy-start.2 = (bf16[2,48,10,32]{1,3,2,0:T(8,128)(2,1)S(1)}, bf16[2,48,10,32]{1,3,2,0:T(8,128)(2,1)}, u32[]{:S(2)}) copy-start(bf16[2,48,10,32]{1,3,2,0:T(8,128)(2,1)} %param.11) | copy-start | bytes 184324
  90.6 1.3 copy-start.3
  91.9 1.4 copy-start
  94.6 47.9 %copy-start.7 = (f32[32]{0:T(128)S(1)}, f32[32]{0:T(128)}, u32[]{:S(2)}) copy-start(f32[32]{0:T(128)} %param.15) | copy-start | bytes 388

commit v3 on v2

--- a/solution.py
+++ b/solution.py
@@ -226,20 +226,19 @@
     bordered = jnp.concatenate([left, joined, right], axis=2)
     bordered = jnp.pad(bordered, ((0, 0), (1, 1), (0, 0), (0, 0)))
     cell_count = nframes * row_count * col_count
-    columns_in = unfold_taps(bordered, row_count, col_count)
-    tap_width = columns_in.shape[3]
     nchan = lax.axis_size("chan")
     nx = nchan // 4
     perm_kernel = kernel.reshape(kernel.shape[:4] + (nx, 2, 2, local_ch))
-    perm_kernel = perm_kernel.transpose(0, 1, 2, 3, 6, 4, 5, 7)
-    flat_kernel = perm_kernel.reshape(3, tap_width, kernel.shape[4])
-    running = jnp.zeros((bias.shape[0] * nchan, cell_count), jnp.float32)
-    for depth in range(3):
-        tap_weight = flat_kernel[depth]
-        window = columns_in[depth : depth + nframes].reshape(cell_count, tap_width)
-        running = running + lax.dot_general(
-            tap_weight, window, (((0,), (1,)), ((), ())), preferred_element_type=jnp.float32
-        )
+    perm_kernel = perm_kernel.transpose(0, 1, 2, 3, 6, 4, 5, 7).reshape(kernel.shape)
+    running = lax.conv_general_dilated(
+        bordered[None],
+        perm_kernel,
+        window_strides=(1, 1, 1),
+        padding="VALID",
+        dimension_numbers=("NDHWC", "DHWIO", "CNDHW"),
+        preferred_element_type=jnp.float32,
+    )
+    running = running.reshape(-1, cell_count)
     summed = scatter_chan(running.reshape(2, nx, 2, local_ch, cell_count))
     result = summed.T + bias
     return result.astype(jnp.bfloat16).reshape(nframes, row_count, col_count, -1)

time: 145 us -> 173 us (1.19)
  matrix products: 3.82 us -> 28.5 us
    another operation x0 -> x2, local copies, waits for them, and re-layouts: none -> 35.6 us  [local(): summed = scatter_chan(running.reshape(2, nx, 2, local_ch, cell_count))]
    conv_general_dilated x0 -> x1, matrix products: none -> 28.5 us  [local(): lax.conv_general_dilated(bordered[None], perm_kernel, window_strides=(1,...]
    slice x5 -> x0, local copies, waits for them, and re-layouts: 21.2 us -> none  [the longest x4 16.8 us: local(): window = columns_in[depth:depth + nframes].reshape(cell_count, tap_width)]
    reshape x2 -> x1, local copies, waits for them, and re-layouts: 11.3 us -> 3.4 us  [local(): perm_kernel = kernel.reshape(kernel.shape[:4] + (nx, 2, 2, local_ch))]
    squeeze x3 -> x0, local copies, waits for them, and re-layouts: 7.07 us -> none  [local(): tap_weight = flat_kernel[depth]]
    reshape x3 -> x1, local copies, waits for them, and re-layouts: 9.95 us -> 4.11 us  [local(): perm_kernel.transpose(0, 1, 2, 3, 6, 4, 5, 7).reshape(kernel.shape)]
    transpose x0 -> x1, local copies, waits for them, and re-layouts: none -> 5.18 us  [local(): perm_kernel.transpose(0, 1, 2, 3, 6, 4, 5, 7).reshape(kernel.shape)]
    dot_general x3 -> x0, matrix products: 3.82 us -> none  [local(): lax.dot_general(tap_weight, window, (((0,), (1,)), ((), ())), preferred_e...]
  transfers between devices with their start and end apart: 2 -> 2, of which waited for: 0 -> 0; matrix products, arithmetic and copies ran while one was open for 20% -> 11% of each run, Pallas kernels for 16% -> 13%
where the time goes in v3:
time: 173 us; the launch traced here: 172 us
  Pallas kernels  70.9 us (41%)
  local copies, waits for them, and re-layouts  59.3 us (34%)
  matrix products  28.5 us (16%)
  other arithmetic  7.41 us (4%)
  starting transfers between devices  5.36 us (3%)
    pallas_call x1, Pallas kernels, scatter_chan(): pl.pallas_call(scatter_kernel, out_shape=jax.ShapeDtypeStruct((rows, cell...  47.9 us
    another operation x2, local copies, waits for them, and re-layouts, local(): summed = scatter_chan(running.reshape(2, nx, 2, local_ch, cell_count))  35.6 us
    conv_general_dilated x1, matrix products, local(): lax.conv_general_dilated(bordered[None], perm_kernel, window_strides=(1,...  28.5 us
    pallas_call x1, Pallas kernels, gather_space(): pl.pallas_call(functools.partial(gather_kernel, n), out_shape=jax.ShapeDt...  23.1 us
    transpose x1, local copies, waits for them, and re-layouts, local(): perm_kernel.transpose(0, 1, 2, 3, 6, 4, 5, 7).reshape(kernel.shape)  5.18 us
    reshape x1, local copies, waits for them, and re-layouts, local(): perm_kernel.transpose(0, 1, 2, 3, 6, 4, 5, 7).reshape(kernel.shape)  4.11 us
    ppermute x1, starting transfers between devices, edge_exchange(): before = lax.ppermute(edges_last, axis, up)  4.08 us
    unnamed x17, local copies, waits for them, and re-layouts  3.75 us
  transfers between devices with their start and end apart: 2, of which 0 were waited for; matrix products, arithmetic and copies ran while one was open for 11% of the time, Pallas kernels for 13%

profile of v3, /device:TPU:6, one launch (start us, length us, event | category | flops | bytes accessed | tf_op | source)
XLA Modules:
  0.0 171.8 jit_solution(6653424055974766498)
XLA Ops:
  0.0 1.0 constant_dynamic-update-slice_fusion.1
  1.0 1.0 constant_dynamic-update-slice_fusion
  2.1 0.6 fusion.20
  2.7 4.1 %collective-permute-start = (bf16[6,48,1,32]{1,3,2,0:T(8,128)(2,1)}, bf16[6,48,1,32]{1,3,2,0:T(8,128)(2,1)}, u32[]{:S(2)}, u32[]{:S(2)}) collective-permute-start(bf16[6,48,1,32]{1,3,2,0:T(8,128)(2,1)} %get-tuple-element.31), channel_id=1, source_target_pairs={{0,16},{16,32},{32,48},{48,64},{64,80},{80,96},{96,112},{112,128},... | collective-permute-start | bytes 55304 | tf_op jit(solution)/shard_map/ppermute | solution.py:167
  6.8 1.3 collective-permute-start.1
  8.1 1.2 convert_reduce_fusion
  9.3 0.1 reduce_sum.61
  9.6 1.3 fusion.2
  11.0 0.1 reduce_sum.64
  11.1 0.2 scatter.9.x_ref
  11.3 0.6 copy-done.4
  11.9 23.1 %shard_map.64 = f32[32,8,128]{2,1,0:T(8,128)} custom-call(f32[8,128]{1,0:T(8,128)} %copy-done.4), custom_call_target="tpu_custom_call" | custom-call | tf_op jit(solution)/shard_map/pallas_call | solution.py:69
  35.0 1.0 slice_reduce_fusion.1
  36.2 0.2 fusion.18
  36.6 1.0 fusion.11
  37.7 3.4 %reshape.198 = bf16[3,3,3,32,4,2,2,32]{7,6,5,4,3,2,1,0:T(2,128)(2,1)} reshape(bf16[3,3,3,32,512]{4,3,2,1,0:T(8,128)(2,1)S(1)} %copy-done.2) | data formatting | bytes 1769472 | tf_op jit(solution)/shard_map/reshape | solution.py:231
  41.1 5.2 %copy.16 = bf16[3,3,3,32,2,4,2,32]{7,6,5,4,3,2,1,0:T(2,128)(2,1)S(1)} copy(bf16[3,3,3,32,2,4,2,32]{7,4,6,5,3,2,1,0:T(2,128)(2,1)} %bitcast.20) | data formatting | bytes 1769472 | tf_op jit(solution)/shard_map/transpose | solution.py:232
  46.2 4.1 %reshape.199 = bf16[3,3,3,32,512]{4,3,2,1,0:T(8,128)(2,1)} reshape(bf16[3,3,3,32,2,4,2,32]{7,6,5,4,3,2,1,0:T(2,128)(2,1)S(1)} %copy.16) | data formatting | bytes 1769472 | tf_op jit(solution)/shard_map/reshape | solution.py:232
  50.4 0.7 slice.68
  51.1 0.9 multiply_convert_fusion.1
  52.0 0.7 slice.71
  52.8 1.5 fusion.12
  54.2 1.6 copy.17
  55.8 28.5 %convolution_reduce_fusion = f32[512,4,48,10]{0,3,2,1:T(8,128)} fusion(bf16[1,6,50,12,32]{4,0,3,2,1:T(2,128)(2,1)S(1)} %copy.17, bf16[3,3,3,32,512]{4,3,2,1,0:T(8,128)(2,1)S(1)} %copy-done.3), kind=kOutput, calls=%fused_computation | convolution fusion | flops 1698693120 | bytes 5047296 | tf_op jit(solution)/shard_map/conv_general_dilated | solution.py:233
  84.3 17.5 %reshape_reshape.3 = f32[2,4,2,32,1920]{3,2,1,0,4:T(2,128)} reshape(f32[512,4,48,10]{0,3,2,1:T(8,128)} %convolution_reduce_fusion) | data formatting | bytes 7864320 | tf_op jit(solution)/shard_map/reshape;reshape | solution.py:242
  101.8 18.2 %copy.18.x_ref = f32[2,4,2,32,1920]{4,3,2,1,0:T(8,128)} copy(f32[2,4,2,32,1920]{3,2,1,0,4:T(2,128)} %reshape_reshape.3) | data formatting | bytes 7864320 | tf_op jit(solution)/shard_map/reshape;reshape | solution.py:242
  120.0 2.1 %copy-done = f32[2,4,2,32,1920]{4,3,2,1,0:T(8,128)S(1)} copy-done((f32[2,4,2,32,1920]{4,3,2,1,0:T(8,128)S(1)}, f32[2,4,2,32,1920]{4,3,2,1,0:T(8,128)}, u32[]{:S(2)}) %copy-start) | copy-done | bytes 3932184
  122.1 47.9 %shard_map.65 = f32[32,1920]{1,0:T(8,128)S(1)} custom-call(f32[2,4,2,32,1920]{4,3,2,1,0:T(8,128)S(1)} %copy-done), custom_call_target="tpu_custom_call" | custom-call | tf_op jit(solution)/shard_map/pallas_call | solution.py:144
  170.0 0.1 fusion.16
  170.1 0.3 copy.19
  170.4 0.2 reshape.200
  170.6 1.2 copy.20
  (30 shorter events, 0.8 us)
Async XLA Ops:
  0.0 36.6 %copy-start.1 = (bf16[4,48,10,32]{1,3,2,0:T(8,128)(2,1)S(1)}, bf16[4,48,10,32]{1,3,2,0:T(8,128)(2,1)}, u32[]{:S(2)}) copy-start(bf16[4,48,10,32]{1,3,2,0:T(8,128)(2,1)} %param.10) | copy-start | bytes 368644
  0.0 36.6 %copy-start.5 = (f32[32]{0:T(128)S(1)}, f32[32]{0:T(128)}, u32[]{:S(2)}) copy-start(f32[32]{0:T(128)} %param.13) | copy-start | bytes 388
  0.0 36.6 %copy-start.6 = (f32[32]{0:T(128)S(1)}, f32[32]{0:T(128)}, u32[]{:S(2)}) copy-start(f32[32]{0:T(128)} %param.12) | copy-start | bytes 388
  0.0 37.6 %copy-start.2 = (bf16[3,3,3,32,512]{4,3,2,1,0:T(8,128)(2,1)S(1)}, bf16[3,3,3,32,512]{4,3,2,1,0:T(8,128)(2,1)}, u32[]{:S(2)}) copy-start(bf16[3,3,3,32,512]{4,3,2,1,0:T(8,128)(2,1)} %param.14) | copy-start | bytes 2654212
  2.7 47.7 %collective-permute-start = (bf16[6,48,1,32]{1,3,2,0:T(8,128)(2,1)}, bf16[6,48,1,32]{1,3,2,0:T(8,128)(2,1)}, u32[]{:S(2)}, u32[]{:S(2)}) collective-permute-start(bf16[6,48,1,32]{1,3,2,0:T(8,128)(2,1)} %get-tuple-element.31), channel_id=1, source_target_pairs={{0,16},{16,32},{32,48},{48,64},{64,80},{80,96},{96,112},{112,128},... | collective-permute-start | bytes 55304 | tf_op jit(solution)/shard_map/ppermute | solution.py:167
  6.8 44.3 %collective-permute-start.1 = (bf16[6,48,1,32]{1,3,2,0:T(8,128)(2,1)}, bf16[6,48,1,32]{1,3,2,0:T(8,128)(2,1)}, u32[]{:S(2)}, u32[]{:S(2)}) collective-permute-start(bf16[6,48,1,32]{1,3,2,0:T(8,128)(2,1)} %get-tuple-element.32), channel_id=1, source_target_pairs={{16,0},{32,16},{48,32},{64,48},{80,64},{96,80},{112,96},{128,112},... | collective-permute-start | bytes 55304 | tf_op jit(solution)/shard_map/ppermute | solution.py:168
  11.3 0.6 copy-start.4
  52.7 3.1 %copy-start.3 = (bf16[3,3,3,32,512]{4,3,2,1,0:T(8,128)(2,1)S(1)}, bf16[3,3,3,32,512]{4,3,2,1,0:T(8,128)(2,1)}, u32[]{:S(2)}) copy-start(bf16[3,3,3,32,512]{4,3,2,1,0:T(8,128)(2,1)} %reshape.199) | copy-start | bytes 2654212
  120.0 2.1 %copy-start = (f32[2,4,2,32,1920]{4,3,2,1,0:T(8,128)S(1)}, f32[2,4,2,32,1920]{4,3,2,1,0:T(8,128)}, u32[]{:S(2)}) copy-start(f32[2,4,2,32,1920]{4,3,2,1,0:T(8,128)} %copy.18.x_ref) | copy-start | bytes 11796484
  122.1 47.9 %copy-start.7 = (f32[32]{0:T(128)S(1)}, f32[32]{0:T(128)}, u32[]{:S(2)}) copy-start(f32[32]{0:T(128)} %param.15) | copy-start | bytes 388

commit v4 on v2

--- a/solution.py
+++ b/solution.py
@@ -86,7 +86,8 @@
     core = c % 2
     yh = (c // 2) % 2
     xx = c // 4
-    nx = x_ref.shape[1]
+    nx, nyh = x_ref.shape[0], x_ref.shape[1]
+    nfirst = nx * nyh
 
     def dev(x_, yh_, core_):
         return (sp, x_ * 4 + yh_ * 2 + core_)
@@ -99,35 +100,46 @@
         pl.semaphore_signal(barrier, 1, device_id=p, device_id_type=MESH)
     pl.semaphore_wait(barrier, len(peers))
 
-    first = pltpu.make_async_remote_copy(
-        src_ref=x_ref.at[1 - core], dst_ref=recv1, send_sem=send_sem.at[0],
-        recv_sem=recv_sem.at[0], device_id=peers[0], device_id_type=MESH)
-    first.start()
-    first.wait()
+    firsts = []
+    for i in range(nx):
+        for j in range(nyh):
+            cp = pltpu.make_async_remote_copy(
+                src_ref=x_ref.at[i, j, 1 - core], dst_ref=recv1.at[i, j],
+                send_sem=send_sem.at[i * nyh + j], recv_sem=recv_sem.at[i * nyh + j],
+                device_id=peers[0], device_id_type=MESH)
+            cp.start()
+            firsts.append(cp)
+    for cp in firsts:
+        cp.wait()
+
+    def fold_first(dest):
+        for j in range(nyh):
+            acc1[dest, j] = x_ref[dest, j, core] + recv1[dest, j]
 
     sends = []
     for k in range(1, nx):
         dest = lax.rem(xx + k, nx)
-        acc1[dest] = x_ref[core, dest] + recv1[dest]
+        fold_first(dest)
         slot = nx - 1 - k
         cp = pltpu.make_async_remote_copy(
-            src_ref=acc1.at[dest], dst_ref=recv2.at[slot], send_sem=send_sem.at[k],
-            recv_sem=recv_sem.at[1 + slot], device_id=peers[k], device_id_type=MESH)
+            src_ref=acc1.at[dest], dst_ref=recv2.at[slot], send_sem=send_sem.at[nfirst + k - 1],
+            recv_sem=recv_sem.at[nfirst + slot], device_id=peers[k], device_id_type=MESH)
         cp.start()
         sends.append(cp)
-    acc1[xx] = x_ref[core, xx] + recv1[xx]
+    fold_first(xx)
     for slot in range(nx - 1):
         pltpu.make_async_remote_copy(
-            src_ref=acc1.at[xx], dst_ref=recv2.at[slot], send_sem=send_sem.at[1 + slot],
-            recv_sem=recv_sem.at[1 + slot], device_id=peers[0], device_id_type=MESH).wait_recv()
+            src_ref=acc1.at[xx], dst_ref=recv2.at[slot], send_sem=send_sem.at[nfirst + slot],
+            recv_sem=recv_sem.at[nfirst + slot], device_id=peers[0], device_id_type=MESH).wait_recv()
     other = 1 - yh
     total = acc1[xx, other]
     for slot in range(nx - 1):
         total = total + recv2[slot, other]
     acc2[other] = total
+    last_sem = nfirst + nx - 1
     last = pltpu.make_async_remote_copy(
-        src_ref=acc2.at[other], dst_ref=recv3, send_sem=send_sem.at[nx],
-        recv_sem=recv_sem.at[nx], device_id=peers[nx], device_id_type=MESH)
+        src_ref=acc2.at[other], dst_ref=recv3, send_sem=send_sem.at[last_sem],
+        recv_sem=recv_sem.at[last_sem], device_id=peers[nx], device_id_type=MESH)
     last.start()
     total = acc1[xx, yh]
     for slot in range(nx - 1):
@@ -139,7 +151,7 @@
 
 
 def scatter_chan(parts):
-    ncore, nx, nyh, rows, cells = parts.shape
+    nx, nyh, ncore, rows, cells = parts.shape
     f32 = jnp.float32
     return pl.pallas_call(
         scatter_kernel,
@@ -152,8 +164,8 @@
             pltpu.VMEM((nx - 1, nyh, rows, cells), f32),
             pltpu.VMEM((nyh, rows, cells), f32),
             pltpu.VMEM((rows, cells), f32),
-            pltpu.SemaphoreType.DMA((nx + 1,)),
-            pltpu.SemaphoreType.DMA((nx + 1,)),
+            pltpu.SemaphoreType.DMA((nx * nyh + nx,)),
+            pltpu.SemaphoreType.DMA((nx * nyh + nx,)),
         ],
         compiler_params=pltpu.CompilerParams(
             collective_id=1, has_side_effects=True, vmem_limit_bytes=48 * 1024 * 1024),
@@ -230,9 +242,7 @@
     tap_width = columns_in.shape[3]
     nchan = lax.axis_size("chan")
     nx = nchan // 4
-    perm_kernel = kernel.reshape(kernel.shape[:4] + (nx, 2, 2, local_ch))
-    perm_kernel = perm_kernel.transpose(0, 1, 2, 3, 6, 4, 5, 7)
-    flat_kernel = perm_kernel.reshape(3, tap_width, kernel.shape[4])
+    flat_kernel = kernel.reshape(3, tap_width, kernel.shape[4])
     running = jnp.zeros((bias.shape[0] * nchan, cell_count), jnp.float32)
     for depth in range(3):
         tap_weight = flat_kernel[depth]
@@ -240,7 +250,7 @@
         running = running + lax.dot_general(
             tap_weight, window, (((0,), (1,)), ((), ())), preferred_element_type=jnp.float32
         )
-    summed = scatter_chan(running.reshape(2, nx, 2, local_ch, cell_count))
+    summed = scatter_chan(running.reshape(nx, 2, 2, local_ch, cell_count))
     result = summed.T + bias
     return result.astype(jnp.bfloat16).reshape(nframes, row_count, col_count, -1)
 

time: 145 us -> 123 us (0.85)
  local copies, waits for them, and re-layouts: 57.8 us -> 34.8 us
    reshape x2 -> x0, local copies, waits for them, and re-layouts: 11.3 us -> none  [local(): perm_kernel = kernel.reshape(kernel.shape[:4] + (nx, 2, 2, local_ch))]
    squeeze x3 -> x0, local copies, waits for them, and re-layouts: 7.07 us -> none  [local(): tap_weight = flat_kernel[depth]]
    slice x1, local copies, waits for them, and re-layouts: 4.4 us -> 1.94 us  [local(): tap_weight = flat_kernel[depth]]
  transfers between devices with their start and end apart: 2 -> 2, of which waited for: 0 -> 0; matrix products, arithmetic and copies ran while one was open for 20% -> 6% of each run, Pallas kernels for 16% -> 19%
where the time goes in v4:
time: 123 us; the launch traced here: 122 us
  Pallas kernels  71.7 us (58%)
  local copies, waits for them, and re-layouts  34.8 us (28%)
  other arithmetic  5.9 us (5%)
  starting transfers between devices  4.77 us (4%)
  matrix products  4.77 us (4%)
    pallas_call x1, Pallas kernels, scatter_chan(): pl.pallas_call(scatter_kernel, out_shape=jax.ShapeDtypeStruct((rows, cell...  48 us
    pallas_call x1, Pallas kernels, gather_space(): pl.pallas_call(functools.partial(gather_kernel, n), out_shape=jax.ShapeDt...  23.7 us
    slice x4, local copies, waits for them, and re-layouts, local(): window = columns_in[depth:depth + nframes].reshape(cell_count, tap_width)  16.8 us
    reshape x3, local copies, waits for them, and re-layouts, local(): window = columns_in[depth:depth + nframes].reshape(cell_count, tap_width)  9.72 us
    dot_general x3, matrix products, local(): lax.dot_general(tap_weight, window, (((0,), (1,)), ((), ())), preferred_e...  4.77 us
    ppermute x1, starting transfers between devices, edge_exchange(): before = lax.ppermute(edges_last, axis, up)  3.48 us
  transfers between devices with their start and end apart: 2, of which 0 were waited for; matrix products, arithmetic and copies ran while one was open for 6% of the time, Pallas kernels for 19%

profile of v4, /device:TPU:6, one launch (start us, length us, event | category | flops | bytes accessed | tf_op | source)
XLA Modules:
  0.0 122.2 jit_solution(10051927434226414271)
XLA Ops:
  0.0 1.0 constant_dynamic-update-slice_fusion.1
  1.0 1.0 constant_dynamic-update-slice_fusion
  2.0 3.5 %collective-permute-start = (bf16[6,48,1,32]{1,3,2,0:T(8,128)(2,1)S(1)}, bf16[6,48,1,32]{1,3,2,0:T(8,128)(2,1)S(1)}, u32[]{:S(2)}, u32[]{:S(2)}) collective-permute-start(bf16[6,48,1,32]{1,3,2,0:T(8,128)(2,1)S(1)} %get-tuple-element.37), channel_id=1, source_target_pairs={{0,16},{16,32},{32,48},{48,64},{64,80},{80,96},{96,112},{112,128},... | collective-permute-start | bytes 55304 | tf_op jit(solution)/shard_map/ppermute | solution.py:179
  5.5 1.3 %collective-permute-start.1 = (bf16[6,48,1,32]{1,3,2,0:T(8,128)(2,1)S(1)}, bf16[6,48,1,32]{1,3,2,0:T(8,128)(2,1)S(1)}, u32[]{:S(2)}, u32[]{:S(2)}) collective-permute-start(bf16[6,48,1,32]{1,3,2,0:T(8,128)(2,1)S(1)} %get-tuple-element.38), channel_id=1, source_target_pairs={{16,0},{32,16},{48,32},{64,48},{80,64},{96,80},{112,96},{128,112},... | collective-permute-start | bytes 55304 | tf_op jit(solution)/shard_map/ppermute | solution.py:180
  6.8 1.2 convert_reduce_fusion
  8.4 1.3 %fusion.2 = f32[32]{0:T(128)S(1)} fusion(bf16[4,48,10,32]{1,3,2,0:T(8,128)(2,1)} %param.10, f32[32]{0:T(128)S(1)} %sub.57), kind=kLoop, calls=%fused_computation.8 | loop fusion | flops 245728 | bytes 123136 | tf_op jit(solution)/shard_map/reduce_sum | solution.py:212
  9.9 0.2 scatter.9.x_ref
  10.1 0.6 copy-done.3
  10.6 23.7 %shard_map.64 = f32[32,8,128]{2,1,0:T(8,128)} custom-call(f32[8,128]{1,0:T(8,128)} %copy-done.3), custom_call_target="tpu_custom_call" | custom-call | tf_op jit(solution)/shard_map/pallas_call | solution.py:69
  34.3 1.0 slice_reduce_fusion.1
  35.4 0.2 fusion.19
  35.9 1.9 %fusion.22 = (bf16[1,3,3,32,512]{4,3,2,1,0:T(8,128)(2,1)S(1)}, bf16[1,3,3,32,512]{4,3,2,1,0:T(8,128)(2,1)}, bf16[1,3,3,32,512]{4,3,2,1,0:T(8,128)(2,1)S(1)}) fusion(bf16[3,3,3,32,512]{4,3,2,1,0:T(8,128)(2,1)} %param.14), kind=kLoop, calls=%fused_computation.54 | loop fusion | bytes 1769472 | tf_op jit(solution)/shard_map/slice | solution.py:248
  37.9 1.0 fusion.11
  39.1 0.4 select_maximum_fusion
  39.7 0.1 fusion.16
  40.1 0.3 slice_dynamic-update-slice_fusion.2
  40.4 0.3 slice_dynamic-update-slice_fusion.1
  40.7 0.3 slice_dynamic-update-slice_fusion
  40.9 2.9 %fusion.21 = (bf16[4,48,10,288]{1,3,2,0:T(8,128)(2,1)}, bf16[4,48,10,288]{1,3,2,0:T(8,128)(2,1)}, bf16[4,48,10,288]{1,3,2,0:T(8,128)(2,1)S(1)}) fusion(bf16[6,48,10,288]{1,3,2,0:T(8,128)(2,1)S(1)} %slice_dynamic-update-slice_fusion), kind=kLoop, calls=%fused_computation.53 | loop fusion | bytes 6635520 | tf_op jit(solution)/shard_map/slice | solution.py:249
  43.8 3.6 %copy.10 = bf16[4,48,10,288]{3,2,1,0:T(8,128)(2,1)} copy(bf16[4,48,10,288]{1,3,2,0:T(8,128)(2,1)S(1)} %get-tuple-element.33) | data formatting | bytes 2211840 | tf_op jit(solution)/shard_map/slice | solution.py:249
  47.4 2.9 %reshape.211 = bf16[1920,288]{1,0:T(8,128)(2,1)S(1)} reshape(bf16[4,48,10,288]{3,2,1,0:T(8,128)(2,1)} %copy.10) | data formatting | bytes 2211840 | tf_op jit(solution)/shard_map/reshape | solution.py:249
  50.3 5.2 %copy.11 = bf16[4,48,10,288]{3,2,1,0:T(8,128)(2,1)} copy(bf16[4,48,10,288]{1,3,2,0:T(8,128)(2,1)} %get-tuple-element.32) | data formatting | bytes 2211840 | tf_op jit(solution)/shard_map/slice | solution.py:249
  55.5 2.9 %reshape.212 = bf16[1920,288]{1,0:T(8,128)(2,1)S(1)} reshape(bf16[4,48,10,288]{3,2,1,0:T(8,128)(2,1)} %copy.11) | data formatting | bytes 2211840 | tf_op jit(solution)/shard_map/reshape | solution.py:249
  58.4 5.2 %copy.12 = bf16[4,48,10,288]{3,2,1,0:T(8,128)(2,1)} copy(bf16[4,48,10,288]{1,3,2,0:T(8,128)(2,1)} %get-tuple-element.31) | data formatting | bytes 2211840 | tf_op jit(solution)/shard_map/slice | solution.py:249
  63.6 3.9 %reshape.213 = bf16[1920,288]{1,0:T(8,128)(2,1)} reshape(bf16[4,48,10,288]{3,2,1,0:T(8,128)(2,1)} %copy.12) | data formatting | bytes 2211840 | tf_op jit(solution)/shard_map/reshape | solution.py:249
  67.5 2.2 %fusion.24 = f32[1920,512]{0,1:T(8,128)S(1)} fusion(bf16[1920,288]{1,0:T(8,128)(2,1)S(1)} %reshape.211, bf16[288,512]{1,0:T(8,128)(2,1)} %bitcast.26), kind=kOutput, calls=%fused_computation.56 | convolution fusion | flops 566231040 | bytes 5332992 | tf_op jit(solution)/shard_map/dot_general | solution.py:250
  69.7 1.3 %fusion.25 = f32[1920,512]{0,1:T(8,128)S(1)} fusion(bf16[1920,288]{1,0:T(8,128)(2,1)S(1)} %reshape.212, bf16[288,512]{1,0:T(8,128)(2,1)S(1)} %bitcast.25), kind=kOutput, calls=%fused_computation.57 | convolution fusion | flops 566231040 | bytes 5332992 | tf_op jit(solution)/shard_map/dot_general | solution.py:250
  71.1 1.3 %add_add_fusion = f32[1920,512]{0,1:T(8,128)S(1)} fusion(f32[1920,512]{0,1:T(8,128)S(1)} %fusion.24, f32[1920,512]{0,1:T(8,128)S(1)} %fusion.25, bf16[1920,288]{1,0:T(8,128)(2,1)S(1)} %copy-done, bf16[288,512]{1,0:T(8,128)(2,1)S(1)} %bitcast.24), kind=kOutput, calls=%fused_computation | convolution fusion | flops 568197120 | bytes 13197312 | tf_op jit(solution)/shard_map/dot_general | solution.py:250
  72.4 48.0 %shard_map.65 = f32[32,1920]{1,0:T(8,128)S(1)} custom-call(f32[4,2,2,32,1920]{4,3,2,1,0:T(8,128)S(1)} %bitcast.23), custom_call_target="tpu_custom_call" | custom-call | tf_op jit(solution)/shard_map/pallas_call | solution.py:156
  120.5 0.3 copy.13
  120.8 0.2 reshape.215
  121.0 1.2 copy.14
  (41 shorter events, 1.8 us)
Async XLA Ops:
  0.0 39.1 %copy-start.2 = (bf16[2,48,10,32]{1,3,2,0:T(8,128)(2,1)S(1)}, bf16[2,48,10,32]{1,3,2,0:T(8,128)(2,1)}, u32[]{:S(2)}) copy-start(bf16[2,48,10,32]{1,3,2,0:T(8,128)(2,1)} %param.11) | copy-start | bytes 184324
  0.0 37.9 %copy-start.1 = (bf16[4,48,10,32]{1,3,2,0:T(8,128)(2,1)S(1)}, bf16[4,48,10,32]{1,3,2,0:T(8,128)(2,1)}, u32[]{:S(2)}) copy-start(bf16[4,48,10,32]{1,3,2,0:T(8,128)(2,1)} %param.10) | copy-start | bytes 368644
  0.0 38.9 %copy-start.5 = (f32[32]{0:T(128)S(1)}, f32[32]{0:T(128)}, u32[]{:S(2)}) copy-start(f32[32]{0:T(128)} %param.12) | copy-start | bytes 388
  0.0 38.9 %copy-start.4 = (f32[32]{0:T(128)S(1)}, f32[32]{0:T(128)}, u32[]{:S(2)}) copy-start(f32[32]{0:T(128)} %param.13) | copy-start | bytes 388
  2.0 36.8 %collective-permute-start = (bf16[6,48,1,32]{1,3,2,0:T(8,128)(2,1)S(1)}, bf16[6,48,1,32]{1,3,2,0:T(8,128)(2,1)S(1)}, u32[]{:S(2)}, u32[]{:S(2)}) collective-permute-start(bf16[6,48,1,32]{1,3,2,0:T(8,128)(2,1)S(1)} %get-tuple-element.37), channel_id=1, source_target_pairs={{0,16},{16,32},{32,48},{48,64},{64,80},{80,96},{96,112},{112,128},... | collective-permute-start | bytes 55304 | tf_op jit(solution)/shard_map/ppermute | solution.py:179
  5.5 33.4 %collective-permute-start.1 = (bf16[6,48,1,32]{1,3,2,0:T(8,128)(2,1)S(1)}, bf16[6,48,1,32]{1,3,2,0:T(8,128)(2,1)S(1)}, u32[]{:S(2)}, u32[]{:S(2)}) collective-permute-start(bf16[6,48,1,32]{1,3,2,0:T(8,128)(2,1)S(1)} %get-tuple-element.38), channel_id=1, source_target_pairs={{16,0},{32,16},{48,32},{64,48},{80,64},{96,80},{112,96},{128,112},... | collective-permute-start | bytes 55304 | tf_op jit(solution)/shard_map/ppermute | solution.py:180
  10.0 0.6 copy-start.3
  69.7 1.4 %copy-start = (bf16[1920,288]{1,0:T(8,128)(2,1)S(1)}, bf16[1920,288]{1,0:T(8,128)(2,1)}, u32[]{:S(2)}) copy-start(bf16[1920,288]{1,0:T(8,128)(2,1)} %reshape.213) | copy-start | bytes 3317764
  72.4 48.0 %copy-start.6 = (f32[32]{0:T(128)S(1)}, f32[32]{0:T(128)}, u32[]{:S(2)}) copy-start(f32[32]{0:T(128)} %param.15) | copy-start | bytes 388

commit v5 on v4

--- a/solution.py
+++ b/solution.py
@@ -80,7 +80,7 @@
     )(tile)
 
 
-def scatter_kernel(x_ref, o_ref, recv1, acc1, recv2, acc2, recv3, send_sem, recv_sem):
+def scatter_kernel(x_ref, o_ref, recv1, acc1, own, recv2, acc2, recv3, send_sem, recv_sem):
     sp = lax.axis_index("space")
     c = lax.axis_index("chan")
     core = c % 2
@@ -112,47 +112,47 @@
     for cp in firsts:
         cp.wait()
 
-    def fold_first(dest):
+    def fold_first(dest, dst):
         for j in range(nyh):
-            acc1[dest, j] = x_ref[dest, j, core] + recv1[dest, j]
+            dst[j] = (x_ref[dest, j, core] + recv1[dest, j]).astype(dst.dtype)
 
     sends = []
     for k in range(1, nx):
         dest = lax.rem(xx + k, nx)
-        fold_first(dest)
+        fold_first(dest, acc1.at[dest])
         slot = nx - 1 - k
         cp = pltpu.make_async_remote_copy(
             src_ref=acc1.at[dest], dst_ref=recv2.at[slot], send_sem=send_sem.at[nfirst + k - 1],
             recv_sem=recv_sem.at[nfirst + slot], device_id=peers[k], device_id_type=MESH)
         cp.start()
         sends.append(cp)
-    fold_first(xx)
+    fold_first(xx, own)
     for slot in range(nx - 1):
         pltpu.make_async_remote_copy(
             src_ref=acc1.at[xx], dst_ref=recv2.at[slot], send_sem=send_sem.at[nfirst + slot],
             recv_sem=recv_sem.at[nfirst + slot], device_id=peers[0], device_id_type=MESH).wait_recv()
     other = 1 - yh
-    total = acc1[xx, other]
+    total = own[other]
     for slot in range(nx - 1):
-        total = total + recv2[slot, other]
-    acc2[other] = total
+        total = total + recv2[slot, other].astype(jnp.float32)
+    acc2[...] = total.astype(acc2.dtype)
     last_sem = nfirst + nx - 1
     last = pltpu.make_async_remote_copy(
-        src_ref=acc2.at[other], dst_ref=recv3, send_sem=send_sem.at[last_sem],
+        src_ref=acc2, dst_ref=recv3, send_sem=send_sem.at[last_sem],
         recv_sem=recv_sem.at[last_sem], device_id=peers[nx], device_id_type=MESH)
     last.start()
-    total = acc1[xx, yh]
+    total = own[yh]
     for slot in range(nx - 1):
-        total = total + recv2[slot, yh]
+        total = total + recv2[slot, yh].astype(jnp.float32)
     for cp in sends:
         cp.wait_send()
     last.wait()
-    o_ref[...] = total + recv3[...]
+    o_ref[...] = total + recv3[...].astype(jnp.float32)
 
 
 def scatter_chan(parts):
     nx, nyh, ncore, rows, cells = parts.shape
-    f32 = jnp.float32
+    f32, bf16 = jnp.float32, jnp.bfloat16
     return pl.pallas_call(
         scatter_kernel,
         out_shape=jax.ShapeDtypeStruct((rows, cells), f32),
@@ -160,10 +160,11 @@
         out_specs=pl.BlockSpec(memory_space=pltpu.VMEM),
         scratch_shapes=[
             pltpu.VMEM((nx, nyh, rows, cells), f32),
-            pltpu.VMEM((nx, nyh, rows, cells), f32),
-            pltpu.VMEM((nx - 1, nyh, rows, cells), f32),
+            pltpu.VMEM((nx, nyh, rows, cells), bf16),
             pltpu.VMEM((nyh, rows, cells), f32),
-            pltpu.VMEM((rows, cells), f32),
+            pltpu.VMEM((nx - 1, nyh, rows, cells), bf16),
+            pltpu.VMEM((rows, cells), bf16),
+            pltpu.VMEM((rows, cells), bf16),
             pltpu.SemaphoreType.DMA((nx * nyh + nx,)),
             pltpu.SemaphoreType.DMA((nx * nyh + nx,)),
         ],

time: 123 us -> 107 us (0.87)
  Pallas kernels: 71.7 us -> 55.8 us
    pallas_call x1, Pallas kernels: 48 us -> 32.2 us  [scatter_chan(): pl.pallas_call(scatter_kernel, out_shape=jax.ShapeDtypeStruct((rows, cell...]
  transfers between devices with their start and end apart: 2 -> 2, of which waited for: 0 -> 0; matrix products, arithmetic and copies ran while one was open for 6% -> 7% of each run, Pallas kernels for 19% -> 22%
where the time goes in v5:
time: 107 us; the launch traced here: 106 us
  Pallas kernels  55.8 us (52%)
  local copies, waits for them, and re-layouts  34.8 us (33%)
  other arithmetic  5.9 us (6%)
  starting transfers between devices  4.77 us (4%)
  matrix products  4.77 us (4%)
    pallas_call x1, Pallas kernels, scatter_chan(): pl.pallas_call(scatter_kernel, out_shape=jax.ShapeDtypeStruct((rows, cell...  32.2 us
    pallas_call x1, Pallas kernels, gather_space(): pl.pallas_call(functools.partial(gather_kernel, n), out_shape=jax.ShapeDt...  23.7 us
    slice x4, local copies, waits for them, and re-layouts, local(): window = columns_in[depth:depth + nframes].reshape(cell_count, tap_width)  16.8 us
    reshape x3, local copies, waits for them, and re-layouts, local(): window = columns_in[depth:depth + nframes].reshape(cell_count, tap_width)  9.72 us
    dot_general x3, matrix products, local(): lax.dot_general(tap_weight, window, (((0,), (1,)), ((), ())), preferred_e...  4.77 us
    ppermute x1, starting transfers between devices, edge_exchange(): before = lax.ppermute(edges_last, axis, up)  3.48 us
    unnamed x20, local copies, waits for them, and re-layouts  2.39 us
  transfers between devices with their start and end apart: 2, of which 0 were waited for; matrix products, arithmetic and copies ran while one was open for 7% of the time, Pallas kernels for 22%

profile of v5, /device:TPU:6, one launch (start us, length us, event | category | flops | bytes accessed | tf_op | source)
XLA Modules:
  0.0 106.4 jit_solution(4868747534246875945)
XLA Ops:
  0.0 1.0 constant_dynamic-update-slice_fusion.1
  1.0 1.0 constant_dynamic-update-slice_fusion
  2.0 3.5 %collective-permute-start = (bf16[6,48,1,32]{1,3,2,0:T(8,128)(2,1)S(1)}, bf16[6,48,1,32]{1,3,2,0:T(8,128)(2,1)S(1)}, u32[]{:S(2)}, u32[]{:S(2)}) collective-permute-start(bf16[6,48,1,32]{1,3,2,0:T(8,128)(2,1)S(1)} %get-tuple-element.37), channel_id=1, source_target_pairs={{0,16},{16,32},{32,48},{48,64},{64,80},{80,96},{96,112},{112,128},... | collective-permute-start | bytes 55304 | tf_op jit(solution)/shard_map/ppermute | solution.py:180
  5.5 1.3 %collective-permute-start.1 = (bf16[6,48,1,32]{1,3,2,0:T(8,128)(2,1)S(1)}, bf16[6,48,1,32]{1,3,2,0:T(8,128)(2,1)S(1)}, u32[]{:S(2)}, u32[]{:S(2)}) collective-permute-start(bf16[6,48,1,32]{1,3,2,0:T(8,128)(2,1)S(1)} %get-tuple-element.38), channel_id=1, source_target_pairs={{16,0},{32,16},{48,32},{64,48},{80,64},{96,80},{112,96},{128,112},... | collective-permute-start | bytes 55304 | tf_op jit(solution)/shard_map/ppermute | solution.py:181
  6.8 1.2 %convert_reduce_fusion = f32[32]{0:T(128)S(1)} fusion(bf16[4,48,10,32]{1,3,2,0:T(8,128)(2,1)} %param.10), kind=kLoop, calls=%fused_computation.6 | loop fusion | flops 122848 | bytes 123008 | tf_op jit(solution)/shard_map/reduce_sum | solution.py:211
  8.4 1.3 %fusion.2 = f32[32]{0:T(128)S(1)} fusion(bf16[4,48,10,32]{1,3,2,0:T(8,128)(2,1)} %param.10, f32[32]{0:T(128)S(1)} %sub.57), kind=kLoop, calls=%fused_computation.8 | loop fusion | flops 245728 | bytes 123136 | tf_op jit(solution)/shard_map/reduce_sum | solution.py:213
  9.9 0.2 scatter.9.x_ref
  10.1 0.6 copy-done.3
  10.6 23.7 %shard_map.64 = f32[32,8,128]{2,1,0:T(8,128)} custom-call(f32[8,128]{1,0:T(8,128)} %copy-done.3), custom_call_target="tpu_custom_call" | custom-call | tf_op jit(solution)/shard_map/pallas_call | solution.py:69
  34.3 1.0 slice_reduce_fusion.1
  35.4 0.2 fusion.19
  35.9 1.9 %fusion.22 = (bf16[1,3,3,32,512]{4,3,2,1,0:T(8,128)(2,1)S(1)}, bf16[1,3,3,32,512]{4,3,2,1,0:T(8,128)(2,1)}, bf16[1,3,3,32,512]{4,3,2,1,0:T(8,128)(2,1)S(1)}) fusion(bf16[3,3,3,32,512]{4,3,2,1,0:T(8,128)(2,1)} %param.14), kind=kLoop, calls=%fused_computation.54 | loop fusion | bytes 1769472 | tf_op jit(solution)/shard_map/slice | solution.py:249
  37.9 1.0 fusion.11
  39.1 0.4 select_maximum_fusion
  39.7 0.1 fusion.16
  40.1 0.3 slice_dynamic-update-slice_fusion.2
  40.4 0.3 slice_dynamic-update-slice_fusion.1
  40.7 0.3 slice_dynamic-update-slice_fusion
  40.9 2.9 %fusion.21 = (bf16[4,48,10,288]{1,3,2,0:T(8,128)(2,1)}, bf16[4,48,10,288]{1,3,2,0:T(8,128)(2,1)}, bf16[4,48,10,288]{1,3,2,0:T(8,128)(2,1)S(1)}) fusion(bf16[6,48,10,288]{1,3,2,0:T(8,128)(2,1)S(1)} %slice_dynamic-update-slice_fusion), kind=kLoop, calls=%fused_computation.53 | loop fusion | bytes 6635520 | tf_op jit(solution)/shard_map/slice | solution.py:250
  43.8 3.6 %copy.10 = bf16[4,48,10,288]{3,2,1,0:T(8,128)(2,1)} copy(bf16[4,48,10,288]{1,3,2,0:T(8,128)(2,1)S(1)} %get-tuple-element.33) | data formatting | bytes 2211840 | tf_op jit(solution)/shard_map/slice | solution.py:250
  47.4 2.9 %reshape.211 = bf16[1920,288]{1,0:T(8,128)(2,1)S(1)} reshape(bf16[4,48,10,288]{3,2,1,0:T(8,128)(2,1)} %copy.10) | data formatting | bytes 2211840 | tf_op jit(solution)/shard_map/reshape | solution.py:250
  50.3 5.2 %copy.11 = bf16[4,48,10,288]{3,2,1,0:T(8,128)(2,1)} copy(bf16[4,48,10,288]{1,3,2,0:T(8,128)(2,1)} %get-tuple-element.32) | data formatting | bytes 2211840 | tf_op jit(solution)/shard_map/slice | solution.py:250
  55.5 2.9 %reshape.212 = bf16[1920,288]{1,0:T(8,128)(2,1)S(1)} reshape(bf16[4,48,10,288]{3,2,1,0:T(8,128)(2,1)} %copy.11) | data formatting | bytes 2211840 | tf_op jit(solution)/shard_map/reshape | solution.py:250
  58.4 5.2 %copy.12 = bf16[4,48,10,288]{3,2,1,0:T(8,128)(2,1)} copy(bf16[4,48,10,288]{1,3,2,0:T(8,128)(2,1)} %get-tuple-element.31) | data formatting | bytes 2211840 | tf_op jit(solution)/shard_map/slice | solution.py:250
  63.6 3.9 %reshape.213 = bf16[1920,288]{1,0:T(8,128)(2,1)} reshape(bf16[4,48,10,288]{3,2,1,0:T(8,128)(2,1)} %copy.12) | data formatting | bytes 2211840 | tf_op jit(solution)/shard_map/reshape | solution.py:250
  67.5 2.2 %fusion.24 = f32[1920,512]{0,1:T(8,128)S(1)} fusion(bf16[1920,288]{1,0:T(8,128)(2,1)S(1)} %reshape.211, bf16[288,512]{1,0:T(8,128)(2,1)} %bitcast.26), kind=kOutput, calls=%fused_computation.56 | convolution fusion | flops 566231040 | bytes 5332992 | tf_op jit(solution)/shard_map/dot_general | solution.py:251
  69.7 1.3 %fusion.25 = f32[1920,512]{0,1:T(8,128)S(1)} fusion(bf16[1920,288]{1,0:T(8,128)(2,1)S(1)} %reshape.212, bf16[288,512]{1,0:T(8,128)(2,1)S(1)} %bitcast.25), kind=kOutput, calls=%fused_computation.57 | convolution fusion | flops 566231040 | bytes 5332992 | tf_op jit(solution)/shard_map/dot_general | solution.py:251
  71.1 1.3 %add_add_fusion = f32[1920,512]{0,1:T(8,128)S(1)} fusion(f32[1920,512]{0,1:T(8,128)S(1)} %fusion.24, f32[1920,512]{0,1:T(8,128)S(1)} %fusion.25, bf16[1920,288]{1,0:T(8,128)(2,1)S(1)} %copy-done, bf16[288,512]{1,0:T(8,128)(2,1)S(1)} %bitcast.24), kind=kOutput, calls=%fused_computation | convolution fusion | flops 568197120 | bytes 13197312 | tf_op jit(solution)/shard_map/dot_general | solution.py:251
  72.4 32.2 %shard_map.65 = f32[32,1920]{1,0:T(8,128)S(1)} custom-call(f32[4,2,2,32,1920]{4,3,2,1,0:T(8,128)S(1)} %bitcast.23), custom_call_target="tpu_custom_call" | custom-call | tf_op jit(solution)/shard_map/pallas_call | solution.py:156
  104.7 0.3 copy.13
  105.0 0.2 reshape.215
  105.2 1.2 %copy.14 = bf16[4,48,10,32]{1,3,2,0:T(8,128)(2,1)} copy(bf16[4,48,10,32]{3,2,1,0:T(8,128)(2,1)S(1)} %reshape.215) | data formatting | bytes 245760 | tf_op jit(solution)/shard_map/reshape | solution.py:256
  (41 shorter events, 1.8 us)
Async XLA Ops:
  0.0 39.1 %copy-start.2 = (bf16[2,48,10,32]{1,3,2,0:T(8,128)(2,1)S(1)}, bf16[2,48,10,32]{1,3,2,0:T(8,128)(2,1)}, u32[]{:S(2)}) copy-start(bf16[2,48,10,32]{1,3,2,0:T(8,128)(2,1)} %param.11) | copy-start | bytes 184324
  0.0 37.9 %copy-start.1 = (bf16[4,48,10,32]{1,3,2,0:T(8,128)(2,1)S(1)}, bf16[4,48,10,32]{1,3,2,0:T(8,128)(2,1)}, u32[]{:S(2)}) copy-start(bf16[4,48,10,32]{1,3,2,0:T(8,128)(2,1)} %param.10) | copy-start | bytes 368644
  0.0 38.9 %copy-start.5 = (f32[32]{0:T(128)S(1)}, f32[32]{0:T(128)}, u32[]{:S(2)}) copy-start(f32[32]{0:T(128)} %param.12) | copy-start | bytes 388
  0.0 38.9 %copy-start.4 = (f32[32]{0:T(128)S(1)}, f32[32]{0:T(128)}, u32[]{:S(2)}) copy-start(f32[32]{0:T(128)} %param.13) | copy-start | bytes 388
  2.0 36.8 %collective-permute-start = (bf16[6,48,1,32]{1,3,2,0:T(8,128)(2,1)S(1)}, bf16[6,48,1,32]{1,3,2,0:T(8,128)(2,1)S(1)}, u32[]{:S(2)}, u32[]{:S(2)}) collective-permute-start(bf16[6,48,1,32]{1,3,2,0:T(8,128)(2,1)S(1)} %get-tuple-element.37), channel_id=1, source_target_pairs={{0,16},{16,32},{32,48},{48,64},{64,80},{80,96},{96,112},{112,128},... | collective-permute-start | bytes 55304 | tf_op jit(solution)/shard_map/ppermute | solution.py:180
  5.5 33.4 %collective-permute-start.1 = (bf16[6,48,1,32]{1,3,2,0:T(8,128)(2,1)S(1)}, bf16[6,48,1,32]{1,3,2,0:T(8,128)(2,1)S(1)}, u32[]{:S(2)}, u32[]{:S(2)}) collective-permute-start(bf16[6,48,1,32]{1,3,2,0:T(8,128)(2,1)S(1)} %get-tuple-element.38), channel_id=1, source_target_pairs={{16,0},{32,16},{48,32},{64,48},{80,64},{96,80},{112,96},{128,112},... | collective-permute-start | bytes 55304 | tf_op jit(solution)/shard_map/ppermute | solution.py:181
  10.0 0.6 copy-start.3
  69.7 1.4 %copy-start = (bf16[1920,288]{1,0:T(8,128)(2,1)S(1)}, bf16[1920,288]{1,0:T(8,128)(2,1)}, u32[]{:S(2)}) copy-start(bf16[1920,288]{1,0:T(8,128)(2,1)} %reshape.213) | copy-start | bytes 3317764
  72.4 32.2 %copy-start.6 = (f32[32]{0:T(128)S(1)}, f32[32]{0:T(128)}, u32[]{:S(2)}) copy-start(f32[32]{0:T(128)} %param.15) | copy-start | bytes 388

commit v6 on v5

--- a/solution.py
+++ b/solution.py
@@ -182,17 +182,6 @@
     return before, after
 
 
-def unfold_taps(source, row_count, col_count):
-    return jnp.concatenate(
-        [
-            source[:, row_tap : row_tap + row_count, col_tap : col_tap + col_count, :]
-            for row_tap in range(3)
-            for col_tap in range(3)
-        ],
-        axis=3,
-    )
-
-
 def local(frames, cache, gamma, beta, kernel, bias):
     nframes, row_count, col_count, local_ch = frames.shape
     ncache = cache.shape[0]
@@ -239,21 +228,32 @@
     bordered = jnp.concatenate([left, joined, right], axis=2)
     bordered = jnp.pad(bordered, ((0, 0), (1, 1), (0, 0), (0, 0)))
     cell_count = nframes * row_count * col_count
-    columns_in = unfold_taps(bordered, row_count, col_count)
+    bordered = bordered.transpose(0, 2, 1, 3)
+    columns_in = jnp.concatenate(
+        [
+            bordered[:, col_tap : col_tap + col_count, row_tap : row_tap + row_count, :]
+            for row_tap in range(3)
+            for col_tap in range(3)
+        ],
+        axis=3,
+    )
     tap_width = columns_in.shape[3]
     nchan = lax.axis_size("chan")
     nx = nchan // 4
     flat_kernel = kernel.reshape(3, tap_width, kernel.shape[4])
     running = jnp.zeros((bias.shape[0] * nchan, cell_count), jnp.float32)
+    plane = row_count * col_count
+    flat_in = columns_in.reshape(columns_in.shape[0] * plane, tap_width)
     for depth in range(3):
         tap_weight = flat_kernel[depth]
-        window = columns_in[depth : depth + nframes].reshape(cell_count, tap_width)
+        window = flat_in[depth * plane : depth * plane + cell_count]
         running = running + lax.dot_general(
             tap_weight, window, (((0,), (1,)), ((), ())), preferred_element_type=jnp.float32
         )
     summed = scatter_chan(running.reshape(nx, 2, 2, local_ch, cell_count))
     result = summed.T + bias
-    return result.astype(jnp.bfloat16).reshape(nframes, row_count, col_count, -1)
+    result = result.astype(jnp.bfloat16).reshape(nframes, col_count, row_count, -1)
+    return result.transpose(0, 2, 1, 3)
 
 
 def solution(mesh):

time: 107 us -> 95.3 us (0.89)
  local copies, waits for them, and re-layouts: 34.8 us -> 23.5 us
    reshape x5 -> x1, local copies, waits for them, and re-layouts: 11.1 us -> 0.52 us  [local(): result.astype(jnp.bfloat16).reshape(nframes, col_count, row_count, -1)]
    slice x4, local copies, waits for them, and re-layouts: 16.8 us -> 14.7 us  [local(): window = flat_in[depth * plane:depth * plane + cell_count]]
    unnamed x20 -> x23, local copies, waits for them, and re-layouts: 2.39 us -> 3.17 us
  transfers between devices with their start and end apart: 2 -> 2, of which waited for: 0 -> 0; matrix products, arithmetic and copies ran while one was open for 7% -> 8% of each run, Pallas kernels for 22% -> 25%
where the time goes in v6:
time: 95.3 us; the launch traced here: 94.7 us
  Pallas kernels  55.8 us (59%)
  local copies, waits for them, and re-layouts  23.5 us (25%)
  other arithmetic  5.49 us (6%)
  starting transfers between devices  4.77 us (5%)
  matrix products  4.77 us (5%)
    pallas_call x1, Pallas kernels, scatter_chan(): pl.pallas_call(scatter_kernel, out_shape=jax.ShapeDtypeStruct((rows, cell...  32.2 us
    pallas_call x1, Pallas kernels, gather_space(): pl.pallas_call(functools.partial(gather_kernel, n), out_shape=jax.ShapeDt...  23.7 us
    slice x4, local copies, waits for them, and re-layouts, local(): window = flat_in[depth * plane:depth * plane + cell_count]  14.7 us
    dot_general x3, matrix products, local(): lax.dot_general(tap_weight, window, (((0,), (1,)), ((), ())), preferred_e...  4.77 us
    ppermute x1, starting transfers between devices, edge_exchange(): before = lax.ppermute(edges_last, axis, up)  3.48 us
    unnamed x23, local copies, waits for them, and re-layouts  3.17 us
    slice x1, local copies, waits for them, and re-layouts, local(): tap_weight = flat_kernel[depth]  1.94 us
  transfers between devices with their start and end apart: 2, of which 0 were waited for; matrix products, arithmetic and copies ran while one was open for 8% of the time, Pallas kernels for 25%

profile of v6, /device:TPU:6, one launch (start us, length us, event | category | flops | bytes accessed | tf_op | source)
XLA Modules:
  0.0 94.7 jit_solution(4581750690048670620)
XLA Ops:
  0.0 1.0 %constant_dynamic-update-slice_fusion.1 = bf16[6,48,10,32]{1,3,2,0:T(8,128)(2,1)S(1)} fusion(bf16[2,48,10,32]{1,3,2,0:T(8,128)(2,1)} %param.11), kind=kLoop, calls=%fused_computation.40 | loop fusion | bytes 225280
  1.0 1.0 %constant_dynamic-update-slice_fusion = bf16[6,48,10,32]{1,3,2,0:T(8,128)(2,1)S(1)} fusion(bf16[6,48,10,32]{1,3,2,0:T(8,128)(2,1)S(1)} %constant_dynamic-update-slice_fusion.1, bf16[4,48,10,32]{1,3,2,0:T(8,128)(2,1)} %param.10), kind=kLoop, calls=%fused_computation.39 | loop fusion | bytes 450560 | tf_op jit(solution)/shard_map/concatenate | solution.py:194
  2.0 3.5 %collective-permute-start = (bf16[6,48,1,32]{1,3,2,0:T(8,128)(2,1)S(1)}, bf16[6,48,1,32]{1,3,2,0:T(8,128)(2,1)S(1)}, u32[]{:S(2)}, u32[]{:S(2)}) collective-permute-start(bf16[6,48,1,32]{1,3,2,0:T(8,128)(2,1)S(1)} %get-tuple-element.37), channel_id=1, source_target_pairs={{0,16},{16,32},{32,48},{48,64},{64,80},{80,96},{96,112},{112,128},... | collective-permute-start | bytes 55304 | tf_op jit(solution)/shard_map/ppermute | solution.py:180
  5.5 1.3 %collective-permute-start.1 = (bf16[6,48,1,32]{1,3,2,0:T(8,128)(2,1)S(1)}, bf16[6,48,1,32]{1,3,2,0:T(8,128)(2,1)S(1)}, u32[]{:S(2)}, u32[]{:S(2)}) collective-permute-start(bf16[6,48,1,32]{1,3,2,0:T(8,128)(2,1)S(1)} %get-tuple-element.38), channel_id=1, source_target_pairs={{16,0},{32,16},{48,32},{64,48},{80,64},{96,80},{112,96},{128,112},... | collective-permute-start | bytes 55304 | tf_op jit(solution)/shard_map/ppermute | solution.py:181
  6.8 1.2 %convert_reduce_fusion = f32[32]{0:T(128)S(1)} fusion(bf16[4,48,10,32]{1,3,2,0:T(8,128)(2,1)} %param.10), kind=kLoop, calls=%fused_computation.6 | loop fusion | flops 122848 | bytes 123008 | tf_op jit(solution)/shard_map/reduce_sum | solution.py:200
  8.1 0.1 reduce_sum.61
  8.4 1.3 %fusion.2 = f32[32]{0:T(128)S(1)} fusion(bf16[4,48,10,32]{1,3,2,0:T(8,128)(2,1)} %param.10, f32[32]{0:T(128)S(1)} %sub.57), kind=kLoop, calls=%fused_computation.8 | loop fusion | flops 245728 | bytes 123136 | tf_op jit(solution)/shard_map/reduce_sum | solution.py:202
  9.9 0.2 scatter.9.x_ref
  10.1 0.6 copy-done.3
  10.6 23.7 %shard_map.64 = f32[32,8,128]{2,1,0:T(8,128)} custom-call(f32[8,128]{1,0:T(8,128)} %copy-done.3), custom_call_target="tpu_custom_call" | custom-call | tf_op jit(solution)/shard_map/pallas_call | solution.py:69
  34.3 1.0 %slice_reduce_fusion.1 = (f32[2]{0:T(128)S(1)}, f32[2]{0:T(128)S(1)}, f32[32,1,2]{2,1,0:T(1,128)S(1)}) fusion(f32[32,8,128]{2,1,0:T(8,128)} %shard_map.64), kind=kLoop, calls=%fused_computation.49 | loop fusion | flops 124 | bytes 784 | tf_op jit(solution)/shard_map/reduce_sum | solution.py:208
  35.4 0.2 fusion.18
  35.9 1.9 %fusion.21 = (bf16[1,3,3,32,512]{4,3,2,1,0:T(8,128)(2,1)S(1)}, bf16[1,3,3,32,512]{4,3,2,1,0:T(8,128)(2,1)}, bf16[1,3,3,32,512]{4,3,2,1,0:T(8,128)(2,1)S(1)}) fusion(bf16[3,3,3,32,512]{4,3,2,1,0:T(8,128)(2,1)} %param.14), kind=kLoop, calls=%fused_computation.51 | loop fusion | bytes 1769472 | tf_op jit(solution)/shard_map/slice | solution.py:248
  37.9 1.0 %fusion.11 = bf16[4,48,10,32]{1,3,2,0:T(8,128)(2,1)S(1)} fusion(bf16[4,48,10,32]{1,3,2,0:T(8,128)(2,1)S(1)} %copy-done.1, f32[32]{0:T(128)} %param.13, f32[32]{0:T(128)} %param.12, f32[32]{0:T(128)S(1)} %mul.88, f32[32]{0:T(128)S(1)} %sub.61), kind=kLoop, calls=%fused_computation.17 | loop fusion | flops 614400 | bytes 246272 | tf_op jit(solution)/shard_map/convert_element_type | solution.py:220
  38.9 0.1 multiply_convert_fusion.1
  39.1 0.4 fusion.12
  39.7 0.3 slice_dynamic-update-slice_fusion.5
  40.0 0.3 slice_dynamic-update-slice_fusion.4
  40.2 0.3 slice_dynamic-update-slice_fusion.3
  40.5 0.3 slice_dynamic-update-slice_fusion.2
  40.8 0.3 slice_dynamic-update-slice_fusion.1
  41.0 0.3 slice_dynamic-update-slice_fusion
  41.3 3.6 %fusion.20 = (bf16[4,10,48,288]{2,3,1,0:T(8,128)(2,1)}, bf16[4,10,48,288]{2,3,1,0:T(8,128)(2,1)}, bf16[4,10,48,288]{2,3,1,0:T(8,128)(2,1)}) fusion(bf16[6,10,48,288]{2,3,1,0:T(8,128)(2,1)S(1)} %slice_dynamic-update-slice_fusion), kind=kLoop, calls=%fused_computation.50 | loop fusion | bytes 6635520 | tf_op jit(solution)/shard_map/slice | solution.py:249
  44.9 3.4 %copy.10 = bf16[4,10,48,288]{3,2,1,0:T(8,128)(2,1)S(1)} copy(bf16[4,10,48,288]{2,3,1,0:T(8,128)(2,1)} %get-tuple-element.33) | data formatting | bytes 2211840 | tf_op jit(solution)/shard_map/slice | solution.py:249
  48.3 3.4 %copy.11 = bf16[4,10,48,288]{3,2,1,0:T(8,128)(2,1)S(1)} copy(bf16[4,10,48,288]{2,3,1,0:T(8,128)(2,1)} %get-tuple-element.32) | data formatting | bytes 2211840 | tf_op jit(solution)/shard_map/slice | solution.py:249
  51.6 4.4 %copy.12 = bf16[4,10,48,288]{3,2,1,0:T(8,128)(2,1)} copy(bf16[4,10,48,288]{2,3,1,0:T(8,128)(2,1)} %get-tuple-element.31) | data formatting | bytes 2211840 | tf_op jit(solution)/shard_map/slice | solution.py:249
  56.0 2.2 %fusion.23 = f32[1920,512]{0,1:T(8,128)S(1)} fusion(bf16[1920,288]{1,0:T(8,128)(2,1)S(1)} %bitcast.33, bf16[288,512]{1,0:T(8,128)(2,1)} %bitcast.38), kind=kOutput, calls=%fused_computation.53 | convolution fusion | flops 566231040 | bytes 5332992 | tf_op jit(solution)/shard_map/dot_general | solution.py:250
  58.3 1.3 %fusion.24 = f32[1920,512]{0,1:T(8,128)S(1)} fusion(bf16[1920,288]{1,0:T(8,128)(2,1)S(1)} %bitcast.32, bf16[288,512]{1,0:T(8,128)(2,1)S(1)} %bitcast.37), kind=kOutput, calls=%fused_computation.54 | convolution fusion | flops 566231040 | bytes 5332992 | tf_op jit(solution)/shard_map/dot_general | solution.py:250
  59.6 1.3 %add_add_fusion = f32[1920,512]{0,1:T(8,128)S(1)} fusion(f32[1920,512]{0,1:T(8,128)S(1)} %fusion.23, f32[1920,512]{0,1:T(8,128)S(1)} %fusion.24, bf16[1920,288]{1,0:T(8,128)(2,1)S(1)} %bitcast.34, bf16[288,512]{1,0:T(8,128)(2,1)S(1)} %bitcast.36), kind=kOutput, calls=%fused_computation | convolution fusion | flops 568197120 | bytes 13197312 | tf_op jit(solution)/shard_map/dot_general | solution.py:250
  61.0 32.2 %shard_map.65 = f32[32,1920]{1,0:T(8,128)S(1)} custom-call(f32[4,2,2,32,1920]{4,3,2,1,0:T(8,128)S(1)} %bitcast.31), custom_call_target="tpu_custom_call" | custom-call | tf_op jit(solution)/shard_map/pallas_call | solution.py:156
  93.2 0.5 reshape.207
  93.7 0.9 copy.13
  (37 shorter events, 1.3 us)
Async XLA Ops:
  0.0 39.1 %copy-start.2 = (bf16[2,48,10,32]{1,3,2,0:T(8,128)(2,1)S(1)}, bf16[2,48,10,32]{1,3,2,0:T(8,128)(2,1)}, u32[]{:S(2)}) copy-start(bf16[2,48,10,32]{1,3,2,0:T(8,128)(2,1)} %param.11) | copy-start | bytes 184324
  0.0 37.9 %copy-start.1 = (bf16[4,48,10,32]{1,3,2,0:T(8,128)(2,1)S(1)}, bf16[4,48,10,32]{1,3,2,0:T(8,128)(2,1)}, u32[]{:S(2)}) copy-start(bf16[4,48,10,32]{1,3,2,0:T(8,128)(2,1)} %param.10) | copy-start | bytes 368644
  0.0 38.9 %copy-start.5 = (f32[32]{0:T(128)S(1)}, f32[32]{0:T(128)}, u32[]{:S(2)}) copy-start(f32[32]{0:T(128)} %param.12) | copy-start | bytes 388
  0.0 38.9 %copy-start.4 = (f32[32]{0:T(128)S(1)}, f32[32]{0:T(128)}, u32[]{:S(2)}) copy-start(f32[32]{0:T(128)} %param.13) | copy-start | bytes 388
  2.0 36.8 %collective-permute-start = (bf16[6,48,1,32]{1,3,2,0:T(8,128)(2,1)S(1)}, bf16[6,48,1,32]{1,3,2,0:T(8,128)(2,1)S(1)}, u32[]{:S(2)}, u32[]{:S(2)}) collective-permute-start(bf16[6,48,1,32]{1,3,2,0:T(8,128)(2,1)S(1)} %get-tuple-element.37), channel_id=1, source_target_pairs={{0,16},{16,32},{32,48},{48,64},{64,80},{80,96},{96,112},{112,128},... | collective-permute-start | bytes 55304 | tf_op jit(solution)/shard_map/ppermute | solution.py:180
  5.5 33.4 %collective-permute-start.1 = (bf16[6,48,1,32]{1,3,2,0:T(8,128)(2,1)S(1)}, bf16[6,48,1,32]{1,3,2,0:T(8,128)(2,1)S(1)}, u32[]{:S(2)}, u32[]{:S(2)}) collective-permute-start(bf16[6,48,1,32]{1,3,2,0:T(8,128)(2,1)S(1)} %get-tuple-element.38), channel_id=1, source_target_pairs={{16,0},{32,16},{48,32},{64,48},{80,64},{96,80},{112,96},{128,112},... | collective-permute-start | bytes 55304 | tf_op jit(solution)/shard_map/ppermute | solution.py:181
  10.0 0.6 copy-start.3
  58.3 1.4 %copy-start = (bf16[4,10,48,288]{3,2,1,0:T(8,128)(2,1)S(1)}, bf16[4,10,48,288]{3,2,1,0:T(8,128)(2,1)}, u32[]{:S(2)}) copy-start(bf16[4,10,48,288]{3,2,1,0:T(8,128)(2,1)} %copy.12) | copy-start | bytes 3317764
  60.9 32.2 %copy-start.6 = (f32[32]{0:T(128)S(1)}, f32[32]{0:T(128)}, u32[]{:S(2)}) copy-start(f32[32]{0:T(128)} %param.15) | copy-start | bytes 388

commit v7 on v6

--- a/solution.py
+++ b/solution.py
@@ -5,6 +5,7 @@
 from jax import lax
 from jax.experimental import pallas as pl
 from jax.experimental.pallas import tpu as pltpu
+from jax.experimental.layout import Layout, with_layout_constraint
 from jax.sharding import PartitionSpec as P
 
 CH = 512
@@ -237,6 +238,7 @@
         ],
         axis=3,
     )
+    columns_in = with_layout_constraint(columns_in, Layout(major_to_minor=(0, 1, 2, 3)))
     tap_width = columns_in.shape[3]
     nchan = lax.axis_size("chan")
     nx = nchan // 4

time: 95.3 us -> 89 us (0.934)
  local copies, waits for them, and re-layouts: 23.5 us -> 18.8 us
  other arithmetic: 5.49 us -> 4.46 us
    slice x4 -> x1, local copies, waits for them, and re-layouts: 14.7 us -> 0.38 us  [local(): window = flat_in[depth * plane:depth * plane + cell_count]]
    concatenate x1, local copies, waits for them, and re-layouts: 0.26 us -> 7.08 us  [local(): jnp.concatenate([bordered[:, col_tap:col_tap + col_count, row_tap:row_tap...]
    slice x1, local copies, waits for them, and re-layouts: 0.01 us -> 2.96 us  [local(): bordered[:, col_tap:col_tap + col_count, row_tap:row_tap + row_count, :]]
    slice x1, local copies, waits for them, and re-layouts: 1.94 us -> 0.79 us  [local(): tap_weight = flat_kernel[depth]]
    concatenate x1 -> x0, local copies, waits for them, and re-layouts: 1.02 us -> none  [local(): raw = jnp.concatenate([cache, frames], axis=0)]
    reduce_sum x2, other arithmetic: 1.28 us -> 0.31 us  [local(): local_mean = jnp.sum(values, axis=(0, 1, 2, 4)) / local_members]
    reduce_sum x2, other arithmetic: 1.38 us -> 0.41 us  [local(): local_m2 = jnp.sum(local_dev * local_dev, axis=(0, 1, 2, 4))]
    unnamed x23 -> x16, local copies, waits for them, and re-layouts: 3.17 us -> 3.53 us
  transfers between devices with their start and end apart: 2 -> 2, of which waited for: 0 -> 0; matrix products, arithmetic and copies ran while one was open for 8% -> 6% of each run, Pallas kernels for 25% -> 26%
where the time goes in v7:
time: 89 us; the launch traced here: 88.2 us
  Pallas kernels  55.2 us (62%)
  local copies, waits for them, and re-layouts  18.8 us (21%)
  starting transfers between devices  5.51 us (6%)
  other arithmetic  4.46 us (5%)
  matrix products  4.06 us (5%)
    pallas_call x1, Pallas kernels, scatter_chan(): pl.pallas_call(scatter_kernel, out_shape=jax.ShapeDtypeStruct((rows, cell...  32.2 us
    pallas_call x1, Pallas kernels, gather_space(): pl.pallas_call(functools.partial(gather_kernel, n), out_shape=jax.ShapeDt...  23 us
    concatenate x1, local copies, waits for them, and re-layouts, local(): jnp.concatenate([bordered[:, col_tap:col_tap + col_count, row_tap:row_tap...  7.08 us
    ppermute x1, starting transfers between devices, edge_exchange(): before = lax.ppermute(edges_last, axis, up)  4.23 us
    dot_general x3, matrix products, local(): lax.dot_general(tap_weight, window, (((0,), (1,)), ((), ())), preferred_e...  4.06 us
    unnamed x16, local copies, waits for them, and re-layouts  3.53 us
    slice x1, local copies, waits for them, and re-layouts, local(): bordered[:, col_tap:col_tap + col_count, row_tap:row_tap + row_count, :]  2.96 us
  transfers between devices with their start and end apart: 2, of which 0 were waited for; matrix products, arithmetic and copies ran while one was open for 6% of the time, Pallas kernels for 26%

profile of v7, /device:TPU:6, one launch (start us, length us, event | category | flops | bytes accessed | tf_op | source)
XLA Modules:
  0.0 88.2 jit_solution(3872251627468302047)
XLA Ops:
  0.0 1.1 %copy.19 = bf16[2,48,10,32]{3,1,2,0:T(8,128)(2,1)S(1)} copy(bf16[2,48,10,32]{1,3,2,0:T(8,128)(2,1)} %param.11) | data formatting | bytes 122880 | tf_op args[1]
  1.2 1.2 %copy.20 = bf16[4,48,10,32]{3,1,2,0:T(8,128)(2,1)S(1)} copy(bf16[4,48,10,32]{1,3,2,0:T(8,128)(2,1)} %param.10) | data formatting | bytes 245760 | tf_op args[0]
  2.4 0.7 pad_maximum_fusion.1
  3.1 4.2 %collective-permute-start = (bf16[6,48,1,32]{3,1,2,0:T(8,128)(2,1)}, bf16[6,48,1,32]{3,1,2,0:T(8,128)(2,1)}, u32[]{:S(2)}, u32[]{:S(2)}) collective-permute-start(bf16[6,48,1,32]{3,1,2,0:T(8,128)(2,1)} %get-tuple-element.46), channel_id=1, source_target_pairs={{0,16},{16,32},{32,48},{48,64},{64,80},{80,96},{96,112},{112,128},... | collective-permute-start | bytes 55304 | tf_op jit(solution)/shard_map/ppermute | solution.py:181
  7.3 1.3 %collective-permute-start.1 = (bf16[6,48,1,32]{3,1,2,0:T(8,128)(2,1)}, bf16[6,48,1,32]{3,1,2,0:T(8,128)(2,1)}, u32[]{:S(2)}, u32[]{:S(2)}) collective-permute-start(bf16[6,48,1,32]{3,1,2,0:T(8,128)(2,1)} %get-tuple-element.47), channel_id=1, source_target_pairs={{16,0},{32,16},{48,32},{64,48},{80,64},{96,80},{112,96},{128,112},... | collective-permute-start | bytes 55304 | tf_op jit(solution)/shard_map/ppermute | solution.py:182
  8.6 0.2 convert_reduce_fusion
  8.8 0.2 copy.22
  9.1 0.1 reduce_sum.61
  9.4 0.3 multiply_reduce_fusion
  9.8 0.1 reduce_sum.64
  9.9 0.2 scatter.9.x_ref
  10.1 0.6 copy-done.3
  10.7 23.0 %shard_map.64 = f32[32,8,128]{2,1,0:T(8,128)} custom-call(f32[8,128]{1,0:T(8,128)} %copy-done.3), custom_call_target="tpu_custom_call" | custom-call | tf_op jit(solution)/shard_map/pallas_call | solution.py:70
  33.7 1.0 %slice_reduce_fusion.1 = (f32[2]{0:T(128)S(1)}, f32[2]{0:T(128)S(1)}, f32[32,1,2]{2,1,0:T(1,128)S(1)}) fusion(f32[32,8,128]{2,1,0:T(8,128)} %shard_map.64), kind=kLoop, calls=%fused_computation.29 | loop fusion | flops 124 | bytes 784 | tf_op jit(solution)/shard_map/reduce_sum | solution.py:209
  35.0 0.2 fusion.7
  35.4 0.3 multiply_convert_fusion
  35.7 0.8 fusion.11
  36.5 0.7 slice.142
  37.3 0.7 slice.144
  38.0 0.9 %multiply_convert_fusion.2 = (bf16[4,48,1,32]{3,1,2,0:T(8,128)(2,1)S(1)}, bf16[4,48,1,32]{3,1,2,0:T(8,128)(2,1)S(1)}) fusion(bf16[6,48,1,32]{3,1,2,0:T(8,128)(2,1)} %collective-permute-done, f32[32]{0:T(128)S(1)} %copy-done.4, f32[32]{0:T(128)S(1)} %copy-done.5, f32[32]{0:T(128)S(1)} %mul.88, f32[32]{0:T(128)S(1)} %sub.61, ...), kind=kLoop, calls=%fused_computation.16 | loop fusion | flops 122880 | bytes 49664 | tf_op jit(solution)/shard_map/convert_element_type | solution.py:221
  39.0 0.4 fusion.1
  39.4 3.0 %fusion.10 = (bf16[6,10,48,32]{3,2,1,0:T(8,128)(2,1)S(1)}, bf16[6,10,48,32]{3,2,1,0:T(8,128)(2,1)}, bf16[6,10,48,32]{3,2,1,0:T(8,128)(2,1)}, bf16[6,10,48,32]{3,...) fusion(bf16[6,12,50,32]{3,2,1,0:T(8,128)(2,1)S(1)} %fusion.1), kind=kLoop, calls=%fused_computation.31 | loop fusion | bytes 3317760 | tf_op jit(solution)/shard_map/slice | solution.py:235
  42.4 7.1 %concatenate.43 = bf16[6,10,48,288]{3,2,1,0:T(8,128)(2,1)S(1)} concatenate(bf16[6,10,48,32]{3,2,1,0:T(8,128)(2,1)} %get-tuple-element.42, bf16[6,10,48,32]{3,2,1,0:T(8,128)(2,1)} %get-tuple-element.41, bf16[6,10,48,32]{3,2,1,0:T(8,128)(2,1)} %get-tuple-element.40, bf16[6,10,48,32]{3,2,1,0:T(8,128)(2,1)} %get-tuple-element.39, bf16[6,10,48,32]{3,2,1,0:T(8,128)(2,1)} %get-tuple-element.38, ...), dimensions={3} | concatenate | bytes 3317760 | tf_op jit(solution)/shard_map/concatenate | solution.py:233
  49.5 0.4 fusion.9
  49.9 0.6 copy-done.1
  50.4 1.3 %fusion.13 = f32[1920,512]{0,1:T(8,128)S(1)} fusion(bf16[1920,288]{1,0:T(8,128)(2,1)S(1)} %bitcast.33, bf16[288,512]{1,0:T(8,128)(2,1)S(1)} %bitcast.38), kind=kOutput, calls=%fused_computation.34 | convolution fusion | flops 566231040 | bytes 5332992 | tf_op jit(solution)/shard_map/dot_general | solution.py:252
  51.7 1.3 %fusion.12 = f32[1920,512]{0,1:T(8,128)S(1)} fusion(bf16[1920,288]{1,0:T(8,128)(2,1)S(1)} %bitcast.32, bf16[288,512]{1,0:T(8,128)(2,1)S(1)} %bitcast.37), kind=kOutput, calls=%fused_computation.33 | convolution fusion | flops 566231040 | bytes 5332992 | tf_op jit(solution)/shard_map/dot_general | solution.py:252
  53.0 1.5 %add_add_fusion = f32[1920,512]{0,1:T(8,128)S(1)} fusion(f32[1920,512]{0,1:T(8,128)S(1)} %fusion.12, f32[1920,512]{0,1:T(8,128)S(1)} %fusion.13, bf16[1920,288]{1,0:T(8,128)(2,1)S(1)} %bitcast.34, bf16[288,512]{1,0:T(8,128)(2,1)S(1)} %bitcast.36), kind=kOutput, calls=%fused_computation | convolution fusion | flops 568197120 | bytes 13197312 | tf_op jit(solution)/shard_map/dot_general | solution.py:252
  54.5 32.2 %shard_map.65 = f32[32,1920]{1,0:T(8,128)S(1)} custom-call(f32[4,2,2,32,1920]{4,3,2,1,0:T(8,128)S(1)} %bitcast.31), custom_call_target="tpu_custom_call" | custom-call | tf_op jit(solution)/shard_map/pallas_call | solution.py:157
  86.7 0.1 fusion.5
  86.8 0.5 reshape.207
  87.3 0.9 %copy.24 = bf16[4,48,10,32]{1,3,2,0:T(8,128)(2,1)} copy(bf16[4,48,10,32]{1,2,0,3:T(8,128)(2,1)S(1)} %bitcast.35) | data formatting | bytes 245760 | tf_op jit(solution)/shard_map/transpose | solution.py:258
  (28 shorter events, 0.8 us)
Async XLA Ops:
  0.0 8.6 %copy-start = (bf16[4,48,10,32]{1,3,2,0:T(8,128)(2,1)S(1)}, bf16[4,48,10,32]{1,3,2,0:T(8,128)(2,1)}, u32[]{:S(2)}) copy-start(bf16[4,48,10,32]{1,3,2,0:T(8,128)(2,1)} %param.10) | copy-start | bytes 368644
  1.1 34.2 %copy-start.4 = (f32[32]{0:T(128)S(1)}, f32[32]{0:T(128)}, u32[]{:S(2)}) copy-start(f32[32]{0:T(128)} %param.13) | copy-start | bytes 388
  1.1 34.2 %copy-start.5 = (f32[32]{0:T(128)S(1)}, f32[32]{0:T(128)}, u32[]{:S(2)}) copy-start(f32[32]{0:T(128)} %param.12) | copy-start | bytes 388
  3.1 32.6 %copy-start.2 = (bf16[3,3,3,32,512]{4,3,2,1,0:T(8,128)(2,1)S(1)}, bf16[3,3,3,32,512]{4,3,2,1,0:T(8,128)(2,1)}, u32[]{:S(2)}) copy-start(bf16[3,3,3,32,512]{4,3,2,1,0:T(8,128)(2,1)} %param.14) | copy-start | bytes 2654212
  3.1 33.4 %collective-permute-start = (bf16[6,48,1,32]{3,1,2,0:T(8,128)(2,1)}, bf16[6,48,1,32]{3,1,2,0:T(8,128)(2,1)}, u32[]{:S(2)}, u32[]{:S(2)}) collective-permute-start(bf16[6,48,1,32]{3,1,2,0:T(8,128)(2,1)} %get-tuple-element.46), channel_id=1, source_target_pairs={{0,16},{16,32},{32,48},{48,64},{64,80},{80,96},{96,112},{112,128},... | collective-permute-start | bytes 55304 | tf_op jit(solution)/shard_map/ppermute | solution.py:181
  7.3 30.0 %collective-permute-start.1 = (bf16[6,48,1,32]{3,1,2,0:T(8,128)(2,1)}, bf16[6,48,1,32]{3,1,2,0:T(8,128)(2,1)}, u32[]{:S(2)}, u32[]{:S(2)}) collective-permute-start(bf16[6,48,1,32]{3,1,2,0:T(8,128)(2,1)} %get-tuple-element.47), channel_id=1, source_target_pairs={{16,0},{32,16},{48,32},{64,48},{80,64},{96,80},{112,96},{128,112},... | collective-permute-start | bytes 55304 | tf_op jit(solution)/shard_map/ppermute | solution.py:182
  10.1 0.6 copy-start.3
  49.5 1.0 %copy-start.1 = (bf16[1,3,3,32,512]{4,3,2,1,0:T(8,128)(2,1)S(1)}, bf16[1,3,3,32,512]{4,3,2,1,0:T(8,128)(2,1)}, u32[]{:S(2)}) copy-start(bf16[1,3,3,32,512]{4,3,2,1,0:T(8,128)(2,1)} %get-tuple-element.45) | copy-start | bytes 884740
  54.5 32.2 %copy-start.6 = (f32[32]{0:T(128)S(1)}, f32[32]{0:T(128)}, u32[]{:S(2)}) copy-start(f32[32]{0:T(128)} %param.15) | copy-start | bytes 388

commit v8 on v7

--- a/solution.py
+++ b/solution.py
@@ -81,14 +81,16 @@
     )(tile)
 
 
-def scatter_kernel(x_ref, o_ref, recv1, acc1, own, recv2, acc2, recv3, send_sem, recv_sem):
+def scatter_kernel(nchunk, x_ref, o_ref, recv1, acc1, own, recv2, acc2, recv3,
+                   sem1s, sem1r, sem2s, sem2r, sem3s, sem3r):
     sp = lax.axis_index("space")
     c = lax.axis_index("chan")
     core = c % 2
     yh = (c // 2) % 2
     xx = c // 4
     nx, nyh = x_ref.shape[0], x_ref.shape[1]
-    nfirst = nx * nyh
+    width = x_ref.shape[-1] // nchunk
+    f32, bf16 = jnp.float32, jnp.bfloat16
 
     def dev(x_, yh_, core_):
         return (sp, x_ * 4 + yh_ * 2 + core_)
@@ -101,73 +103,97 @@
         pl.semaphore_signal(barrier, 1, device_id=p, device_id_type=MESH)
     pl.semaphore_wait(barrier, len(peers))
 
+    def cols(q):
+        return pl.ds(q * width, width)
+
     firsts = []
-    for i in range(nx):
+    for q in range(nchunk):
+        for i in range(nx):
+            for j in range(nyh):
+                n = (q * nx + i) * nyh + j
+                cp = pltpu.make_async_remote_copy(
+                    src_ref=x_ref.at[i, j, 1 - core, :, cols(q)], dst_ref=recv1.at[q, i, j],
+                    send_sem=sem1s.at[n], recv_sem=sem1r.at[n],
+                    device_id=peers[0], device_id_type=MESH)
+                cp.start()
+                firsts.append(cp)
+
+    def second(q):
+        for cp in firsts[q * nx * nyh : (q + 1) * nx * nyh]:
+            cp.wait()
+        sends = []
+        for k in range(1, nx):
+            dest = lax.rem(xx + k, nx)
+            for j in range(nyh):
+                acc1[q, dest, j] = (x_ref[dest, j, core, :, cols(q)] + recv1[q, dest, j]).astype(bf16)
+            slot = nx - 1 - k
+            cp = pltpu.make_async_remote_copy(
+                src_ref=acc1.at[q, dest], dst_ref=recv2.at[q, slot],
+                send_sem=sem2s.at[q * (nx - 1) + k - 1], recv_sem=sem2r.at[q * (nx - 1) + slot],
+                device_id=peers[k], device_id_type=MESH)
+            cp.start()
+            sends.append(cp)
         for j in range(nyh):
-            cp = pltpu.make_async_remote_copy(
-                src_ref=x_ref.at[i, j, 1 - core], dst_ref=recv1.at[i, j],
-                send_sem=send_sem.at[i * nyh + j], recv_sem=recv_sem.at[i * nyh + j],
-                device_id=peers[0], device_id_type=MESH)
-            cp.start()
-            firsts.append(cp)
-    for cp in firsts:
+            own[q, j] = x_ref[xx, j, core, :, cols(q)] + recv1[q, xx, j]
+        return sends
+
+    def third(q):
+        for slot in range(nx - 1):
+            pltpu.make_async_remote_copy(
+                src_ref=acc1.at[q, xx], dst_ref=recv2.at[q, slot],
+                send_sem=sem2s.at[q * (nx - 1) + slot], recv_sem=sem2r.at[q * (nx - 1) + slot],
+                device_id=peers[0], device_id_type=MESH).wait_recv()
+        other = 1 - yh
+        total = own[q, other]
+        for slot in range(nx - 1):
+            total = total + recv2[q, slot, other].astype(f32)
+        acc2[q] = total.astype(bf16)
+        cp = pltpu.make_async_remote_copy(
+            src_ref=acc2.at[q], dst_ref=recv3.at[q], send_sem=sem3s.at[q],
+            recv_sem=sem3r.at[q], device_id=peers[nx], device_id_type=MESH)
+        cp.start()
+        total = own[q, yh]
+        for slot in range(nx - 1):
+            total = total + recv2[q, slot, yh].astype(f32)
+        own[q, yh] = total
+        return cp
+
+    seconds, lasts = [], []
+    for q in range(nchunk):
+        seconds.append(second(q))
+        if q >= 1:
+            lasts.append(third(q - 1))
+    lasts.append(third(nchunk - 1))
+    for sends in seconds:
+        for cp in sends:
+            cp.wait_send()
+    for q, cp in enumerate(lasts):
         cp.wait()
-
-    def fold_first(dest, dst):
-        for j in range(nyh):
-            dst[j] = (x_ref[dest, j, core] + recv1[dest, j]).astype(dst.dtype)
-
-    sends = []
-    for k in range(1, nx):
-        dest = lax.rem(xx + k, nx)
-        fold_first(dest, acc1.at[dest])
-        slot = nx - 1 - k
-        cp = pltpu.make_async_remote_copy(
-            src_ref=acc1.at[dest], dst_ref=recv2.at[slot], send_sem=send_sem.at[nfirst + k - 1],
-            recv_sem=recv_sem.at[nfirst + slot], device_id=peers[k], device_id_type=MESH)
-        cp.start()
-        sends.append(cp)
-    fold_first(xx, own)
-    for slot in range(nx - 1):
-        pltpu.make_async_remote_copy(
-            src_ref=acc1.at[xx], dst_ref=recv2.at[slot], send_sem=send_sem.at[nfirst + slot],
-            recv_sem=recv_sem.at[nfirst + slot], device_id=peers[0], device_id_type=MESH).wait_recv()
-    other = 1 - yh
-    total = own[other]
-    for slot in range(nx - 1):
-        total = total + recv2[slot, other].astype(jnp.float32)
-    acc2[...] = total.astype(acc2.dtype)
-    last_sem = nfirst + nx - 1
-    last = pltpu.make_async_remote_copy(
-        src_ref=acc2, dst_ref=recv3, send_sem=send_sem.at[last_sem],
-        recv_sem=recv_sem.at[last_sem], device_id=peers[nx], device_id_type=MESH)
-    last.start()
-    total = own[yh]
-    for slot in range(nx - 1):
-        total = total + recv2[slot, yh].astype(jnp.float32)
-    for cp in sends:
-        cp.wait_send()
-    last.wait()
-    o_ref[...] = total + recv3[...].astype(jnp.float32)
-
-
-def scatter_chan(parts):
+        o_ref[:, cols(q)] = own[q, yh] + recv3[q].astype(f32)
+
+
+def scatter_chan(parts, nchunk=3):
     nx, nyh, ncore, rows, cells = parts.shape
+    width = cells // nchunk
     f32, bf16 = jnp.float32, jnp.bfloat16
     return pl.pallas_call(
-        scatter_kernel,
+        functools.partial(scatter_kernel, nchunk),
         out_shape=jax.ShapeDtypeStruct((rows, cells), f32),
         in_specs=[pl.BlockSpec(memory_space=pltpu.VMEM)],
         out_specs=pl.BlockSpec(memory_space=pltpu.VMEM),
         scratch_shapes=[
-            pltpu.VMEM((nx, nyh, rows, cells), f32),
-            pltpu.VMEM((nx, nyh, rows, cells), bf16),
-            pltpu.VMEM((nyh, rows, cells), f32),
-            pltpu.VMEM((nx - 1, nyh, rows, cells), bf16),
-            pltpu.VMEM((rows, cells), bf16),
-            pltpu.VMEM((rows, cells), bf16),
-            pltpu.SemaphoreType.DMA((nx * nyh + nx,)),
-            pltpu.SemaphoreType.DMA((nx * nyh + nx,)),
+            pltpu.VMEM((nchunk, nx, nyh, rows, width), f32),
+            pltpu.VMEM((nchunk, nx, nyh, rows, width), bf16),
+            pltpu.VMEM((nchunk, nyh, rows, width), f32),
+            pltpu.VMEM((nchunk, nx - 1, nyh, rows, width), bf16),
+            pltpu.VMEM((nchunk, rows, width), bf16),
+            pltpu.VMEM((nchunk, rows, width), bf16),
+            pltpu.SemaphoreType.DMA((nchunk * nx * nyh,)),
+            pltpu.SemaphoreType.DMA((nchunk * nx * nyh,)),
+            pltpu.SemaphoreType.DMA((nchunk * (nx - 1),)),
+            pltpu.SemaphoreType.DMA((nchunk * (nx - 1),)),
+            pltpu.SemaphoreType.DMA((nchunk,)),
+            pltpu.SemaphoreType.DMA((nchunk,)),
         ],
         compiler_params=pltpu.CompilerParams(
             collective_id=1, has_side_effects=True, vmem_limit_bytes=48 * 1024 * 1024),

time: 89 us -> 83.7 us (0.940)
  Pallas kernels: 55.2 us -> 49.6 us
    pallas_call x1, Pallas kernels: 32.2 us -> 26.6 us  [scatter_chan(): pl.pallas_call(functools.partial(scatter_kernel, nchunk), out_shape=jax.S...]
  transfers between devices with their start and end apart: 2 -> 2, of which waited for: 0 -> 0; matrix products, arithmetic and copies ran while one was open for 6% -> 6% of each run, Pallas kernels for 26% -> 28%
where the time goes in v8:
time: 83.7 us; the launch traced here: 82.7 us
  Pallas kernels  49.6 us (59%)
  local copies, waits for them, and re-layouts  18.8 us (22%)
  starting transfers between devices  5.51 us (7%)
  other arithmetic  4.46 us (5%)
  matrix products  4.06 us (5%)
    pallas_call x1, Pallas kernels, scatter_chan(): pl.pallas_call(functools.partial(scatter_kernel, nchunk), out_shape=jax.S...  26.6 us
    pallas_call x1, Pallas kernels, gather_space(): pl.pallas_call(functools.partial(gather_kernel, n), out_shape=jax.ShapeDt...  23 us
    concatenate x1, local copies, waits for them, and re-layouts, local(): jnp.concatenate([bordered[:, col_tap:col_tap + col_count, row_tap:row_tap...  7.08 us
    ppermute x1, starting transfers between devices, edge_exchange(): before = lax.ppermute(edges_last, axis, up)  4.23 us
    dot_general x3, matrix products, local(): lax.dot_general(tap_weight, window, (((0,), (1,)), ((), ())), preferred_e...  4.06 us
    unnamed x16, local copies, waits for them, and re-layouts  3.53 us
    slice x1, local copies, waits for them, and re-layouts, local(): bordered[:, col_tap:col_tap + col_count, row_tap:row_tap + row_count, :]  2.96 us
  transfers between devices with their start and end apart: 2, of which 0 were waited for; matrix products, arithmetic and copies ran while one was open for 6% of the time, Pallas kernels for 28%

profile of v8, /device:TPU:6, one launch (start us, length us, event | category | flops | bytes accessed | tf_op | source)
XLA Modules:
  0.0 82.7 jit_solution(4826185751198290278)
XLA Ops:
  0.0 1.1 %copy.19 = bf16[2,48,10,32]{3,1,2,0:T(8,128)(2,1)S(1)} copy(bf16[2,48,10,32]{1,3,2,0:T(8,128)(2,1)} %param.11) | data formatting | bytes 122880 | tf_op args[1]
  1.2 1.2 %copy.20 = bf16[4,48,10,32]{3,1,2,0:T(8,128)(2,1)S(1)} copy(bf16[4,48,10,32]{1,3,2,0:T(8,128)(2,1)} %param.10) | data formatting | bytes 245760 | tf_op args[0]
  2.4 0.7 pad_maximum_fusion.1
  3.1 4.2 %collective-permute-start = (bf16[6,48,1,32]{3,1,2,0:T(8,128)(2,1)}, bf16[6,48,1,32]{3,1,2,0:T(8,128)(2,1)}, u32[]{:S(2)}, u32[]{:S(2)}) collective-permute-start(bf16[6,48,1,32]{3,1,2,0:T(8,128)(2,1)} %get-tuple-element.46), channel_id=1, source_target_pairs={{0,16},{16,32},{32,48},{48,64},{64,80},{80,96},{96,112},{112,128},... | collective-permute-start | bytes 55304 | tf_op jit(solution)/shard_map/ppermute | solution.py:207
  7.3 1.3 %collective-permute-start.1 = (bf16[6,48,1,32]{3,1,2,0:T(8,128)(2,1)}, bf16[6,48,1,32]{3,1,2,0:T(8,128)(2,1)}, u32[]{:S(2)}, u32[]{:S(2)}) collective-permute-start(bf16[6,48,1,32]{3,1,2,0:T(8,128)(2,1)} %get-tuple-element.47), channel_id=1, source_target_pairs={{16,0},{32,16},{48,32},{64,48},{80,64},{96,80},{112,96},{128,112},... | collective-permute-start | bytes 55304 | tf_op jit(solution)/shard_map/ppermute | solution.py:208
  8.6 0.2 convert_reduce_fusion
  8.8 0.2 copy.22
  9.1 0.1 reduce_sum.61
  9.4 0.3 multiply_reduce_fusion
  9.8 0.1 reduce_sum.64
  9.9 0.2 scatter.9.x_ref
  10.1 0.6 copy-done.3
  10.7 23.0 %shard_map.64 = f32[32,8,128]{2,1,0:T(8,128)} custom-call(f32[8,128]{1,0:T(8,128)} %copy-done.3), custom_call_target="tpu_custom_call" | custom-call | tf_op jit(solution)/shard_map/pallas_call | solution.py:70
  33.7 1.0 %slice_reduce_fusion.1 = (f32[2]{0:T(128)S(1)}, f32[2]{0:T(128)S(1)}, f32[32,1,2]{2,1,0:T(1,128)S(1)}) fusion(f32[32,8,128]{2,1,0:T(8,128)} %shard_map.64), kind=kLoop, calls=%fused_computation.29 | loop fusion | flops 124 | bytes 784 | tf_op jit(solution)/shard_map/reduce_sum | solution.py:235
  35.0 0.2 fusion.7
  35.4 0.3 multiply_convert_fusion
  35.7 0.8 fusion.11
  36.5 0.7 slice.142
  37.3 0.7 slice.144
  38.0 0.9 %multiply_convert_fusion.2 = (bf16[4,48,1,32]{3,1,2,0:T(8,128)(2,1)S(1)}, bf16[4,48,1,32]{3,1,2,0:T(8,128)(2,1)S(1)}) fusion(bf16[6,48,1,32]{3,1,2,0:T(8,128)(2,1)} %collective-permute-done, f32[32]{0:T(128)S(1)} %copy-done.4, f32[32]{0:T(128)S(1)} %copy-done.5, f32[32]{0:T(128)S(1)} %mul.88, f32[32]{0:T(128)S(1)} %sub.61, ...), kind=kLoop, calls=%fused_computation.16 | loop fusion | flops 122880 | bytes 49664 | tf_op jit(solution)/shard_map/convert_element_type | solution.py:247
  39.0 0.4 fusion.1
  39.4 3.0 %fusion.10 = (bf16[6,10,48,32]{3,2,1,0:T(8,128)(2,1)S(1)}, bf16[6,10,48,32]{3,2,1,0:T(8,128)(2,1)}, bf16[6,10,48,32]{3,2,1,0:T(8,128)(2,1)}, bf16[6,10,48,32]{3,...) fusion(bf16[6,12,50,32]{3,2,1,0:T(8,128)(2,1)S(1)} %fusion.1), kind=kLoop, calls=%fused_computation.31 | loop fusion | bytes 3317760 | tf_op jit(solution)/shard_map/slice | solution.py:261
  42.4 7.1 %concatenate.43 = bf16[6,10,48,288]{3,2,1,0:T(8,128)(2,1)S(1)} concatenate(bf16[6,10,48,32]{3,2,1,0:T(8,128)(2,1)} %get-tuple-element.42, bf16[6,10,48,32]{3,2,1,0:T(8,128)(2,1)} %get-tuple-element.41, bf16[6,10,48,32]{3,2,1,0:T(8,128)(2,1)} %get-tuple-element.40, bf16[6,10,48,32]{3,2,1,0:T(8,128)(2,1)} %get-tuple-element.39, bf16[6,10,48,32]{3,2,1,0:T(8,128)(2,1)} %get-tuple-element.38, ...), dimensions={3} | concatenate | bytes 3317760 | tf_op jit(solution)/shard_map/concatenate | solution.py:259
  49.5 0.4 fusion.9
  49.9 0.6 copy-done.1
  50.4 1.3 %fusion.13 = f32[1920,512]{0,1:T(8,128)S(1)} fusion(bf16[1920,288]{1,0:T(8,128)(2,1)S(1)} %bitcast.33, bf16[288,512]{1,0:T(8,128)(2,1)S(1)} %bitcast.38), kind=kOutput, calls=%fused_computation.34 | convolution fusion | flops 566231040 | bytes 5332992 | tf_op jit(solution)/shard_map/dot_general | solution.py:278
  51.7 1.3 %fusion.12 = f32[1920,512]{0,1:T(8,128)S(1)} fusion(bf16[1920,288]{1,0:T(8,128)(2,1)S(1)} %bitcast.32, bf16[288,512]{1,0:T(8,128)(2,1)S(1)} %bitcast.37), kind=kOutput, calls=%fused_computation.33 | convolution fusion | flops 566231040 | bytes 5332992 | tf_op jit(solution)/shard_map/dot_general | solution.py:278
  53.0 1.5 %add_add_fusion = f32[1920,512]{0,1:T(8,128)S(1)} fusion(f32[1920,512]{0,1:T(8,128)S(1)} %fusion.12, f32[1920,512]{0,1:T(8,128)S(1)} %fusion.13, bf16[1920,288]{1,0:T(8,128)(2,1)S(1)} %bitcast.34, bf16[288,512]{1,0:T(8,128)(2,1)S(1)} %bitcast.36), kind=kOutput, calls=%fused_computation | convolution fusion | flops 568197120 | bytes 13197312 | tf_op jit(solution)/shard_map/dot_general | solution.py:278
  54.5 26.6 %shard_map.65 = f32[32,1920]{1,0:T(8,128)S(1)} custom-call(f32[4,2,2,32,1920]{4,3,2,1,0:T(8,128)S(1)} %bitcast.31), custom_call_target="tpu_custom_call" | custom-call | tf_op jit(solution)/shard_map/pallas_call | solution.py:179
  81.1 0.1 fusion.5
  81.2 0.5 reshape.207
  81.7 0.9 %copy.24 = bf16[4,48,10,32]{1,3,2,0:T(8,128)(2,1)} copy(bf16[4,48,10,32]{1,2,0,3:T(8,128)(2,1)S(1)} %bitcast.35) | data formatting | bytes 245760 | tf_op jit(solution)/shard_map/transpose | solution.py:284
  (28 shorter events, 0.8 us)
Async XLA Ops:
  0.0 8.6 %copy-start = (bf16[4,48,10,32]{1,3,2,0:T(8,128)(2,1)S(1)}, bf16[4,48,10,32]{1,3,2,0:T(8,128)(2,1)}, u32[]{:S(2)}) copy-start(bf16[4,48,10,32]{1,3,2,0:T(8,128)(2,1)} %param.10) | copy-start | bytes 368644
  1.1 34.2 %copy-start.4 = (f32[32]{0:T(128)S(1)}, f32[32]{0:T(128)}, u32[]{:S(2)}) copy-start(f32[32]{0:T(128)} %param.13) | copy-start | bytes 388
  1.1 34.2 %copy-start.5 = (f32[32]{0:T(128)S(1)}, f32[32]{0:T(128)}, u32[]{:S(2)}) copy-start(f32[32]{0:T(128)} %param.12) | copy-start | bytes 388
  3.1 32.6 %copy-start.2 = (bf16[3,3,3,32,512]{4,3,2,1,0:T(8,128)(2,1)S(1)}, bf16[3,3,3,32,512]{4,3,2,1,0:T(8,128)(2,1)}, u32[]{:S(2)}) copy-start(bf16[3,3,3,32,512]{4,3,2,1,0:T(8,128)(2,1)} %param.14) | copy-start | bytes 2654212
  3.1 33.4 %collective-permute-start = (bf16[6,48,1,32]{3,1,2,0:T(8,128)(2,1)}, bf16[6,48,1,32]{3,1,2,0:T(8,128)(2,1)}, u32[]{:S(2)}, u32[]{:S(2)}) collective-permute-start(bf16[6,48,1,32]{3,1,2,0:T(8,128)(2,1)} %get-tuple-element.46), channel_id=1, source_target_pairs={{0,16},{16,32},{32,48},{48,64},{64,80},{80,96},{96,112},{112,128},... | collective-permute-start | bytes 55304 | tf_op jit(solution)/shard_map/ppermute | solution.py:207
  7.3 30.0 %collective-permute-start.1 = (bf16[6,48,1,32]{3,1,2,0:T(8,128)(2,1)}, bf16[6,48,1,32]{3,1,2,0:T(8,128)(2,1)}, u32[]{:S(2)}, u32[]{:S(2)}) collective-permute-start(bf16[6,48,1,32]{3,1,2,0:T(8,128)(2,1)} %get-tuple-element.47), channel_id=1, source_target_pairs={{16,0},{32,16},{48,32},{64,48},{80,64},{96,80},{112,96},{128,112},... | collective-permute-start | bytes 55304 | tf_op jit(solution)/shard_map/ppermute | solution.py:208
  10.1 0.6 copy-start.3
  49.5 1.0 %copy-start.1 = (bf16[1,3,3,32,512]{4,3,2,1,0:T(8,128)(2,1)S(1)}, bf16[1,3,3,32,512]{4,3,2,1,0:T(8,128)(2,1)}, u32[]{:S(2)}) copy-start(bf16[1,3,3,32,512]{4,3,2,1,0:T(8,128)(2,1)} %get-tuple-element.45) | copy-start | bytes 884740
  54.5 26.6 %copy-start.6 = (f32[32]{0:T(128)S(1)}, f32[32]{0:T(128)}, u32[]{:S(2)}) copy-start(f32[32]{0:T(128)} %param.15) | copy-start | bytes 388

commit v9 on v8

--- a/solution.py
+++ b/solution.py
@@ -172,7 +172,7 @@
         o_ref[:, cols(q)] = own[q, yh] + recv3[q].astype(f32)
 
 
-def scatter_chan(parts, nchunk=3):
+def scatter_chan(parts, nchunk=5):
     nx, nyh, ncore, rows, cells = parts.shape
     width = cells // nchunk
     f32, bf16 = jnp.float32, jnp.bfloat16

time: 83.7 us -> 84.9 us (1.014)
  Pallas kernels: 49.6 us -> 50.6 us
    pallas_call x1, Pallas kernels: 26.6 us -> 27.6 us  [scatter_chan(): pl.pallas_call(functools.partial(scatter_kernel, nchunk), out_shape=jax.S...]
where the time goes in v9:
time: 84.9 us; the launch traced here: 83.7 us
  Pallas kernels  50.6 us (60%)
  local copies, waits for them, and re-layouts  18.8 us (22%)
  starting transfers between devices  5.51 us (6%)
  other arithmetic  4.46 us (5%)
  matrix products  4.06 us (5%)
    pallas_call x1, Pallas kernels, scatter_chan(): pl.pallas_call(functools.partial(scatter_kernel, nchunk), out_shape=jax.S...  27.6 us
    pallas_call x1, Pallas kernels, gather_space(): pl.pallas_call(functools.partial(gather_kernel, n), out_shape=jax.ShapeDt...  23 us
    concatenate x1, local copies, waits for them, and re-layouts, local(): jnp.concatenate([bordered[:, col_tap:col_tap + col_count, row_tap:row_tap...  7.08 us
    ppermute x1, starting transfers between devices, edge_exchange(): before = lax.ppermute(edges_last, axis, up)  4.23 us
    dot_general x3, matrix products, local(): lax.dot_general(tap_weight, window, (((0,), (1,)), ((), ())), preferred_e...  4.06 us
    unnamed x16, local copies, waits for them, and re-layouts  3.53 us
    slice x1, local copies, waits for them, and re-layouts, local(): bordered[:, col_tap:col_tap + col_count, row_tap:row_tap + row_count, :]  2.96 us
  transfers between devices with their start and end apart: 2, of which 0 were waited for; matrix products, arithmetic and copies ran while one was open for 6% of the time, Pallas kernels for 28%

profile of v9, /device:TPU:6, one launch (start us, length us, event | category | flops | bytes accessed | tf_op | source)
XLA Modules:
  0.0 83.7 jit_solution(12173779784893142650)
XLA Ops:
  0.0 1.1 %copy.19 = bf16[2,48,10,32]{3,1,2,0:T(8,128)(2,1)S(1)} copy(bf16[2,48,10,32]{1,3,2,0:T(8,128)(2,1)} %param.11) | data formatting | bytes 122880 | tf_op args[1]
  1.2 1.2 %copy.20 = bf16[4,48,10,32]{3,1,2,0:T(8,128)(2,1)S(1)} copy(bf16[4,48,10,32]{1,3,2,0:T(8,128)(2,1)} %param.10) | data formatting | bytes 245760 | tf_op args[0]
  2.4 0.7 pad_maximum_fusion.1
  3.1 4.2 %collective-permute-start = (bf16[6,48,1,32]{3,1,2,0:T(8,128)(2,1)}, bf16[6,48,1,32]{3,1,2,0:T(8,128)(2,1)}, u32[]{:S(2)}, u32[]{:S(2)}) collective-permute-start(bf16[6,48,1,32]{3,1,2,0:T(8,128)(2,1)} %get-tuple-element.46), channel_id=1, source_target_pairs={{0,16},{16,32},{32,48},{48,64},{64,80},{80,96},{96,112},{112,128},... | collective-permute-start | bytes 55304 | tf_op jit(solution)/shard_map/ppermute | solution.py:207
  7.3 1.3 %collective-permute-start.1 = (bf16[6,48,1,32]{3,1,2,0:T(8,128)(2,1)}, bf16[6,48,1,32]{3,1,2,0:T(8,128)(2,1)}, u32[]{:S(2)}, u32[]{:S(2)}) collective-permute-start(bf16[6,48,1,32]{3,1,2,0:T(8,128)(2,1)} %get-tuple-element.47), channel_id=1, source_target_pairs={{16,0},{32,16},{48,32},{64,48},{80,64},{96,80},{112,96},{128,112},... | collective-permute-start | bytes 55304 | tf_op jit(solution)/shard_map/ppermute | solution.py:208
  8.6 0.2 convert_reduce_fusion
  8.8 0.2 copy.22
  9.1 0.1 reduce_sum.61
  9.4 0.3 multiply_reduce_fusion
  9.8 0.1 reduce_sum.64
  9.9 0.2 scatter.9.x_ref
  10.1 0.6 copy-done.3
  10.7 23.0 %shard_map.64 = f32[32,8,128]{2,1,0:T(8,128)} custom-call(f32[8,128]{1,0:T(8,128)} %copy-done.3), custom_call_target="tpu_custom_call" | custom-call | tf_op jit(solution)/shard_map/pallas_call | solution.py:70
  33.7 1.0 %slice_reduce_fusion.1 = (f32[2]{0:T(128)S(1)}, f32[2]{0:T(128)S(1)}, f32[32,1,2]{2,1,0:T(1,128)S(1)}) fusion(f32[32,8,128]{2,1,0:T(8,128)} %shard_map.64), kind=kLoop, calls=%fused_computation.29 | loop fusion | flops 124 | bytes 784 | tf_op jit(solution)/shard_map/reduce_sum | solution.py:235
  35.0 0.2 fusion.7
  35.4 0.3 multiply_convert_fusion
  35.7 0.8 fusion.11
  36.5 0.7 slice.142
  37.3 0.7 slice.144
  38.0 0.9 %multiply_convert_fusion.2 = (bf16[4,48,1,32]{3,1,2,0:T(8,128)(2,1)S(1)}, bf16[4,48,1,32]{3,1,2,0:T(8,128)(2,1)S(1)}) fusion(bf16[6,48,1,32]{3,1,2,0:T(8,128)(2,1)} %collective-permute-done, f32[32]{0:T(128)S(1)} %copy-done.4, f32[32]{0:T(128)S(1)} %copy-done.5, f32[32]{0:T(128)S(1)} %mul.88, f32[32]{0:T(128)S(1)} %sub.61, ...), kind=kLoop, calls=%fused_computation.16 | loop fusion | flops 122880 | bytes 49664 | tf_op jit(solution)/shard_map/convert_element_type | solution.py:247
  39.0 0.4 fusion.1
  39.4 3.0 %fusion.10 = (bf16[6,10,48,32]{3,2,1,0:T(8,128)(2,1)S(1)}, bf16[6,10,48,32]{3,2,1,0:T(8,128)(2,1)}, bf16[6,10,48,32]{3,2,1,0:T(8,128)(2,1)}, bf16[6,10,48,32]{3,...) fusion(bf16[6,12,50,32]{3,2,1,0:T(8,128)(2,1)S(1)} %fusion.1), kind=kLoop, calls=%fused_computation.31 | loop fusion | bytes 3317760 | tf_op jit(solution)/shard_map/slice | solution.py:261
  42.4 7.1 %concatenate.43 = bf16[6,10,48,288]{3,2,1,0:T(8,128)(2,1)S(1)} concatenate(bf16[6,10,48,32]{3,2,1,0:T(8,128)(2,1)} %get-tuple-element.42, bf16[6,10,48,32]{3,2,1,0:T(8,128)(2,1)} %get-tuple-element.41, bf16[6,10,48,32]{3,2,1,0:T(8,128)(2,1)} %get-tuple-element.40, bf16[6,10,48,32]{3,2,1,0:T(8,128)(2,1)} %get-tuple-element.39, bf16[6,10,48,32]{3,2,1,0:T(8,128)(2,1)} %get-tuple-element.38, ...), dimensions={3} | concatenate | bytes 3317760 | tf_op jit(solution)/shard_map/concatenate | solution.py:259
  49.5 0.4 fusion.9
  49.9 0.6 copy-done.1
  50.4 1.3 %fusion.13 = f32[1920,512]{0,1:T(8,128)S(1)} fusion(bf16[1920,288]{1,0:T(8,128)(2,1)S(1)} %bitcast.33, bf16[288,512]{1,0:T(8,128)(2,1)S(1)} %bitcast.38), kind=kOutput, calls=%fused_computation.34 | convolution fusion | flops 566231040 | bytes 5332992 | tf_op jit(solution)/shard_map/dot_general | solution.py:278
  51.7 1.3 %fusion.12 = f32[1920,512]{0,1:T(8,128)S(1)} fusion(bf16[1920,288]{1,0:T(8,128)(2,1)S(1)} %bitcast.32, bf16[288,512]{1,0:T(8,128)(2,1)S(1)} %bitcast.37), kind=kOutput, calls=%fused_computation.33 | convolution fusion | flops 566231040 | bytes 5332992 | tf_op jit(solution)/shard_map/dot_general | solution.py:278
  53.0 1.5 %add_add_fusion = f32[1920,512]{0,1:T(8,128)S(1)} fusion(f32[1920,512]{0,1:T(8,128)S(1)} %fusion.12, f32[1920,512]{0,1:T(8,128)S(1)} %fusion.13, bf16[1920,288]{1,0:T(8,128)(2,1)S(1)} %bitcast.34, bf16[288,512]{1,0:T(8,128)(2,1)S(1)} %bitcast.36), kind=kOutput, calls=%fused_computation | convolution fusion | flops 568197120 | bytes 13197312 | tf_op jit(solution)/shard_map/dot_general | solution.py:278
  54.5 27.6 %shard_map.65 = f32[32,1920]{1,0:T(8,128)S(1)} custom-call(f32[4,2,2,32,1920]{4,3,2,1,0:T(8,128)S(1)} %bitcast.31), custom_call_target="tpu_custom_call" | custom-call | tf_op jit(solution)/shard_map/pallas_call | solution.py:179
  82.1 0.1 fusion.5
  82.2 0.5 reshape.207
  82.7 0.9 %copy.24 = bf16[4,48,10,32]{1,3,2,0:T(8,128)(2,1)} copy(bf16[4,48,10,32]{1,2,0,3:T(8,128)(2,1)S(1)} %bitcast.35) | data formatting | bytes 245760 | tf_op jit(solution)/shard_map/transpose | solution.py:284
  (28 shorter events, 0.8 us)
Async XLA Ops:
  0.0 8.6 %copy-start = (bf16[4,48,10,32]{1,3,2,0:T(8,128)(2,1)S(1)}, bf16[4,48,10,32]{1,3,2,0:T(8,128)(2,1)}, u32[]{:S(2)}) copy-start(bf16[4,48,10,32]{1,3,2,0:T(8,128)(2,1)} %param.10) | copy-start | bytes 368644
  1.1 34.2 %copy-start.4 = (f32[32]{0:T(128)S(1)}, f32[32]{0:T(128)}, u32[]{:S(2)}) copy-start(f32[32]{0:T(128)} %param.13) | copy-start | bytes 388
  1.1 34.2 %copy-start.5 = (f32[32]{0:T(128)S(1)}, f32[32]{0:T(128)}, u32[]{:S(2)}) copy-start(f32[32]{0:T(128)} %param.12) | copy-start | bytes 388
  3.1 32.6 %copy-start.2 = (bf16[3,3,3,32,512]{4,3,2,1,0:T(8,128)(2,1)S(1)}, bf16[3,3,3,32,512]{4,3,2,1,0:T(8,128)(2,1)}, u32[]{:S(2)}) copy-start(bf16[3,3,3,32,512]{4,3,2,1,0:T(8,128)(2,1)} %param.14) | copy-start | bytes 2654212
  3.1 33.4 %collective-permute-start = (bf16[6,48,1,32]{3,1,2,0:T(8,128)(2,1)}, bf16[6,48,1,32]{3,1,2,0:T(8,128)(2,1)}, u32[]{:S(2)}, u32[]{:S(2)}) collective-permute-start(bf16[6,48,1,32]{3,1,2,0:T(8,128)(2,1)} %get-tuple-element.46), channel_id=1, source_target_pairs={{0,16},{16,32},{32,48},{48,64},{64,80},{80,96},{96,112},{112,128},... | collective-permute-start | bytes 55304 | tf_op jit(solution)/shard_map/ppermute | solution.py:207
  7.3 30.0 %collective-permute-start.1 = (bf16[6,48,1,32]{3,1,2,0:T(8,128)(2,1)}, bf16[6,48,1,32]{3,1,2,0:T(8,128)(2,1)}, u32[]{:S(2)}, u32[]{:S(2)}) collective-permute-start(bf16[6,48,1,32]{3,1,2,0:T(8,128)(2,1)} %get-tuple-element.47), channel_id=1, source_target_pairs={{16,0},{32,16},{48,32},{64,48},{80,64},{96,80},{112,96},{128,112},... | collective-permute-start | bytes 55304 | tf_op jit(solution)/shard_map/ppermute | solution.py:208
  10.1 0.6 copy-start.3
  49.5 1.0 %copy-start.1 = (bf16[1,3,3,32,512]{4,3,2,1,0:T(8,128)(2,1)S(1)}, bf16[1,3,3,32,512]{4,3,2,1,0:T(8,128)(2,1)}, u32[]{:S(2)}) copy-start(bf16[1,3,3,32,512]{4,3,2,1,0:T(8,128)(2,1)} %get-tuple-element.45) | copy-start | bytes 884740
  54.5 27.6 %copy-start.6 = (f32[32]{0:T(128)S(1)}, f32[32]{0:T(128)}, u32[]{:S(2)}) copy-start(f32[32]{0:T(128)} %param.15) | copy-start | bytes 388

commit v10 on v8

--- a/solution.py
+++ b/solution.py
@@ -15,9 +15,12 @@
 epsilon = 1e-06
 
 
-def gather_kernel(n, x_ref, o_ref, buf, send_sem, recv_sem):
+def gather_kernel(n, x_ref, lo_ref, hi_ref, o_ref, left_ref, right_ref,
+                  buf, left_buf, right_buf, send_sem, recv_sem, edge_send, edge_recv):
     me = lax.axis_index("space")
     ch = lax.axis_index("chan")
+    right = lax.rem(me + 1, n)
+    left = lax.rem(me + n - 1, n)
     barrier = pltpu.get_barrier_semaphore()
 
     def signal(k, carry):
@@ -27,6 +30,15 @@
 
     lax.fori_loop(1, n, signal, 0)
     pl.semaphore_wait(barrier, n - 1)
+
+    to_right = pltpu.make_async_remote_copy(
+        src_ref=hi_ref, dst_ref=left_buf, send_sem=edge_send.at[0], recv_sem=edge_recv.at[0],
+        device_id=(right, ch), device_id_type=MESH)
+    to_left = pltpu.make_async_remote_copy(
+        src_ref=lo_ref, dst_ref=right_buf, send_sem=edge_send.at[1], recv_sem=edge_recv.at[1],
+        device_id=(left, ch), device_id_type=MESH)
+    to_right.start()
+    to_left.start()
 
     def copy_to(peer):
         return pltpu.make_async_remote_copy(
@@ -63,22 +75,35 @@
     lax.fori_loop(1, n, finish, 0)
     buf[me] = x_ref[...]
     o_ref[...] = buf[...]
-
-
-def gather_space(tile):
+    to_right.wait()
+    to_left.wait()
+    left_ref[...] = left_buf[...]
+    right_ref[...] = right_buf[...]
+
+
+def gather_space(tile, lo, hi):
     n = lax.axis_size("space")
+    vmem = pl.BlockSpec(memory_space=pltpu.VMEM)
     return pl.pallas_call(
         functools.partial(gather_kernel, n),
-        out_shape=jax.ShapeDtypeStruct((n,) + tile.shape, tile.dtype),
-        in_specs=[pl.BlockSpec(memory_space=pltpu.VMEM)],
-        out_specs=pl.BlockSpec(memory_space=pltpu.VMEM),
+        out_shape=(
+            jax.ShapeDtypeStruct((n,) + tile.shape, tile.dtype),
+            jax.ShapeDtypeStruct(hi.shape, hi.dtype),
+            jax.ShapeDtypeStruct(lo.shape, lo.dtype),
+        ),
+        in_specs=[vmem, vmem, vmem],
+        out_specs=(vmem, vmem, vmem),
         scratch_shapes=[
             pltpu.VMEM((n,) + tile.shape, tile.dtype),
+            pltpu.VMEM(hi.shape, hi.dtype),
+            pltpu.VMEM(lo.shape, lo.dtype),
             pltpu.SemaphoreType.DMA((n,)),
             pltpu.SemaphoreType.DMA((n,)),
+            pltpu.SemaphoreType.DMA((2,)),
+            pltpu.SemaphoreType.DMA((2,)),
         ],
         compiler_params=pltpu.CompilerParams(collective_id=0, has_side_effects=True),
-    )(tile)
+    )(tile, lo, hi)
 
 
 def scatter_kernel(nchunk, x_ref, o_ref, recv1, acc1, own, recv2, acc2, recv3,
@@ -200,15 +225,6 @@
     )(parts)
 
 
-def edge_exchange(edges_last, edges_first, axis):
-    peers = lax.axis_size(axis)
-    up = [(i, (i + 1) % peers) for i in range(peers - 1)]
-    down = [(j, i) for i, j in up]
-    before = lax.ppermute(edges_last, axis, up)
-    after = lax.ppermute(edges_first, axis, down)
-    return before, after
-
-
 def local(frames, cache, gamma, beta, kernel, bias):
     nframes, row_count, col_count, local_ch = frames.shape
     ncache = cache.shape[0]
@@ -219,7 +235,6 @@
     local_members = float(nframes * row_count * col_count * group_size)
 
     raw = jnp.concatenate([cache, frames], axis=0)
-    before, after = edge_exchange(raw[:, :, col_count - 1 :], raw[:, :, :1], "space")
 
     values = frames.astype(jnp.float32).reshape(
         nframes, row_count, col_count, local_groups, group_size
@@ -229,7 +244,9 @@
     local_m2 = jnp.sum(local_dev * local_dev, axis=(0, 1, 2, 4))
     tile = jnp.zeros((8, 128), jnp.float32)
     tile = tile.at[0, :local_groups].set(local_mean).at[1, :local_groups].set(local_m2)
-    gathered = gather_space(tile)
+    gathered, before, after = gather_space(tile, raw[:, :, 0], raw[:, :, col_count - 1])
+    before = before[:, :, None]
+    after = after[:, :, None]
     means = gathered[:, 0, :local_groups]
     m2s = gathered[:, 1, :local_groups]
     group_mean = jnp.mean(means, axis=0)

time: 83.7 us -> 81.4 us (0.973)
  starting transfers between devices: 5.51 us -> 0 us
  other arithmetic: 4.46 us -> 6.48 us
    ppermute x2 -> x0, starting transfers between devices: 5.51 us -> none  [the longest x1 4.23 us: edge_exchange(): before = lax.ppermute(edges_last, axis, up)]
    concatenate x0 -> x2, local copies, waits for them, and re-layouts: none -> 1.49 us  [the longest x1 0.75 us: local(): left = jnp.concatenate([before[:ncache], activate(before[ncache:])], axis=0)]
    slice x2 -> x0, local copies, waits for them, and re-layouts: 1.48 us -> none  [the longest x1 0.74 us: local(): left = jnp.concatenate([before[:ncache], activate(before[ncache:])], axis=0)]
    pallas_call x1, Pallas kernels: 23 us -> 24.5 us  [gather_space(): pl.pallas_call(functools.partial(gather_kernel, n), out_shape=(jax.ShapeD...]
    pallas_call x1, Pallas kernels: 26.6 us -> 25.4 us  [scatter_chan(): pl.pallas_call(functools.partial(scatter_kernel, nchunk), out_shape=jax.S...]
    reduce_sum x2, other arithmetic: 0.31 us -> 1.36 us  [local(): local_mean = jnp.sum(values, axis=(0, 1, 2, 4)) / local_members]
    reduce_sum x2, other arithmetic: 0.41 us -> 1.39 us  [local(): local_m2 = jnp.sum(local_dev * local_dev, axis=(0, 1, 2, 4))]
    convert_element_type x2 -> x1, other arithmetic: 1.25 us -> 0.33 us  [activate(): return jax.nn.silu(normed).astype(jnp.bfloat16)]
  transfers between devices with their start and end apart: 2 -> 0, of which waited for: 0 -> 0; matrix products, arithmetic and copies ran while one was open for 6% -> 0% of each run, Pallas kernels for 28% -> 0%
where the time goes in v10:
time: 81.4 us; the launch traced here: 79.9 us
  Pallas kernels  49.9 us (61%)
  local copies, waits for them, and re-layouts  19.3 us (24%)
  other arithmetic  6.48 us (8%)
  matrix products  4.06 us (5%)
    pallas_call x1, Pallas kernels, scatter_chan(): pl.pallas_call(functools.partial(scatter_kernel, nchunk), out_shape=jax.S...  25.4 us
    pallas_call x1, Pallas kernels, gather_space(): pl.pallas_call(functools.partial(gather_kernel, n), out_shape=(jax.ShapeD...  24.5 us
    concatenate x1, local copies, waits for them, and re-layouts, local(): jnp.concatenate([bordered[:, col_tap:col_tap + col_count, row_tap:row_tap...  7.08 us
    dot_general x3, matrix products, local(): lax.dot_general(tap_weight, window, (((0,), (1,)), ((), ())), preferred_e...  4.06 us
    unnamed x17, local copies, waits for them, and re-layouts  4.03 us
    slice x1, local copies, waits for them, and re-layouts, local(): bordered[:, col_tap:col_tap + col_count, row_tap:row_tap + row_count, :]  2.96 us

profile of v10, /device:TPU:6, one launch (start us, length us, event | category | flops | bytes accessed | tf_op | source)
XLA Modules:
  0.0 79.9 jit_solution(12438762730051585442)
XLA Ops:
  0.0 1.2 %convert_reduce_fusion = f32[32]{0:T(128)S(1)} fusion(bf16[4,48,10,32]{1,3,2,0:T(8,128)(2,1)} %param.10), kind=kLoop, calls=%fused_computation.12 | loop fusion | flops 122848 | bytes 123008 | tf_op jit(solution)/shard_map/reduce_sum | solution.py:242
  1.3 0.1 reduce_sum.61
  1.6 1.3 %multiply_reduce_fusion = f32[32]{0:T(128)S(1)} fusion(f32[32]{0:T(128)S(1)} %sub.59, bf16[4,48,10,32]{1,3,2,0:T(8,128)(2,1)} %param.10), kind=kLoop, calls=%fused_computation.11 | loop fusion | flops 245728 | bytes 123136 | tf_op jit(solution)/shard_map/reduce_sum | solution.py:244
  3.0 0.1 reduce_sum.64
  3.1 0.2 scatter.9.x_ref
  3.3 1.1 %copy.27 = bf16[2,48,10,32]{3,1,2,0:T(8,128)(2,1)S(1)} copy(bf16[2,48,10,32]{1,3,2,0:T(8,128)(2,1)} %param.11) | data formatting | bytes 122880 | tf_op args[1]
  4.4 1.1 %copy.23 = bf16[2,48,10,32]{3,1,0,2:T(8,128)(2,1)S(1)} copy(bf16[2,48,10,32]{1,3,2,0:T(8,128)(2,1)} %param.11) | data formatting | bytes 122880 | tf_op args[1]
  5.5 1.3 %copy.24 = bf16[4,48,10,32]{3,1,0,2:T(8,128)(2,1)S(1)} copy(bf16[4,48,10,32]{1,3,2,0:T(8,128)(2,1)} %param.10) | data formatting | bytes 245760 | tf_op args[0]
  6.8 0.7 fusion.6
  7.5 24.5 %shard_map.64 = (f32[32,8,128]{2,1,0:T(8,128)}, bf16[6,48,32]{2,1,0:T(8,128)(2,1)}, bf16[6,48,32]{2,1,0:T(8,128)(2,1)}) custom-call(f32[8,128]{1,0:T(8,128)} %copy-done.3, bf16[6,48,32]{2,1,0:T(8,128)(2,1)} %get-tuple-element.53.lo_ref, bf16[6,48,32]{2,1,0:T(8,128)(2,1)} %get-tuple-element.52.hi_ref), custom_call_target="tpu_custom_call" | custom-call | tf_op jit(solution)/shard_map/pallas_call | solution.py:87
  32.0 1.0 %slice_reduce_fusion.1 = (f32[2]{0:T(128)S(1)}, f32[2]{0:T(128)S(1)}, f32[32,1,2]{2,1,0:T(1,128)S(1)}) fusion(f32[32,8,128]{2,1,0:T(8,128)} %get-tuple-element.33), kind=kLoop, calls=%fused_computation.35 | loop fusion | flops 124 | bytes 784 | tf_op jit(solution)/shard_map/reduce_sum | solution.py:252
  33.1 0.1 sub.63
  33.3 0.2 fusion.11
  33.5 0.1 mul.94
  33.6 0.8 slice_bitcast_fusion.1
  34.4 0.7 slice_bitcast_fusion
  35.1 0.9 %fusion.8 = (bf16[4,48,1,32]{3,1,0,2:T(8,128)(2,1)S(1)}, bf16[4,48,1,32]{3,1,2,0:T(8,128)(2,1)S(1)}) fusion(f32[32]{0:T(128)S(1)} %copy-done.4, f32[32]{0:T(128)S(1)} %copy-done.5, f32[32]{0:T(128)S(1)} %mul.94, f32[32]{0:T(128)S(1)} %sub.63, bf16[6,48,32]{2,1,0:T(8,128)(2,1)} %get-tuple-element.32, bf16[6,48,32]{2,1,0:T(8,128)(2,1)} %get-tuple-element.34), kind=kLoop, calls=%fused_computation.23 | loop fusion | flops 122880 | bytes 49664 | tf_op jit(solution)/shard_map/concatenate | solution.py:268
  36.1 0.8 fusion.15
  36.9 0.2 copy.26
  37.1 0.3 multiply_convert_fusion
  37.5 0.4 fusion.1
  37.9 3.0 %fusion.14 = (bf16[6,10,48,32]{3,2,1,0:T(8,128)(2,1)S(1)}, bf16[6,10,48,32]{3,2,1,0:T(8,128)(2,1)}, bf16[6,10,48,32]{3,2,1,0:T(8,128)(2,1)}, bf16[6,10,48,32]{3,...) fusion(bf16[6,12,50,32]{3,2,1,0:T(8,128)(2,1)S(1)} %fusion.1), kind=kLoop, calls=%fused_computation.37 | loop fusion | bytes 3317760 | tf_op jit(solution)/shard_map/slice | solution.py:278
  40.9 7.1 %concatenate.55 = bf16[6,10,48,288]{3,2,1,0:T(8,128)(2,1)S(1)} concatenate(bf16[6,10,48,32]{3,2,1,0:T(8,128)(2,1)} %get-tuple-element.48, bf16[6,10,48,32]{3,2,1,0:T(8,128)(2,1)} %get-tuple-element.47, bf16[6,10,48,32]{3,2,1,0:T(8,128)(2,1)} %get-tuple-element.46, bf16[6,10,48,32]{3,2,1,0:T(8,128)(2,1)} %get-tuple-element.45, bf16[6,10,48,32]{3,2,1,0:T(8,128)(2,1)} %get-tuple-element.44, ...), dimensions={3} | concatenate | bytes 3317760 | tf_op jit(solution)/shard_map/concatenate | solution.py:276
  48.0 0.4 fusion.13
  48.4 0.6 copy-done.1
  48.9 1.3 %fusion.17 = f32[1920,512]{0,1:T(8,128)S(1)} fusion(bf16[1920,288]{1,0:T(8,128)(2,1)S(1)} %bitcast.49, bf16[288,512]{1,0:T(8,128)(2,1)S(1)} %bitcast.54), kind=kOutput, calls=%fused_computation.40 | convolution fusion | flops 566231040 | bytes 5332992 | tf_op jit(solution)/shard_map/dot_general | solution.py:295
  50.2 1.3 %fusion.16 = f32[1920,512]{0,1:T(8,128)S(1)} fusion(bf16[1920,288]{1,0:T(8,128)(2,1)S(1)} %bitcast.48, bf16[288,512]{1,0:T(8,128)(2,1)S(1)} %bitcast.53), kind=kOutput, calls=%fused_computation.39 | convolution fusion | flops 566231040 | bytes 5332992 | tf_op jit(solution)/shard_map/dot_general | solution.py:295
  51.5 1.5 %add_add_fusion = f32[1920,512]{0,1:T(8,128)S(1)} fusion(f32[1920,512]{0,1:T(8,128)S(1)} %fusion.16, f32[1920,512]{0,1:T(8,128)S(1)} %fusion.17, bf16[1920,288]{1,0:T(8,128)(2,1)S(1)} %bitcast.50, bf16[288,512]{1,0:T(8,128)(2,1)S(1)} %bitcast.52), kind=kOutput, calls=%fused_computation | convolution fusion | flops 568197120 | bytes 13197312 | tf_op jit(solution)/shard_map/dot_general | solution.py:295
  53.0 25.4 %shard_map.65 = f32[32,1920]{1,0:T(8,128)S(1)} custom-call(f32[4,2,2,32,1920]{4,3,2,1,0:T(8,128)S(1)} %bitcast.47), custom_call_target="tpu_custom_call" | custom-call | tf_op jit(solution)/shard_map/pallas_call | solution.py:204
  78.4 0.1 fusion.5
  78.5 0.5 reshape.225
  79.0 0.9 %copy.30 = bf16[4,48,10,32]{1,3,2,0:T(8,128)(2,1)} copy(bf16[4,48,10,32]{1,2,0,3:T(8,128)(2,1)S(1)} %bitcast.51) | data formatting | bytes 245760 | tf_op jit(solution)/shard_map/transpose | solution.py:301
  (26 shorter events, 0.7 us)
Async XLA Ops:
  0.0 35.1 %copy-start.4 = (f32[32]{0:T(128)S(1)}, f32[32]{0:T(128)}, u32[]{:S(2)}) copy-start(f32[32]{0:T(128)} %param.13) | copy-start | bytes 388
  0.0 35.1 %copy-start.5 = (f32[32]{0:T(128)S(1)}, f32[32]{0:T(128)}, u32[]{:S(2)}) copy-start(f32[32]{0:T(128)} %param.12) | copy-start | bytes 388
  0.0 36.1 %copy-start.2 = (bf16[3,3,3,32,512]{4,3,2,1,0:T(8,128)(2,1)S(1)}, bf16[3,3,3,32,512]{4,3,2,1,0:T(8,128)(2,1)}, u32[]{:S(2)}) copy-start(bf16[3,3,3,32,512]{4,3,2,1,0:T(8,128)(2,1)} %param.14) | copy-start | bytes 2654212
  3.3 4.2 %copy-start.3 = (f32[8,128]{1,0:T(8,128)}, f32[8,128]{1,0:T(8,128)S(1)}, u32[]{:S(2)}) copy-start(f32[8,128]{1,0:T(8,128)S(1)} %scatter.9.x_ref) | copy-start | bytes 12292
  5.5 31.4 %copy-start = (bf16[4,48,10,32]{1,3,2,0:T(8,128)(2,1)S(1)}, bf16[4,48,10,32]{1,3,2,0:T(8,128)(2,1)}, u32[]{:S(2)}) copy-start(bf16[4,48,10,32]{1,3,2,0:T(8,128)(2,1)} %param.10) | copy-start | bytes 368644
  47.9 1.0 %copy-start.1 = (bf16[1,3,3,32,512]{4,3,2,1,0:T(8,128)(2,1)S(1)}, bf16[1,3,3,32,512]{4,3,2,1,0:T(8,128)(2,1)}, u32[]{:S(2)}) copy-start(bf16[1,3,3,32,512]{4,3,2,1,0:T(8,128)(2,1)} %get-tuple-element.51) | copy-start | bytes 884740
  53.0 25.4 %copy-start.6 = (f32[32]{0:T(128)S(1)}, f32[32]{0:T(128)}, u32[]{:S(2)}) copy-start(f32[32]{0:T(128)} %param.15) | copy-start | bytes 388

commit v11 on v10

--- a/solution.py
+++ b/solution.py
@@ -15,21 +15,24 @@
 epsilon = 1e-06
 
 
-def gather_kernel(n, x_ref, lo_ref, hi_ref, o_ref, left_ref, right_ref,
-                  buf, left_buf, right_buf, send_sem, recv_sem, edge_send, edge_recv):
+def gather_kernel(n, nrow, x_ref, lo_ref, hi_ref, o_ref, left_ref, right_ref,
+                  part, full, left_buf, right_buf, local_sem, a_send, a_recv, b_send, b_recv,
+                  edge_send, edge_recv):
     me = lax.axis_index("space")
     ch = lax.axis_index("chan")
+    ncol = n // nrow
+    zz = me // nrow
+    yy = me % nrow
     right = lax.rem(me + 1, n)
     left = lax.rem(me + n - 1, n)
+    row_peers = [(zz * nrow + lax.rem(yy + k, nrow), lax.rem(yy + k, nrow)) for k in range(1, nrow)]
+    col_peers = [(lax.rem(zz + k, ncol) * nrow + yy, lax.rem(zz + k, ncol)) for k in range(1, ncol)]
     barrier = pltpu.get_barrier_semaphore()
-
-    def signal(k, carry):
-        peer = lax.rem(me + k, n)
+    for peer, _ in row_peers + col_peers:
         pl.semaphore_signal(barrier, 1, device_id=(peer, ch), device_id_type=MESH)
-        return carry
-
-    lax.fori_loop(1, n, signal, 0)
-    pl.semaphore_wait(barrier, n - 1)
+    for peer in (left, right):
+        pl.semaphore_signal(barrier, 1, device_id=(peer, ch), device_id_type=MESH)
+    pl.semaphore_wait(barrier, len(row_peers) + len(col_peers) + 2)
 
     to_right = pltpu.make_async_remote_copy(
         src_ref=hi_ref, dst_ref=left_buf, send_sem=edge_send.at[0], recv_sem=edge_recv.at[0],
@@ -40,70 +43,71 @@
     to_right.start()
     to_left.start()
 
-    def copy_to(peer):
-        return pltpu.make_async_remote_copy(
-            src_ref=x_ref,
-            dst_ref=buf.at[me],
-            send_sem=send_sem.at[peer],
-            recv_sem=recv_sem.at[me],
-            device_id=(peer, ch),
-            device_id_type=MESH,
-        )
-
-    def copy_from(peer):
-        return pltpu.make_async_remote_copy(
-            src_ref=x_ref,
-            dst_ref=buf.at[peer],
-            send_sem=send_sem.at[peer],
-            recv_sem=recv_sem.at[peer],
-            device_id=(peer, ch),
-            device_id_type=MESH,
-        )
-
-    def start(k, carry):
-        copy_to(lax.rem(me + k, n)).start()
-        return carry
-
-    lax.fori_loop(1, n, start, 0)
-
-    def finish(k, carry):
-        peer = lax.rem(me + k, n)
-        copy_to(peer).wait_send()
-        copy_from(peer).wait_recv()
-        return carry
-
-    lax.fori_loop(1, n, finish, 0)
-    buf[me] = x_ref[...]
-    o_ref[...] = buf[...]
+    sends = []
+    for peer, slot in row_peers:
+        cp = pltpu.make_async_remote_copy(
+            src_ref=x_ref, dst_ref=part.at[yy], send_sem=a_send.at[slot], recv_sem=a_recv.at[yy],
+            device_id=(peer, ch), device_id_type=MESH)
+        cp.start()
+        sends.append(cp)
+    own = pltpu.make_async_copy(x_ref, part.at[yy], local_sem.at[0])
+    own.start()
+    for peer, slot in row_peers:
+        pltpu.make_async_remote_copy(
+            src_ref=x_ref, dst_ref=part.at[slot], send_sem=a_send.at[slot], recv_sem=a_recv.at[slot],
+            device_id=(peer, ch), device_id_type=MESH).wait_recv()
+    own.wait()
+    for peer, slot in col_peers:
+        cp = pltpu.make_async_remote_copy(
+            src_ref=part, dst_ref=full.at[zz], send_sem=b_send.at[slot], recv_sem=b_recv.at[zz],
+            device_id=(peer, ch), device_id_type=MESH)
+        cp.start()
+        sends.append(cp)
+    own = pltpu.make_async_copy(part, full.at[zz], local_sem.at[1])
+    own.start()
+    for peer, slot in col_peers:
+        pltpu.make_async_remote_copy(
+            src_ref=part, dst_ref=full.at[slot], send_sem=b_send.at[slot], recv_sem=b_recv.at[slot],
+            device_id=(peer, ch), device_id_type=MESH).wait_recv()
+    own.wait()
+    for cp in sends:
+        cp.wait_send()
+    o_ref[...] = full[...]
     to_right.wait()
     to_left.wait()
     left_ref[...] = left_buf[...]
     right_ref[...] = right_buf[...]
 
 
-def gather_space(tile, lo, hi):
+def gather_space(tile, lo, hi, nrow=4):
     n = lax.axis_size("space")
+    ncol = n // nrow
     vmem = pl.BlockSpec(memory_space=pltpu.VMEM)
-    return pl.pallas_call(
-        functools.partial(gather_kernel, n),
+    gathered, before, after = pl.pallas_call(
+        functools.partial(gather_kernel, n, nrow),
         out_shape=(
-            jax.ShapeDtypeStruct((n,) + tile.shape, tile.dtype),
+            jax.ShapeDtypeStruct((ncol, nrow) + tile.shape, tile.dtype),
             jax.ShapeDtypeStruct(hi.shape, hi.dtype),
             jax.ShapeDtypeStruct(lo.shape, lo.dtype),
         ),
         in_specs=[vmem, vmem, vmem],
         out_specs=(vmem, vmem, vmem),
         scratch_shapes=[
-            pltpu.VMEM((n,) + tile.shape, tile.dtype),
+            pltpu.VMEM((nrow,) + tile.shape, tile.dtype),
+            pltpu.VMEM((ncol, nrow) + tile.shape, tile.dtype),
             pltpu.VMEM(hi.shape, hi.dtype),
             pltpu.VMEM(lo.shape, lo.dtype),
-            pltpu.SemaphoreType.DMA((n,)),
-            pltpu.SemaphoreType.DMA((n,)),
+            pltpu.SemaphoreType.DMA((2,)),
+            pltpu.SemaphoreType.DMA((nrow,)),
+            pltpu.SemaphoreType.DMA((nrow,)),
+            pltpu.SemaphoreType.DMA((ncol,)),
+            pltpu.SemaphoreType.DMA((ncol,)),
             pltpu.SemaphoreType.DMA((2,)),
             pltpu.SemaphoreType.DMA((2,)),
         ],
         compiler_params=pltpu.CompilerParams(collective_id=0, has_side_effects=True),
     )(tile, lo, hi)
+    return gathered.reshape((n,) + tile.shape), before, after
 
 
 def scatter_kernel(nchunk, x_ref, o_ref, recv1, acc1, own, recv2, acc2, recv3,

time: 81.4 us -> 81.7 us (level)
  the two profiles are of different devices: /device:TPU:6 before, /device:TPU:1 now
where the time goes in v11:
time: 81.7 us; the launch traced here: 80.8 us
  Pallas kernels  50.8 us (62%)
  local copies, waits for them, and re-layouts  19.3 us (24%)
  other arithmetic  6.48 us (8%)
  matrix products  4.06 us (5%)
    pallas_call x1, Pallas kernels, scatter_chan(): pl.pallas_call(functools.partial(scatter_kernel, nchunk), out_shape=jax.S...  26.9 us
    pallas_call x1, Pallas kernels, gather_space(): pl.pallas_call(functools.partial(gather_kernel, n, nrow), out_shape=(jax....  23.8 us
    concatenate x1, local copies, waits for them, and re-layouts, local(): jnp.concatenate([bordered[:, col_tap:col_tap + col_count, row_tap:row_tap...  7.08 us
    unnamed x18, local copies, waits for them, and re-layouts  4.11 us
    dot_general x3, matrix products, local(): lax.dot_general(tap_weight, window, (((0,), (1,)), ((), ())), preferred_e...  4.06 us
    slice x1, local copies, waits for them, and re-layouts, local(): bordered[:, col_tap:col_tap + col_count, row_tap:row_tap + row_count, :]  2.96 us

profile of v11, /device:TPU:1, one launch (start us, length us, event | category | flops | bytes accessed | tf_op | source)
XLA Modules:
  0.0 80.8 jit_solution(7997856564115304217)
XLA Ops:
  0.0 1.2 %convert_reduce_fusion = f32[32]{0:T(128)S(1)} fusion(bf16[4,48,10,32]{1,3,2,0:T(8,128)(2,1)} %param.10), kind=kLoop, calls=%fused_computation.12 | loop fusion | flops 122848 | bytes 123008 | tf_op jit(solution)/shard_map/reduce_sum | solution.py:246
  1.3 0.1 reduce_sum.60
  1.3 0.1 reduce_sum.61
  1.6 1.3 %multiply_reduce_fusion = f32[32]{0:T(128)S(1)} fusion(f32[32]{0:T(128)S(1)} %sub.59, bf16[4,48,10,32]{1,3,2,0:T(8,128)(2,1)} %param.10), kind=kLoop, calls=%fused_computation.11 | loop fusion | flops 245728 | bytes 123136 | tf_op jit(solution)/shard_map/reduce_sum | solution.py:248
  3.0 0.1 reduce_sum.64
  3.1 0.2 scatter.9.x_ref
  3.3 1.1 %copy.27 = bf16[2,48,10,32]{3,1,2,0:T(8,128)(2,1)S(1)} copy(bf16[2,48,10,32]{1,3,2,0:T(8,128)(2,1)} %param.11) | data formatting | bytes 122880 | tf_op args[1]
  4.4 1.1 %copy.23 = bf16[2,48,10,32]{3,1,0,2:T(8,128)(2,1)S(1)} copy(bf16[2,48,10,32]{1,3,2,0:T(8,128)(2,1)} %param.11) | data formatting | bytes 122880 | tf_op args[1]
  5.5 1.3 %copy.24 = bf16[4,48,10,32]{3,1,0,2:T(8,128)(2,1)S(1)} copy(bf16[4,48,10,32]{1,3,2,0:T(8,128)(2,1)} %param.10) | data formatting | bytes 245760 | tf_op args[0]
  6.8 0.7 fusion.6
  7.5 23.8 %shard_map.64 = (f32[8,4,8,128]{3,2,1,0:T(8,128)}, bf16[6,48,32]{2,1,0:T(8,128)(2,1)}, bf16[6,48,32]{2,1,0:T(8,128)(2,1)}) custom-call(f32[8,128]{1,0:T(8,128)} %copy-done.3, bf16[6,48,32]{2,1,0:T(8,128)(2,1)} %get-tuple-element.53.lo_ref, bf16[6,48,32]{2,1,0:T(8,128)(2,1)} %get-tuple-element.52.hi_ref), custom_call_target="tpu_custom_call" | custom-call | tf_op jit(solution)/shard_map/pallas_call | solution.py:86
  31.3 1.0 %slice_reduce_fusion.1 = (f32[2]{0:T(128)S(1)}, f32[2]{0:T(128)S(1)}, f32[32,1,2]{2,1,0:T(1,128)S(1)}) fusion(f32[32,8,128]{2,1,0:T(8,128)} %bitcast.56), kind=kLoop, calls=%fused_computation.35 | loop fusion | flops 124 | bytes 784 | tf_op jit(solution)/shard_map/reduce_sum | solution.py:256
  32.6 0.2 fusion.11
  32.8 0.1 mul.94
  32.9 0.8 slice_bitcast_fusion.1
  33.7 0.7 slice_bitcast_fusion
  34.4 0.9 %fusion.8 = (bf16[4,48,1,32]{3,1,0,2:T(8,128)(2,1)S(1)}, bf16[4,48,1,32]{3,1,2,0:T(8,128)(2,1)S(1)}) fusion(f32[32]{0:T(128)S(1)} %copy-done.4, f32[32]{0:T(128)S(1)} %copy-done.5, f32[32]{0:T(128)S(1)} %mul.94, f32[32]{0:T(128)S(1)} %sub.63, bf16[6,48,32]{2,1,0:T(8,128)(2,1)} %get-tuple-element.32, bf16[6,48,32]{2,1,0:T(8,128)(2,1)} %get-tuple-element.34), kind=kLoop, calls=%fused_computation.23 | loop fusion | flops 122880 | bytes 49664 | tf_op jit(solution)/shard_map/concatenate | solution.py:272
  35.4 0.8 fusion.15
  36.2 0.2 copy.26
  36.4 0.3 multiply_convert_fusion
  36.8 0.4 fusion.1
  37.2 3.0 %fusion.14 = (bf16[6,10,48,32]{3,2,1,0:T(8,128)(2,1)S(1)}, bf16[6,10,48,32]{3,2,1,0:T(8,128)(2,1)}, bf16[6,10,48,32]{3,2,1,0:T(8,128)(2,1)}, bf16[6,10,48,32]{3,...) fusion(bf16[6,12,50,32]{3,2,1,0:T(8,128)(2,1)S(1)} %fusion.1), kind=kLoop, calls=%fused_computation.37 | loop fusion | bytes 3317760 | tf_op jit(solution)/shard_map/slice | solution.py:282
  40.2 7.1 %concatenate.55 = bf16[6,10,48,288]{3,2,1,0:T(8,128)(2,1)S(1)} concatenate(bf16[6,10,48,32]{3,2,1,0:T(8,128)(2,1)} %get-tuple-element.48, bf16[6,10,48,32]{3,2,1,0:T(8,128)(2,1)} %get-tuple-element.47, bf16[6,10,48,32]{3,2,1,0:T(8,128)(2,1)} %get-tuple-element.46, bf16[6,10,48,32]{3,2,1,0:T(8,128)(2,1)} %get-tuple-element.45, bf16[6,10,48,32]{3,2,1,0:T(8,128)(2,1)} %get-tuple-element.44, ...), dimensions={3} | concatenate | bytes 3317760 | tf_op jit(solution)/shard_map/concatenate | solution.py:280
  47.3 0.4 fusion.13
  47.7 0.6 copy-done.1
  48.2 1.3 %fusion.17 = f32[1920,512]{0,1:T(8,128)S(1)} fusion(bf16[1920,288]{1,0:T(8,128)(2,1)S(1)} %bitcast.50, bf16[288,512]{1,0:T(8,128)(2,1)S(1)} %bitcast.55), kind=kOutput, calls=%fused_computation.40 | convolution fusion | flops 566231040 | bytes 5332992 | tf_op jit(solution)/shard_map/dot_general | solution.py:299
  49.5 1.3 %fusion.16 = f32[1920,512]{0,1:T(8,128)S(1)} fusion(bf16[1920,288]{1,0:T(8,128)(2,1)S(1)} %bitcast.49, bf16[288,512]{1,0:T(8,128)(2,1)S(1)} %bitcast.54), kind=kOutput, calls=%fused_computation.39 | convolution fusion | flops 566231040 | bytes 5332992 | tf_op jit(solution)/shard_map/dot_general | solution.py:299
  50.8 1.5 %add_add_fusion = f32[1920,512]{0,1:T(8,128)S(1)} fusion(f32[1920,512]{0,1:T(8,128)S(1)} %fusion.16, f32[1920,512]{0,1:T(8,128)S(1)} %fusion.17, bf16[1920,288]{1,0:T(8,128)(2,1)S(1)} %bitcast.51, bf16[288,512]{1,0:T(8,128)(2,1)S(1)} %bitcast.53), kind=kOutput, calls=%fused_computation | convolution fusion | flops 568197120 | bytes 13197312 | tf_op jit(solution)/shard_map/dot_general | solution.py:299
  52.3 26.9 %shard_map.65 = f32[32,1920]{1,0:T(8,128)S(1)} custom-call(f32[4,2,2,32,1920]{4,3,2,1,0:T(8,128)S(1)} %bitcast.48), custom_call_target="tpu_custom_call" | custom-call | tf_op jit(solution)/shard_map/pallas_call | solution.py:208
  79.3 0.1 fusion.5
  79.4 0.5 reshape.229
  79.9 0.9 %copy.30 = bf16[4,48,10,32]{1,3,2,0:T(8,128)(2,1)} copy(bf16[4,48,10,32]{1,2,0,3:T(8,128)(2,1)S(1)} %bitcast.52) | data formatting | bytes 245760 | tf_op jit(solution)/shard_map/transpose | solution.py:305
  (26 shorter events, 0.7 us)
Async XLA Ops:
  0.0 34.4 %copy-start.4 = (f32[32]{0:T(128)S(1)}, f32[32]{0:T(128)}, u32[]{:S(2)}) copy-start(f32[32]{0:T(128)} %param.13) | copy-start | bytes 388
  0.0 34.4 %copy-start.5 = (f32[32]{0:T(128)S(1)}, f32[32]{0:T(128)}, u32[]{:S(2)}) copy-start(f32[32]{0:T(128)} %param.12) | copy-start | bytes 388
  0.0 35.4 %copy-start.2 = (bf16[3,3,3,32,512]{4,3,2,1,0:T(8,128)(2,1)S(1)}, bf16[3,3,3,32,512]{4,3,2,1,0:T(8,128)(2,1)}, u32[]{:S(2)}) copy-start(bf16[3,3,3,32,512]{4,3,2,1,0:T(8,128)(2,1)} %param.14) | copy-start | bytes 2654212
  3.3 4.2 %copy-start.3 = (f32[8,128]{1,0:T(8,128)}, f32[8,128]{1,0:T(8,128)S(1)}, u32[]{:S(2)}) copy-start(f32[8,128]{1,0:T(8,128)S(1)} %scatter.9.x_ref) | copy-start | bytes 12292
  5.5 30.7 %copy-start = (bf16[4,48,10,32]{1,3,2,0:T(8,128)(2,1)S(1)}, bf16[4,48,10,32]{1,3,2,0:T(8,128)(2,1)}, u32[]{:S(2)}) copy-start(bf16[4,48,10,32]{1,3,2,0:T(8,128)(2,1)} %param.10) | copy-start | bytes 368644
  47.3 1.0 %copy-start.1 = (bf16[1,3,3,32,512]{4,3,2,1,0:T(8,128)(2,1)S(1)}, bf16[1,3,3,32,512]{4,3,2,1,0:T(8,128)(2,1)}, u32[]{:S(2)}) copy-start(bf16[1,3,3,32,512]{4,3,2,1,0:T(8,128)(2,1)} %get-tuple-element.51) | copy-start | bytes 884740
  52.3 27.0 %copy-start.6 = (f32[32]{0:T(128)S(1)}, f32[32]{0:T(128)}, u32[]{:S(2)}) copy-start(f32[32]{0:T(128)} %param.15) | copy-start | bytes 388

commit v12 on v10

--- a/solution.py
+++ b/solution.py
@@ -106,7 +106,7 @@
     )(tile, lo, hi)
 
 
-def scatter_kernel(nchunk, x_ref, o_ref, recv1, acc1, own, recv2, acc2, recv3,
+def scatter_kernel(nchunk, x_ref, o_ref, half, recv1, acc1, own, recv2, acc2, recv3,
                    sem1s, sem1r, sem2s, sem2r, sem3s, sem3r):
     sp = lax.axis_index("space")
     c = lax.axis_index("chan")
@@ -136,8 +136,9 @@
         for i in range(nx):
             for j in range(nyh):
                 n = (q * nx + i) * nyh + j
+                half[q, i, j] = x_ref[i, j, 1 - core, :, cols(q)].astype(bf16)
                 cp = pltpu.make_async_remote_copy(
-                    src_ref=x_ref.at[i, j, 1 - core, :, cols(q)], dst_ref=recv1.at[q, i, j],
+                    src_ref=half.at[q, i, j], dst_ref=recv1.at[q, i, j],
                     send_sem=sem1s.at[n], recv_sem=sem1r.at[n],
                     device_id=peers[0], device_id_type=MESH)
                 cp.start()
@@ -150,7 +151,9 @@
         for k in range(1, nx):
             dest = lax.rem(xx + k, nx)
             for j in range(nyh):
-                acc1[q, dest, j] = (x_ref[dest, j, core, :, cols(q)] + recv1[q, dest, j]).astype(bf16)
+                acc1[q, dest, j] = (
+                    x_ref[dest, j, core, :, cols(q)] + recv1[q, dest, j].astype(f32)
+                ).astype(bf16)
             slot = nx - 1 - k
             cp = pltpu.make_async_remote_copy(
                 src_ref=acc1.at[q, dest], dst_ref=recv2.at[q, slot],
@@ -159,7 +162,7 @@
             cp.start()
             sends.append(cp)
         for j in range(nyh):
-            own[q, j] = x_ref[xx, j, core, :, cols(q)] + recv1[q, xx, j]
+            own[q, j] = x_ref[xx, j, core, :, cols(q)] + recv1[q, xx, j].astype(f32)
         return sends
 
     def third(q):
@@ -207,7 +210,8 @@
         in_specs=[pl.BlockSpec(memory_space=pltpu.VMEM)],
         out_specs=pl.BlockSpec(memory_space=pltpu.VMEM),
         scratch_shapes=[
-            pltpu.VMEM((nchunk, nx, nyh, rows, width), f32),
+            pltpu.VMEM((nchunk, nx, nyh, rows, width), bf16),
+            pltpu.VMEM((nchunk, nx, nyh, rows, width), bf16),
             pltpu.VMEM((nchunk, nx, nyh, rows, width), bf16),
             pltpu.VMEM((nchunk, nyh, rows, width), f32),
             pltpu.VMEM((nchunk, nx - 1, nyh, rows, width), bf16),

time: 81.4 us -> 80.9 us (level)
  no operation moved by 1% of the time
where the time goes in v12:
time: 80.9 us; the launch traced here: 79.5 us
  Pallas kernels  49.4 us (61%)
  local copies, waits for them, and re-layouts  19.3 us (24%)
  other arithmetic  6.48 us (8%)
  matrix products  4.06 us (5%)
    pallas_call x1, Pallas kernels, scatter_chan(): pl.pallas_call(functools.partial(scatter_kernel, nchunk), out_shape=jax.S...  24.9 us
    pallas_call x1, Pallas kernels, gather_space(): pl.pallas_call(functools.partial(gather_kernel, n), out_shape=(jax.ShapeD...  24.5 us
    concatenate x1, local copies, waits for them, and re-layouts, local(): jnp.concatenate([bordered[:, col_tap:col_tap + col_count, row_tap:row_tap...  7.08 us
    dot_general x3, matrix products, local(): lax.dot_general(tap_weight, window, (((0,), (1,)), ((), ())), preferred_e...  4.06 us
    unnamed x17, local copies, waits for them, and re-layouts  4.03 us
    slice x1, local copies, waits for them, and re-layouts, local(): bordered[:, col_tap:col_tap + col_count, row_tap:row_tap + row_count, :]  2.96 us

profile of v12, /device:TPU:6, one launch (start us, length us, event | category | flops | bytes accessed | tf_op | source)
XLA Modules:
  0.0 79.5 jit_solution(5667900719352302803)
XLA Ops:
  0.0 1.2 %convert_reduce_fusion = f32[32]{0:T(128)S(1)} fusion(bf16[4,48,10,32]{1,3,2,0:T(8,128)(2,1)} %param.10), kind=kLoop, calls=%fused_computation.12 | loop fusion | flops 122848 | bytes 123008 | tf_op jit(solution)/shard_map/reduce_sum | solution.py:246
  1.3 0.1 reduce_sum.61
  1.6 1.3 %multiply_reduce_fusion = f32[32]{0:T(128)S(1)} fusion(f32[32]{0:T(128)S(1)} %sub.59, bf16[4,48,10,32]{1,3,2,0:T(8,128)(2,1)} %param.10), kind=kLoop, calls=%fused_computation.11 | loop fusion | flops 245728 | bytes 123136 | tf_op jit(solution)/shard_map/reduce_sum | solution.py:248
  3.0 0.1 reduce_sum.64
  3.1 0.2 scatter.9.x_ref
  3.3 1.1 %copy.27 = bf16[2,48,10,32]{3,1,2,0:T(8,128)(2,1)S(1)} copy(bf16[2,48,10,32]{1,3,2,0:T(8,128)(2,1)} %param.11) | data formatting | bytes 122880 | tf_op args[1]
  4.4 1.1 %copy.23 = bf16[2,48,10,32]{3,1,0,2:T(8,128)(2,1)S(1)} copy(bf16[2,48,10,32]{1,3,2,0:T(8,128)(2,1)} %param.11) | data formatting | bytes 122880 | tf_op args[1]
  5.5 1.3 %copy.24 = bf16[4,48,10,32]{3,1,0,2:T(8,128)(2,1)S(1)} copy(bf16[4,48,10,32]{1,3,2,0:T(8,128)(2,1)} %param.10) | data formatting | bytes 245760 | tf_op args[0]
  6.8 0.7 fusion.6
  7.5 24.5 %shard_map.64 = (f32[32,8,128]{2,1,0:T(8,128)}, bf16[6,48,32]{2,1,0:T(8,128)(2,1)}, bf16[6,48,32]{2,1,0:T(8,128)(2,1)}) custom-call(f32[8,128]{1,0:T(8,128)} %copy-done.3, bf16[6,48,32]{2,1,0:T(8,128)(2,1)} %get-tuple-element.53.lo_ref, bf16[6,48,32]{2,1,0:T(8,128)(2,1)} %get-tuple-element.52.hi_ref), custom_call_target="tpu_custom_call" | custom-call | tf_op jit(solution)/shard_map/pallas_call | solution.py:87
  32.0 1.0 %slice_reduce_fusion.1 = (f32[2]{0:T(128)S(1)}, f32[2]{0:T(128)S(1)}, f32[32,1,2]{2,1,0:T(1,128)S(1)}) fusion(f32[32,8,128]{2,1,0:T(8,128)} %get-tuple-element.33), kind=kLoop, calls=%fused_computation.35 | loop fusion | flops 124 | bytes 784 | tf_op jit(solution)/shard_map/reduce_sum | solution.py:256
  33.1 0.1 sub.63
  33.3 0.2 fusion.11
  33.5 0.1 mul.94
  33.6 0.8 slice_bitcast_fusion.1
  34.4 0.7 slice_bitcast_fusion
  35.1 0.9 %fusion.8 = (bf16[4,48,1,32]{3,1,0,2:T(8,128)(2,1)S(1)}, bf16[4,48,1,32]{3,1,2,0:T(8,128)(2,1)S(1)}) fusion(f32[32]{0:T(128)S(1)} %copy-done.4, f32[32]{0:T(128)S(1)} %copy-done.5, f32[32]{0:T(128)S(1)} %mul.94, f32[32]{0:T(128)S(1)} %sub.63, bf16[6,48,32]{2,1,0:T(8,128)(2,1)} %get-tuple-element.32, bf16[6,48,32]{2,1,0:T(8,128)(2,1)} %get-tuple-element.34), kind=kLoop, calls=%fused_computation.23 | loop fusion | flops 122880 | bytes 49664 | tf_op jit(solution)/shard_map/concatenate | solution.py:272
  36.1 0.8 fusion.15
  36.9 0.2 copy.26
  37.1 0.3 multiply_convert_fusion
  37.5 0.4 fusion.1
  37.9 3.0 %fusion.14 = (bf16[6,10,48,32]{3,2,1,0:T(8,128)(2,1)S(1)}, bf16[6,10,48,32]{3,2,1,0:T(8,128)(2,1)}, bf16[6,10,48,32]{3,2,1,0:T(8,128)(2,1)}, bf16[6,10,48,32]{3,...) fusion(bf16[6,12,50,32]{3,2,1,0:T(8,128)(2,1)S(1)} %fusion.1), kind=kLoop, calls=%fused_computation.37 | loop fusion | bytes 3317760 | tf_op jit(solution)/shard_map/slice | solution.py:282
  40.9 7.1 %concatenate.55 = bf16[6,10,48,288]{3,2,1,0:T(8,128)(2,1)S(1)} concatenate(bf16[6,10,48,32]{3,2,1,0:T(8,128)(2,1)} %get-tuple-element.48, bf16[6,10,48,32]{3,2,1,0:T(8,128)(2,1)} %get-tuple-element.47, bf16[6,10,48,32]{3,2,1,0:T(8,128)(2,1)} %get-tuple-element.46, bf16[6,10,48,32]{3,2,1,0:T(8,128)(2,1)} %get-tuple-element.45, bf16[6,10,48,32]{3,2,1,0:T(8,128)(2,1)} %get-tuple-element.44, ...), dimensions={3} | concatenate | bytes 3317760 | tf_op jit(solution)/shard_map/concatenate | solution.py:280
  48.0 0.4 fusion.13
  48.4 0.6 copy-done.1
  48.9 1.3 %fusion.17 = f32[1920,512]{0,1:T(8,128)S(1)} fusion(bf16[1920,288]{1,0:T(8,128)(2,1)S(1)} %bitcast.49, bf16[288,512]{1,0:T(8,128)(2,1)S(1)} %bitcast.54), kind=kOutput, calls=%fused_computation.40 | convolution fusion | flops 566231040 | bytes 5332992 | tf_op jit(solution)/shard_map/dot_general | solution.py:299
  50.2 1.3 %fusion.16 = f32[1920,512]{0,1:T(8,128)S(1)} fusion(bf16[1920,288]{1,0:T(8,128)(2,1)S(1)} %bitcast.48, bf16[288,512]{1,0:T(8,128)(2,1)S(1)} %bitcast.53), kind=kOutput, calls=%fused_computation.39 | convolution fusion | flops 566231040 | bytes 5332992 | tf_op jit(solution)/shard_map/dot_general | solution.py:299
  51.5 1.5 %add_add_fusion = f32[1920,512]{0,1:T(8,128)S(1)} fusion(f32[1920,512]{0,1:T(8,128)S(1)} %fusion.16, f32[1920,512]{0,1:T(8,128)S(1)} %fusion.17, bf16[1920,288]{1,0:T(8,128)(2,1)S(1)} %bitcast.50, bf16[288,512]{1,0:T(8,128)(2,1)S(1)} %bitcast.52), kind=kOutput, calls=%fused_computation | convolution fusion | flops 568197120 | bytes 13197312 | tf_op jit(solution)/shard_map/dot_general | solution.py:299
  53.0 24.9 %shard_map.65 = f32[32,1920]{1,0:T(8,128)S(1)} custom-call(f32[4,2,2,32,1920]{4,3,2,1,0:T(8,128)S(1)} %bitcast.47), custom_call_target="tpu_custom_call" | custom-call | tf_op jit(solution)/shard_map/pallas_call | solution.py:207
  77.9 0.1 fusion.5
  78.0 0.5 reshape.225
  78.5 0.9 %copy.30 = bf16[4,48,10,32]{1,3,2,0:T(8,128)(2,1)} copy(bf16[4,48,10,32]{1,2,0,3:T(8,128)(2,1)S(1)} %bitcast.51) | data formatting | bytes 245760 | tf_op jit(solution)/shard_map/transpose | solution.py:305
  (26 shorter events, 0.7 us)
Async XLA Ops:
  0.0 35.1 %copy-start.4 = (f32[32]{0:T(128)S(1)}, f32[32]{0:T(128)}, u32[]{:S(2)}) copy-start(f32[32]{0:T(128)} %param.13) | copy-start | bytes 388
  0.0 35.1 %copy-start.5 = (f32[32]{0:T(128)S(1)}, f32[32]{0:T(128)}, u32[]{:S(2)}) copy-start(f32[32]{0:T(128)} %param.12) | copy-start | bytes 388
  0.0 36.1 %copy-start.2 = (bf16[3,3,3,32,512]{4,3,2,1,0:T(8,128)(2,1)S(1)}, bf16[3,3,3,32,512]{4,3,2,1,0:T(8,128)(2,1)}, u32[]{:S(2)}) copy-start(bf16[3,3,3,32,512]{4,3,2,1,0:T(8,128)(2,1)} %param.14) | copy-start | bytes 2654212
  3.3 4.2 %copy-start.3 = (f32[8,128]{1,0:T(8,128)}, f32[8,128]{1,0:T(8,128)S(1)}, u32[]{:S(2)}) copy-start(f32[8,128]{1,0:T(8,128)S(1)} %scatter.9.x_ref) | copy-start | bytes 12292
  5.5 31.4 %copy-start = (bf16[4,48,10,32]{1,3,2,0:T(8,128)(2,1)S(1)}, bf16[4,48,10,32]{1,3,2,0:T(8,128)(2,1)}, u32[]{:S(2)}) copy-start(bf16[4,48,10,32]{1,3,2,0:T(8,128)(2,1)} %param.10) | copy-start | bytes 368644
  47.9 1.0 %copy-start.1 = (bf16[1,3,3,32,512]{4,3,2,1,0:T(8,128)(2,1)S(1)}, bf16[1,3,3,32,512]{4,3,2,1,0:T(8,128)(2,1)}, u32[]{:S(2)}) copy-start(bf16[1,3,3,32,512]{4,3,2,1,0:T(8,128)(2,1)} %get-tuple-element.51) | copy-start | bytes 884740
  53.0 24.9 %copy-start.6 = (f32[32]{0:T(128)S(1)}, f32[32]{0:T(128)}, u32[]{:S(2)}) copy-start(f32[32]{0:T(128)} %param.15) | copy-start | bytes 388

commit v13 on v10

--- a/solution.py
+++ b/solution.py
@@ -106,7 +106,7 @@
     )(tile, lo, hi)
 
 
-def scatter_kernel(nchunk, x_ref, o_ref, recv1, acc1, own, recv2, acc2, recv3,
+def scatter_kernel(nchunk, x_ref, o_ref, recv1, acc1, own, recv2, relay, acc2, recv3,
                    sem1s, sem1r, sem2s, sem2r, sem3s, sem3r):
     sp = lax.axis_index("space")
     c = lax.axis_index("chan")
@@ -143,31 +143,46 @@
                 cp.start()
                 firsts.append(cp)
 
+    east = lax.rem(xx + 1, nx)
+    west = lax.rem(xx + nx - 1, nx)
+    across = lax.rem(xx + 2, nx)
+
+    def rcopy(src, dst, q, n, peer):
+        return pltpu.make_async_remote_copy(
+            src_ref=src, dst_ref=dst, send_sem=sem2s.at[q * 6 + n], recv_sem=sem2r.at[q * 6 + n],
+            device_id=peer, device_id_type=MESH)
+
     def second(q):
         for cp in firsts[q * nx * nyh : (q + 1) * nx * nyh]:
             cp.wait()
-        sends = []
-        for k in range(1, nx):
-            dest = lax.rem(xx + k, nx)
+        for dest in (east, west, across):
             for j in range(nyh):
                 acc1[q, dest, j] = (x_ref[dest, j, core, :, cols(q)] + recv1[q, dest, j]).astype(bf16)
-            slot = nx - 1 - k
-            cp = pltpu.make_async_remote_copy(
-                src_ref=acc1.at[q, dest], dst_ref=recv2.at[q, slot],
-                send_sem=sem2s.at[q * (nx - 1) + k - 1], recv_sem=sem2r.at[q * (nx - 1) + slot],
-                device_id=peers[k], device_id_type=MESH)
+        sends = [
+            rcopy(acc1.at[q, east], recv2.at[q, 0], q, 0, peers[1]),
+            rcopy(acc1.at[q, west], recv2.at[q, 1], q, 1, peers[3]),
+            rcopy(acc1.at[q, across, 0], relay.at[q, 0], q, 2, peers[1]),
+            rcopy(acc1.at[q, across, 1], relay.at[q, 1], q, 3, peers[3]),
+        ]
+        for cp in sends:
             cp.start()
-            sends.append(cp)
         for j in range(nyh):
             own[q, j] = x_ref[xx, j, core, :, cols(q)] + recv1[q, xx, j]
+        rcopy(acc1.at[q, across, 0], relay.at[q, 0], q, 2, peers[1]).wait_recv()
+        fwd = rcopy(relay.at[q, 0], recv2.at[q, 2, 0], q, 4, peers[1])
+        fwd.start()
+        sends.append(fwd)
+        rcopy(acc1.at[q, across, 1], relay.at[q, 1], q, 3, peers[3]).wait_recv()
+        fwd = rcopy(relay.at[q, 1], recv2.at[q, 2, 1], q, 5, peers[3])
+        fwd.start()
+        sends.append(fwd)
         return sends
 
     def third(q):
-        for slot in range(nx - 1):
-            pltpu.make_async_remote_copy(
-                src_ref=acc1.at[q, xx], dst_ref=recv2.at[q, slot],
-                send_sem=sem2s.at[q * (nx - 1) + slot], recv_sem=sem2r.at[q * (nx - 1) + slot],
-                device_id=peers[0], device_id_type=MESH).wait_recv()
+        rcopy(acc1.at[q, east], recv2.at[q, 0], q, 0, peers[1]).wait_recv()
+        rcopy(acc1.at[q, west], recv2.at[q, 1], q, 1, peers[3]).wait_recv()
+        rcopy(relay.at[q, 0], recv2.at[q, 2, 0], q, 4, peers[1]).wait_recv()
+        rcopy(relay.at[q, 1], recv2.at[q, 2, 1], q, 5, peers[3]).wait_recv()
         other = 1 - yh
         total = own[q, other]
         for slot in range(nx - 1):
@@ -211,12 +226,13 @@
             pltpu.VMEM((nchunk, nx, nyh, rows, width), bf16),
             pltpu.VMEM((nchunk, nyh, rows, width), f32),
             pltpu.VMEM((nchunk, nx - 1, nyh, rows, width), bf16),
+            pltpu.VMEM((nchunk, nyh, rows, width), bf16),
             pltpu.VMEM((nchunk, rows, width), bf16),
             pltpu.VMEM((nchunk, rows, width), bf16),
             pltpu.SemaphoreType.DMA((nchunk * nx * nyh,)),
             pltpu.SemaphoreType.DMA((nchunk * nx * nyh,)),
-            pltpu.SemaphoreType.DMA((nchunk * (nx - 1),)),
-            pltpu.SemaphoreType.DMA((nchunk * (nx - 1),)),
+            pltpu.SemaphoreType.DMA((nchunk * 6,)),
+            pltpu.SemaphoreType.DMA((nchunk * 6,)),
             pltpu.SemaphoreType.DMA((nchunk,)),
             pltpu.SemaphoreType.DMA((nchunk,)),
         ],

time: 81.4 us -> 86.7 us (1.065)
  Pallas kernels: 49.9 us -> 55.7 us
    pallas_call x1, Pallas kernels: 25.4 us -> 31.2 us  [scatter_chan(): pl.pallas_call(functools.partial(scatter_kernel, nchunk), out_shape=jax.S...]
where the time goes in v13:
time: 86.7 us; the launch traced here: 85.8 us
  Pallas kernels  55.7 us (64%)
  local copies, waits for them, and re-layouts  19.3 us (22%)
  other arithmetic  6.48 us (7%)
  matrix products  4.06 us (5%)
    pallas_call x1, Pallas kernels, scatter_chan(): pl.pallas_call(functools.partial(scatter_kernel, nchunk), out_shape=jax.S...  31.2 us
    pallas_call x1, Pallas kernels, gather_space(): pl.pallas_call(functools.partial(gather_kernel, n), out_shape=(jax.ShapeD...  24.5 us
    concatenate x1, local copies, waits for them, and re-layouts, local(): jnp.concatenate([bordered[:, col_tap:col_tap + col_count, row_tap:row_tap...  7.08 us
    dot_general x3, matrix products, local(): lax.dot_general(tap_weight, window, (((0,), (1,)), ((), ())), preferred_e...  4.06 us
    unnamed x17, local copies, waits for them, and re-layouts  4.03 us
    slice x1, local copies, waits for them, and re-layouts, local(): bordered[:, col_tap:col_tap + col_count, row_tap:row_tap + row_count, :]  2.96 us

profile of v13, /device:TPU:6, one launch (start us, length us, event | category | flops | bytes accessed | tf_op | source)
XLA Modules:
  0.0 85.8 jit_solution(13784350577538381987)
XLA Ops:
  0.0 1.2 %convert_reduce_fusion = f32[32]{0:T(128)S(1)} fusion(bf16[4,48,10,32]{1,3,2,0:T(8,128)(2,1)} %param.10), kind=kLoop, calls=%fused_computation.12 | loop fusion | flops 122848 | bytes 123008 | tf_op jit(solution)/shard_map/reduce_sum | solution.py:258
  1.3 0.1 reduce_sum.61
  1.6 1.3 %multiply_reduce_fusion = f32[32]{0:T(128)S(1)} fusion(f32[32]{0:T(128)S(1)} %sub.59, bf16[4,48,10,32]{1,3,2,0:T(8,128)(2,1)} %param.10), kind=kLoop, calls=%fused_computation.11 | loop fusion | flops 245728 | bytes 123136 | tf_op jit(solution)/shard_map/reduce_sum | solution.py:260
  3.0 0.1 reduce_sum.64
  3.1 0.2 scatter.9.x_ref
  3.3 1.1 %copy.27 = bf16[2,48,10,32]{3,1,2,0:T(8,128)(2,1)S(1)} copy(bf16[2,48,10,32]{1,3,2,0:T(8,128)(2,1)} %param.11) | data formatting | bytes 122880 | tf_op args[1]
  4.4 1.1 %copy.23 = bf16[2,48,10,32]{3,1,0,2:T(8,128)(2,1)S(1)} copy(bf16[2,48,10,32]{1,3,2,0:T(8,128)(2,1)} %param.11) | data formatting | bytes 122880 | tf_op args[1]
  5.5 1.3 %copy.24 = bf16[4,48,10,32]{3,1,0,2:T(8,128)(2,1)S(1)} copy(bf16[4,48,10,32]{1,3,2,0:T(8,128)(2,1)} %param.10) | data formatting | bytes 245760 | tf_op args[0]
  6.8 0.7 fusion.6
  7.5 24.5 %shard_map.64 = (f32[32,8,128]{2,1,0:T(8,128)}, bf16[6,48,32]{2,1,0:T(8,128)(2,1)}, bf16[6,48,32]{2,1,0:T(8,128)(2,1)}) custom-call(f32[8,128]{1,0:T(8,128)} %copy-done.3, bf16[6,48,32]{2,1,0:T(8,128)(2,1)} %get-tuple-element.53.lo_ref, bf16[6,48,32]{2,1,0:T(8,128)(2,1)} %get-tuple-element.52.hi_ref), custom_call_target="tpu_custom_call" | custom-call | tf_op jit(solution)/shard_map/pallas_call | solution.py:87
  32.0 1.0 %slice_reduce_fusion.1 = (f32[2]{0:T(128)S(1)}, f32[2]{0:T(128)S(1)}, f32[32,1,2]{2,1,0:T(1,128)S(1)}) fusion(f32[32,8,128]{2,1,0:T(8,128)} %get-tuple-element.33), kind=kLoop, calls=%fused_computation.35 | loop fusion | flops 124 | bytes 784 | tf_op jit(solution)/shard_map/reduce_sum | solution.py:268
  33.1 0.1 sub.63
  33.3 0.2 fusion.11
  33.5 0.1 mul.94
  33.6 0.8 slice_bitcast_fusion.1
  34.4 0.7 slice_bitcast_fusion
  35.1 0.9 %fusion.8 = (bf16[4,48,1,32]{3,1,0,2:T(8,128)(2,1)S(1)}, bf16[4,48,1,32]{3,1,2,0:T(8,128)(2,1)S(1)}) fusion(f32[32]{0:T(128)S(1)} %copy-done.4, f32[32]{0:T(128)S(1)} %copy-done.5, f32[32]{0:T(128)S(1)} %mul.94, f32[32]{0:T(128)S(1)} %sub.63, bf16[6,48,32]{2,1,0:T(8,128)(2,1)} %get-tuple-element.32, bf16[6,48,32]{2,1,0:T(8,128)(2,1)} %get-tuple-element.34), kind=kLoop, calls=%fused_computation.23 | loop fusion | flops 122880 | bytes 49664 | tf_op jit(solution)/shard_map/concatenate | solution.py:284
  36.1 0.8 fusion.15
  36.9 0.2 copy.26
  37.1 0.3 multiply_convert_fusion
  37.5 0.4 fusion.1
  37.9 3.0 %fusion.14 = (bf16[6,10,48,32]{3,2,1,0:T(8,128)(2,1)S(1)}, bf16[6,10,48,32]{3,2,1,0:T(8,128)(2,1)}, bf16[6,10,48,32]{3,2,1,0:T(8,128)(2,1)}, bf16[6,10,48,32]{3,...) fusion(bf16[6,12,50,32]{3,2,1,0:T(8,128)(2,1)S(1)} %fusion.1), kind=kLoop, calls=%fused_computation.37 | loop fusion | bytes 3317760 | tf_op jit(solution)/shard_map/slice | solution.py:294
  40.9 7.1 %concatenate.55 = bf16[6,10,48,288]{3,2,1,0:T(8,128)(2,1)S(1)} concatenate(bf16[6,10,48,32]{3,2,1,0:T(8,128)(2,1)} %get-tuple-element.48, bf16[6,10,48,32]{3,2,1,0:T(8,128)(2,1)} %get-tuple-element.47, bf16[6,10,48,32]{3,2,1,0:T(8,128)(2,1)} %get-tuple-element.46, bf16[6,10,48,32]{3,2,1,0:T(8,128)(2,1)} %get-tuple-element.45, bf16[6,10,48,32]{3,2,1,0:T(8,128)(2,1)} %get-tuple-element.44, ...), dimensions={3} | concatenate | bytes 3317760 | tf_op jit(solution)/shard_map/concatenate | solution.py:292
  48.0 0.4 fusion.13
  48.4 0.6 copy-done.1
  48.9 1.3 %fusion.17 = f32[1920,512]{0,1:T(8,128)S(1)} fusion(bf16[1920,288]{1,0:T(8,128)(2,1)S(1)} %bitcast.49, bf16[288,512]{1,0:T(8,128)(2,1)S(1)} %bitcast.54), kind=kOutput, calls=%fused_computation.40 | convolution fusion | flops 566231040 | bytes 5332992 | tf_op jit(solution)/shard_map/dot_general | solution.py:311
  50.2 1.3 %fusion.16 = f32[1920,512]{0,1:T(8,128)S(1)} fusion(bf16[1920,288]{1,0:T(8,128)(2,1)S(1)} %bitcast.48, bf16[288,512]{1,0:T(8,128)(2,1)S(1)} %bitcast.53), kind=kOutput, calls=%fused_computation.39 | convolution fusion | flops 566231040 | bytes 5332992 | tf_op jit(solution)/shard_map/dot_general | solution.py:311
  51.5 1.5 %add_add_fusion = f32[1920,512]{0,1:T(8,128)S(1)} fusion(f32[1920,512]{0,1:T(8,128)S(1)} %fusion.16, f32[1920,512]{0,1:T(8,128)S(1)} %fusion.17, bf16[1920,288]{1,0:T(8,128)(2,1)S(1)} %bitcast.50, bf16[288,512]{1,0:T(8,128)(2,1)S(1)} %bitcast.52), kind=kOutput, calls=%fused_computation | convolution fusion | flops 568197120 | bytes 13197312 | tf_op jit(solution)/shard_map/dot_general | solution.py:311
  53.0 31.2 %shard_map.65 = f32[32,1920]{1,0:T(8,128)S(1)} custom-call(f32[4,2,2,32,1920]{4,3,2,1,0:T(8,128)S(1)} %bitcast.47), custom_call_target="tpu_custom_call" | custom-call | tf_op jit(solution)/shard_map/pallas_call | solution.py:219
  84.2 0.1 fusion.5
  84.3 0.5 reshape.225
  84.8 0.9 %copy.30 = bf16[4,48,10,32]{1,3,2,0:T(8,128)(2,1)} copy(bf16[4,48,10,32]{1,2,0,3:T(8,128)(2,1)S(1)} %bitcast.51) | data formatting | bytes 245760 | tf_op jit(solution)/shard_map/transpose | solution.py:317
  (26 shorter events, 0.7 us)
Async XLA Ops:
  0.0 35.1 %copy-start.4 = (f32[32]{0:T(128)S(1)}, f32[32]{0:T(128)}, u32[]{:S(2)}) copy-start(f32[32]{0:T(128)} %param.13) | copy-start | bytes 388
  0.0 35.1 %copy-start.5 = (f32[32]{0:T(128)S(1)}, f32[32]{0:T(128)}, u32[]{:S(2)}) copy-start(f32[32]{0:T(128)} %param.12) | copy-start | bytes 388
  0.0 36.1 %copy-start.2 = (bf16[3,3,3,32,512]{4,3,2,1,0:T(8,128)(2,1)S(1)}, bf16[3,3,3,32,512]{4,3,2,1,0:T(8,128)(2,1)}, u32[]{:S(2)}) copy-start(bf16[3,3,3,32,512]{4,3,2,1,0:T(8,128)(2,1)} %param.14) | copy-start | bytes 2654212
  3.3 4.2 %copy-start.3 = (f32[8,128]{1,0:T(8,128)}, f32[8,128]{1,0:T(8,128)S(1)}, u32[]{:S(2)}) copy-start(f32[8,128]{1,0:T(8,128)S(1)} %scatter.9.x_ref) | copy-start | bytes 12292
  5.5 31.4 %copy-start = (bf16[4,48,10,32]{1,3,2,0:T(8,128)(2,1)S(1)}, bf16[4,48,10,32]{1,3,2,0:T(8,128)(2,1)}, u32[]{:S(2)}) copy-start(bf16[4,48,10,32]{1,3,2,0:T(8,128)(2,1)} %param.10) | copy-start | bytes 368644
  47.9 1.0 %copy-start.1 = (bf16[1,3,3,32,512]{4,3,2,1,0:T(8,128)(2,1)S(1)}, bf16[1,3,3,32,512]{4,3,2,1,0:T(8,128)(2,1)}, u32[]{:S(2)}) copy-start(bf16[1,3,3,32,512]{4,3,2,1,0:T(8,128)(2,1)} %get-tuple-element.51) | copy-start | bytes 884740
  53.0 31.2 %copy-start.6 = (f32[32]{0:T(128)S(1)}, f32[32]{0:T(128)}, u32[]{:S(2)}) copy-start(f32[32]{0:T(128)} %param.15) | copy-start | bytes 388

commit v14 on v10

--- a/solution.py
+++ b/solution.py
@@ -273,28 +273,22 @@
     bordered = jnp.pad(bordered, ((0, 0), (1, 1), (0, 0), (0, 0)))
     cell_count = nframes * row_count * col_count
     bordered = bordered.transpose(0, 2, 1, 3)
-    columns_in = jnp.concatenate(
-        [
-            bordered[:, col_tap : col_tap + col_count, row_tap : row_tap + row_count, :]
-            for row_tap in range(3)
-            for col_tap in range(3)
-        ],
-        axis=3,
-    )
-    columns_in = with_layout_constraint(columns_in, Layout(major_to_minor=(0, 1, 2, 3)))
-    tap_width = columns_in.shape[3]
+    rows_in = jnp.concatenate(
+        [bordered[:, :, row_tap : row_tap + row_count, :] for row_tap in range(3)], axis=3
+    )
+    rows_in = with_layout_constraint(rows_in, Layout(major_to_minor=(0, 1, 2, 3)))
+    tap_width = rows_in.shape[3]
     nchan = lax.axis_size("chan")
     nx = nchan // 4
-    flat_kernel = kernel.reshape(3, tap_width, kernel.shape[4])
     running = jnp.zeros((bias.shape[0] * nchan, cell_count), jnp.float32)
-    plane = row_count * col_count
-    flat_in = columns_in.reshape(columns_in.shape[0] * plane, tap_width)
     for depth in range(3):
-        tap_weight = flat_kernel[depth]
-        window = flat_in[depth * plane : depth * plane + cell_count]
-        running = running + lax.dot_general(
-            tap_weight, window, (((0,), (1,)), ((), ())), preferred_element_type=jnp.float32
-        )
+        for col_tap in range(3):
+            tap_weight = kernel[depth, :, col_tap].reshape(tap_width, kernel.shape[4])
+            window = rows_in[depth : depth + nframes, col_tap : col_tap + col_count]
+            window = window.reshape(cell_count, tap_width)
+            running = running + lax.dot_general(
+                tap_weight, window, (((0,), (1,)), ((), ())), preferred_element_type=jnp.float32
+            )
     summed = scatter_chan(running.reshape(nx, 2, 2, local_ch, cell_count))
     result = summed.T + bias
     result = result.astype(jnp.bfloat16).reshape(nframes, col_count, row_count, -1)

time: 81.4 us -> 91.7 us (1.13)
  matrix products: 4.06 us -> 24.3 us
  local copies, waits for them, and re-layouts: 19.3 us -> 8.69 us
    dot_general x3 -> x9, matrix products: 4.06 us -> 24.3 us  [local(): lax.dot_general(tap_weight, window, (((0,), (1,)), ((), ())), preferred_e...]
    concatenate x1 -> x0, local copies, waits for them, and re-layouts: 7.08 us -> none  [local(): jnp.concatenate([bordered[:, col_tap:col_tap + col_count, row_tap:row_tap...]
    slice x3, local copies, waits for them, and re-layouts: 4.13 us -> 1.22 us  [the longest x1 0.57 us: local(): window = rows_in[depth:depth + nframes, col_tap:col_tap + col_count]]
    unnamed x17 -> x15, local copies, waits for them, and re-layouts: 4.03 us -> 3.4 us
where the time goes in v14:
time: 91.7 us; the launch traced here: 90.6 us
  Pallas kernels  50 us (55%)
  matrix products  24.3 us (26%)
  local copies, waits for them, and re-layouts  8.69 us (9%)
  other arithmetic  7.34 us (8%)
    pallas_call x1, Pallas kernels, scatter_chan(): pl.pallas_call(functools.partial(scatter_kernel, nchunk), out_shape=jax.S...  25.5 us
    pallas_call x1, Pallas kernels, gather_space(): pl.pallas_call(functools.partial(gather_kernel, n), out_shape=(jax.ShapeD...  24.5 us
    dot_general x9, matrix products, local(): lax.dot_general(tap_weight, window, (((0,), (1,)), ((), ())), preferred_e...  24.3 us
    unnamed x15, local copies, waits for them, and re-layouts  3.4 us

profile of v14, /device:TPU:6, one launch (start us, length us, event | category | flops | bytes accessed | tf_op | source)
XLA Modules:
  0.0 90.6 jit_solution(17112079868574002352)
XLA Ops:
  0.0 1.3 %convert_reduce_fusion = f32[32]{0:T(128)S(1)} fusion(bf16[4,48,10,32]{1,3,2,0:T(8,128)(2,1)} %param.10), kind=kLoop, calls=%fused_computation.13 | loop fusion | flops 122848 | bytes 123008 | tf_op jit(solution)/shard_map/reduce_sum | solution.py:242
  1.7 1.3 %multiply_reduce_fusion = f32[32]{0:T(128)S(1)} fusion(f32[32]{0:T(128)S(1)} %sub.59, bf16[4,48,10,32]{1,3,2,0:T(8,128)(2,1)} %param.10), kind=kLoop, calls=%fused_computation.12 | loop fusion | flops 245728 | bytes 123136 | tf_op jit(solution)/shard_map/reduce_sum | solution.py:244
  3.0 0.1 reduce_sum.64
  3.1 0.2 scatter.9.x_ref
  3.3 1.1 %copy.27 = bf16[2,48,10,32]{3,1,2,0:T(8,128)(2,1)S(1)} copy(bf16[2,48,10,32]{1,3,2,0:T(8,128)(2,1)} %param.11) | data formatting | bytes 122880 | tf_op args[1]
  4.4 1.1 %copy.23 = bf16[2,48,10,32]{3,1,0,2:T(8,128)(2,1)S(1)} copy(bf16[2,48,10,32]{1,3,2,0:T(8,128)(2,1)} %param.11) | data formatting | bytes 122880 | tf_op args[1]
  5.5 1.2 %copy.24 = bf16[4,48,10,32]{3,1,0,2:T(8,128)(2,1)S(1)} copy(bf16[4,48,10,32]{1,3,2,0:T(8,128)(2,1)} %param.10) | data formatting | bytes 245760 | tf_op args[0]
  6.7 0.7 fusion.6
  7.4 24.5 %shard_map.64 = (f32[32,8,128]{2,1,0:T(8,128)}, bf16[6,48,32]{2,1,0:T(8,128)(2,1)}, bf16[6,48,32]{2,1,0:T(8,128)(2,1)}) custom-call(f32[8,128]{1,0:T(8,128)} %copy-done.2, bf16[6,48,32]{2,1,0:T(8,128)(2,1)} %get-tuple-element.59.lo_ref, bf16[6,48,32]{2,1,0:T(8,128)(2,1)} %get-tuple-element.58.hi_ref), custom_call_target="tpu_custom_call" | custom-call | tf_op jit(solution)/shard_map/pallas_call | solution.py:87
  31.9 1.0 %slice_reduce_fusion.1 = (f32[2]{0:T(128)S(1)}, f32[2]{0:T(128)S(1)}, f32[32,1,2]{2,1,0:T(1,128)S(1)}) fusion(f32[32,8,128]{2,1,0:T(8,128)} %get-tuple-element.33), kind=kLoop, calls=%fused_computation.36 | loop fusion | flops 124 | bytes 784 | tf_op jit(solution)/shard_map/reduce_sum | solution.py:252
  33.2 0.2 fusion.11
  33.6 0.8 slice_bitcast_fusion.1
  34.3 0.7 slice_bitcast_fusion
  35.1 0.9 %fusion.8 = (bf16[4,48,1,32]{3,1,0,2:T(8,128)(2,1)S(1)}, bf16[4,48,1,32]{3,1,2,0:T(8,128)(2,1)S(1)}) fusion(f32[32]{0:T(128)} %param.13, f32[32]{0:T(128)} %param.12, f32[32]{0:T(128)S(1)} %mul.94, f32[32]{0:T(128)S(1)} %sub.63, bf16[6,48,32]{2,1,0:T(8,128)(2,1)} %get-tuple-element.32, bf16[6,48,32]{2,1,0:T(8,128)(2,1)} %get-tuple-element.34), kind=kLoop, calls=%fused_computation.24 | loop fusion | flops 122880 | bytes 49664 | tf_op jit(solution)/shard_map/concatenate | solution.py:268
  36.2 0.2 copy.26
  36.4 0.3 multiply_convert_fusion
  36.8 0.4 fusion.1
  37.2 0.6 fusion.13
  37.8 0.8 pad_maximum_fusion
  38.6 0.6 fusion.15
  39.2 0.7 fusion.23
  39.9 0.7 fusion.22
  40.6 0.7 fusion.21
  41.3 2.6 %fusion.20 = f32[1920,512]{0,1:T(8,128)} fusion(bf16[1920,96]{1,0:T(8,128)(2,1)S(1)} %bitcast.77, bf16[96,512]{1,0:T(8,128)(2,1)S(1)} %bitcast.86), kind=kOutput, calls=%fused_computation.44 | convolution fusion | flops 188743680 | bytes 4399104 | tf_op jit(solution)/shard_map/dot_general | solution.py:289
  43.9 2.6 %fusion.19 = f32[1920,512]{0,1:T(8,128)} fusion(bf16[1920,96]{1,0:T(8,128)(2,1)S(1)} %bitcast.76, bf16[96,512]{1,0:T(8,128)(2,1)S(1)} %bitcast.85), kind=kOutput, calls=%fused_computation.43 | convolution fusion | flops 188743680 | bytes 4399104 | tf_op jit(solution)/shard_map/dot_general | solution.py:289
  46.5 2.7 %fusion.18 = f32[1920,512]{0,1:T(8,128)} fusion(bf16[1920,96]{1,0:T(8,128)(2,1)S(1)} %bitcast.75, bf16[96,512]{1,0:T(8,128)(2,1)S(1)} %bitcast.84), kind=kOutput, calls=%fused_computation.42 | convolution fusion | flops 188743680 | bytes 4399104 | tf_op jit(solution)/shard_map/dot_general | solution.py:289
  49.2 2.6 %fusion.17 = f32[1920,512]{0,1:T(8,128)} fusion(bf16[1920,96]{1,0:T(8,128)(2,1)S(1)} %bitcast.74, bf16[96,512]{1,0:T(8,128)(2,1)S(1)} %bitcast.83), kind=kOutput, calls=%fused_computation.41 | convolution fusion | flops 188743680 | bytes 4399104 | tf_op jit(solution)/shard_map/dot_general | solution.py:289
  51.9 2.7 %fusion.16 = f32[1920,512]{0,1:T(8,128)} fusion(bf16[1920,96]{1,0:T(8,128)(2,1)S(1)} %bitcast.73, bf16[96,512]{1,0:T(8,128)(2,1)S(1)} %bitcast.82), kind=kOutput, calls=%fused_computation.40 | convolution fusion | flops 188743680 | bytes 4399104 | tf_op jit(solution)/shard_map/dot_general | solution.py:289
  54.5 9.0 %add_add_fusion = f32[1920,512]{0,1:T(8,128)S(1)} fusion(f32[1920,512]{0,1:T(8,128)S(1)} %fusion.23, f32[1920,512]{0,1:T(8,128)S(1)} %fusion.22, f32[1920,512]{0,1:T(8,128)S(1)} %fusion.21, f32[1920,512]{0,1:T(8,128)} %fusion.20, f32[1920,512]{0,1:T(8,128)} %fusion.19, f32[1920,512]{0,1:T(8,128)} %fusion.18, f32[1920,512]{0,1:T(8,128)} %fusion.16, ...), kind=kOutput, calls=%fused_computation | convolution fusion | flops 196608000 | bytes 35856384 | tf_op jit(solution)/shard_map/dot_general | solution.py:289
  63.5 25.5 %shard_map.65 = f32[32,1920]{1,0:T(8,128)S(1)} custom-call(f32[4,2,2,32,1920]{4,3,2,1,0:T(8,128)S(1)} %bitcast.71), custom_call_target="tpu_custom_call" | custom-call | tf_op jit(solution)/shard_map/pallas_call | solution.py:204
  89.1 0.5 reshape.250
  89.6 0.9 %copy.30 = bf16[4,48,10,32]{1,3,2,0:T(8,128)(2,1)} copy(bf16[4,48,10,32]{1,2,0,3:T(8,128)(2,1)S(1)} %bitcast.72) | data formatting | bytes 245760 | tf_op jit(solution)/shard_map/transpose | solution.py:295
  (30 shorter events, 1.1 us)
Async XLA Ops:
  0.0 36.2 %copy-start = (bf16[4,48,10,32]{1,3,2,0:T(8,128)(2,1)S(1)}, bf16[4,48,10,32]{1,3,2,0:T(8,128)(2,1)}, u32[]{:S(2)}) copy-start(bf16[4,48,10,32]{1,3,2,0:T(8,128)(2,1)} %param.10) | copy-start | bytes 368644
  0.0 36.4 %copy-start.3 = (f32[32]{0:T(128)S(1)}, f32[32]{0:T(128)}, u32[]{:S(2)}) copy-start(f32[32]{0:T(128)} %param.13) | copy-start | bytes 388
  0.0 36.4 %copy-start.4 = (f32[32]{0:T(128)S(1)}, f32[32]{0:T(128)}, u32[]{:S(2)}) copy-start(f32[32]{0:T(128)} %param.12) | copy-start | bytes 388
  0.0 36.1 %copy-start.1 = (bf16[3,3,3,32,512]{4,3,2,1,0:T(8,128)(2,1)S(1)}, bf16[3,3,3,32,512]{4,3,2,1,0:T(8,128)(2,1)}, u32[]{:S(2)}) copy-start(bf16[3,3,3,32,512]{4,3,2,1,0:T(8,128)(2,1)} %param.14) | copy-start | bytes 2654212
  3.3 4.1 %copy-start.2 = (f32[8,128]{1,0:T(8,128)}, f32[8,128]{1,0:T(8,128)S(1)}, u32[]{:S(2)}) copy-start(f32[8,128]{1,0:T(8,128)S(1)} %scatter.9.x_ref) | copy-start | bytes 12292
  63.5 25.5 %copy-start.5 = (f32[32]{0:T(128)S(1)}, f32[32]{0:T(128)}, u32[]{:S(2)}) copy-start(f32[32]{0:T(128)} %param.15) | copy-start | bytes 388

commit v15 on v10

--- a/solution.py
+++ b/solution.py
@@ -273,19 +273,18 @@
     bordered = jnp.pad(bordered, ((0, 0), (1, 1), (0, 0), (0, 0)))
     cell_count = nframes * row_count * col_count
     bordered = bordered.transpose(0, 2, 1, 3)
+    rows_in = jnp.concatenate(
+        [bordered[:, :, row_tap : row_tap + row_count, :] for row_tap in range(3)], axis=3
+    )
+    rows_in = with_layout_constraint(rows_in, Layout(major_to_minor=(0, 1, 2, 3)))
     columns_in = jnp.concatenate(
-        [
-            bordered[:, col_tap : col_tap + col_count, row_tap : row_tap + row_count, :]
-            for row_tap in range(3)
-            for col_tap in range(3)
-        ],
-        axis=3,
+        [rows_in[:, col_tap : col_tap + col_count] for col_tap in range(3)], axis=3
     )
     columns_in = with_layout_constraint(columns_in, Layout(major_to_minor=(0, 1, 2, 3)))
     tap_width = columns_in.shape[3]
     nchan = lax.axis_size("chan")
     nx = nchan // 4
-    flat_kernel = kernel.reshape(3, tap_width, kernel.shape[4])
+    flat_kernel = kernel.transpose(0, 2, 1, 3, 4).reshape(3, tap_width, kernel.shape[4])
     running = jnp.zeros((bias.shape[0] * nchan, cell_count), jnp.float32)
     plane = row_count * col_count
     flat_in = columns_in.reshape(columns_in.shape[0] * plane, tap_width)

time: 81.4 us -> 72.4 us (0.89)
  local copies, waits for them, and re-layouts: 19.3 us -> 8.89 us
  other arithmetic: 6.48 us -> 8.44 us
    concatenate x1 -> x0, local copies, waits for them, and re-layouts: 7.08 us -> none  [local(): jnp.concatenate([bordered[:, col_tap:col_tap + col_count, row_tap:row_tap...]
    slice x1 -> x2, local copies, waits for them, and re-layouts: 2.96 us -> 0.84 us  [the longest x1 0.56 us: local(): bordered[:, :, row_tap:row_tap + row_count, :]]
    concatenate x0 -> x2, other arithmetic: none -> 1.95 us  [the longest x1 1.14 us: local(): jnp.concatenate([rows_in[:, col_tap:col_tap + col_count] for col_tap in r...]
    unnamed x17 -> x16, local copies, waits for them, and re-layouts: 4.03 us -> 3.46 us
where the time goes in v15:
time: 72.4 us; the launch traced here: 71.3 us
  Pallas kernels  49.9 us (69%)
  local copies, waits for them, and re-layouts  8.89 us (12%)
  other arithmetic  8.44 us (12%)
  matrix products  3.81 us (5%)
    pallas_call x1, Pallas kernels, scatter_chan(): pl.pallas_call(functools.partial(scatter_kernel, nchunk), out_shape=jax.S...  25.4 us
    pallas_call x1, Pallas kernels, gather_space(): pl.pallas_call(functools.partial(gather_kernel, n), out_shape=(jax.ShapeD...  24.5 us
    dot_general x3, matrix products, local(): lax.dot_general(tap_weight, window, (((0,), (1,)), ((), ())), preferred_e...  3.81 us
    unnamed x16, local copies, waits for them, and re-layouts  3.46 us

profile of v15, /device:TPU:6, one launch (start us, length us, event | category | flops | bytes accessed | tf_op | source)
XLA Modules:
  0.0 71.3 jit_solution(4253750267089144775)
XLA Ops:
  0.0 1.2 %convert_reduce_fusion = f32[32]{0:T(128)S(1)} fusion(bf16[4,48,10,32]{1,3,2,0:T(8,128)(2,1)} %param.10), kind=kLoop, calls=%fused_computation.15 | loop fusion | flops 122848 | bytes 123008 | tf_op jit(solution)/shard_map/reduce_sum | solution.py:242
  1.3 0.1 reduce_sum.60
  1.3 0.1 reduce_sum.61
  1.5 0.1 sub.59
  1.6 1.3 %multiply_reduce_fusion = f32[32]{0:T(128)S(1)} fusion(f32[32]{0:T(128)S(1)} %sub.59, bf16[4,48,10,32]{1,3,2,0:T(8,128)(2,1)} %param.10), kind=kLoop, calls=%fused_computation.14 | loop fusion | flops 245728 | bytes 123136 | tf_op jit(solution)/shard_map/reduce_sum | solution.py:244
  3.0 0.1 reduce_sum.64
  3.1 0.2 scatter.9.x_ref
  3.3 1.1 %copy.28 = bf16[2,48,10,32]{3,1,2,0:T(8,128)(2,1)S(1)} copy(bf16[2,48,10,32]{1,3,2,0:T(8,128)(2,1)} %param.11) | data formatting | bytes 122880 | tf_op args[1]
  4.4 1.1 %copy.24 = bf16[2,48,10,32]{3,1,0,2:T(8,128)(2,1)S(1)} copy(bf16[2,48,10,32]{1,3,2,0:T(8,128)(2,1)} %param.11) | data formatting | bytes 122880 | tf_op args[1]
  5.5 1.2 %copy.25 = bf16[4,48,10,32]{3,1,0,2:T(8,128)(2,1)S(1)} copy(bf16[4,48,10,32]{1,3,2,0:T(8,128)(2,1)} %param.10) | data formatting | bytes 245760 | tf_op args[0]
  6.7 0.7 fusion.6
  7.4 24.5 %shard_map.64 = (f32[32,8,128]{2,1,0:T(8,128)}, bf16[6,48,32]{2,1,0:T(8,128)(2,1)}, bf16[6,48,32]{2,1,0:T(8,128)(2,1)}) custom-call(f32[8,128]{1,0:T(8,128)} %copy-done.2, bf16[6,48,32]{2,1,0:T(8,128)(2,1)} %get-tuple-element.50.lo_ref, bf16[6,48,32]{2,1,0:T(8,128)(2,1)} %get-tuple-element.49.hi_ref), custom_call_target="tpu_custom_call" | custom-call | tf_op jit(solution)/shard_map/pallas_call | solution.py:87
  31.9 1.0 %slice_reduce_fusion.1 = (f32[2]{0:T(128)S(1)}, f32[2]{0:T(128)S(1)}, f32[32,1,2]{2,1,0:T(1,128)S(1)}) fusion(f32[32,8,128]{2,1,0:T(8,128)} %get-tuple-element.33), kind=kLoop, calls=%fused_computation.38 | loop fusion | flops 124 | bytes 784 | tf_op jit(solution)/shard_map/reduce_sum | solution.py:252
  33.2 0.2 fusion.11
  33.6 0.8 %slice_bitcast_fusion.1 = bf16[2,48,1,32]{3,1,0,2:T(8,128)(2,1)S(1)} fusion(bf16[6,48,32]{2,1,0:T(8,128)(2,1)} %get-tuple-element.32), kind=kLoop, calls=%fused_computation.29 | loop fusion | bytes 12288 | tf_op jit(solution)/shard_map/concatenate | solution.py:268
  34.4 0.7 %slice_bitcast_fusion = bf16[2,48,1,32]{3,1,2,0:T(8,128)(2,1)S(1)} fusion(bf16[6,48,32]{2,1,0:T(8,128)(2,1)} %get-tuple-element.34), kind=kLoop, calls=%fused_computation.28 | loop fusion | bytes 12288 | tf_op jit(solution)/shard_map/concatenate | solution.py:269
  35.1 0.9 %fusion.8 = (bf16[4,48,1,32]{3,1,0,2:T(8,128)(2,1)S(1)}, bf16[4,48,1,32]{3,1,2,0:T(8,128)(2,1)S(1)}) fusion(f32[32]{0:T(128)S(1)} %copy-done.3, f32[32]{0:T(128)S(1)} %copy-done.4, f32[32]{0:T(128)S(1)} %mul.94, f32[32]{0:T(128)S(1)} %sub.63, bf16[6,48,32]{2,1,0:T(8,128)(2,1)} %get-tuple-element.32, bf16[6,48,32]{2,1,0:T(8,128)(2,1)} %get-tuple-element.34), kind=kLoop, calls=%fused_computation.26 | loop fusion | flops 122880 | bytes 49664 | tf_op jit(solution)/shard_map/concatenate | solution.py:268
  36.3 0.2 copy.27
  36.5 0.3 multiply_convert_fusion
  36.8 0.4 fusion.1
  37.3 0.6 fusion.14
  37.8 0.8 %pad_maximum_fusion.1 = bf16[6,12,48,96]{3,2,1,0:T(8,128)(2,1)S(1)} fusion(bf16[6,12,48,32]{3,2,1,0:T(8,128)(2,1)S(1)} %get-tuple-element.41, bf16[6,12,48,32]{3,2,1,0:T(8,128)(2,1)S(1)} %get-tuple-element.42, bf16[6,12,48,32]{3,2,1,0:T(8,128)(2,1)S(1)} %get-tuple-element.40), kind=kLoop, calls=%fused_computation.12 | loop fusion | flops 1990656 | bytes 1327104 | tf_op jit(solution)/shard_map/concatenate | solution.py:276
  38.6 0.3 fusion.16
  38.9 1.1 %pad_maximum_fusion = bf16[6,10,48,288]{3,2,1,0:T(8,128)(2,1)S(1)} fusion(bf16[6,10,48,96]{3,2,1,0:T(8,128)(2,1)S(1)} %get-tuple-element.48, bf16[6,10,48,96]{3,2,1,0:T(8,128)(2,1)S(1)} %get-tuple-element.47, bf16[6,10,48,96]{3,2,1,0:T(8,128)(2,1)S(1)} %get-tuple-element.46), kind=kLoop, calls=%fused_computation.3 | loop fusion | flops 4976640 | bytes 3317760 | tf_op jit(solution)/shard_map/concatenate | solution.py:280
  40.1 0.4 fusion.13
  40.5 1.3 %fusion.18 = f32[1920,512]{0,1:T(8,128)S(1)} fusion(bf16[1920,288]{1,0:T(8,128)(2,1)S(1)} %bitcast.52, bf16[288,512]{1,0:T(8,128)(2,1)S(1)} %bitcast.58), kind=kOutput, calls=%fused_computation.44 | convolution fusion | flops 566231040 | bytes 5332992 | tf_op jit(solution)/shard_map/dot_general | solution.py:294
  41.7 1.3 %fusion.17 = f32[1920,512]{0,1:T(8,128)S(1)} fusion(bf16[1920,288]{1,0:T(8,128)(2,1)S(1)} %bitcast.51, bf16[288,512]{1,0:T(8,128)(2,1)S(1)} %bitcast.57), kind=kOutput, calls=%fused_computation.43 | convolution fusion | flops 566231040 | bytes 5332992 | tf_op jit(solution)/shard_map/dot_general | solution.py:294
  43.0 1.3 %add_add_fusion = f32[1920,512]{0,1:T(8,128)S(1)} fusion(f32[1920,512]{0,1:T(8,128)S(1)} %fusion.17, f32[1920,512]{0,1:T(8,128)S(1)} %fusion.18, bf16[1920,288]{1,0:T(8,128)(2,1)S(1)} %bitcast.53, bf16[288,512]{1,0:T(8,128)(2,1)S(1)} %bitcast.56), kind=kOutput, calls=%fused_computation | convolution fusion | flops 568197120 | bytes 13197312 | tf_op jit(solution)/shard_map/dot_general | solution.py:294
  44.3 25.4 %shard_map.65 = f32[32,1920]{1,0:T(8,128)S(1)} custom-call(f32[4,2,2,32,1920]{4,3,2,1,0:T(8,128)S(1)} %bitcast.50), custom_call_target="tpu_custom_call" | custom-call | tf_op jit(solution)/shard_map/pallas_call | solution.py:204
  69.7 0.1 fusion.5
  69.8 0.5 reshape.225
  70.3 0.9 %copy.32 = bf16[4,48,10,32]{1,3,2,0:T(8,128)(2,1)} copy(bf16[4,48,10,32]{1,2,0,3:T(8,128)(2,1)S(1)} %bitcast.55) | data formatting | bytes 245760 | tf_op jit(solution)/shard_map/transpose | solution.py:300
  (27 shorter events, 0.8 us)
Async XLA Ops:
  0.0 35.1 %copy-start.3 = (f32[32]{0:T(128)S(1)}, f32[32]{0:T(128)}, u32[]{:S(2)}) copy-start(f32[32]{0:T(128)} %param.13) | copy-start | bytes 388
  0.0 35.1 %copy-start.4 = (f32[32]{0:T(128)S(1)}, f32[32]{0:T(128)}, u32[]{:S(2)}) copy-start(f32[32]{0:T(128)} %param.12) | copy-start | bytes 388
  0.0 36.1 %copy-start.1 = (bf16[3,3,3,32,512]{4,3,2,1,0:T(8,128)(2,1)S(1)}, bf16[3,3,3,32,512]{4,3,2,1,0:T(8,128)(2,1)}, u32[]{:S(2)}) copy-start(bf16[3,3,3,32,512]{4,3,2,1,0:T(8,128)(2,1)} %param.14) | copy-start | bytes 2654212
  3.3 4.1 %copy-start.2 = (f32[8,128]{1,0:T(8,128)}, f32[8,128]{1,0:T(8,128)S(1)}, u32[]{:S(2)}) copy-start(f32[8,128]{1,0:T(8,128)S(1)} %scatter.9.x_ref) | copy-start | bytes 12292
  33.6 2.7 %copy-start = (bf16[4,48,10,32]{1,3,2,0:T(8,128)(2,1)S(1)}, bf16[4,48,10,32]{1,3,2,0:T(8,128)(2,1)}, u32[]{:S(2)}) copy-start(bf16[4,48,10,32]{1,3,2,0:T(8,128)(2,1)} %param.10) | copy-start | bytes 368644
  44.3 25.4 %copy-start.5 = (f32[32]{0:T(128)S(1)}, f32[32]{0:T(128)}, u32[]{:S(2)}) copy-start(f32[32]{0:T(128)} %param.15) | copy-start | bytes 388

commit v16 on v15

--- a/solution.py
+++ b/solution.py
@@ -234,7 +234,9 @@
     me = lax.axis_index("space")
     local_members = float(nframes * row_count * col_count * group_size)
 
-    raw = jnp.concatenate([cache, frames], axis=0)
+
+    def edge(col):
+        return jnp.concatenate([cache[:, :, col], frames[:, :, col]], axis=0).transpose(0, 2, 1)
 
     values = frames.astype(jnp.float32).reshape(
         nframes, row_count, col_count, local_groups, group_size
@@ -244,9 +246,9 @@
     local_m2 = jnp.sum(local_dev * local_dev, axis=(0, 1, 2, 4))
     tile = jnp.zeros((8, 128), jnp.float32)
     tile = tile.at[0, :local_groups].set(local_mean).at[1, :local_groups].set(local_m2)
-    gathered, before, after = gather_space(tile, raw[:, :, 0], raw[:, :, col_count - 1])
-    before = before[:, :, None]
-    after = after[:, :, None]
+    gathered, before, after = gather_space(tile, edge(0), edge(col_count - 1))
+    before = before.transpose(0, 2, 1)[:, :, None]
+    after = after.transpose(0, 2, 1)[:, :, None]
     means = gathered[:, 0, :local_groups]
     m2s = gathered[:, 1, :local_groups]
     group_mean = jnp.mean(means, axis=0)

time: 72.4 us -> 70.3 us (0.971)
  Pallas kernels: 49.9 us -> 48.7 us
  local copies, waits for them, and re-layouts: 8.89 us -> 8.04 us
    unnamed x16, local copies, waits for them, and re-layouts: 3.46 us -> 0.81 us
    pallas_call x0 -> x2, local copies, waits for them, and re-layouts: none -> 1.81 us  [gather_space(): pl.pallas_call(functools.partial(gather_kernel, n), out_shape=(jax.ShapeD...]
    squeeze x0 -> x2, local copies, waits for them, and re-layouts: none -> 1.53 us  [the longest x1 0.78 us: edge(): frames[:, :, col]]
    pallas_call x1, Pallas kernels: 24.5 us -> 23.4 us  [gather_space(): pl.pallas_call(functools.partial(gather_kernel, n), out_shape=(jax.ShapeD...]
    concatenate x1, local copies, waits for them, and re-layouts: 0.8 us -> 0.01 us  [local(): left = jnp.concatenate([before[:ncache], activate(before[ncache:])], axis=0)]
    concatenate x1, local copies, waits for them, and re-layouts: 0.74 us -> 0.01 us  [local(): right = jnp.concatenate([after[:ncache], activate(after[ncache:])], axis=0)]
where the time goes in v16:
time: 70.3 us; the launch traced here: 69.1 us
  Pallas kernels  48.7 us (69%)
  other arithmetic  8.27 us (12%)
  local copies, waits for them, and re-layouts  8.04 us (11%)
  matrix products  3.81 us (5%)
    pallas_call x1, Pallas kernels, scatter_chan(): pl.pallas_call(functools.partial(scatter_kernel, nchunk), out_shape=jax.S...  25.3 us
    pallas_call x1, Pallas kernels, gather_space(): pl.pallas_call(functools.partial(gather_kernel, n), out_shape=(jax.ShapeD...  23.4 us
    dot_general x3, matrix products, local(): lax.dot_general(tap_weight, window, (((0,), (1,)), ((), ())), preferred_e...  3.81 us
    pallas_call x2, local copies, waits for them, and re-layouts, gather_space(): pl.pallas_call(functools.partial(gather_kernel, n), out_shape=(jax.ShapeD...  1.81 us

profile of v16, /device:TPU:6, one launch (start us, length us, event | category | flops | bytes accessed | tf_op | source)
XLA Modules:
  0.0 69.1 jit_solution(15725470231550398980)
XLA Ops:
  0.0 1.2 %convert_reduce_fusion = f32[32]{0:T(128)S(1)} fusion(bf16[4,48,10,32]{1,3,2,0:T(8,128)(2,1)} %param.10), kind=kLoop, calls=%fused_computation.15 | loop fusion | flops 122848 | bytes 123008 | tf_op jit(solution)/shard_map/reduce_sum | solution.py:244
  1.3 0.1 reduce_sum.61
  1.6 1.3 %multiply_reduce_fusion = f32[32]{0:T(128)S(1)} fusion(f32[32]{0:T(128)S(1)} %sub.59, bf16[4,48,10,32]{1,3,2,0:T(8,128)(2,1)} %param.10), kind=kLoop, calls=%fused_computation.14 | loop fusion | flops 245728 | bytes 123136 | tf_op jit(solution)/shard_map/reduce_sum | solution.py:246
  3.0 0.1 reduce_sum.64
  3.1 0.2 scatter.9.x_ref
  3.3 0.7 %slice_bitcast_fusion.4 = (bf16[2,48,32]{1,2,0:T(8,128)(2,1)S(1)}, bf16[2,48,32]{1,2,0:T(8,128)(2,1)S(1)}) fusion(bf16[2,48,10,32]{1,3,2,0:T(8,128)(2,1)} %param.11), kind=kLoop, calls=%fused_computation.32 | loop fusion | bytes 24576 | tf_op jit(solution)/shard_map/squeeze | solution.py:239
  4.1 0.8 %slice_bitcast_fusion = (bf16[4,48,32]{1,2,0:T(8,128)(2,1)S(1)}, bf16[4,48,32]{1,2,0:T(8,128)(2,1)S(1)}) fusion(bf16[4,48,10,32]{1,3,2,0:T(8,128)(2,1)} %param.10), kind=kLoop, calls=%fused_computation.27 | loop fusion | bytes 49152 | tf_op jit(solution)/shard_map/squeeze | solution.py:239
  4.8 0.7 maximum_bitcast_fusion
  5.5 23.4 %shard_map.64 = (f32[32,8,128]{2,1,0:T(8,128)}, bf16[6,32,48]{2,1,0:T(8,128)(2,1)}, bf16[6,32,48]{2,1,0:T(8,128)(2,1)}) custom-call(f32[8,128]{1,0:T(8,128)} %copy-done.3, bf16[6,32,48]{2,1,0:T(8,128)(2,1)} %get-tuple-element.58.lo_ref, bf16[6,32,48]{2,1,0:T(8,128)(2,1)} %get-tuple-element.59.hi_ref), custom_call_target="tpu_custom_call" | custom-call | tf_op jit(solution)/shard_map/pallas_call | solution.py:87
  28.9 1.0 %slice_reduce_fusion.1 = (f32[2]{0:T(128)S(1)}, f32[2]{0:T(128)S(1)}, f32[32,1,2]{2,1,0:T(1,128)S(1)}) fusion(f32[32,8,128]{2,1,0:T(8,128)} %get-tuple-element.33), kind=kLoop, calls=%fused_computation.41 | loop fusion | flops 124 | bytes 784 | tf_op jit(solution)/shard_map/reduce_sum | solution.py:254
  30.1 0.2 fusion.10
  30.5 0.9 %copy.38 = bf16[6,32,48]{1,2,0:T(8,128)(2,1)S(1)} copy(bf16[6,32,48]{2,1,0:T(8,128)(2,1)} %get-tuple-element.32) | data formatting | bytes 36864 | tf_op jit(solution)/shard_map/pallas_call | solution.py:87
  31.4 0.9 %copy.42 = bf16[6,32,48]{1,2,0:T(8,128)(2,1)S(1)} copy(bf16[6,32,48]{2,1,0:T(8,128)(2,1)} %get-tuple-element.34) | data formatting | bytes 36864 | tf_op jit(solution)/shard_map/pallas_call | solution.py:87
  32.3 0.8 %fusion.7 = (bf16[4,48,1,32]{3,1,0,2:T(8,128)(2,1)S(1)}, bf16[4,48,1,32]{3,1,2,0:T(8,128)(2,1)S(1)}) fusion(bf16[6,48,32]{2,1,0:T(8,128)(2,1)S(1)} %bitcast.80, f32[32]{0:T(128)} %param.13, f32[32]{0:T(128)} %param.12, f32[32]{0:T(128)S(1)} %mul.94, f32[32]{0:T(128)S(1)} %sub.63, bf16[6,48,32]{2,1,0:T(8,128)(2,1)S(1)} %bitcast.82), kind=kLoop, calls=%fused_computation.23 | loop fusion | flops 122880 | bytes 49664 | tf_op jit(solution)/shard_map/concatenate | solution.py:270
  33.2 0.2 copy.41
  33.5 0.1 fusion.14
  33.6 0.5 copy-done
  34.1 0.2 copy.40
  34.4 0.3 multiply_convert_fusion
  34.7 0.4 fusion.1
  35.1 0.6 fusion.13
  35.7 0.8 %pad_maximum_fusion.1 = bf16[6,12,48,96]{3,2,1,0:T(8,128)(2,1)S(1)} fusion(bf16[6,12,48,32]{3,2,1,0:T(8,128)(2,1)S(1)} %get-tuple-element.41, bf16[6,12,48,32]{3,2,1,0:T(8,128)(2,1)S(1)} %get-tuple-element.42, bf16[6,12,48,32]{3,2,1,0:T(8,128)(2,1)S(1)} %get-tuple-element.40), kind=kLoop, calls=%fused_computation.12 | loop fusion | flops 1990656 | bytes 1327104 | tf_op jit(solution)/shard_map/concatenate | solution.py:278
  36.5 0.3 fusion.15
  36.8 1.1 %pad_maximum_fusion = bf16[6,10,48,288]{3,2,1,0:T(8,128)(2,1)S(1)} fusion(bf16[6,10,48,96]{3,2,1,0:T(8,128)(2,1)S(1)} %get-tuple-element.48, bf16[6,10,48,96]{3,2,1,0:T(8,128)(2,1)S(1)} %get-tuple-element.47, bf16[6,10,48,96]{3,2,1,0:T(8,128)(2,1)S(1)} %get-tuple-element.46), kind=kLoop, calls=%fused_computation.3 | loop fusion | flops 4976640 | bytes 3317760 | tf_op jit(solution)/shard_map/concatenate | solution.py:282
  38.0 0.4 fusion.12
  38.3 1.3 %fusion.17 = f32[1920,512]{0,1:T(8,128)S(1)} fusion(bf16[1920,288]{1,0:T(8,128)(2,1)S(1)} %bitcast.72, bf16[288,512]{1,0:T(8,128)(2,1)S(1)} %bitcast.78), kind=kOutput, calls=%fused_computation.47 | convolution fusion | flops 566231040 | bytes 5332992 | tf_op jit(solution)/shard_map/dot_general | solution.py:296
  39.6 1.3 %fusion.16 = f32[1920,512]{0,1:T(8,128)S(1)} fusion(bf16[1920,288]{1,0:T(8,128)(2,1)S(1)} %bitcast.71, bf16[288,512]{1,0:T(8,128)(2,1)S(1)} %bitcast.77), kind=kOutput, calls=%fused_computation.46 | convolution fusion | flops 566231040 | bytes 5332992 | tf_op jit(solution)/shard_map/dot_general | solution.py:296
  40.9 1.3 %add_add_fusion = f32[1920,512]{0,1:T(8,128)S(1)} fusion(f32[1920,512]{0,1:T(8,128)S(1)} %fusion.16, f32[1920,512]{0,1:T(8,128)S(1)} %fusion.17, bf16[1920,288]{1,0:T(8,128)(2,1)S(1)} %bitcast.73, bf16[288,512]{1,0:T(8,128)(2,1)S(1)} %bitcast.76), kind=kOutput, calls=%fused_computation | convolution fusion | flops 568197120 | bytes 13197312 | tf_op jit(solution)/shard_map/dot_general | solution.py:296
  42.2 25.3 %shard_map.65 = f32[32,1920]{1,0:T(8,128)S(1)} custom-call(f32[4,2,2,32,1920]{4,3,2,1,0:T(8,128)S(1)} %bitcast.70), custom_call_target="tpu_custom_call" | custom-call | tf_op jit(solution)/shard_map/pallas_call | solution.py:204
  67.5 0.1 fusion.5
  67.6 0.5 reshape.225
  68.1 0.9 %copy.47 = bf16[4,48,10,32]{1,3,2,0:T(8,128)(2,1)} copy(bf16[4,48,10,32]{1,2,0,3:T(8,128)(2,1)S(1)} %bitcast.75) | data formatting | bytes 245760 | tf_op jit(solution)/shard_map/transpose | solution.py:302
  (31 shorter events, 0.9 us)
Async XLA Ops:
  0.0 33.2 %copy-start.2 = (bf16[2,48,10,32]{1,3,2,0:T(8,128)(2,1)S(1)}, bf16[2,48,10,32]{1,3,2,0:T(8,128)(2,1)}, u32[]{:S(2)}) copy-start(bf16[2,48,10,32]{1,3,2,0:T(8,128)(2,1)} %param.11) | copy-start | bytes 184324
  0.0 33.4 %copy-start.1 = (bf16[3,3,3,32,512]{4,3,2,1,0:T(8,128)(2,1)S(1)}, bf16[3,3,3,32,512]{4,3,2,1,0:T(8,128)(2,1)}, u32[]{:S(2)}) copy-start(bf16[3,3,3,32,512]{4,3,2,1,0:T(8,128)(2,1)} %param.14) | copy-start | bytes 2654212
  3.3 2.2 %copy-start.3 = (f32[8,128]{1,0:T(8,128)}, f32[8,128]{1,0:T(8,128)S(1)}, u32[]{:S(2)}) copy-start(f32[8,128]{1,0:T(8,128)S(1)} %scatter.9.x_ref) | copy-start | bytes 12292
  33.1 1.0 %copy-start = (bf16[4,48,10,32]{1,3,2,0:T(8,128)(2,1)S(1)}, bf16[4,48,10,32]{1,3,2,0:T(8,128)(2,1)}, u32[]{:S(2)}) copy-start(bf16[4,48,10,32]{1,3,2,0:T(8,128)(2,1)} %param.10) | copy-start | bytes 368644
  33.4 1.0 %copy-start.4 = (f32[32]{0:T(128)S(1)}, f32[32]{0:T(128)}, u32[]{:S(2)}) copy-start(f32[32]{0:T(128)} %param.13) | copy-start | bytes 388
  33.4 1.0 %copy-start.5 = (f32[32]{0:T(128)S(1)}, f32[32]{0:T(128)}, u32[]{:S(2)}) copy-start(f32[32]{0:T(128)} %param.12) | copy-start | bytes 388
  42.2 25.3 %copy-start.6 = (f32[32]{0:T(128)S(1)}, f32[32]{0:T(128)}, u32[]{:S(2)}) copy-start(f32[32]{0:T(128)} %param.15) | copy-start | bytes 388

commit v17 on v16

--- a/solution.py
+++ b/solution.py
@@ -15,7 +15,7 @@
 epsilon = 1e-06
 
 
-def gather_kernel(n, x_ref, lo_ref, hi_ref, o_ref, left_ref, right_ref,
+def gather_kernel(n, x_ref, cache_ref, frames_ref, o_ref, left_ref, right_ref,
                   buf, left_buf, right_buf, send_sem, recv_sem, edge_send, edge_recv):
     me = lax.axis_index("space")
     ch = lax.axis_index("chan")
@@ -31,14 +31,19 @@
     lax.fori_loop(1, n, signal, 0)
     pl.semaphore_wait(barrier, n - 1)
 
-    to_right = pltpu.make_async_remote_copy(
-        src_ref=hi_ref, dst_ref=left_buf, send_sem=edge_send.at[0], recv_sem=edge_recv.at[0],
-        device_id=(right, ch), device_id_type=MESH)
-    to_left = pltpu.make_async_remote_copy(
-        src_ref=lo_ref, dst_ref=right_buf, send_sem=edge_send.at[1], recv_sem=edge_recv.at[1],
-        device_id=(left, ch), device_id_type=MESH)
-    to_right.start()
-    to_left.start()
+    ncache = cache_ref.shape[0]
+    last = cache_ref.shape[1] - 1
+    edges = []
+    for k, (src, lo_row) in enumerate(((cache_ref, 0), (frames_ref, ncache))):
+        rows = pl.ds(lo_row, src.shape[0])
+        edges.append(pltpu.make_async_remote_copy(
+            src_ref=src.at[:, last], dst_ref=left_buf.at[rows], send_sem=edge_send.at[k],
+            recv_sem=edge_recv.at[k], device_id=(right, ch), device_id_type=MESH))
+        edges.append(pltpu.make_async_remote_copy(
+            src_ref=src.at[:, 0], dst_ref=right_buf.at[rows], send_sem=edge_send.at[2 + k],
+            recv_sem=edge_recv.at[2 + k], device_id=(left, ch), device_id_type=MESH))
+    for cp in edges:
+        cp.start()
 
     def copy_to(peer):
         return pltpu.make_async_remote_copy(
@@ -75,35 +80,37 @@
     lax.fori_loop(1, n, finish, 0)
     buf[me] = x_ref[...]
     o_ref[...] = buf[...]
-    to_right.wait()
-    to_left.wait()
+    for cp in edges:
+        cp.wait()
     left_ref[...] = left_buf[...]
     right_ref[...] = right_buf[...]
 
 
-def gather_space(tile, lo, hi):
+def gather_space(tile, cache_t, frames_t):
     n = lax.axis_size("space")
     vmem = pl.BlockSpec(memory_space=pltpu.VMEM)
+    hbm = pl.BlockSpec(memory_space=pl.ANY)
+    edge = (cache_t.shape[0] + frames_t.shape[0],) + cache_t.shape[2:]
     return pl.pallas_call(
         functools.partial(gather_kernel, n),
         out_shape=(
             jax.ShapeDtypeStruct((n,) + tile.shape, tile.dtype),
-            jax.ShapeDtypeStruct(hi.shape, hi.dtype),
-            jax.ShapeDtypeStruct(lo.shape, lo.dtype),
+            jax.ShapeDtypeStruct(edge, cache_t.dtype),
+            jax.ShapeDtypeStruct(edge, cache_t.dtype),
         ),
-        in_specs=[vmem, vmem, vmem],
+        in_specs=[vmem, hbm, hbm],
         out_specs=(vmem, vmem, vmem),
         scratch_shapes=[
             pltpu.VMEM((n,) + tile.shape, tile.dtype),
-            pltpu.VMEM(hi.shape, hi.dtype),
-            pltpu.VMEM(lo.shape, lo.dtype),
+            pltpu.VMEM(edge, cache_t.dtype),
+            pltpu.VMEM(edge, cache_t.dtype),
             pltpu.SemaphoreType.DMA((n,)),
             pltpu.SemaphoreType.DMA((n,)),
-            pltpu.SemaphoreType.DMA((2,)),
-            pltpu.SemaphoreType.DMA((2,)),
+            pltpu.SemaphoreType.DMA((4,)),
+            pltpu.SemaphoreType.DMA((4,)),
         ],
         compiler_params=pltpu.CompilerParams(collective_id=0, has_side_effects=True),
-    )(tile, lo, hi)
+    )(tile, cache_t, frames_t)
 
 
 def scatter_kernel(nchunk, x_ref, o_ref, recv1, acc1, own, recv2, acc2, recv3,
@@ -235,9 +242,6 @@
     local_members = float(nframes * row_count * col_count * group_size)
 
 
-    def edge(col):
-        return jnp.concatenate([cache[:, :, col], frames[:, :, col]], axis=0).transpose(0, 2, 1)
-
     values = frames.astype(jnp.float32).reshape(
         nframes, row_count, col_count, local_groups, group_size
     )
@@ -246,7 +250,9 @@
     local_m2 = jnp.sum(local_dev * local_dev, axis=(0, 1, 2, 4))
     tile = jnp.zeros((8, 128), jnp.float32)
     tile = tile.at[0, :local_groups].set(local_mean).at[1, :local_groups].set(local_m2)
-    gathered, before, after = gather_space(tile, edge(0), edge(col_count - 1))
+    gathered, before, after = gather_space(
+        tile, cache.transpose(0, 2, 3, 1), frames.transpose(0, 2, 3, 1)
+    )
     before = before.transpose(0, 2, 1)[:, :, None]
     after = after.transpose(0, 2, 1)[:, :, None]
     means = gathered[:, 0, :local_groups]

time: 70.3 us -> 68.6 us (0.976)
  local copies, waits for them, and re-layouts: 8.04 us -> 7.1 us
    squeeze x2 -> x0, local copies, waits for them, and re-layouts: 1.53 us -> none  [the longest x1 0.78 us: edge(): frames[:, :, col]]
where the time goes in v17:
time: 68.6 us; the launch traced here: 67.6 us
  Pallas kernels  48.8 us (71%)
  other arithmetic  7.62 us (11%)
  local copies, waits for them, and re-layouts  7.1 us (10%)
  matrix products  3.81 us (6%)
    pallas_call x1, Pallas kernels, scatter_chan(): pl.pallas_call(functools.partial(scatter_kernel, nchunk), out_shape=jax.S...  25.3 us
    pallas_call x1, Pallas kernels, gather_space(): pl.pallas_call(functools.partial(gather_kernel, n), out_shape=(jax.ShapeD...  23.5 us
    dot_general x3, matrix products, local(): lax.dot_general(tap_weight, window, (((0,), (1,)), ((), ())), preferred_e...  3.81 us
    pallas_call x2, local copies, waits for them, and re-layouts, gather_space(): pl.pallas_call(functools.partial(gather_kernel, n), out_shape=(jax.ShapeD...  1.81 us
    unnamed x16, local copies, waits for them, and re-layouts  1.39 us
    reduce_sum x2, other arithmetic, local(): local_m2 = jnp.sum(local_dev * local_dev, axis=(0, 1, 2, 4))  1.39 us

profile of v17, /device:TPU:6, one launch (start us, length us, event | category | flops | bytes accessed | tf_op | source)
XLA Modules:
  0.0 67.6 jit_solution(7117565914033371420)
XLA Ops:
  0.0 1.2 %convert_reduce_fusion = f32[32]{0:T(128)S(1)} fusion(bf16[4,48,10,32]{1,3,2,0:T(8,128)(2,1)} %param.10), kind=kLoop, calls=%fused_computation.15 | loop fusion | flops 122848 | bytes 123008 | tf_op jit(solution)/shard_map/reduce_sum | solution.py:248
  1.3 0.1 reduce_sum.60
  1.3 0.1 reduce_sum.61
  1.6 1.3 %multiply_reduce_fusion = f32[32]{0:T(128)S(1)} fusion(f32[32]{0:T(128)S(1)} %sub.59, bf16[4,48,10,32]{1,3,2,0:T(8,128)(2,1)} %param.10), kind=kLoop, calls=%fused_computation.14 | loop fusion | flops 245728 | bytes 123136 | tf_op jit(solution)/shard_map/reduce_sum | solution.py:250
  3.0 0.1 reduce_sum.64
  3.1 0.2 scatter.9.x_ref
  3.3 0.6 copy-done.3
  3.9 23.5 %shard_map.64 = (f32[32,8,128]{2,1,0:T(8,128)}, bf16[6,32,48]{2,1,0:T(8,128)(2,1)}, bf16[6,32,48]{2,1,0:T(8,128)(2,1)}) custom-call(f32[8,128]{1,0:T(8,128)} %copy-done.3, bf16[2,10,32,48]{3,2,1,0:T(8,128)(2,1)} %bitcast.62, bf16[4,10,32,48]{3,2,1,0:T(8,128)(2,1)} %bitcast.56), custom_call_target="tpu_custom_call" | custom-call | tf_op jit(solution)/shard_map/pallas_call | solution.py:94
  27.4 1.0 %slice_reduce_fusion.1 = (f32[2]{0:T(128)S(1)}, f32[2]{0:T(128)S(1)}, f32[32,1,2]{2,1,0:T(1,128)S(1)}) fusion(f32[32,8,128]{2,1,0:T(8,128)} %get-tuple-element.33), kind=kLoop, calls=%fused_computation.35 | loop fusion | flops 124 | bytes 784 | tf_op jit(solution)/shard_map/reduce_sum | solution.py:260
  28.5 0.1 sub.63
  28.7 0.2 fusion.10
  29.0 0.9 %copy.26 = bf16[6,32,48]{1,2,0:T(8,128)(2,1)S(1)} copy(bf16[6,32,48]{2,1,0:T(8,128)(2,1)} %get-tuple-element.32) | data formatting | bytes 36864 | tf_op jit(solution)/shard_map/pallas_call | solution.py:94
  29.9 0.9 %copy.30 = bf16[6,32,48]{1,2,0:T(8,128)(2,1)S(1)} copy(bf16[6,32,48]{2,1,0:T(8,128)(2,1)} %get-tuple-element.34) | data formatting | bytes 36864 | tf_op jit(solution)/shard_map/pallas_call | solution.py:94
  30.8 0.8 %fusion.7 = (bf16[4,48,1,32]{3,1,0,2:T(8,128)(2,1)S(1)}, bf16[4,48,1,32]{3,1,2,0:T(8,128)(2,1)S(1)}) fusion(bf16[6,48,32]{2,1,0:T(8,128)(2,1)S(1)} %bitcast.64, f32[32]{0:T(128)} %param.13, f32[32]{0:T(128)} %param.12, f32[32]{0:T(128)S(1)} %mul.94, f32[32]{0:T(128)S(1)} %sub.63, bf16[6,48,32]{2,1,0:T(8,128)(2,1)S(1)} %bitcast.66), kind=kLoop, calls=%fused_computation.23 | loop fusion | flops 122880 | bytes 49664 | tf_op jit(solution)/shard_map/concatenate | solution.py:276
  31.7 0.2 copy.29
  32.0 0.1 fusion.14
  32.1 0.5 copy-done
  32.6 0.2 copy.28
  32.9 0.3 multiply_convert_fusion
  33.2 0.4 fusion.1
  33.6 0.6 fusion.13
  34.2 0.8 %pad_maximum_fusion.1 = bf16[6,12,48,96]{3,2,1,0:T(8,128)(2,1)S(1)} fusion(bf16[6,12,48,32]{3,2,1,0:T(8,128)(2,1)S(1)} %get-tuple-element.41, bf16[6,12,48,32]{3,2,1,0:T(8,128)(2,1)S(1)} %get-tuple-element.42, bf16[6,12,48,32]{3,2,1,0:T(8,128)(2,1)S(1)} %get-tuple-element.40), kind=kLoop, calls=%fused_computation.12 | loop fusion | flops 1990656 | bytes 1327104 | tf_op jit(solution)/shard_map/concatenate | solution.py:284
  35.0 0.3 fusion.15
  35.3 1.1 %pad_maximum_fusion = bf16[6,10,48,288]{3,2,1,0:T(8,128)(2,1)S(1)} fusion(bf16[6,10,48,96]{3,2,1,0:T(8,128)(2,1)S(1)} %get-tuple-element.48, bf16[6,10,48,96]{3,2,1,0:T(8,128)(2,1)S(1)} %get-tuple-element.47, bf16[6,10,48,96]{3,2,1,0:T(8,128)(2,1)S(1)} %get-tuple-element.46), kind=kLoop, calls=%fused_computation.3 | loop fusion | flops 4976640 | bytes 3317760 | tf_op jit(solution)/shard_map/concatenate | solution.py:288
  36.5 0.4 fusion.12
  36.8 1.3 %fusion.17 = f32[1920,512]{0,1:T(8,128)S(1)} fusion(bf16[1920,288]{1,0:T(8,128)(2,1)S(1)} %bitcast.54, bf16[288,512]{1,0:T(8,128)(2,1)S(1)} %bitcast.61), kind=kOutput, calls=%fused_computation.41 | convolution fusion | flops 566231040 | bytes 5332992 | tf_op jit(solution)/shard_map/dot_general | solution.py:302
  38.1 1.3 %fusion.16 = f32[1920,512]{0,1:T(8,128)S(1)} fusion(bf16[1920,288]{1,0:T(8,128)(2,1)S(1)} %bitcast.53, bf16[288,512]{1,0:T(8,128)(2,1)S(1)} %bitcast.60), kind=kOutput, calls=%fused_computation.40 | convolution fusion | flops 566231040 | bytes 5332992 | tf_op jit(solution)/shard_map/dot_general | solution.py:302
  39.4 1.3 %add_add_fusion = f32[1920,512]{0,1:T(8,128)S(1)} fusion(f32[1920,512]{0,1:T(8,128)S(1)} %fusion.16, f32[1920,512]{0,1:T(8,128)S(1)} %fusion.17, bf16[1920,288]{1,0:T(8,128)(2,1)S(1)} %bitcast.55, bf16[288,512]{1,0:T(8,128)(2,1)S(1)} %bitcast.59), kind=kOutput, calls=%fused_computation | convolution fusion | flops 568197120 | bytes 13197312 | tf_op jit(solution)/shard_map/dot_general | solution.py:302
  40.7 25.3 %shard_map.65 = f32[32,1920]{1,0:T(8,128)S(1)} custom-call(f32[4,2,2,32,1920]{4,3,2,1,0:T(8,128)S(1)} %bitcast.52), custom_call_target="tpu_custom_call" | custom-call | tf_op jit(solution)/shard_map/pallas_call | solution.py:211
  66.1 0.1 fusion.5
  66.1 0.5 reshape.225
  66.7 0.9 %copy.35 = bf16[4,48,10,32]{1,3,2,0:T(8,128)(2,1)} copy(bf16[4,48,10,32]{1,2,0,3:T(8,128)(2,1)S(1)} %bitcast.58) | data formatting | bytes 245760 | tf_op jit(solution)/shard_map/transpose | solution.py:308
  (28 shorter events, 0.7 us)
Async XLA Ops:
  0.0 31.7 %copy-start.2 = (bf16[2,48,10,32]{1,3,2,0:T(8,128)(2,1)S(1)}, bf16[2,48,10,32]{1,3,2,0:T(8,128)(2,1)}, u32[]{:S(2)}) copy-start(bf16[2,48,10,32]{1,3,2,0:T(8,128)(2,1)} %param.11) | copy-start | bytes 184324
  0.0 31.9 %copy-start.1 = (bf16[3,3,3,32,512]{4,3,2,1,0:T(8,128)(2,1)S(1)}, bf16[3,3,3,32,512]{4,3,2,1,0:T(8,128)(2,1)}, u32[]{:S(2)}) copy-start(bf16[3,3,3,32,512]{4,3,2,1,0:T(8,128)(2,1)} %param.14) | copy-start | bytes 2654212
  3.3 0.6 copy-start.3
  31.6 1.0 %copy-start = (bf16[4,48,10,32]{1,3,2,0:T(8,128)(2,1)S(1)}, bf16[4,48,10,32]{1,3,2,0:T(8,128)(2,1)}, u32[]{:S(2)}) copy-start(bf16[4,48,10,32]{1,3,2,0:T(8,128)(2,1)} %param.10) | copy-start | bytes 368644
  31.9 1.0 %copy-start.4 = (f32[32]{0:T(128)S(1)}, f32[32]{0:T(128)}, u32[]{:S(2)}) copy-start(f32[32]{0:T(128)} %param.13) | copy-start | bytes 388
  31.9 1.0 %copy-start.5 = (f32[32]{0:T(128)S(1)}, f32[32]{0:T(128)}, u32[]{:S(2)}) copy-start(f32[32]{0:T(128)} %param.12) | copy-start | bytes 388
  40.7 25.4 %copy-start.6 = (f32[32]{0:T(128)S(1)}, f32[32]{0:T(128)}, u32[]{:S(2)}) copy-start(f32[32]{0:T(128)} %param.15) | copy-start | bytes 388

commit v18 on v17

--- a/solution.py
+++ b/solution.py
@@ -15,7 +15,7 @@
 epsilon = 1e-06
 
 
-def gather_kernel(n, x_ref, cache_ref, frames_ref, o_ref, left_ref, right_ref,
+def gather_kernel(n, members, x_ref, cache_ref, frames_ref, o_ref, left_ref, right_ref,
                   buf, left_buf, right_buf, send_sem, recv_sem, edge_send, edge_recv):
     me = lax.axis_index("space")
     ch = lax.axis_index("chan")
@@ -79,22 +79,29 @@
 
     lax.fori_loop(1, n, finish, 0)
     buf[me] = x_ref[...]
-    o_ref[...] = buf[...]
+    gathered = buf[...]
+    means = gathered[:, 0, :]
+    group_mean = jnp.sum(means, axis=0, keepdims=True) / n
+    spread = jnp.sum(gathered[:, 1, :], axis=0, keepdims=True) + members * jnp.sum(
+        (means - group_mean) ** 2, axis=0, keepdims=True
+    )
+    inv = lax.rsqrt(spread / (members * n) + epsilon)
+    o_ref[...] = jnp.concatenate([group_mean, inv, jnp.zeros((6,) + inv.shape[1:], inv.dtype)], axis=0)
     for cp in edges:
         cp.wait()
     left_ref[...] = left_buf[...]
     right_ref[...] = right_buf[...]
 
 
-def gather_space(tile, cache_t, frames_t):
+def gather_space(tile, cache_t, frames_t, members):
     n = lax.axis_size("space")
     vmem = pl.BlockSpec(memory_space=pltpu.VMEM)
     hbm = pl.BlockSpec(memory_space=pl.ANY)
     edge = (cache_t.shape[0] + frames_t.shape[0],) + cache_t.shape[2:]
     return pl.pallas_call(
-        functools.partial(gather_kernel, n),
+        functools.partial(gather_kernel, n, members),
         out_shape=(
-            jax.ShapeDtypeStruct((n,) + tile.shape, tile.dtype),
+            jax.ShapeDtypeStruct(tile.shape, tile.dtype),
             jax.ShapeDtypeStruct(edge, cache_t.dtype),
             jax.ShapeDtypeStruct(edge, cache_t.dtype),
         ),
@@ -250,19 +257,13 @@
     local_m2 = jnp.sum(local_dev * local_dev, axis=(0, 1, 2, 4))
     tile = jnp.zeros((8, 128), jnp.float32)
     tile = tile.at[0, :local_groups].set(local_mean).at[1, :local_groups].set(local_m2)
-    gathered, before, after = gather_space(
-        tile, cache.transpose(0, 2, 3, 1), frames.transpose(0, 2, 3, 1)
+    combined, before, after = gather_space(
+        tile, cache.transpose(0, 2, 3, 1), frames.transpose(0, 2, 3, 1), local_members
     )
     before = before.transpose(0, 2, 1)[:, :, None]
     after = after.transpose(0, 2, 1)[:, :, None]
-    means = gathered[:, 0, :local_groups]
-    m2s = gathered[:, 1, :local_groups]
-    group_mean = jnp.mean(means, axis=0)
-    spread = jnp.sum(m2s, axis=0) + local_members * jnp.sum(
-        (means - group_mean) ** 2, axis=0
-    )
-    group_var = spread / (local_members * nspace)
-    inv = lax.rsqrt(group_var + epsilon)
+    group_mean = combined[0, :local_groups]
+    inv = combined[1, :local_groups]
 
     def activate(x):
         shape = x.shape

time: 68.6 us -> 68.1 us (level)
  other arithmetic: 7.62 us -> 6.38 us
    reduce_sum x2 -> x0, other arithmetic: 1.22 us -> none  [the longest x1 1.03 us: local(): group_mean = jnp.mean(means, axis=0)]
    sub x2 -> x3, local copies, waits for them, and re-layouts: 0.15 us -> 0.9 us  [activate(): scaled = (v - group_mean[:, None]) * inv[:, None]]
where the time goes in v18:
time: 68.1 us; the launch traced here: 67 us
  Pallas kernels  48.8 us (72%)
  local copies, waits for them, and re-layouts  7.76 us (11%)
  other arithmetic  6.38 us (9%)
  matrix products  3.8 us (6%)
    pallas_call x1, Pallas kernels, scatter_chan(): pl.pallas_call(functools.partial(scatter_kernel, nchunk), out_shape=jax.S...  25.3 us
    pallas_call x1, Pallas kernels, gather_space(): pl.pallas_call(functools.partial(gather_kernel, n, members), out_shape=(j...  23.5 us
    dot_general x3, matrix products, local(): lax.dot_general(tap_weight, window, (((0,), (1,)), ((), ())), preferred_e...  3.8 us
    pallas_call x2, local copies, waits for them, and re-layouts, gather_space(): pl.pallas_call(functools.partial(gather_kernel, n, members), out_shape=(j...  1.8 us
    unnamed x16, local copies, waits for them, and re-layouts  1.39 us
    reduce_sum x2, other arithmetic, local(): local_m2 = jnp.sum(local_dev * local_dev, axis=(0, 1, 2, 4))  1.39 us
    reduce_sum x2, other arithmetic, local(): local_mean = jnp.sum(values, axis=(0, 1, 2, 4)) / local_members  1.37 us

profile of v18, /device:TPU:6, one launch (start us, length us, event | category | flops | bytes accessed | tf_op | source)
XLA Modules:
  0.0 67.0 jit_solution(7911458293412942650)
XLA Ops:
  0.0 1.2 %convert_reduce_fusion = f32[32]{0:T(128)S(1)} fusion(bf16[4,48,10,32]{1,3,2,0:T(8,128)(2,1)} %param.10), kind=kLoop, calls=%fused_computation.15 | loop fusion | flops 122848 | bytes 123008 | tf_op jit(solution)/shard_map/reduce_sum | solution.py:255
  1.3 0.1 reduce_sum.24
  1.3 0.1 reduce_sum.25
  1.5 0.1 sub.53
  1.6 1.3 %multiply_reduce_fusion = f32[32]{0:T(128)S(1)} fusion(f32[32]{0:T(128)S(1)} %sub.53, bf16[4,48,10,32]{1,3,2,0:T(8,128)(2,1)} %param.10), kind=kLoop, calls=%fused_computation.14 | loop fusion | flops 245728 | bytes 123136 | tf_op jit(solution)/shard_map/reduce_sum | solution.py:257
  2.9 0.1 reduce_sum.36
  3.0 0.1 reduce_sum.37
  3.1 0.2 scatter.9.x_ref
  3.3 0.6 copy-done.3
  3.9 23.5 %shard_map.64 = (f32[8,128]{1,0:T(8,128)}, bf16[6,32,48]{2,1,0:T(8,128)(2,1)}, bf16[6,32,48]{2,1,0:T(8,128)(2,1)}) custom-call(f32[8,128]{1,0:T(8,128)} %copy-done.3, bf16[2,10,32,48]{3,2,1,0:T(8,128)(2,1)} %bitcast.60, bf16[4,10,32,48]{3,2,1,0:T(8,128)(2,1)} %bitcast.54), custom_call_target="tpu_custom_call" | custom-call | tf_op jit(solution)/shard_map/pallas_call | solution.py:101
  27.4 0.8 %slice_bitcast_fusion.3 = (f32[2]{0:T(128)S(1)}, f32[2]{0:T(128)S(1)}) fusion(f32[8,128]{1,0:T(8,128)} %get-tuple-element.33), kind=kLoop, calls=%fused_computation.28 | loop fusion | bytes 32 | tf_op jit(solution)/shard_map/sub | solution.py:271
  28.4 0.9 %copy.24 = bf16[6,32,48]{1,2,0:T(8,128)(2,1)S(1)} copy(bf16[6,32,48]{2,1,0:T(8,128)(2,1)} %get-tuple-element.32) | data formatting | bytes 36864 | tf_op jit(solution)/shard_map/pallas_call | solution.py:101
  29.4 0.9 %copy.27 = bf16[6,32,48]{1,2,0:T(8,128)(2,1)S(1)} copy(bf16[6,32,48]{2,1,0:T(8,128)(2,1)} %get-tuple-element.34) | data formatting | bytes 36864 | tf_op jit(solution)/shard_map/pallas_call | solution.py:101
  30.3 0.8 %fusion.7 = (bf16[4,48,1,32]{3,1,0,2:T(8,128)(2,1)S(1)}, bf16[4,48,1,32]{3,1,2,0:T(8,128)(2,1)S(1)}) fusion(bf16[6,48,32]{2,1,0:T(8,128)(2,1)S(1)} %bitcast.62, f32[32]{0:T(128)} %param.13, f32[32]{0:T(128)} %param.12, f32[32]{0:T(128)S(1)} %mul.91, f32[32]{0:T(128)S(1)} %sub.58, bf16[6,48,32]{2,1,0:T(8,128)(2,1)S(1)} %bitcast.64), kind=kLoop, calls=%fused_computation.23 | loop fusion | flops 122880 | bytes 49664 | tf_op jit(solution)/shard_map/concatenate | solution.py:277
  31.1 0.2 copy.26
  31.4 0.1 fusion.12
  31.5 0.5 copy-done
  32.0 0.2 copy.25
  32.3 0.3 multiply_convert_fusion
  32.6 0.4 fusion.1
  33.1 0.6 fusion.11
  33.6 0.8 %pad_maximum_fusion.1 = bf16[6,12,48,96]{3,2,1,0:T(8,128)(2,1)S(1)} fusion(bf16[6,12,48,32]{3,2,1,0:T(8,128)(2,1)S(1)} %get-tuple-element.39, bf16[6,12,48,32]{3,2,1,0:T(8,128)(2,1)S(1)} %get-tuple-element.40, bf16[6,12,48,32]{3,2,1,0:T(8,128)(2,1)S(1)} %get-tuple-element.38), kind=kLoop, calls=%fused_computation.12 | loop fusion | flops 1990656 | bytes 1327104 | tf_op jit(solution)/shard_map/concatenate | solution.py:285
  34.4 0.3 fusion.13
  34.7 1.1 %pad_maximum_fusion = bf16[6,10,48,288]{3,2,1,0:T(8,128)(2,1)S(1)} fusion(bf16[6,10,48,96]{3,2,1,0:T(8,128)(2,1)S(1)} %get-tuple-element.46, bf16[6,10,48,96]{3,2,1,0:T(8,128)(2,1)S(1)} %get-tuple-element.45, bf16[6,10,48,96]{3,2,1,0:T(8,128)(2,1)S(1)} %get-tuple-element.44), kind=kLoop, calls=%fused_computation.3 | loop fusion | flops 4976640 | bytes 3317760 | tf_op jit(solution)/shard_map/concatenate | solution.py:289
  35.9 0.4 fusion.10
  36.3 1.3 %fusion.15 = f32[1920,512]{0,1:T(8,128)S(1)} fusion(bf16[1920,288]{1,0:T(8,128)(2,1)S(1)} %bitcast.52, bf16[288,512]{1,0:T(8,128)(2,1)S(1)} %bitcast.59), kind=kOutput, calls=%fused_computation.36 | convolution fusion | flops 566231040 | bytes 5332992 | tf_op jit(solution)/shard_map/dot_general | solution.py:303
  37.5 1.3 %fusion.14 = f32[1920,512]{0,1:T(8,128)S(1)} fusion(bf16[1920,288]{1,0:T(8,128)(2,1)S(1)} %bitcast.51, bf16[288,512]{1,0:T(8,128)(2,1)S(1)} %bitcast.58), kind=kOutput, calls=%fused_computation.35 | convolution fusion | flops 566231040 | bytes 5332992 | tf_op jit(solution)/shard_map/dot_general | solution.py:303
  38.8 1.3 %add_add_fusion = f32[1920,512]{0,1:T(8,128)S(1)} fusion(f32[1920,512]{0,1:T(8,128)S(1)} %fusion.14, f32[1920,512]{0,1:T(8,128)S(1)} %fusion.15, bf16[1920,288]{1,0:T(8,128)(2,1)S(1)} %bitcast.53, bf16[288,512]{1,0:T(8,128)(2,1)S(1)} %bitcast.57), kind=kOutput, calls=%fused_computation | convolution fusion | flops 568197120 | bytes 13197312 | tf_op jit(solution)/shard_map/dot_general | solution.py:303
  40.1 25.3 %shard_map.65 = f32[32,1920]{1,0:T(8,128)S(1)} custom-call(f32[4,2,2,32,1920]{4,3,2,1,0:T(8,128)S(1)} %bitcast.50), custom_call_target="tpu_custom_call" | custom-call | tf_op jit(solution)/shard_map/pallas_call | solution.py:218
  65.5 0.1 fusion.5
  65.6 0.5 reshape.221
  66.1 0.9 %copy.32 = bf16[4,48,10,32]{1,3,2,0:T(8,128)(2,1)} copy(bf16[4,48,10,32]{1,2,0,3:T(8,128)(2,1)S(1)} %bitcast.56) | data formatting | bytes 245760 | tf_op jit(solution)/shard_map/transpose | solution.py:309
  (24 shorter events, 0.6 us)
Async XLA Ops:
  0.0 31.1 %copy-start.2 = (bf16[2,48,10,32]{1,3,2,0:T(8,128)(2,1)S(1)}, bf16[2,48,10,32]{1,3,2,0:T(8,128)(2,1)}, u32[]{:S(2)}) copy-start(bf16[2,48,10,32]{1,3,2,0:T(8,128)(2,1)} %param.11) | copy-start | bytes 184324
  0.0 31.3 %copy-start.1 = (bf16[3,3,3,32,512]{4,3,2,1,0:T(8,128)(2,1)S(1)}, bf16[3,3,3,32,512]{4,3,2,1,0:T(8,128)(2,1)}, u32[]{:S(2)}) copy-start(bf16[3,3,3,32,512]{4,3,2,1,0:T(8,128)(2,1)} %param.14) | copy-start | bytes 2654212
  3.3 0.6 copy-start.3
  31.1 1.0 %copy-start = (bf16[4,48,10,32]{1,3,2,0:T(8,128)(2,1)S(1)}, bf16[4,48,10,32]{1,3,2,0:T(8,128)(2,1)}, u32[]{:S(2)}) copy-start(bf16[4,48,10,32]{1,3,2,0:T(8,128)(2,1)} %param.10) | copy-start | bytes 368644
  31.3 1.0 %copy-start.4 = (f32[32]{0:T(128)S(1)}, f32[32]{0:T(128)}, u32[]{:S(2)}) copy-start(f32[32]{0:T(128)} %param.13) | copy-start | bytes 388
  31.3 1.0 %copy-start.5 = (f32[32]{0:T(128)S(1)}, f32[32]{0:T(128)}, u32[]{:S(2)}) copy-start(f32[32]{0:T(128)} %param.12) | copy-start | bytes 388
  40.1 25.4 %copy-start.6 = (f32[32]{0:T(128)S(1)}, f32[32]{0:T(128)}, u32[]{:S(2)}) copy-start(f32[32]{0:T(128)} %param.15) | copy-start | bytes 388

commit v19 on v17

--- a/solution.py
+++ b/solution.py
@@ -303,9 +303,9 @@
             tap_weight, window, (((0,), (1,)), ((), ())), preferred_element_type=jnp.float32
         )
     summed = scatter_chan(running.reshape(nx, 2, 2, local_ch, cell_count))
-    result = summed.T + bias
-    result = result.astype(jnp.bfloat16).reshape(nframes, col_count, row_count, -1)
-    return result.transpose(0, 2, 1, 3)
+    result = (summed + bias[:, None]).astype(jnp.bfloat16)
+    result = result.reshape(-1, nframes, col_count, row_count)
+    return result.transpose(1, 3, 2, 0)
 
 
 def solution(mesh):

time: 68.6 us -> 68.6 us (level)
  no operation moved by 1% of the time
where the time goes in v19:
time: 68.6 us; the launch traced here: 67.6 us
  Pallas kernels  48.8 us (71%)
  other arithmetic  7.62 us (11%)
  local copies, waits for them, and re-layouts  7.1 us (10%)
  matrix products  3.81 us (6%)
    pallas_call x1, Pallas kernels, scatter_chan(): pl.pallas_call(functools.partial(scatter_kernel, nchunk), out_shape=jax.S...  25.3 us
    pallas_call x1, Pallas kernels, gather_space(): pl.pallas_call(functools.partial(gather_kernel, n), out_shape=(jax.ShapeD...  23.5 us
    dot_general x3, matrix products, local(): lax.dot_general(tap_weight, window, (((0,), (1,)), ((), ())), preferred_e...  3.81 us
    pallas_call x2, local copies, waits for them, and re-layouts, gather_space(): pl.pallas_call(functools.partial(gather_kernel, n), out_shape=(jax.ShapeD...  1.81 us
    unnamed x16, local copies, waits for them, and re-layouts  1.39 us
    reduce_sum x2, other arithmetic, local(): local_m2 = jnp.sum(local_dev * local_dev, axis=(0, 1, 2, 4))  1.39 us

profile of v19, /device:TPU:6, one launch (start us, length us, event | category | flops | bytes accessed | tf_op | source)
XLA Modules:
  0.0 67.6 jit_solution(7117565914033371420)
XLA Ops:
  0.0 1.2 %convert_reduce_fusion = f32[32]{0:T(128)S(1)} fusion(bf16[4,48,10,32]{1,3,2,0:T(8,128)(2,1)} %param.10), kind=kLoop, calls=%fused_computation.15 | loop fusion | flops 122848 | bytes 123008 | tf_op jit(solution)/shard_map/reduce_sum | solution.py:248
  1.3 0.1 reduce_sum.60
  1.3 0.1 reduce_sum.61
  1.6 1.3 %multiply_reduce_fusion = f32[32]{0:T(128)S(1)} fusion(f32[32]{0:T(128)S(1)} %sub.59, bf16[4,48,10,32]{1,3,2,0:T(8,128)(2,1)} %param.10), kind=kLoop, calls=%fused_computation.14 | loop fusion | flops 245728 | bytes 123136 | tf_op jit(solution)/shard_map/reduce_sum | solution.py:250
  3.0 0.1 reduce_sum.64
  3.1 0.2 scatter.9.x_ref
  3.3 0.6 copy-done.3
  3.9 23.5 %shard_map.64 = (f32[32,8,128]{2,1,0:T(8,128)}, bf16[6,32,48]{2,1,0:T(8,128)(2,1)}, bf16[6,32,48]{2,1,0:T(8,128)(2,1)}) custom-call(f32[8,128]{1,0:T(8,128)} %copy-done.3, bf16[2,10,32,48]{3,2,1,0:T(8,128)(2,1)} %bitcast.58, bf16[4,10,32,48]{3,2,1,0:T(8,128)(2,1)} %bitcast.52), custom_call_target="tpu_custom_call" | custom-call | tf_op jit(solution)/shard_map/pallas_call | solution.py:94
  27.4 1.0 %slice_reduce_fusion.1 = (f32[2]{0:T(128)S(1)}, f32[2]{0:T(128)S(1)}, f32[32,1,2]{2,1,0:T(1,128)S(1)}) fusion(f32[32,8,128]{2,1,0:T(8,128)} %get-tuple-element.33), kind=kLoop, calls=%fused_computation.34 | loop fusion | flops 124 | bytes 784 | tf_op jit(solution)/shard_map/reduce_sum | solution.py:260
  28.5 0.1 sub.63
  28.7 0.2 fusion.9
  29.0 0.9 %copy.26 = bf16[6,32,48]{1,2,0:T(8,128)(2,1)S(1)} copy(bf16[6,32,48]{2,1,0:T(8,128)(2,1)} %get-tuple-element.32) | data formatting | bytes 36864 | tf_op jit(solution)/shard_map/pallas_call | solution.py:94
  29.9 0.9 %copy.30 = bf16[6,32,48]{1,2,0:T(8,128)(2,1)S(1)} copy(bf16[6,32,48]{2,1,0:T(8,128)(2,1)} %get-tuple-element.34) | data formatting | bytes 36864 | tf_op jit(solution)/shard_map/pallas_call | solution.py:94
  30.8 0.8 %fusion.6 = (bf16[4,48,1,32]{3,1,0,2:T(8,128)(2,1)S(1)}, bf16[4,48,1,32]{3,1,2,0:T(8,128)(2,1)S(1)}) fusion(bf16[6,48,32]{2,1,0:T(8,128)(2,1)S(1)} %bitcast.60, f32[32]{0:T(128)} %param.13, f32[32]{0:T(128)} %param.12, f32[32]{0:T(128)S(1)} %mul.94, f32[32]{0:T(128)S(1)} %sub.63, bf16[6,48,32]{2,1,0:T(8,128)(2,1)S(1)} %bitcast.62), kind=kLoop, calls=%fused_computation.22 | loop fusion | flops 122880 | bytes 49664 | tf_op jit(solution)/shard_map/concatenate | solution.py:276
  31.7 0.2 copy.29
  32.0 0.1 fusion.13
  32.1 0.5 copy-done
  32.6 0.2 copy.28
  32.9 0.3 multiply_convert_fusion
  33.2 0.4 fusion.1
  33.6 0.6 fusion.12
  34.2 0.8 %pad_maximum_fusion.1 = bf16[6,12,48,96]{3,2,1,0:T(8,128)(2,1)S(1)} fusion(bf16[6,12,48,32]{3,2,1,0:T(8,128)(2,1)S(1)} %get-tuple-element.41, bf16[6,12,48,32]{3,2,1,0:T(8,128)(2,1)S(1)} %get-tuple-element.42, bf16[6,12,48,32]{3,2,1,0:T(8,128)(2,1)S(1)} %get-tuple-element.40), kind=kLoop, calls=%fused_computation.12 | loop fusion | flops 1990656 | bytes 1327104 | tf_op jit(solution)/shard_map/concatenate | solution.py:284
  35.0 0.3 fusion.14
  35.3 1.1 %pad_maximum_fusion = bf16[6,10,48,288]{3,2,1,0:T(8,128)(2,1)S(1)} fusion(bf16[6,10,48,96]{3,2,1,0:T(8,128)(2,1)S(1)} %get-tuple-element.48, bf16[6,10,48,96]{3,2,1,0:T(8,128)(2,1)S(1)} %get-tuple-element.47, bf16[6,10,48,96]{3,2,1,0:T(8,128)(2,1)S(1)} %get-tuple-element.46), kind=kLoop, calls=%fused_computation.3 | loop fusion | flops 4976640 | bytes 3317760 | tf_op jit(solution)/shard_map/concatenate | solution.py:288
  36.5 0.4 fusion.11
  36.8 1.3 %fusion.16 = f32[1920,512]{0,1:T(8,128)S(1)} fusion(bf16[1920,288]{1,0:T(8,128)(2,1)S(1)} %bitcast.50, bf16[288,512]{1,0:T(8,128)(2,1)S(1)} %bitcast.57), kind=kOutput, calls=%fused_computation.40 | convolution fusion | flops 566231040 | bytes 5332992 | tf_op jit(solution)/shard_map/dot_general | solution.py:302
  38.1 1.3 %fusion.15 = f32[1920,512]{0,1:T(8,128)S(1)} fusion(bf16[1920,288]{1,0:T(8,128)(2,1)S(1)} %bitcast.49, bf16[288,512]{1,0:T(8,128)(2,1)S(1)} %bitcast.56), kind=kOutput, calls=%fused_computation.39 | convolution fusion | flops 566231040 | bytes 5332992 | tf_op jit(solution)/shard_map/dot_general | solution.py:302
  39.4 1.3 %add_add_fusion = f32[1920,512]{0,1:T(8,128)S(1)} fusion(f32[1920,512]{0,1:T(8,128)S(1)} %fusion.15, f32[1920,512]{0,1:T(8,128)S(1)} %fusion.16, bf16[1920,288]{1,0:T(8,128)(2,1)S(1)} %bitcast.51, bf16[288,512]{1,0:T(8,128)(2,1)S(1)} %bitcast.55), kind=kOutput, calls=%fused_computation | convolution fusion | flops 568197120 | bytes 13197312 | tf_op jit(solution)/shard_map/dot_general | solution.py:302
  40.7 25.3 %shard_map.65 = f32[32,1920]{1,0:T(8,128)S(1)} custom-call(f32[4,2,2,32,1920]{4,3,2,1,0:T(8,128)S(1)} %bitcast.48), custom_call_target="tpu_custom_call" | custom-call | tf_op jit(solution)/shard_map/pallas_call | solution.py:211
  66.1 0.1 add_convert_fusion
  66.1 0.5 reshape.225
  66.7 0.9 %copy.35 = bf16[4,48,10,32]{1,3,2,0:T(8,128)(2,1)} copy(bf16[4,48,10,32]{1,2,0,3:T(8,128)(2,1)S(1)} %bitcast.54) | data formatting | bytes 245760 | tf_op jit(solution)/shard_map/transpose | solution.py:308
  (28 shorter events, 0.7 us)
Async XLA Ops:
  0.0 31.7 %copy-start.2 = (bf16[2,48,10,32]{1,3,2,0:T(8,128)(2,1)S(1)}, bf16[2,48,10,32]{1,3,2,0:T(8,128)(2,1)}, u32[]{:S(2)}) copy-start(bf16[2,48,10,32]{1,3,2,0:T(8,128)(2,1)} %param.11) | copy-start | bytes 184324
  0.0 31.9 %copy-start.1 = (bf16[3,3,3,32,512]{4,3,2,1,0:T(8,128)(2,1)S(1)}, bf16[3,3,3,32,512]{4,3,2,1,0:T(8,128)(2,1)}, u32[]{:S(2)}) copy-start(bf16[3,3,3,32,512]{4,3,2,1,0:T(8,128)(2,1)} %param.14) | copy-start | bytes 2654212
  3.3 0.6 copy-start.3
  31.6 1.0 %copy-start = (bf16[4,48,10,32]{1,3,2,0:T(8,128)(2,1)S(1)}, bf16[4,48,10,32]{1,3,2,0:T(8,128)(2,1)}, u32[]{:S(2)}) copy-start(bf16[4,48,10,32]{1,3,2,0:T(8,128)(2,1)} %param.10) | copy-start | bytes 368644
  31.9 1.0 %copy-start.4 = (f32[32]{0:T(128)S(1)}, f32[32]{0:T(128)}, u32[]{:S(2)}) copy-start(f32[32]{0:T(128)} %param.13) | copy-start | bytes 388
  31.9 1.0 %copy-start.5 = (f32[32]{0:T(128)S(1)}, f32[32]{0:T(128)}, u32[]{:S(2)}) copy-start(f32[32]{0:T(128)} %param.12) | copy-start | bytes 388
  40.7 25.4 %copy-start.6 = (f32[32]{0:T(128)S(1)}, f32[32]{0:T(128)}, u32[]{:S(2)}) copy-start(f32[32]{0:T(128)} %param.15) | copy-start | bytes 388

commit v20 on v17

--- a/solution.py
+++ b/solution.py
@@ -82,8 +82,9 @@
     o_ref[...] = buf[...]
     for cp in edges:
         cp.wait()
-    left_ref[...] = left_buf[...]
-    right_ref[...] = right_buf[...]
+    for t in range(left_ref.shape[0]):
+        left_ref[t] = left_buf[t].astype(jnp.float32).T.astype(left_ref.dtype)
+        right_ref[t] = right_buf[t].astype(jnp.float32).T.astype(right_ref.dtype)
 
 
 def gather_space(tile, cache_t, frames_t):
@@ -91,12 +92,13 @@
     vmem = pl.BlockSpec(memory_space=pltpu.VMEM)
     hbm = pl.BlockSpec(memory_space=pl.ANY)
     edge = (cache_t.shape[0] + frames_t.shape[0],) + cache_t.shape[2:]
+    edge_t = edge[:1] + edge[:0:-1]
     return pl.pallas_call(
         functools.partial(gather_kernel, n),
         out_shape=(
             jax.ShapeDtypeStruct((n,) + tile.shape, tile.dtype),
-            jax.ShapeDtypeStruct(edge, cache_t.dtype),
-            jax.ShapeDtypeStruct(edge, cache_t.dtype),
+            jax.ShapeDtypeStruct(edge_t, cache_t.dtype),
+            jax.ShapeDtypeStruct(edge_t, cache_t.dtype),
         ),
         in_specs=[vmem, hbm, hbm],
         out_specs=(vmem, vmem, vmem),
@@ -253,8 +255,8 @@
     gathered, before, after = gather_space(
         tile, cache.transpose(0, 2, 3, 1), frames.transpose(0, 2, 3, 1)
     )
-    before = before.transpose(0, 2, 1)[:, :, None]
-    after = after.transpose(0, 2, 1)[:, :, None]
+    before = before[:, :, None]
+    after = after[:, :, None]
     means = gathered[:, 0, :local_groups]
     m2s = gathered[:, 1, :local_groups]
     group_mean = jnp.mean(means, axis=0)

time: 68.6 us -> 68.6 us (level)
    pallas_call x2 -> x0, local copies, waits for them, and re-layouts: 1.81 us -> none  [gather_space(): pl.pallas_call(functools.partial(gather_kernel, n), out_shape=(jax.ShapeD...]
    concatenate x1, local copies, waits for them, and re-layouts: 0.01 us -> 0.8 us  [local(): left = jnp.concatenate([before[:ncache], activate(before[ncache:])], axis=0)]
    concatenate x1, local copies, waits for them, and re-layouts: 0.01 us -> 0.74 us  [local(): right = jnp.concatenate([after[:ncache], activate(after[ncache:])], axis=0)]
    unnamed x16 -> x14, local copies, waits for them, and re-layouts: 1.39 us -> 1.41 us
where the time goes in v20:
time: 68.6 us; the launch traced here: 67.6 us
  Pallas kernels  48.9 us (71%)
  other arithmetic  7.78 us (11%)
  local copies, waits for them, and re-layouts  6.84 us (10%)
  matrix products  3.81 us (6%)
    pallas_call x1, Pallas kernels, scatter_chan(): pl.pallas_call(functools.partial(scatter_kernel, nchunk), out_shape=jax.S...  25.3 us
    pallas_call x1, Pallas kernels, gather_space(): pl.pallas_call(functools.partial(gather_kernel, n), out_shape=(jax.ShapeD...  23.6 us
    dot_general x3, matrix products, local(): lax.dot_general(tap_weight, window, (((0,), (1,)), ((), ())), preferred_e...  3.81 us
    unnamed x14, local copies, waits for them, and re-layouts  1.41 us
    reduce_sum x2, other arithmetic, local(): local_m2 = jnp.sum(local_dev * local_dev, axis=(0, 1, 2, 4))  1.39 us

profile of v20, /device:TPU:6, one launch (start us, length us, event | category | flops | bytes accessed | tf_op | source)
XLA Modules:
  0.0 67.6 jit_solution(6324288593710070609)
XLA Ops:
  0.0 1.2 %convert_reduce_fusion = f32[32]{0:T(128)S(1)} fusion(bf16[4,48,10,32]{1,3,2,0:T(8,128)(2,1)} %param.10), kind=kLoop, calls=%fused_computation.15 | loop fusion | flops 122848 | bytes 123008 | tf_op jit(solution)/shard_map/reduce_sum | solution.py:250
  1.2 0.1 reduce_sum.60
  1.3 0.1 reduce_sum.61
  1.5 0.1 sub.59
  1.6 1.3 %multiply_reduce_fusion = f32[32]{0:T(128)S(1)} fusion(f32[32]{0:T(128)S(1)} %sub.59, bf16[4,48,10,32]{1,3,2,0:T(8,128)(2,1)} %param.10), kind=kLoop, calls=%fused_computation.14 | loop fusion | flops 245728 | bytes 123136 | tf_op jit(solution)/shard_map/reduce_sum | solution.py:252
  3.0 0.1 reduce_sum.64
  3.1 0.2 scatter.9.x_ref
  3.3 1.1 %copy.22 = bf16[2,48,10,32]{3,1,2,0:T(8,128)(2,1)S(1)} copy(bf16[2,48,10,32]{1,3,2,0:T(8,128)(2,1)} %param.11) | data formatting | bytes 122880 | tf_op args[1]
  4.4 23.6 %shard_map.64 = (f32[32,8,128]{2,1,0:T(8,128)}, bf16[6,48,32]{2,1,0:T(8,128)(2,1)}, bf16[6,48,32]{2,1,0:T(8,128)(2,1)}) custom-call(f32[8,128]{1,0:T(8,128)} %copy-done.2, bf16[2,10,32,48]{3,2,1,0:T(8,128)(2,1)} %bitcast.58, bf16[4,10,32,48]{3,2,1,0:T(8,128)(2,1)} %bitcast.52), custom_call_target="tpu_custom_call" | custom-call | tf_op jit(solution)/shard_map/pallas_call | solution.py:96
  28.0 1.0 %slice_reduce_fusion.1 = (f32[2]{0:T(128)S(1)}, f32[2]{0:T(128)S(1)}, f32[32,1,2]{2,1,0:T(1,128)S(1)}) fusion(f32[32,8,128]{2,1,0:T(8,128)} %get-tuple-element.33), kind=kLoop, calls=%fused_computation.35 | loop fusion | flops 124 | bytes 784 | tf_op jit(solution)/shard_map/reduce_sum | solution.py:262
  29.2 0.2 fusion.10
  29.5 0.1 mul.94
  29.6 0.8 %slice_bitcast_fusion.1 = bf16[2,48,1,32]{3,1,0,2:T(8,128)(2,1)S(1)} fusion(bf16[6,48,32]{2,1,0:T(8,128)(2,1)} %get-tuple-element.32), kind=kLoop, calls=%fused_computation.26 | loop fusion | bytes 12288 | tf_op jit(solution)/shard_map/concatenate | solution.py:278
  30.4 0.7 %slice_bitcast_fusion = bf16[2,48,1,32]{3,1,2,0:T(8,128)(2,1)S(1)} fusion(bf16[6,48,32]{2,1,0:T(8,128)(2,1)} %get-tuple-element.34), kind=kLoop, calls=%fused_computation.25 | loop fusion | bytes 12288 | tf_op jit(solution)/shard_map/concatenate | solution.py:279
  31.1 0.9 %fusion.7 = (bf16[4,48,1,32]{3,1,0,2:T(8,128)(2,1)S(1)}, bf16[4,48,1,32]{3,1,2,0:T(8,128)(2,1)S(1)}) fusion(f32[32]{0:T(128)} %param.13, f32[32]{0:T(128)} %param.12, f32[32]{0:T(128)S(1)} %mul.94, f32[32]{0:T(128)S(1)} %sub.63, bf16[6,48,32]{2,1,0:T(8,128)(2,1)} %get-tuple-element.32, bf16[6,48,32]{2,1,0:T(8,128)(2,1)} %get-tuple-element.34), kind=kLoop, calls=%fused_computation.23 | loop fusion | flops 122880 | bytes 49664 | tf_op jit(solution)/shard_map/concatenate | solution.py:278
  32.3 0.1 fusion.14
  32.4 0.2 copy.21
  32.6 0.2 copy-done.3
  32.8 0.3 multiply_convert_fusion
  33.2 0.4 fusion.1
  33.6 0.6 fusion.13
  34.2 0.8 %pad_maximum_fusion.1 = bf16[6,12,48,96]{3,2,1,0:T(8,128)(2,1)S(1)} fusion(bf16[6,12,48,32]{3,2,1,0:T(8,128)(2,1)S(1)} %get-tuple-element.41, bf16[6,12,48,32]{3,2,1,0:T(8,128)(2,1)S(1)} %get-tuple-element.42, bf16[6,12,48,32]{3,2,1,0:T(8,128)(2,1)S(1)} %get-tuple-element.40), kind=kLoop, calls=%fused_computation.12 | loop fusion | flops 1990656 | bytes 1327104 | tf_op jit(solution)/shard_map/concatenate | solution.py:286
  35.0 0.3 fusion.15
  35.3 1.1 %pad_maximum_fusion = bf16[6,10,48,288]{3,2,1,0:T(8,128)(2,1)S(1)} fusion(bf16[6,10,48,96]{3,2,1,0:T(8,128)(2,1)S(1)} %get-tuple-element.48, bf16[6,10,48,96]{3,2,1,0:T(8,128)(2,1)S(1)} %get-tuple-element.47, bf16[6,10,48,96]{3,2,1,0:T(8,128)(2,1)S(1)} %get-tuple-element.46), kind=kLoop, calls=%fused_computation.3 | loop fusion | flops 4976640 | bytes 3317760 | tf_op jit(solution)/shard_map/concatenate | solution.py:290
  36.4 0.4 fusion.12
  36.8 1.3 %fusion.17 = f32[1920,512]{0,1:T(8,128)S(1)} fusion(bf16[1920,288]{1,0:T(8,128)(2,1)S(1)} %bitcast.50, bf16[288,512]{1,0:T(8,128)(2,1)S(1)} %bitcast.57), kind=kOutput, calls=%fused_computation.41 | convolution fusion | flops 566231040 | bytes 5332992 | tf_op jit(solution)/shard_map/dot_general | solution.py:304
  38.1 1.3 %fusion.16 = f32[1920,512]{0,1:T(8,128)S(1)} fusion(bf16[1920,288]{1,0:T(8,128)(2,1)S(1)} %bitcast.49, bf16[288,512]{1,0:T(8,128)(2,1)S(1)} %bitcast.56), kind=kOutput, calls=%fused_computation.40 | convolution fusion | flops 566231040 | bytes 5332992 | tf_op jit(solution)/shard_map/dot_general | solution.py:304
  39.4 1.3 %add_add_fusion = f32[1920,512]{0,1:T(8,128)S(1)} fusion(f32[1920,512]{0,1:T(8,128)S(1)} %fusion.16, f32[1920,512]{0,1:T(8,128)S(1)} %fusion.17, bf16[1920,288]{1,0:T(8,128)(2,1)S(1)} %bitcast.51, bf16[288,512]{1,0:T(8,128)(2,1)S(1)} %bitcast.55), kind=kOutput, calls=%fused_computation | convolution fusion | flops 568197120 | bytes 13197312 | tf_op jit(solution)/shard_map/dot_general | solution.py:304
  40.7 25.3 %shard_map.65 = f32[32,1920]{1,0:T(8,128)S(1)} custom-call(f32[4,2,2,32,1920]{4,3,2,1,0:T(8,128)S(1)} %bitcast.48), custom_call_target="tpu_custom_call" | custom-call | tf_op jit(solution)/shard_map/pallas_call | solution.py:213
  66.0 0.1 fusion.5
  66.1 0.5 reshape.225
  66.6 0.9 %copy.26 = bf16[4,48,10,32]{1,3,2,0:T(8,128)(2,1)} copy(bf16[4,48,10,32]{1,2,0,3:T(8,128)(2,1)S(1)} %bitcast.54) | data formatting | bytes 245760 | tf_op jit(solution)/shard_map/transpose | solution.py:310
  (24 shorter events, 0.7 us)
Async XLA Ops:
  0.0 32.1 %copy-start.1 = (bf16[3,3,3,32,512]{4,3,2,1,0:T(8,128)(2,1)S(1)}, bf16[3,3,3,32,512]{4,3,2,1,0:T(8,128)(2,1)}, u32[]{:S(2)}) copy-start(bf16[3,3,3,32,512]{4,3,2,1,0:T(8,128)(2,1)} %param.14) | copy-start | bytes 2654212
  3.3 1.1 %copy-start.2 = (f32[8,128]{1,0:T(8,128)}, f32[8,128]{1,0:T(8,128)S(1)}, u32[]{:S(2)}) copy-start(f32[8,128]{1,0:T(8,128)S(1)} %scatter.9.x_ref) | copy-start | bytes 12292
  29.6 2.8 %copy-start = (bf16[4,48,10,32]{1,3,2,0:T(8,128)(2,1)S(1)}, bf16[4,48,10,32]{1,3,2,0:T(8,128)(2,1)}, u32[]{:S(2)}) copy-start(bf16[4,48,10,32]{1,3,2,0:T(8,128)(2,1)} %param.10) | copy-start | bytes 368644
  32.2 0.7 copy-start.3
  32.2 0.7 copy-start.4
  40.6 25.3 %copy-start.5 = (f32[32]{0:T(128)S(1)}, f32[32]{0:T(128)}, u32[]{:S(2)}) copy-start(f32[32]{0:T(128)} %param.15) | copy-start | bytes 388

commit v21 on v17

--- a/solution.py
+++ b/solution.py
@@ -113,7 +113,7 @@
     )(tile, cache_t, frames_t)
 
 
-def scatter_kernel(nchunk, x_ref, o_ref, recv1, acc1, own, recv2, acc2, recv3,
+def scatter_kernel(widths, x_ref, o_ref, recv1, acc1, own, recv2, acc2, recv3,
                    sem1s, sem1r, sem2s, sem2r, sem3s, sem3r):
     sp = lax.axis_index("space")
     c = lax.axis_index("chan")
@@ -121,7 +121,8 @@
     yh = (c // 2) % 2
     xx = c // 4
     nx, nyh = x_ref.shape[0], x_ref.shape[1]
-    width = x_ref.shape[-1] // nchunk
+    nchunk = len(widths)
+    starts = [sum(widths[:q]) for q in range(nchunk)]
     f32, bf16 = jnp.float32, jnp.bfloat16
 
     def dev(x_, yh_, core_):
@@ -136,7 +137,10 @@
     pl.semaphore_wait(barrier, len(peers))
 
     def cols(q):
-        return pl.ds(q * width, width)
+        return pl.ds(starts[q], widths[q])
+
+    def fit(q):
+        return pl.ds(0, widths[q])
 
     firsts = []
     for q in range(nchunk):
@@ -144,7 +148,7 @@
             for j in range(nyh):
                 n = (q * nx + i) * nyh + j
                 cp = pltpu.make_async_remote_copy(
-                    src_ref=x_ref.at[i, j, 1 - core, :, cols(q)], dst_ref=recv1.at[q, i, j],
+                    src_ref=x_ref.at[i, j, 1 - core, :, cols(q)], dst_ref=recv1.at[q, i, j, :, fit(q)],
                     send_sem=sem1s.at[n], recv_sem=sem1r.at[n],
                     device_id=peers[0], device_id_type=MESH)
                 cp.start()
@@ -157,37 +161,39 @@
         for k in range(1, nx):
             dest = lax.rem(xx + k, nx)
             for j in range(nyh):
-                acc1[q, dest, j] = (x_ref[dest, j, core, :, cols(q)] + recv1[q, dest, j]).astype(bf16)
+                acc1[q, dest, j, :, fit(q)] = (
+                    x_ref[dest, j, core, :, cols(q)] + recv1[q, dest, j, :, fit(q)]
+                ).astype(bf16)
             slot = nx - 1 - k
             cp = pltpu.make_async_remote_copy(
-                src_ref=acc1.at[q, dest], dst_ref=recv2.at[q, slot],
+                src_ref=acc1.at[q, dest, :, :, fit(q)], dst_ref=recv2.at[q, slot, :, :, fit(q)],
                 send_sem=sem2s.at[q * (nx - 1) + k - 1], recv_sem=sem2r.at[q * (nx - 1) + slot],
                 device_id=peers[k], device_id_type=MESH)
             cp.start()
             sends.append(cp)
         for j in range(nyh):
-            own[q, j] = x_ref[xx, j, core, :, cols(q)] + recv1[q, xx, j]
+            own[q, j, :, fit(q)] = x_ref[xx, j, core, :, cols(q)] + recv1[q, xx, j, :, fit(q)]
         return sends
 
     def third(q):
         for slot in range(nx - 1):
             pltpu.make_async_remote_copy(
-                src_ref=acc1.at[q, xx], dst_ref=recv2.at[q, slot],
+                src_ref=acc1.at[q, xx, :, :, fit(q)], dst_ref=recv2.at[q, slot, :, :, fit(q)],
                 send_sem=sem2s.at[q * (nx - 1) + slot], recv_sem=sem2r.at[q * (nx - 1) + slot],
                 device_id=peers[0], device_id_type=MESH).wait_recv()
         other = 1 - yh
-        total = own[q, other]
+        total = own[q, other, :, fit(q)]
         for slot in range(nx - 1):
-            total = total + recv2[q, slot, other].astype(f32)
-        acc2[q] = total.astype(bf16)
+            total = total + recv2[q, slot, other, :, fit(q)].astype(f32)
+        acc2[q, :, fit(q)] = total.astype(bf16)
         cp = pltpu.make_async_remote_copy(
-            src_ref=acc2.at[q], dst_ref=recv3.at[q], send_sem=sem3s.at[q],
+            src_ref=acc2.at[q, :, fit(q)], dst_ref=recv3.at[q, :, fit(q)], send_sem=sem3s.at[q],
             recv_sem=sem3r.at[q], device_id=peers[nx], device_id_type=MESH)
         cp.start()
-        total = own[q, yh]
+        total = own[q, yh, :, fit(q)]
         for slot in range(nx - 1):
-            total = total + recv2[q, slot, yh].astype(f32)
-        own[q, yh] = total
+            total = total + recv2[q, slot, yh, :, fit(q)].astype(f32)
+        own[q, yh, :, fit(q)] = total
         return cp
 
     seconds, lasts = [], []
@@ -201,15 +207,16 @@
             cp.wait_send()
     for q, cp in enumerate(lasts):
         cp.wait()
-        o_ref[:, cols(q)] = own[q, yh] + recv3[q].astype(f32)
-
-
-def scatter_chan(parts, nchunk=3):
+        o_ref[:, cols(q)] = own[q, yh, :, fit(q)] + recv3[q, :, fit(q)].astype(f32)
+
+
+def scatter_chan(parts, widths=(384, 1152, 384)):
     nx, nyh, ncore, rows, cells = parts.shape
-    width = cells // nchunk
+    nchunk, width = len(widths), max(widths)
+    assert sum(widths) == cells
     f32, bf16 = jnp.float32, jnp.bfloat16
     return pl.pallas_call(
-        functools.partial(scatter_kernel, nchunk),
+        functools.partial(scatter_kernel, widths),
         out_shape=jax.ShapeDtypeStruct((rows, cells), f32),
         in_specs=[pl.BlockSpec(memory_space=pltpu.VMEM)],
         out_specs=pl.BlockSpec(memory_space=pltpu.VMEM),

time: 68.6 us -> 68.6 us (level)
  no operation moved by 1% of the time
where the time goes in v21:
time: 68.6 us; the launch traced here: 68.2 us
  Pallas kernels  49.4 us (72%)
  other arithmetic  7.62 us (11%)
  local copies, waits for them, and re-layouts  7.1 us (10%)
  matrix products  3.81 us (6%)
    pallas_call x1, Pallas kernels, scatter_chan(): pl.pallas_call(functools.partial(scatter_kernel, widths), out_shape=jax.S...  25.9 us
    pallas_call x1, Pallas kernels, gather_space(): pl.pallas_call(functools.partial(gather_kernel, n), out_shape=(jax.ShapeD...  23.5 us
    dot_general x3, matrix products, local(): lax.dot_general(tap_weight, window, (((0,), (1,)), ((), ())), preferred_e...  3.81 us
    pallas_call x2, local copies, waits for them, and re-layouts, gather_space(): pl.pallas_call(functools.partial(gather_kernel, n), out_shape=(jax.ShapeD...  1.81 us
    unnamed x16, local copies, waits for them, and re-layouts  1.39 us
    reduce_sum x2, other arithmetic, local(): local_m2 = jnp.sum(local_dev * local_dev, axis=(0, 1, 2, 4))  1.39 us

profile of v21, /device:TPU:6, one launch (start us, length us, event | category | flops | bytes accessed | tf_op | source)
XLA Modules:
  0.0 68.2 jit_solution(5326123334102783438)
XLA Ops:
  0.0 1.2 %convert_reduce_fusion = f32[32]{0:T(128)S(1)} fusion(bf16[4,48,10,32]{1,3,2,0:T(8,128)(2,1)} %param.10), kind=kLoop, calls=%fused_computation.15 | loop fusion | flops 122848 | bytes 123008 | tf_op jit(solution)/shard_map/reduce_sum | solution.py:255
  1.3 0.1 reduce_sum.60
  1.3 0.1 reduce_sum.61
  1.6 1.3 %multiply_reduce_fusion = f32[32]{0:T(128)S(1)} fusion(f32[32]{0:T(128)S(1)} %sub.59, bf16[4,48,10,32]{1,3,2,0:T(8,128)(2,1)} %param.10), kind=kLoop, calls=%fused_computation.14 | loop fusion | flops 245728 | bytes 123136 | tf_op jit(solution)/shard_map/reduce_sum | solution.py:257
  3.0 0.1 reduce_sum.64
  3.1 0.2 scatter.9.x_ref
  3.3 0.6 copy-done.3
  3.9 23.5 %shard_map.64 = (f32[32,8,128]{2,1,0:T(8,128)}, bf16[6,32,48]{2,1,0:T(8,128)(2,1)}, bf16[6,32,48]{2,1,0:T(8,128)(2,1)}) custom-call(f32[8,128]{1,0:T(8,128)} %copy-done.3, bf16[2,10,32,48]{3,2,1,0:T(8,128)(2,1)} %bitcast.62, bf16[4,10,32,48]{3,2,1,0:T(8,128)(2,1)} %bitcast.56), custom_call_target="tpu_custom_call" | custom-call | tf_op jit(solution)/shard_map/pallas_call | solution.py:94
  27.4 1.0 %slice_reduce_fusion.1 = (f32[2]{0:T(128)S(1)}, f32[2]{0:T(128)S(1)}, f32[32,1,2]{2,1,0:T(1,128)S(1)}) fusion(f32[32,8,128]{2,1,0:T(8,128)} %get-tuple-element.33), kind=kLoop, calls=%fused_computation.35 | loop fusion | flops 124 | bytes 784 | tf_op jit(solution)/shard_map/reduce_sum | solution.py:267
  28.5 0.1 sub.63
  28.7 0.2 fusion.10
  29.0 0.9 %copy.26 = bf16[6,32,48]{1,2,0:T(8,128)(2,1)S(1)} copy(bf16[6,32,48]{2,1,0:T(8,128)(2,1)} %get-tuple-element.32) | data formatting | bytes 36864 | tf_op jit(solution)/shard_map/pallas_call | solution.py:94
  29.9 0.9 %copy.30 = bf16[6,32,48]{1,2,0:T(8,128)(2,1)S(1)} copy(bf16[6,32,48]{2,1,0:T(8,128)(2,1)} %get-tuple-element.34) | data formatting | bytes 36864 | tf_op jit(solution)/shard_map/pallas_call | solution.py:94
  30.8 0.8 %fusion.7 = (bf16[4,48,1,32]{3,1,0,2:T(8,128)(2,1)S(1)}, bf16[4,48,1,32]{3,1,2,0:T(8,128)(2,1)S(1)}) fusion(bf16[6,48,32]{2,1,0:T(8,128)(2,1)S(1)} %bitcast.64, f32[32]{0:T(128)} %param.13, f32[32]{0:T(128)} %param.12, f32[32]{0:T(128)S(1)} %mul.94, f32[32]{0:T(128)S(1)} %sub.63, bf16[6,48,32]{2,1,0:T(8,128)(2,1)S(1)} %bitcast.66), kind=kLoop, calls=%fused_computation.23 | loop fusion | flops 122880 | bytes 49664 | tf_op jit(solution)/shard_map/concatenate | solution.py:283
  31.7 0.2 copy.29
  32.0 0.1 fusion.14
  32.1 0.5 copy-done
  32.6 0.2 copy.28
  32.9 0.3 multiply_convert_fusion
  33.2 0.4 fusion.1
  33.6 0.6 fusion.13
  34.2 0.8 %pad_maximum_fusion.1 = bf16[6,12,48,96]{3,2,1,0:T(8,128)(2,1)S(1)} fusion(bf16[6,12,48,32]{3,2,1,0:T(8,128)(2,1)S(1)} %get-tuple-element.41, bf16[6,12,48,32]{3,2,1,0:T(8,128)(2,1)S(1)} %get-tuple-element.42, bf16[6,12,48,32]{3,2,1,0:T(8,128)(2,1)S(1)} %get-tuple-element.40), kind=kLoop, calls=%fused_computation.12 | loop fusion | flops 1990656 | bytes 1327104 | tf_op jit(solution)/shard_map/concatenate | solution.py:291
  35.0 0.3 fusion.15
  35.3 1.1 %pad_maximum_fusion = bf16[6,10,48,288]{3,2,1,0:T(8,128)(2,1)S(1)} fusion(bf16[6,10,48,96]{3,2,1,0:T(8,128)(2,1)S(1)} %get-tuple-element.48, bf16[6,10,48,96]{3,2,1,0:T(8,128)(2,1)S(1)} %get-tuple-element.47, bf16[6,10,48,96]{3,2,1,0:T(8,128)(2,1)S(1)} %get-tuple-element.46), kind=kLoop, calls=%fused_computation.3 | loop fusion | flops 4976640 | bytes 3317760 | tf_op jit(solution)/shard_map/concatenate | solution.py:295
  36.5 0.4 fusion.12
  36.8 1.3 %fusion.17 = f32[1920,512]{0,1:T(8,128)S(1)} fusion(bf16[1920,288]{1,0:T(8,128)(2,1)S(1)} %bitcast.54, bf16[288,512]{1,0:T(8,128)(2,1)S(1)} %bitcast.61), kind=kOutput, calls=%fused_computation.41 | convolution fusion | flops 566231040 | bytes 5332992 | tf_op jit(solution)/shard_map/dot_general | solution.py:309
  38.1 1.3 %fusion.16 = f32[1920,512]{0,1:T(8,128)S(1)} fusion(bf16[1920,288]{1,0:T(8,128)(2,1)S(1)} %bitcast.53, bf16[288,512]{1,0:T(8,128)(2,1)S(1)} %bitcast.60), kind=kOutput, calls=%fused_computation.40 | convolution fusion | flops 566231040 | bytes 5332992 | tf_op jit(solution)/shard_map/dot_general | solution.py:309
  39.4 1.3 %add_add_fusion = f32[1920,512]{0,1:T(8,128)S(1)} fusion(f32[1920,512]{0,1:T(8,128)S(1)} %fusion.16, f32[1920,512]{0,1:T(8,128)S(1)} %fusion.17, bf16[1920,288]{1,0:T(8,128)(2,1)S(1)} %bitcast.55, bf16[288,512]{1,0:T(8,128)(2,1)S(1)} %bitcast.59), kind=kOutput, calls=%fused_computation | convolution fusion | flops 568197120 | bytes 13197312 | tf_op jit(solution)/shard_map/dot_general | solution.py:309
  40.7 25.9 %shard_map.65 = f32[32,1920]{1,0:T(8,128)S(1)} custom-call(f32[4,2,2,32,1920]{4,3,2,1,0:T(8,128)S(1)} %bitcast.52), custom_call_target="tpu_custom_call" | custom-call | tf_op jit(solution)/shard_map/pallas_call | solution.py:218
  66.6 0.1 fusion.5
  66.7 0.5 reshape.225
  67.3 0.9 %copy.35 = bf16[4,48,10,32]{1,3,2,0:T(8,128)(2,1)} copy(bf16[4,48,10,32]{1,2,0,3:T(8,128)(2,1)S(1)} %bitcast.58) | data formatting | bytes 245760 | tf_op jit(solution)/shard_map/transpose | solution.py:315
  (28 shorter events, 0.7 us)
Async XLA Ops:
  0.0 31.7 %copy-start.2 = (bf16[2,48,10,32]{1,3,2,0:T(8,128)(2,1)S(1)}, bf16[2,48,10,32]{1,3,2,0:T(8,128)(2,1)}, u32[]{:S(2)}) copy-start(bf16[2,48,10,32]{1,3,2,0:T(8,128)(2,1)} %param.11) | copy-start | bytes 184324
  0.0 31.9 %copy-start.1 = (bf16[3,3,3,32,512]{4,3,2,1,0:T(8,128)(2,1)S(1)}, bf16[3,3,3,32,512]{4,3,2,1,0:T(8,128)(2,1)}, u32[]{:S(2)}) copy-start(bf16[3,3,3,32,512]{4,3,2,1,0:T(8,128)(2,1)} %param.14) | copy-start | bytes 2654212
  3.3 0.6 copy-start.3
  31.6 1.0 %copy-start = (bf16[4,48,10,32]{1,3,2,0:T(8,128)(2,1)S(1)}, bf16[4,48,10,32]{1,3,2,0:T(8,128)(2,1)}, u32[]{:S(2)}) copy-start(bf16[4,48,10,32]{1,3,2,0:T(8,128)(2,1)} %param.10) | copy-start | bytes 368644
  31.9 1.0 %copy-start.4 = (f32[32]{0:T(128)S(1)}, f32[32]{0:T(128)}, u32[]{:S(2)}) copy-start(f32[32]{0:T(128)} %param.13) | copy-start | bytes 388
  31.9 1.0 %copy-start.5 = (f32[32]{0:T(128)S(1)}, f32[32]{0:T(128)}, u32[]{:S(2)}) copy-start(f32[32]{0:T(128)} %param.12) | copy-start | bytes 388
  40.7 25.9 %copy-start.6 = (f32[32]{0:T(128)S(1)}, f32[32]{0:T(128)}, u32[]{:S(2)}) copy-start(f32[32]{0:T(128)} %param.15) | copy-start | bytes 388

commit v22 on v21

--- a/solution.py
+++ b/solution.py
@@ -15,7 +15,7 @@
 epsilon = 1e-06
 
 
-def gather_kernel(n, x_ref, cache_ref, frames_ref, o_ref, left_ref, right_ref,
+def gather_kernel(n, members, x_ref, cache_ref, frames_ref, o_ref, left_ref, right_ref,
                   buf, left_buf, right_buf, send_sem, recv_sem, edge_send, edge_recv):
     me = lax.axis_index("space")
     ch = lax.axis_index("chan")
@@ -79,24 +79,33 @@
 
     lax.fori_loop(1, n, finish, 0)
     buf[me] = x_ref[...]
-    o_ref[...] = buf[...]
+    gathered = buf[...]
+    means = gathered[:, 0, :]
+    group_mean = jnp.sum(means, axis=0, keepdims=True) / n
+    spread = jnp.sum(gathered[:, 1, :], axis=0, keepdims=True) + members * jnp.sum(
+        (means - group_mean) ** 2, axis=0, keepdims=True
+    )
+    inv = lax.rsqrt(spread / (members * n) + epsilon)
+    o_ref[...] = jnp.concatenate([group_mean, inv, jnp.zeros((6,) + inv.shape[1:], inv.dtype)], axis=0)
     for cp in edges:
         cp.wait()
-    left_ref[...] = left_buf[...]
-    right_ref[...] = right_buf[...]
-
-
-def gather_space(tile, cache_t, frames_t):
+    for t in range(left_ref.shape[0]):
+        left_ref[t] = left_buf[t].astype(jnp.float32).T.astype(left_ref.dtype)
+        right_ref[t] = right_buf[t].astype(jnp.float32).T.astype(right_ref.dtype)
+
+
+def gather_space(tile, cache_t, frames_t, members):
     n = lax.axis_size("space")
     vmem = pl.BlockSpec(memory_space=pltpu.VMEM)
     hbm = pl.BlockSpec(memory_space=pl.ANY)
     edge = (cache_t.shape[0] + frames_t.shape[0],) + cache_t.shape[2:]
+    edge_t = edge[:1] + edge[:0:-1]
     return pl.pallas_call(
-        functools.partial(gather_kernel, n),
+        functools.partial(gather_kernel, n, members),
         out_shape=(
-            jax.ShapeDtypeStruct((n,) + tile.shape, tile.dtype),
-            jax.ShapeDtypeStruct(edge, cache_t.dtype),
-            jax.ShapeDtypeStruct(edge, cache_t.dtype),
+            jax.ShapeDtypeStruct(tile.shape, tile.dtype),
+            jax.ShapeDtypeStruct(edge_t, cache_t.dtype),
+            jax.ShapeDtypeStruct(edge_t, cache_t.dtype),
         ),
         in_specs=[vmem, hbm, hbm],
         out_specs=(vmem, vmem, vmem),
@@ -257,19 +266,13 @@
     local_m2 = jnp.sum(local_dev * local_dev, axis=(0, 1, 2, 4))
     tile = jnp.zeros((8, 128), jnp.float32)
     tile = tile.at[0, :local_groups].set(local_mean).at[1, :local_groups].set(local_m2)
-    gathered, before, after = gather_space(
-        tile, cache.transpose(0, 2, 3, 1), frames.transpose(0, 2, 3, 1)
-    )
-    before = before.transpose(0, 2, 1)[:, :, None]
-    after = after.transpose(0, 2, 1)[:, :, None]
-    means = gathered[:, 0, :local_groups]
-    m2s = gathered[:, 1, :local_groups]
-    group_mean = jnp.mean(means, axis=0)
-    spread = jnp.sum(m2s, axis=0) + local_members * jnp.sum(
-        (means - group_mean) ** 2, axis=0
-    )
-    group_var = spread / (local_members * nspace)
-    inv = lax.rsqrt(group_var + epsilon)
+    combined, before, after = gather_space(
+        tile, cache.transpose(0, 2, 3, 1), frames.transpose(0, 2, 3, 1), local_members
+    )
+    before = before[:, :, None]
+    after = after[:, :, None]
+    group_mean = combined[0, :local_groups]
+    inv = combined[1, :local_groups]
 
     def activate(x):
         shape = x.shape

time: 68.6 us -> 68.6 us (level)
  other arithmetic: 7.62 us -> 6.55 us
  local copies, waits for them, and re-layouts: 7.1 us -> 8.07 us
    pallas_call x2 -> x0, local copies, waits for them, and re-layouts: 1.81 us -> none  [gather_space(): pl.pallas_call(functools.partial(gather_kernel, n), out_shape=(jax.ShapeD...]
    reduce_sum x2 -> x0, other arithmetic: 1.22 us -> none  [the longest x1 1.03 us: local(): group_mean = jnp.mean(means, axis=0)]
    sub x2 -> x3, local copies, waits for them, and re-layouts: 0.15 us -> 0.91 us  [activate(): scaled = (v - group_mean[:, None]) * inv[:, None]]
    concatenate x1, local copies, waits for them, and re-layouts: 0.01 us -> 0.74 us  [local(): right = jnp.concatenate([after[:ncache], activate(after[ncache:])], axis=0)]
    concatenate x1, local copies, waits for them, and re-layouts: 0.01 us -> 0.74 us  [local(): left = jnp.concatenate([before[:ncache], activate(before[ncache:])], axis=0)]
    unnamed x16 -> x14, local copies, waits for them, and re-layouts: 1.39 us -> 2.04 us
where the time goes in v22:
time: 68.6 us; the launch traced here: 68.2 us
  Pallas kernels  49.5 us (72%)
  local copies, waits for them, and re-layouts  8.07 us (12%)
  other arithmetic  6.55 us (10%)
  matrix products  3.8 us (6%)
    pallas_call x1, Pallas kernels, scatter_chan(): pl.pallas_call(functools.partial(scatter_kernel, widths), out_shape=jax.S...  25.9 us
    pallas_call x1, Pallas kernels, gather_space(): pl.pallas_call(functools.partial(gather_kernel, n, members), out_shape=(j...  23.6 us
    dot_general x3, matrix products, local(): lax.dot_general(tap_weight, window, (((0,), (1,)), ((), ())), preferred_e...  3.8 us
    unnamed x14, local copies, waits for them, and re-layouts  2.04 us
    reduce_sum x2, other arithmetic, local(): local_m2 = jnp.sum(local_dev * local_dev, axis=(0, 1, 2, 4))  1.39 us

profile of v22, /device:TPU:6, one launch (start us, length us, event | category | flops | bytes accessed | tf_op | source)
XLA Modules:
  0.0 68.2 jit_solution(13074500928989456423)
XLA Ops:
  0.0 1.2 %convert_reduce_fusion = f32[32]{0:T(128)S(1)} fusion(bf16[4,48,10,32]{1,3,2,0:T(8,128)(2,1)} %param.10), kind=kLoop, calls=%fused_computation.15 | loop fusion | flops 122848 | bytes 123008 | tf_op jit(solution)/shard_map/reduce_sum | solution.py:264
  1.2 0.1 reduce_sum.24
  1.3 0.1 reduce_sum.25
  1.5 0.1 sub.53
  1.6 1.3 %multiply_reduce_fusion = f32[32]{0:T(128)S(1)} fusion(f32[32]{0:T(128)S(1)} %sub.53, bf16[4,48,10,32]{1,3,2,0:T(8,128)(2,1)} %param.10), kind=kLoop, calls=%fused_computation.14 | loop fusion | flops 245728 | bytes 123136 | tf_op jit(solution)/shard_map/reduce_sum | solution.py:266
  3.0 0.1 reduce_sum.37
  3.1 0.2 scatter.9.x_ref
  3.3 0.6 copy-done.2
  3.9 23.6 %shard_map.64 = (f32[8,128]{1,0:T(8,128)}, bf16[6,48,32]{2,1,0:T(8,128)(2,1)}, bf16[6,48,32]{2,1,0:T(8,128)(2,1)}) custom-call(f32[8,128]{1,0:T(8,128)} %copy-done.2, bf16[2,10,32,48]{3,2,1,0:T(8,128)(2,1)} %bitcast.56, bf16[4,10,32,48]{3,2,1,0:T(8,128)(2,1)} %bitcast.50), custom_call_target="tpu_custom_call" | custom-call | tf_op jit(solution)/shard_map/pallas_call | solution.py:103
  27.5 0.8 %slice_bitcast_fusion.3 = (f32[2]{0:T(128)S(1)}, f32[2]{0:T(128)S(1)}) fusion(f32[8,128]{1,0:T(8,128)} %get-tuple-element.33), kind=kLoop, calls=%fused_computation.28 | loop fusion | bytes 32 | tf_op jit(solution)/shard_map/sub | solution.py:280
  28.3 0.1 sub.58
  28.5 0.7 %slice_bitcast_fusion.1 = bf16[2,48,1,32]{3,1,0,2:T(8,128)(2,1)S(1)} fusion(bf16[6,48,32]{2,1,0:T(8,128)(2,1)} %get-tuple-element.32), kind=kLoop, calls=%fused_computation.26 | loop fusion | bytes 12288 | tf_op jit(solution)/shard_map/concatenate | solution.py:286
  29.3 0.7 %slice_bitcast_fusion = bf16[2,48,1,32]{3,1,2,0:T(8,128)(2,1)S(1)} fusion(bf16[6,48,32]{2,1,0:T(8,128)(2,1)} %get-tuple-element.34), kind=kLoop, calls=%fused_computation.25 | loop fusion | bytes 12288 | tf_op jit(solution)/shard_map/concatenate | solution.py:287
  30.0 0.9 %fusion.7 = (bf16[4,48,1,32]{3,1,0,2:T(8,128)(2,1)S(1)}, bf16[4,48,1,32]{3,1,2,0:T(8,128)(2,1)S(1)}) fusion(f32[32]{0:T(128)} %param.13, f32[32]{0:T(128)} %param.12, f32[32]{0:T(128)S(1)} %mul.91, f32[32]{0:T(128)S(1)} %sub.58, bf16[6,48,32]{2,1,0:T(8,128)(2,1)} %get-tuple-element.32, bf16[6,48,32]{2,1,0:T(8,128)(2,1)} %get-tuple-element.34), kind=kLoop, calls=%fused_computation.23 | loop fusion | flops 122880 | bytes 49664 | tf_op jit(solution)/shard_map/concatenate | solution.py:286
  31.0 1.1 %copy.19 = bf16[2,48,10,32]{3,1,2,0:T(8,128)(2,1)S(1)} copy(bf16[2,48,10,32]{1,3,2,0:T(8,128)(2,1)} %param.11) | data formatting | bytes 122880 | tf_op args[1]
  32.3 0.1 fusion.12
  32.4 0.2 copy.18
  32.6 0.2 copy-done.3
  32.8 0.3 multiply_convert_fusion
  33.2 0.4 fusion.1
  33.6 0.6 fusion.11
  34.2 0.8 %pad_maximum_fusion.1 = bf16[6,12,48,96]{3,2,1,0:T(8,128)(2,1)S(1)} fusion(bf16[6,12,48,32]{3,2,1,0:T(8,128)(2,1)S(1)} %get-tuple-element.39, bf16[6,12,48,32]{3,2,1,0:T(8,128)(2,1)S(1)} %get-tuple-element.40, bf16[6,12,48,32]{3,2,1,0:T(8,128)(2,1)S(1)} %get-tuple-element.38), kind=kLoop, calls=%fused_computation.12 | loop fusion | flops 1990656 | bytes 1327104 | tf_op jit(solution)/shard_map/concatenate | solution.py:294
  35.0 0.3 fusion.13
  35.3 1.1 %pad_maximum_fusion = bf16[6,10,48,288]{3,2,1,0:T(8,128)(2,1)S(1)} fusion(bf16[6,10,48,96]{3,2,1,0:T(8,128)(2,1)S(1)} %get-tuple-element.46, bf16[6,10,48,96]{3,2,1,0:T(8,128)(2,1)S(1)} %get-tuple-element.45, bf16[6,10,48,96]{3,2,1,0:T(8,128)(2,1)S(1)} %get-tuple-element.44), kind=kLoop, calls=%fused_computation.3 | loop fusion | flops 4976640 | bytes 3317760 | tf_op jit(solution)/shard_map/concatenate | solution.py:298
  36.4 0.4 fusion.10
  36.8 1.3 %fusion.15 = f32[1920,512]{0,1:T(8,128)S(1)} fusion(bf16[1920,288]{1,0:T(8,128)(2,1)S(1)} %bitcast.48, bf16[288,512]{1,0:T(8,128)(2,1)S(1)} %bitcast.55), kind=kOutput, calls=%fused_computation.36 | convolution fusion | flops 566231040 | bytes 5332992 | tf_op jit(solution)/shard_map/dot_general | solution.py:312
  38.1 1.3 %fusion.14 = f32[1920,512]{0,1:T(8,128)S(1)} fusion(bf16[1920,288]{1,0:T(8,128)(2,1)S(1)} %bitcast.47, bf16[288,512]{1,0:T(8,128)(2,1)S(1)} %bitcast.54), kind=kOutput, calls=%fused_computation.35 | convolution fusion | flops 566231040 | bytes 5332992 | tf_op jit(solution)/shard_map/dot_general | solution.py:312
  39.4 1.3 %add_add_fusion = f32[1920,512]{0,1:T(8,128)S(1)} fusion(f32[1920,512]{0,1:T(8,128)S(1)} %fusion.14, f32[1920,512]{0,1:T(8,128)S(1)} %fusion.15, bf16[1920,288]{1,0:T(8,128)(2,1)S(1)} %bitcast.49, bf16[288,512]{1,0:T(8,128)(2,1)S(1)} %bitcast.53), kind=kOutput, calls=%fused_computation | convolution fusion | flops 568197120 | bytes 13197312 | tf_op jit(solution)/shard_map/dot_general | solution.py:312
  40.7 25.9 %shard_map.65 = f32[32,1920]{1,0:T(8,128)S(1)} custom-call(f32[4,2,2,32,1920]{4,3,2,1,0:T(8,128)S(1)} %bitcast.46), custom_call_target="tpu_custom_call" | custom-call | tf_op jit(solution)/shard_map/pallas_call | solution.py:227
  66.6 0.1 fusion.5
  66.7 0.5 reshape.221
  67.2 0.9 %copy.23 = bf16[4,48,10,32]{1,3,2,0:T(8,128)(2,1)} copy(bf16[4,48,10,32]{1,2,0,3:T(8,128)(2,1)S(1)} %bitcast.52) | data formatting | bytes 245760 | tf_op jit(solution)/shard_map/transpose | solution.py:318
  (20 shorter events, 0.6 us)
Async XLA Ops:
  0.0 32.2 %copy-start.1 = (bf16[3,3,3,32,512]{4,3,2,1,0:T(8,128)(2,1)S(1)}, bf16[3,3,3,32,512]{4,3,2,1,0:T(8,128)(2,1)}, u32[]{:S(2)}) copy-start(bf16[3,3,3,32,512]{4,3,2,1,0:T(8,128)(2,1)} %param.14) | copy-start | bytes 2654212
  3.3 0.6 copy-start.2
  31.0 1.4 %copy-start = (bf16[4,48,10,32]{1,3,2,0:T(8,128)(2,1)S(1)}, bf16[4,48,10,32]{1,3,2,0:T(8,128)(2,1)}, u32[]{:S(2)}) copy-start(bf16[4,48,10,32]{1,3,2,0:T(8,128)(2,1)} %param.10) | copy-start | bytes 368644
  32.2 0.7 copy-start.3
  32.2 0.7 copy-start.4
  40.7 26.0 %copy-start.5 = (f32[32]{0:T(128)S(1)}, f32[32]{0:T(128)}, u32[]{:S(2)}) copy-start(f32[32]{0:T(128)} %param.15) | copy-start | bytes 388

commit v23 on v21

--- a/solution.py
+++ b/solution.py
@@ -113,7 +113,7 @@
     )(tile, cache_t, frames_t)
 
 
-def scatter_kernel(widths, x_ref, o_ref, recv1, acc1, own, recv2, acc2, recv3,
+def scatter_kernel(widths, x_ref, bias_ref, o_ref, recv1, acc1, own, recv2, acc2, recv3,
                    sem1s, sem1r, sem2s, sem2r, sem3s, sem3r):
     sp = lax.axis_index("space")
     c = lax.axis_index("chan")
@@ -207,18 +207,19 @@
             cp.wait_send()
     for q, cp in enumerate(lasts):
         cp.wait()
-        o_ref[:, cols(q)] = own[q, yh, :, fit(q)] + recv3[q, :, fit(q)].astype(f32)
-
-
-def scatter_chan(parts, widths=(384, 1152, 384)):
+        total = own[q, yh, :, fit(q)] + recv3[q, :, fit(q)].astype(f32)
+        o_ref[:, cols(q)] = (total + bias_ref[...]).astype(o_ref.dtype)
+
+
+def scatter_chan(parts, bias, widths=(384, 1152, 384)):
     nx, nyh, ncore, rows, cells = parts.shape
     nchunk, width = len(widths), max(widths)
     assert sum(widths) == cells
     f32, bf16 = jnp.float32, jnp.bfloat16
     return pl.pallas_call(
         functools.partial(scatter_kernel, widths),
-        out_shape=jax.ShapeDtypeStruct((rows, cells), f32),
-        in_specs=[pl.BlockSpec(memory_space=pltpu.VMEM)],
+        out_shape=jax.ShapeDtypeStruct((rows, cells), bf16),
+        in_specs=[pl.BlockSpec(memory_space=pltpu.VMEM)] * 2,
         out_specs=pl.BlockSpec(memory_space=pltpu.VMEM),
         scratch_shapes=[
             pltpu.VMEM((nchunk, nx, nyh, rows, width), f32),
@@ -236,7 +237,7 @@
         ],
         compiler_params=pltpu.CompilerParams(
             collective_id=1, has_side_effects=True, vmem_limit_bytes=48 * 1024 * 1024),
-    )(parts)
+    )(parts, bias)
 
 
 def local(frames, cache, gamma, beta, kernel, bias):
@@ -309,9 +310,8 @@
         running = running + lax.dot_general(
             tap_weight, window, (((0,), (1,)), ((), ())), preferred_element_type=jnp.float32
         )
-    summed = scatter_chan(running.reshape(nx, 2, 2, local_ch, cell_count))
-    result = summed.T + bias
-    result = result.astype(jnp.bfloat16).reshape(nframes, col_count, row_count, -1)
+    summed = scatter_chan(running.reshape(nx, 2, 2, local_ch, cell_count), bias[:, None])
+    result = summed.T.reshape(nframes, col_count, row_count, -1)
     return result.transpose(0, 2, 1, 3)
 
 

time: 68.6 us -> 72.8 us (1.061)
  local copies, waits for them, and re-layouts: 7.1 us -> 9.49 us
  matrix products: 3.81 us -> 5.7 us
    unnamed x16 -> x18, local copies, waits for them, and re-layouts: 1.39 us -> 3.71 us
    dot_general x3, matrix products: 3.81 us -> 5.7 us  [local(): lax.dot_general(tap_weight, window, (((0,), (1,)), ((), ())), preferred_e...]
where the time goes in v23:
time: 72.8 us; the launch traced here: 72.4 us
  Pallas kernels  49.4 us (68%)
  local copies, waits for them, and re-layouts  9.49 us (13%)
  other arithmetic  7.49 us (10%)
  matrix products  5.7 us (8%)
    pallas_call x1, Pallas kernels, scatter_chan(): pl.pallas_call(functools.partial(scatter_kernel, widths), out_shape=jax.S...  25.8 us
    pallas_call x1, Pallas kernels, gather_space(): pl.pallas_call(functools.partial(gather_kernel, n), out_shape=(jax.ShapeD...  23.6 us
    dot_general x3, matrix products, local(): lax.dot_general(tap_weight, window, (((0,), (1,)), ((), ())), preferred_e...  5.7 us
    unnamed x18, local copies, waits for them, and re-layouts  3.71 us
    pallas_call x2, local copies, waits for them, and re-layouts, gather_space(): pl.pallas_call(functools.partial(gather_kernel, n), out_shape=(jax.ShapeD...  1.82 us

profile of v23, /device:TPU:6, one launch (start us, length us, event | category | flops | bytes accessed | tf_op | source)
XLA Modules:
  0.0 72.4 jit_solution(2310599149439077878)
XLA Ops:
  0.0 1.2 %convert_reduce_fusion = f32[32]{0:T(128)S(1)} fusion(bf16[4,48,10,32]{1,3,2,0:T(8,128)(2,1)} %param.10), kind=kLoop, calls=%fused_computation.15 | loop fusion | flops 122848 | bytes 123008 | tf_op jit(solution)/shard_map/reduce_sum | solution.py:256
  1.2 0.1 reduce_sum.60
  1.3 0.1 reduce_sum.61
  1.5 0.1 sub.59
  1.6 1.3 %multiply_reduce_fusion = f32[32]{0:T(128)S(1)} fusion(f32[32]{0:T(128)S(1)} %sub.59, bf16[4,48,10,32]{1,3,2,0:T(8,128)(2,1)} %param.10), kind=kLoop, calls=%fused_computation.14 | loop fusion | flops 245728 | bytes 123136 | tf_op jit(solution)/shard_map/reduce_sum | solution.py:258
  3.0 0.1 reduce_sum.64
  3.1 0.2 scatter.9.x_ref
  3.3 0.6 copy-done.4
  3.9 23.6 %shard_map.64 = (f32[32,8,128]{2,1,0:T(8,128)}, bf16[6,32,48]{2,1,0:T(8,128)(2,1)}, bf16[6,32,48]{2,1,0:T(8,128)(2,1)}) custom-call(f32[8,128]{1,0:T(8,128)} %copy-done.4, bf16[2,10,32,48]{3,2,1,0:T(8,128)(2,1)} %bitcast.63, bf16[4,10,32,48]{3,2,1,0:T(8,128)(2,1)} %bitcast.57), custom_call_target="tpu_custom_call" | custom-call | tf_op jit(solution)/shard_map/pallas_call | solution.py:94
  27.5 1.0 %slice_reduce_fusion.1 = (f32[2]{0:T(128)S(1)}, f32[2]{0:T(128)S(1)}, f32[32,1,2]{2,1,0:T(1,128)S(1)}) fusion(f32[32,8,128]{2,1,0:T(8,128)} %get-tuple-element.33), kind=kLoop, calls=%fused_computation.33 | loop fusion | flops 124 | bytes 784 | tf_op jit(solution)/shard_map/reduce_sum | solution.py:268
  28.6 0.2 fusion.9
  29.1 0.9 %copy.32 = bf16[6,32,48]{1,2,0:T(8,128)(2,1)S(1)} copy(bf16[6,32,48]{2,1,0:T(8,128)(2,1)} %get-tuple-element.34) | data formatting | bytes 36864 | tf_op jit(solution)/shard_map/pallas_call | solution.py:94
  30.0 0.9 %copy.28 = bf16[6,32,48]{1,2,0:T(8,128)(2,1)S(1)} copy(bf16[6,32,48]{2,1,0:T(8,128)(2,1)} %get-tuple-element.32) | data formatting | bytes 36864 | tf_op jit(solution)/shard_map/pallas_call | solution.py:94
  30.9 0.8 %fusion.6 = (bf16[4,48,1,32]{3,1,0,2:T(8,128)(2,1)S(1)}, bf16[4,48,1,32]{3,1,2,0:T(8,128)(2,1)S(1)}) fusion(bf16[6,48,32]{2,1,0:T(8,128)(2,1)S(1)} %bitcast.66, f32[32]{0:T(128)} %param.13, f32[32]{0:T(128)} %param.12, f32[32]{0:T(128)S(1)} %mul.94, f32[32]{0:T(128)S(1)} %sub.63, bf16[6,48,32]{2,1,0:T(8,128)(2,1)S(1)} %bitcast.64), kind=kLoop, calls=%fused_computation.21 | loop fusion | flops 122880 | bytes 49664 | tf_op jit(solution)/shard_map/concatenate | solution.py:284
  31.8 0.2 copy.30
  32.1 0.3 multiply_convert_fusion
  32.4 0.2 copy.31
  32.6 0.4 fusion.1
  33.0 0.6 fusion.12
  33.6 0.8 %pad_maximum_fusion.1 = bf16[6,12,48,96]{3,2,1,0:T(8,128)(2,1)S(1)} fusion(bf16[6,12,48,32]{3,2,1,0:T(8,128)(2,1)S(1)} %get-tuple-element.41, bf16[6,12,48,32]{3,2,1,0:T(8,128)(2,1)S(1)} %get-tuple-element.42, bf16[6,12,48,32]{3,2,1,0:T(8,128)(2,1)S(1)} %get-tuple-element.40), kind=kLoop, calls=%fused_computation.12 | loop fusion | flops 1990656 | bytes 1327104 | tf_op jit(solution)/shard_map/concatenate | solution.py:292
  34.4 0.3 fusion.14
  34.7 1.1 %pad_maximum_fusion = bf16[6,10,48,288]{3,2,1,0:T(8,128)(2,1)S(1)} fusion(bf16[6,10,48,96]{3,2,1,0:T(8,128)(2,1)S(1)} %get-tuple-element.48, bf16[6,10,48,96]{3,2,1,0:T(8,128)(2,1)S(1)} %get-tuple-element.47, bf16[6,10,48,96]{3,2,1,0:T(8,128)(2,1)S(1)} %get-tuple-element.46), kind=kLoop, calls=%fused_computation.3 | loop fusion | flops 4976640 | bytes 3317760 | tf_op jit(solution)/shard_map/concatenate | solution.py:296
  35.8 0.4 fusion.11
  36.2 0.8 %copy-done.2 = bf16[3,3,3,32,512]{4,3,2,1,0:T(8,128)(2,1)S(1)} copy-done((bf16[3,3,3,32,512]{4,3,2,1,0:T(8,128)(2,1)S(1)}, bf16[3,3,3,32,512]{4,3,2,1,0:T(8,128)(2,1)}, u32[]{:S(2)}) %copy-start.2) | copy-done | bytes 884760
  37.1 1.3 %fusion.15 = f32[1920,512]{0,1:T(8,128)S(1)} fusion(bf16[1920,288]{1,0:T(8,128)(2,1)S(1)} %bitcast.55, bf16[288,512]{1,0:T(8,128)(2,1)S(1)} %bitcast.62), kind=kOutput, calls=%fused_computation.38 | convolution fusion | flops 566231040 | bytes 5332992 | tf_op jit(solution)/shard_map/dot_general | solution.py:310
  38.4 1.3 %fusion.16 = f32[1920,512]{0,1:T(8,128)S(1)} fusion(bf16[1920,288]{1,0:T(8,128)(2,1)S(1)} %bitcast.54, bf16[288,512]{1,0:T(8,128)(2,1)S(1)} %bitcast.61), kind=kOutput, calls=%fused_computation.39 | convolution fusion | flops 566231040 | bytes 5332992 | tf_op jit(solution)/shard_map/dot_general | solution.py:310
  39.7 3.2 %add_add_fusion = f32[1920,512]{0,1:T(8,128)} fusion(f32[1920,512]{0,1:T(8,128)S(1)} %fusion.15, f32[1920,512]{0,1:T(8,128)S(1)} %fusion.16, bf16[1920,288]{1,0:T(8,128)(2,1)S(1)} %bitcast.56, bf16[288,512]{1,0:T(8,128)(2,1)S(1)} %bitcast.60), kind=kOutput, calls=%fused_computation | convolution fusion | flops 568197120 | bytes 13197312 | tf_op jit(solution)/shard_map/dot_general | solution.py:310
  42.9 0.1 copy.37.bias_ref
  43.0 2.1 %copy-done = f32[1920,512]{0,1:T(8,128)S(1)} copy-done((f32[1920,512]{0,1:T(8,128)S(1)}, f32[1920,512]{0,1:T(8,128)}, u32[]{:S(2)}) %copy-start) | copy-done | bytes 3932184
  45.1 25.8 %shard_map.65 = bf16[32,1920]{1,0:T(8,128)(2,1)S(1)} custom-call(f32[4,2,2,32,1920]{4,3,2,1,0:T(8,128)S(1)} %bitcast.52, f32[32,1]{1,0:T(8,128)S(1)} %copy.37.bias_ref), custom_call_target="tpu_custom_call" | custom-call | tf_op jit(solution)/shard_map/pallas_call | solution.py:219
  70.9 0.5 reshape.224
  71.4 0.9 %copy.38 = bf16[4,48,10,32]{1,3,2,0:T(8,128)(2,1)} copy(bf16[4,48,10,32]{1,2,0,3:T(8,128)(2,1)S(1)} %bitcast.59) | data formatting | bytes 245760 | tf_op jit(solution)/shard_map/transpose | solution.py:315
  (30 shorter events, 0.8 us)
Async XLA Ops:
  0.0 31.8 %copy-start.1 = (bf16[4,48,10,32]{1,3,2,0:T(8,128)(2,1)S(1)}, bf16[4,48,10,32]{1,3,2,0:T(8,128)(2,1)}, u32[]{:S(2)}) copy-start(bf16[4,48,10,32]{1,3,2,0:T(8,128)(2,1)} %param.10) | copy-start | bytes 368644
  0.0 32.0 %copy-start.6 = (f32[32]{0:T(128)S(1)}, f32[32]{0:T(128)}, u32[]{:S(2)}) copy-start(f32[32]{0:T(128)} %param.12) | copy-start | bytes 388
  0.0 32.0 %copy-start.5 = (f32[32]{0:T(128)S(1)}, f32[32]{0:T(128)}, u32[]{:S(2)}) copy-start(f32[32]{0:T(128)} %param.13) | copy-start | bytes 388
  3.3 0.6 copy-start.4
  3.9 28.5 %copy-start.3 = (bf16[2,48,10,32]{1,3,2,0:T(8,128)(2,1)S(1)}, bf16[2,48,10,32]{1,3,2,0:T(8,128)(2,1)}, u32[]{:S(2)}) copy-start(bf16[2,48,10,32]{1,3,2,0:T(8,128)(2,1)} %param.11) | copy-start | bytes 184324
  35.8 1.2 %copy-start.2 = (bf16[3,3,3,32,512]{4,3,2,1,0:T(8,128)(2,1)S(1)}, bf16[3,3,3,32,512]{4,3,2,1,0:T(8,128)(2,1)}, u32[]{:S(2)}) copy-start(bf16[3,3,3,32,512]{4,3,2,1,0:T(8,128)(2,1)} %param.14) | copy-start | bytes 2654212
  39.7 3.2 %copy-start.7 = (f32[32]{0:T(128)S(1)}, f32[32]{0:T(128)}, u32[]{:S(2)}) copy-start(f32[32]{0:T(128)} %param.15) | copy-start | bytes 388
  42.9 2.1 %copy-start = (f32[1920,512]{0,1:T(8,128)S(1)}, f32[1920,512]{0,1:T(8,128)}, u32[]{:S(2)}) copy-start(f32[1920,512]{0,1:T(8,128)} %add_add_fusion) | copy-start | bytes 11796484

commit v24 on v21

--- a/solution.py
+++ b/solution.py
@@ -299,16 +299,15 @@
     tap_width = columns_in.shape[3]
     nchan = lax.axis_size("chan")
     nx = nchan // 4
-    flat_kernel = kernel.transpose(0, 2, 1, 3, 4).reshape(3, tap_width, kernel.shape[4])
-    running = jnp.zeros((bias.shape[0] * nchan, cell_count), jnp.float32)
-    plane = row_count * col_count
-    flat_in = columns_in.reshape(columns_in.shape[0] * plane, tap_width)
-    for depth in range(3):
-        tap_weight = flat_kernel[depth]
-        window = flat_in[depth * plane : depth * plane + cell_count]
-        running = running + lax.dot_general(
-            tap_weight, window, (((0,), (1,)), ((), ())), preferred_element_type=jnp.float32
-        )
+    full_kernel = kernel.transpose(0, 2, 1, 3, 4).reshape(3 * tap_width, kernel.shape[4])
+    depth_in = jnp.concatenate(
+        [columns_in[depth : depth + nframes] for depth in range(3)], axis=3
+    )
+    depth_in = with_layout_constraint(depth_in, Layout(major_to_minor=(0, 1, 2, 3)))
+    window = depth_in.reshape(cell_count, 3 * tap_width)
+    running = lax.dot_general(
+        full_kernel, window, (((0,), (1,)), ((), ())), preferred_element_type=jnp.float32
+    )
     summed = scatter_chan(running.reshape(nx, 2, 2, local_ch, cell_count))
     result = summed.T + bias
     result = result.astype(jnp.bfloat16).reshape(nframes, col_count, row_count, -1)

time: 68.6 us -> 68.9 us (level)
  other arithmetic: 7.62 us -> 10 us
  matrix products: 3.81 us -> 2.35 us
    concatenate x0 -> x1, other arithmetic: none -> 2.42 us  [local(): jnp.concatenate([columns_in[depth:depth + nframes] for depth in range(3)]...]
    dot_general x3 -> x1, matrix products: 3.81 us -> 2.35 us  [local(): lax.dot_general(full_kernel, window, (((0,), (1,)), ((), ())), preferred_...]
where the time goes in v24:
time: 68.9 us; the launch traced here: 68.5 us
  Pallas kernels  49.4 us (72%)
  other arithmetic  10 us (15%)
  local copies, waits for them, and re-layouts  6.46 us (9%)
  matrix products  2.35 us (3%)
    pallas_call x1, Pallas kernels, scatter_chan(): pl.pallas_call(functools.partial(scatter_kernel, widths), out_shape=jax.S...  25.9 us
    pallas_call x1, Pallas kernels, gather_space(): pl.pallas_call(functools.partial(gather_kernel, n), out_shape=(jax.ShapeD...  23.5 us
    concatenate x1, other arithmetic, local(): jnp.concatenate([columns_in[depth:depth + nframes] for depth in range(3)]...  2.42 us
    dot_general x1, matrix products, local(): lax.dot_general(full_kernel, window, (((0,), (1,)), ((), ())), preferred_...  2.35 us
    pallas_call x2, local copies, waits for them, and re-layouts, gather_space(): pl.pallas_call(functools.partial(gather_kernel, n), out_shape=(jax.ShapeD...  1.82 us
    reduce_sum x2, other arithmetic, local(): local_m2 = jnp.sum(local_dev * local_dev, axis=(0, 1, 2, 4))  1.42 us

profile of v24, /device:TPU:6, one launch (start us, length us, event | category | flops | bytes accessed | tf_op | source)
XLA Modules:
  0.0 68.5 jit_solution(16224983529417447192)
XLA Ops:
  0.0 1.2 %convert_reduce_fusion = f32[32]{0:T(128)S(1)} fusion(bf16[4,48,10,32]{1,3,2,0:T(8,128)(2,1)} %param.10), kind=kLoop, calls=%fused_computation.14 | loop fusion | flops 122848 | bytes 123008 | tf_op jit(solution)/shard_map/reduce_sum | solution.py:255
  1.2 0.1 reduce_sum.60
  1.3 0.1 reduce_sum.61
  1.5 0.1 sub.59
  1.6 1.3 %multiply_reduce_fusion = f32[32]{0:T(128)S(1)} fusion(f32[32]{0:T(128)S(1)} %sub.59, bf16[4,48,10,32]{1,3,2,0:T(8,128)(2,1)} %param.10), kind=kLoop, calls=%fused_computation.13 | loop fusion | flops 245728 | bytes 123136 | tf_op jit(solution)/shard_map/reduce_sum | solution.py:257
  2.9 0.1 reduce_sum.63
  3.0 0.1 reduce_sum.64
  3.1 0.2 scatter.9.x_ref
  3.3 0.6 copy-done.3
  3.9 23.5 %shard_map.64 = (f32[32,8,128]{2,1,0:T(8,128)}, bf16[6,32,48]{2,1,0:T(8,128)(2,1)}, bf16[6,32,48]{2,1,0:T(8,128)(2,1)}) custom-call(f32[8,128]{1,0:T(8,128)} %copy-done.3, bf16[2,10,32,48]{3,2,1,0:T(8,128)(2,1)} %bitcast.48, bf16[4,10,32,48]{3,2,1,0:T(8,128)(2,1)} %bitcast.44), custom_call_target="tpu_custom_call" | custom-call | tf_op jit(solution)/shard_map/pallas_call | solution.py:94
  27.4 1.0 %slice_reduce_fusion.1 = (f32[2]{0:T(128)S(1)}, f32[2]{0:T(128)S(1)}, f32[32,1,2]{2,1,0:T(1,128)S(1)}) fusion(f32[32,8,128]{2,1,0:T(8,128)} %get-tuple-element.33), kind=kLoop, calls=%fused_computation.34 | loop fusion | flops 124 | bytes 784 | tf_op jit(solution)/shard_map/reduce_sum | solution.py:267
  28.5 0.2 fusion.10
  28.8 0.1 mul.94
  28.9 0.1 sub.63
  29.0 0.9 %copy.30 = bf16[6,32,48]{1,2,0:T(8,128)(2,1)S(1)} copy(bf16[6,32,48]{2,1,0:T(8,128)(2,1)} %get-tuple-element.34) | data formatting | bytes 36864 | tf_op jit(solution)/shard_map/pallas_call | solution.py:94
  29.9 0.9 %copy.26 = bf16[6,32,48]{1,2,0:T(8,128)(2,1)S(1)} copy(bf16[6,32,48]{2,1,0:T(8,128)(2,1)} %get-tuple-element.32) | data formatting | bytes 36864 | tf_op jit(solution)/shard_map/pallas_call | solution.py:94
  30.8 0.8 %fusion.7 = (bf16[4,48,1,32]{3,1,0,2:T(8,128)(2,1)S(1)}, bf16[4,48,1,32]{3,1,2,0:T(8,128)(2,1)S(1)}) fusion(bf16[6,48,32]{2,1,0:T(8,128)(2,1)S(1)} %bitcast.51, f32[32]{0:T(128)} %param.13, f32[32]{0:T(128)} %param.12, f32[32]{0:T(128)S(1)} %mul.94, f32[32]{0:T(128)S(1)} %sub.63, bf16[6,48,32]{2,1,0:T(8,128)(2,1)S(1)} %bitcast.49), kind=kLoop, calls=%fused_computation.22 | loop fusion | flops 122880 | bytes 49664 | tf_op jit(solution)/shard_map/concatenate | solution.py:283
  31.7 0.2 copy.28
  32.0 0.3 multiply_convert_fusion
  32.3 0.2 copy.29
  32.5 0.4 fusion.1
  32.9 0.6 fusion.13
  33.5 0.8 %pad_maximum_fusion.2 = bf16[6,12,48,96]{3,2,1,0:T(8,128)(2,1)S(1)} fusion(bf16[6,12,48,32]{3,2,1,0:T(8,128)(2,1)S(1)} %get-tuple-element.41, bf16[6,12,48,32]{3,2,1,0:T(8,128)(2,1)S(1)} %get-tuple-element.42, bf16[6,12,48,32]{3,2,1,0:T(8,128)(2,1)S(1)} %get-tuple-element.40), kind=kLoop, calls=%fused_computation.12 | loop fusion | flops 1990656 | bytes 1327104 | tf_op jit(solution)/shard_map/concatenate | solution.py:291
  34.3 0.3 fusion.14
  34.6 1.1 %pad_maximum_fusion.1 = bf16[6,10,48,288]{3,2,1,0:T(8,128)(2,1)S(1)} fusion(bf16[6,10,48,96]{3,2,1,0:T(8,128)(2,1)S(1)} %get-tuple-element.45, bf16[6,10,48,96]{3,2,1,0:T(8,128)(2,1)S(1)} %get-tuple-element.44, bf16[6,10,48,96]{3,2,1,0:T(8,128)(2,1)S(1)} %get-tuple-element.43), kind=kLoop, calls=%fused_computation.3 | loop fusion | flops 4976640 | bytes 3317760 | tf_op jit(solution)/shard_map/concatenate | solution.py:295
  35.7 0.4 fusion.12
  36.1 2.4 %pad_maximum_fusion = bf16[4,10,48,864]{3,2,1,0:T(8,128)(2,1)S(1)} fusion(bf16[4,10,48,288]{3,2,1,0:T(8,128)(2,1)S(1)} %get-tuple-element.39, bf16[4,10,48,288]{3,2,1,0:T(8,128)(2,1)S(1)} %get-tuple-element.38, bf16[4,10,48,288]{3,2,1,0:T(8,128)(2,1)S(1)} %get-tuple-element.37), kind=kLoop, calls=%fused_computation | loop fusion | flops 9953280 | bytes 6635520 | tf_op jit(solution)/shard_map/concatenate | solution.py:303
  38.6 2.3 %fusion.15 = f32[1920,512]{0,1:T(8,128)S(1)} fusion(bf16[1920,864]{1,0:T(8,128)(2,1)S(1)} %bitcast.45, bf16[864,512]{1,0:T(8,128)(2,1)S(1)} %bitcast.47), kind=kOutput, calls=%fused_computation.38 | convolution fusion | flops 1698693120 | bytes 8134656 | tf_op jit(solution)/shard_map/dot_general | solution.py:308
  41.0 25.9 %shard_map.65 = f32[32,1920]{1,0:T(8,128)S(1)} custom-call(f32[4,2,2,32,1920]{4,3,2,1,0:T(8,128)S(1)} %bitcast.43), custom_call_target="tpu_custom_call" | custom-call | tf_op jit(solution)/shard_map/pallas_call | solution.py:218
  67.0 0.1 fusion.5
  67.0 0.5 reshape.222
  67.6 0.9 %copy.35 = bf16[4,48,10,32]{1,3,2,0:T(8,128)(2,1)} copy(bf16[4,48,10,32]{1,2,0,3:T(8,128)(2,1)S(1)} %bitcast.46) | data formatting | bytes 245760 | tf_op jit(solution)/shard_map/transpose | solution.py:314
  (26 shorter events, 0.5 us)
Async XLA Ops:
  0.0 31.7 %copy-start = (bf16[4,48,10,32]{1,3,2,0:T(8,128)(2,1)S(1)}, bf16[4,48,10,32]{1,3,2,0:T(8,128)(2,1)}, u32[]{:S(2)}) copy-start(bf16[4,48,10,32]{1,3,2,0:T(8,128)(2,1)} %param.10) | copy-start | bytes 368644
  0.0 31.9 %copy-start.5 = (f32[32]{0:T(128)S(1)}, f32[32]{0:T(128)}, u32[]{:S(2)}) copy-start(f32[32]{0:T(128)} %param.12) | copy-start | bytes 388
  0.0 31.9 %copy-start.4 = (f32[32]{0:T(128)S(1)}, f32[32]{0:T(128)}, u32[]{:S(2)}) copy-start(f32[32]{0:T(128)} %param.13) | copy-start | bytes 388
  1.6 30.7 %copy-start.2 = (bf16[2,48,10,32]{1,3,2,0:T(8,128)(2,1)S(1)}, bf16[2,48,10,32]{1,3,2,0:T(8,128)(2,1)}, u32[]{:S(2)}) copy-start(bf16[2,48,10,32]{1,3,2,0:T(8,128)(2,1)} %param.11) | copy-start | bytes 184324
  3.3 0.6 copy-start.3
  36.1 2.4 %copy-start.1 = (bf16[3,3,3,32,512]{4,3,2,1,0:T(8,128)(2,1)S(1)}, bf16[3,3,3,32,512]{4,3,2,1,0:T(8,128)(2,1)}, u32[]{:S(2)}) copy-start(bf16[3,3,3,32,512]{4,3,2,1,0:T(8,128)(2,1)} %param.14) | copy-start | bytes 2654212
  41.0 26.0 %copy-start.6 = (f32[32]{0:T(128)S(1)}, f32[32]{0:T(128)}, u32[]{:S(2)}) copy-start(f32[32]{0:T(128)} %param.15) | copy-start | bytes 388

commit v25 on v21

--- a/solution.py
+++ b/solution.py
@@ -210,7 +210,7 @@
         o_ref[:, cols(q)] = own[q, yh, :, fit(q)] + recv3[q, :, fit(q)].astype(f32)
 
 
-def scatter_chan(parts, widths=(384, 1152, 384)):
+def scatter_chan(parts, widths=(256, 1408, 256)):
     nx, nyh, ncore, rows, cells = parts.shape
     nchunk, width = len(widths), max(widths)
     assert sum(widths) == cells

time: 68.6 us -> 70.3 us (1.025)
  Pallas kernels: 49.4 us -> 51.1 us
    pallas_call x1, Pallas kernels: 25.9 us -> 27.7 us  [scatter_chan(): pl.pallas_call(functools.partial(scatter_kernel, widths), out_shape=jax.S...]
where the time goes in v25:
time: 70.3 us; the launch traced here: 69.9 us
  Pallas kernels  51.1 us (73%)
  other arithmetic  7.62 us (11%)
  local copies, waits for them, and re-layouts  7.1 us (10%)
  matrix products  3.81 us (5%)
    pallas_call x1, Pallas kernels, scatter_chan(): pl.pallas_call(functools.partial(scatter_kernel, widths), out_shape=jax.S...  27.7 us
    pallas_call x1, Pallas kernels, gather_space(): pl.pallas_call(functools.partial(gather_kernel, n), out_shape=(jax.ShapeD...  23.5 us
    dot_general x3, matrix products, local(): lax.dot_general(tap_weight, window, (((0,), (1,)), ((), ())), preferred_e...  3.81 us
    pallas_call x2, local copies, waits for them, and re-layouts, gather_space(): pl.pallas_call(functools.partial(gather_kernel, n), out_shape=(jax.ShapeD...  1.81 us

profile of v25, /device:TPU:6, one launch (start us, length us, event | category | flops | bytes accessed | tf_op | source)
XLA Modules:
  0.0 69.9 jit_solution(3060684082114340024)
XLA Ops:
  0.0 1.2 %convert_reduce_fusion = f32[32]{0:T(128)S(1)} fusion(bf16[4,48,10,32]{1,3,2,0:T(8,128)(2,1)} %param.10), kind=kLoop, calls=%fused_computation.15 | loop fusion | flops 122848 | bytes 123008 | tf_op jit(solution)/shard_map/reduce_sum | solution.py:255
  1.3 0.1 reduce_sum.60
  1.3 0.1 reduce_sum.61
  1.6 1.3 %multiply_reduce_fusion = f32[32]{0:T(128)S(1)} fusion(f32[32]{0:T(128)S(1)} %sub.59, bf16[4,48,10,32]{1,3,2,0:T(8,128)(2,1)} %param.10), kind=kLoop, calls=%fused_computation.14 | loop fusion | flops 245728 | bytes 123136 | tf_op jit(solution)/shard_map/reduce_sum | solution.py:257
  3.0 0.1 reduce_sum.64
  3.1 0.2 scatter.9.x_ref
  3.3 0.6 copy-done.3
  3.9 23.5 %shard_map.64 = (f32[32,8,128]{2,1,0:T(8,128)}, bf16[6,32,48]{2,1,0:T(8,128)(2,1)}, bf16[6,32,48]{2,1,0:T(8,128)(2,1)}) custom-call(f32[8,128]{1,0:T(8,128)} %copy-done.3, bf16[2,10,32,48]{3,2,1,0:T(8,128)(2,1)} %bitcast.62, bf16[4,10,32,48]{3,2,1,0:T(8,128)(2,1)} %bitcast.56), custom_call_target="tpu_custom_call" | custom-call | tf_op jit(solution)/shard_map/pallas_call | solution.py:94
  27.4 1.0 %slice_reduce_fusion.1 = (f32[2]{0:T(128)S(1)}, f32[2]{0:T(128)S(1)}, f32[32,1,2]{2,1,0:T(1,128)S(1)}) fusion(f32[32,8,128]{2,1,0:T(8,128)} %get-tuple-element.33), kind=kLoop, calls=%fused_computation.35 | loop fusion | flops 124 | bytes 784 | tf_op jit(solution)/shard_map/reduce_sum | solution.py:267
  28.5 0.1 sub.63
  28.7 0.2 fusion.10
  29.0 0.9 %copy.26 = bf16[6,32,48]{1,2,0:T(8,128)(2,1)S(1)} copy(bf16[6,32,48]{2,1,0:T(8,128)(2,1)} %get-tuple-element.32) | data formatting | bytes 36864 | tf_op jit(solution)/shard_map/pallas_call | solution.py:94
  29.9 0.9 %copy.30 = bf16[6,32,48]{1,2,0:T(8,128)(2,1)S(1)} copy(bf16[6,32,48]{2,1,0:T(8,128)(2,1)} %get-tuple-element.34) | data formatting | bytes 36864 | tf_op jit(solution)/shard_map/pallas_call | solution.py:94
  30.8 0.8 %fusion.7 = (bf16[4,48,1,32]{3,1,0,2:T(8,128)(2,1)S(1)}, bf16[4,48,1,32]{3,1,2,0:T(8,128)(2,1)S(1)}) fusion(bf16[6,48,32]{2,1,0:T(8,128)(2,1)S(1)} %bitcast.64, f32[32]{0:T(128)} %param.13, f32[32]{0:T(128)} %param.12, f32[32]{0:T(128)S(1)} %mul.94, f32[32]{0:T(128)S(1)} %sub.63, bf16[6,48,32]{2,1,0:T(8,128)(2,1)S(1)} %bitcast.66), kind=kLoop, calls=%fused_computation.23 | loop fusion | flops 122880 | bytes 49664 | tf_op jit(solution)/shard_map/concatenate | solution.py:283
  31.7 0.2 copy.29
  32.0 0.1 fusion.14
  32.1 0.5 copy-done
  32.6 0.2 copy.28
  32.9 0.3 multiply_convert_fusion
  33.2 0.4 fusion.1
  33.6 0.6 fusion.13
  34.2 0.8 %pad_maximum_fusion.1 = bf16[6,12,48,96]{3,2,1,0:T(8,128)(2,1)S(1)} fusion(bf16[6,12,48,32]{3,2,1,0:T(8,128)(2,1)S(1)} %get-tuple-element.41, bf16[6,12,48,32]{3,2,1,0:T(8,128)(2,1)S(1)} %get-tuple-element.42, bf16[6,12,48,32]{3,2,1,0:T(8,128)(2,1)S(1)} %get-tuple-element.40), kind=kLoop, calls=%fused_computation.12 | loop fusion | flops 1990656 | bytes 1327104 | tf_op jit(solution)/shard_map/concatenate | solution.py:291
  35.0 0.3 fusion.15
  35.3 1.1 %pad_maximum_fusion = bf16[6,10,48,288]{3,2,1,0:T(8,128)(2,1)S(1)} fusion(bf16[6,10,48,96]{3,2,1,0:T(8,128)(2,1)S(1)} %get-tuple-element.48, bf16[6,10,48,96]{3,2,1,0:T(8,128)(2,1)S(1)} %get-tuple-element.47, bf16[6,10,48,96]{3,2,1,0:T(8,128)(2,1)S(1)} %get-tuple-element.46), kind=kLoop, calls=%fused_computation.3 | loop fusion | flops 4976640 | bytes 3317760 | tf_op jit(solution)/shard_map/concatenate | solution.py:295
  36.5 0.4 fusion.12
  36.8 1.3 %fusion.17 = f32[1920,512]{0,1:T(8,128)S(1)} fusion(bf16[1920,288]{1,0:T(8,128)(2,1)S(1)} %bitcast.54, bf16[288,512]{1,0:T(8,128)(2,1)S(1)} %bitcast.61), kind=kOutput, calls=%fused_computation.41 | convolution fusion | flops 566231040 | bytes 5332992 | tf_op jit(solution)/shard_map/dot_general | solution.py:309
  38.1 1.3 %fusion.16 = f32[1920,512]{0,1:T(8,128)S(1)} fusion(bf16[1920,288]{1,0:T(8,128)(2,1)S(1)} %bitcast.53, bf16[288,512]{1,0:T(8,128)(2,1)S(1)} %bitcast.60), kind=kOutput, calls=%fused_computation.40 | convolution fusion | flops 566231040 | bytes 5332992 | tf_op jit(solution)/shard_map/dot_general | solution.py:309
  39.4 1.3 %add_add_fusion = f32[1920,512]{0,1:T(8,128)S(1)} fusion(f32[1920,512]{0,1:T(8,128)S(1)} %fusion.16, f32[1920,512]{0,1:T(8,128)S(1)} %fusion.17, bf16[1920,288]{1,0:T(8,128)(2,1)S(1)} %bitcast.55, bf16[288,512]{1,0:T(8,128)(2,1)S(1)} %bitcast.59), kind=kOutput, calls=%fused_computation | convolution fusion | flops 568197120 | bytes 13197312 | tf_op jit(solution)/shard_map/dot_general | solution.py:309
  40.7 27.7 %shard_map.65 = f32[32,1920]{1,0:T(8,128)S(1)} custom-call(f32[4,2,2,32,1920]{4,3,2,1,0:T(8,128)S(1)} %bitcast.52), custom_call_target="tpu_custom_call" | custom-call | tf_op jit(solution)/shard_map/pallas_call | solution.py:218
  68.4 0.1 fusion.5
  68.5 0.5 reshape.225
  69.0 0.9 %copy.35 = bf16[4,48,10,32]{1,3,2,0:T(8,128)(2,1)} copy(bf16[4,48,10,32]{1,2,0,3:T(8,128)(2,1)S(1)} %bitcast.58) | data formatting | bytes 245760 | tf_op jit(solution)/shard_map/transpose | solution.py:315
  (28 shorter events, 0.7 us)
Async XLA Ops:
  0.0 31.7 %copy-start.2 = (bf16[2,48,10,32]{1,3,2,0:T(8,128)(2,1)S(1)}, bf16[2,48,10,32]{1,3,2,0:T(8,128)(2,1)}, u32[]{:S(2)}) copy-start(bf16[2,48,10,32]{1,3,2,0:T(8,128)(2,1)} %param.11) | copy-start | bytes 184324
  0.0 31.9 %copy-start.1 = (bf16[3,3,3,32,512]{4,3,2,1,0:T(8,128)(2,1)S(1)}, bf16[3,3,3,32,512]{4,3,2,1,0:T(8,128)(2,1)}, u32[]{:S(2)}) copy-start(bf16[3,3,3,32,512]{4,3,2,1,0:T(8,128)(2,1)} %param.14) | copy-start | bytes 2654212
  3.3 0.6 copy-start.3
  31.6 1.0 %copy-start = (bf16[4,48,10,32]{1,3,2,0:T(8,128)(2,1)S(1)}, bf16[4,48,10,32]{1,3,2,0:T(8,128)(2,1)}, u32[]{:S(2)}) copy-start(bf16[4,48,10,32]{1,3,2,0:T(8,128)(2,1)} %param.10) | copy-start | bytes 368644
  31.9 1.0 %copy-start.4 = (f32[32]{0:T(128)S(1)}, f32[32]{0:T(128)}, u32[]{:S(2)}) copy-start(f32[32]{0:T(128)} %param.13) | copy-start | bytes 388
  31.9 1.0 %copy-start.5 = (f32[32]{0:T(128)S(1)}, f32[32]{0:T(128)}, u32[]{:S(2)}) copy-start(f32[32]{0:T(128)} %param.12) | copy-start | bytes 388
  40.7 27.7 %copy-start.6 = (f32[32]{0:T(128)S(1)}, f32[32]{0:T(128)}, u32[]{:S(2)}) copy-start(f32[32]{0:T(128)} %param.15) | copy-start | bytes 388

commit v26 on v25

--- a/solution.py
+++ b/solution.py
@@ -210,7 +210,7 @@
         o_ref[:, cols(q)] = own[q, yh, :, fit(q)] + recv3[q, :, fit(q)].astype(f32)
 
 
-def scatter_chan(parts, widths=(256, 1408, 256)):
+def scatter_chan(parts, widths=(512, 896, 512)):
     nx, nyh, ncore, rows, cells = parts.shape
     nchunk, width = len(widths), max(widths)
     assert sum(widths) == cells

time: 70.3 us -> 68.6 us (0.976)
  the two profiles are of different devices: /device:TPU:6 before, /device:TPU:1 now
where the time goes in v26:
time: 68.6 us; the launch traced here: 68.2 us
  Pallas kernels  49.4 us (72%)
  other arithmetic  7.62 us (11%)
  local copies, waits for them, and re-layouts  7.1 us (10%)
  matrix products  3.81 us (6%)
    pallas_call x1, Pallas kernels, scatter_chan(): pl.pallas_call(functools.partial(scatter_kernel, widths), out_shape=jax.S...  26.5 us
    pallas_call x1, Pallas kernels, gather_space(): pl.pallas_call(functools.partial(gather_kernel, n), out_shape=(jax.ShapeD...  23 us
    dot_general x3, matrix products, local(): lax.dot_general(tap_weight, window, (((0,), (1,)), ((), ())), preferred_e...  3.81 us
    pallas_call x2, local copies, waits for them, and re-layouts, gather_space(): pl.pallas_call(functools.partial(gather_kernel, n), out_shape=(jax.ShapeD...  1.81 us
    unnamed x16, local copies, waits for them, and re-layouts  1.39 us
    reduce_sum x2, other arithmetic, local(): local_m2 = jnp.sum(local_dev * local_dev, axis=(0, 1, 2, 4))  1.39 us

profile of v26, /device:TPU:1, one launch (start us, length us, event | category | flops | bytes accessed | tf_op | source)
XLA Modules:
  0.0 68.2 jit_solution(1025812633837608294)
XLA Ops:
  0.0 1.2 %convert_reduce_fusion = f32[32]{0:T(128)S(1)} fusion(bf16[4,48,10,32]{1,3,2,0:T(8,128)(2,1)} %param.10), kind=kLoop, calls=%fused_computation.15 | loop fusion | flops 122848 | bytes 123008 | tf_op jit(solution)/shard_map/reduce_sum | solution.py:255
  1.3 0.1 reduce_sum.60
  1.3 0.1 reduce_sum.61
  1.5 0.1 sub.59
  1.6 1.3 %multiply_reduce_fusion = f32[32]{0:T(128)S(1)} fusion(f32[32]{0:T(128)S(1)} %sub.59, bf16[4,48,10,32]{1,3,2,0:T(8,128)(2,1)} %param.10), kind=kLoop, calls=%fused_computation.14 | loop fusion | flops 245728 | bytes 123136 | tf_op jit(solution)/shard_map/reduce_sum | solution.py:257
  3.0 0.1 reduce_sum.64
  3.1 0.2 scatter.9.x_ref
  3.3 0.6 copy-done.3
  3.9 23.0 %shard_map.64 = (f32[32,8,128]{2,1,0:T(8,128)}, bf16[6,32,48]{2,1,0:T(8,128)(2,1)}, bf16[6,32,48]{2,1,0:T(8,128)(2,1)}) custom-call(f32[8,128]{1,0:T(8,128)} %copy-done.3, bf16[2,10,32,48]{3,2,1,0:T(8,128)(2,1)} %bitcast.62, bf16[4,10,32,48]{3,2,1,0:T(8,128)(2,1)} %bitcast.56), custom_call_target="tpu_custom_call" | custom-call | tf_op jit(solution)/shard_map/pallas_call | solution.py:94
  26.9 1.0 %slice_reduce_fusion.1 = (f32[2]{0:T(128)S(1)}, f32[2]{0:T(128)S(1)}, f32[32,1,2]{2,1,0:T(1,128)S(1)}) fusion(f32[32,8,128]{2,1,0:T(8,128)} %get-tuple-element.33), kind=kLoop, calls=%fused_computation.35 | loop fusion | flops 124 | bytes 784 | tf_op jit(solution)/shard_map/reduce_sum | solution.py:267
  28.2 0.2 fusion.10
  28.5 0.9 %copy.26 = bf16[6,32,48]{1,2,0:T(8,128)(2,1)S(1)} copy(bf16[6,32,48]{2,1,0:T(8,128)(2,1)} %get-tuple-element.32) | data formatting | bytes 36864 | tf_op jit(solution)/shard_map/pallas_call | solution.py:94
  29.4 0.9 %copy.30 = bf16[6,32,48]{1,2,0:T(8,128)(2,1)S(1)} copy(bf16[6,32,48]{2,1,0:T(8,128)(2,1)} %get-tuple-element.34) | data formatting | bytes 36864 | tf_op jit(solution)/shard_map/pallas_call | solution.py:94
  30.4 0.8 %fusion.7 = (bf16[4,48,1,32]{3,1,0,2:T(8,128)(2,1)S(1)}, bf16[4,48,1,32]{3,1,2,0:T(8,128)(2,1)S(1)}) fusion(bf16[6,48,32]{2,1,0:T(8,128)(2,1)S(1)} %bitcast.64, f32[32]{0:T(128)} %param.13, f32[32]{0:T(128)} %param.12, f32[32]{0:T(128)S(1)} %mul.94, f32[32]{0:T(128)S(1)} %sub.63, bf16[6,48,32]{2,1,0:T(8,128)(2,1)S(1)} %bitcast.66), kind=kLoop, calls=%fused_computation.23 | loop fusion | flops 122880 | bytes 49664 | tf_op jit(solution)/shard_map/concatenate | solution.py:283
  31.2 0.2 copy.29
  31.5 0.1 fusion.14
  31.6 0.5 copy-done
  32.1 0.2 copy.28
  32.4 0.3 multiply_convert_fusion
  32.7 0.4 fusion.1
  33.1 0.6 fusion.13
  33.7 0.8 %pad_maximum_fusion.1 = bf16[6,12,48,96]{3,2,1,0:T(8,128)(2,1)S(1)} fusion(bf16[6,12,48,32]{3,2,1,0:T(8,128)(2,1)S(1)} %get-tuple-element.41, bf16[6,12,48,32]{3,2,1,0:T(8,128)(2,1)S(1)} %get-tuple-element.42, bf16[6,12,48,32]{3,2,1,0:T(8,128)(2,1)S(1)} %get-tuple-element.40), kind=kLoop, calls=%fused_computation.12 | loop fusion | flops 1990656 | bytes 1327104 | tf_op jit(solution)/shard_map/concatenate | solution.py:291
  34.5 0.3 fusion.15
  34.8 1.1 %pad_maximum_fusion = bf16[6,10,48,288]{3,2,1,0:T(8,128)(2,1)S(1)} fusion(bf16[6,10,48,96]{3,2,1,0:T(8,128)(2,1)S(1)} %get-tuple-element.48, bf16[6,10,48,96]{3,2,1,0:T(8,128)(2,1)S(1)} %get-tuple-element.47, bf16[6,10,48,96]{3,2,1,0:T(8,128)(2,1)S(1)} %get-tuple-element.46), kind=kLoop, calls=%fused_computation.3 | loop fusion | flops 4976640 | bytes 3317760 | tf_op jit(solution)/shard_map/concatenate | solution.py:295
  36.0 0.4 fusion.12
  36.4 1.3 %fusion.17 = f32[1920,512]{0,1:T(8,128)S(1)} fusion(bf16[1920,288]{1,0:T(8,128)(2,1)S(1)} %bitcast.54, bf16[288,512]{1,0:T(8,128)(2,1)S(1)} %bitcast.61), kind=kOutput, calls=%fused_computation.41 | convolution fusion | flops 566231040 | bytes 5332992 | tf_op jit(solution)/shard_map/dot_general | solution.py:309
  37.6 1.3 %fusion.16 = f32[1920,512]{0,1:T(8,128)S(1)} fusion(bf16[1920,288]{1,0:T(8,128)(2,1)S(1)} %bitcast.53, bf16[288,512]{1,0:T(8,128)(2,1)S(1)} %bitcast.60), kind=kOutput, calls=%fused_computation.40 | convolution fusion | flops 566231040 | bytes 5332992 | tf_op jit(solution)/shard_map/dot_general | solution.py:309
  38.9 1.3 %add_add_fusion = f32[1920,512]{0,1:T(8,128)S(1)} fusion(f32[1920,512]{0,1:T(8,128)S(1)} %fusion.16, f32[1920,512]{0,1:T(8,128)S(1)} %fusion.17, bf16[1920,288]{1,0:T(8,128)(2,1)S(1)} %bitcast.55, bf16[288,512]{1,0:T(8,128)(2,1)S(1)} %bitcast.59), kind=kOutput, calls=%fused_computation | convolution fusion | flops 568197120 | bytes 13197312 | tf_op jit(solution)/shard_map/dot_general | solution.py:309
  40.2 26.5 %shard_map.65 = f32[32,1920]{1,0:T(8,128)S(1)} custom-call(f32[4,2,2,32,1920]{4,3,2,1,0:T(8,128)S(1)} %bitcast.52), custom_call_target="tpu_custom_call" | custom-call | tf_op jit(solution)/shard_map/pallas_call | solution.py:218
  66.7 0.1 fusion.5
  66.8 0.5 reshape.225
  67.3 0.9 %copy.35 = bf16[4,48,10,32]{1,3,2,0:T(8,128)(2,1)} copy(bf16[4,48,10,32]{1,2,0,3:T(8,128)(2,1)S(1)} %bitcast.58) | data formatting | bytes 245760 | tf_op jit(solution)/shard_map/transpose | solution.py:315
  (28 shorter events, 0.7 us)
Async XLA Ops:
  0.0 31.2 %copy-start.2 = (bf16[2,48,10,32]{1,3,2,0:T(8,128)(2,1)S(1)}, bf16[2,48,10,32]{1,3,2,0:T(8,128)(2,1)}, u32[]{:S(2)}) copy-start(bf16[2,48,10,32]{1,3,2,0:T(8,128)(2,1)} %param.11) | copy-start | bytes 184324
  0.0 31.4 %copy-start.1 = (bf16[3,3,3,32,512]{4,3,2,1,0:T(8,128)(2,1)S(1)}, bf16[3,3,3,32,512]{4,3,2,1,0:T(8,128)(2,1)}, u32[]{:S(2)}) copy-start(bf16[3,3,3,32,512]{4,3,2,1,0:T(8,128)(2,1)} %param.14) | copy-start | bytes 2654212
  3.3 0.6 copy-start.3
  31.2 1.0 %copy-start = (bf16[4,48,10,32]{1,3,2,0:T(8,128)(2,1)S(1)}, bf16[4,48,10,32]{1,3,2,0:T(8,128)(2,1)}, u32[]{:S(2)}) copy-start(bf16[4,48,10,32]{1,3,2,0:T(8,128)(2,1)} %param.10) | copy-start | bytes 368644
  31.4 1.0 %copy-start.4 = (f32[32]{0:T(128)S(1)}, f32[32]{0:T(128)}, u32[]{:S(2)}) copy-start(f32[32]{0:T(128)} %param.13) | copy-start | bytes 388
  31.4 1.0 %copy-start.5 = (f32[32]{0:T(128)S(1)}, f32[32]{0:T(128)}, u32[]{:S(2)}) copy-start(f32[32]{0:T(128)} %param.12) | copy-start | bytes 388
  40.2 26.5 %copy-start.6 = (f32[32]{0:T(128)S(1)}, f32[32]{0:T(128)}, u32[]{:S(2)}) copy-start(f32[32]{0:T(128)} %param.15) | copy-start | bytes 388
